TPU v7x, 128 devices: a whole 4x4x4 slice. The times are simulated.
128 devices in a mesh: doc: 2 (over core), coarse: 4 (over z), fine: 16 (over y, x).
Axes of the slice: x: 4, y: 4, z: 4, core: 2. Of those that a mesh axis runs over, the one named last changes fastest.
Arguments:
- q_light: bfloat16 [2, 8192, 1024], P('doc', ('coarse', 'fine')), may hold values from -8 to 8
- k_light: bfloat16 [2, 8192, 1024], P('doc', ('coarse', 'fine')), may hold values from -8 to 8
- v_light: bfloat16 [2, 8192, 1024], P('doc', ('coarse', 'fine')), may hold values from -6 to 6
- q_heavy: bfloat16 [2, 8192, 1024], P('doc', ('coarse', 'fine')), may hold values from -8 to 8
- k_heavy: bfloat16 [2, 8192, 1024], P('doc', ('coarse', 'fine')), may hold values from -8 to 8
- v_heavy: bfloat16 [2, 8192, 1024], P('doc', ('coarse', 'fine')), may hold values from -6 to 6
- enc_kv: bfloat16 [2, 8192, 128], P('doc', ('coarse', 'fine')), may hold values from -8 to 8
- dec_queries: bfloat16 [2, 512, 1024], P('doc'), may hold values from -8 to 8
- query_ids: int32 [2, 64], P('doc'), may hold values from 0 to 63, as said below
- key_ids: int32 [2, 32], P('doc'), may hold values from 0 to 63, as said below
Outputs:
- encoded: bfloat16 [2, 8192, 1024], P('doc', ('coarse', 'fine'))
- decoded: bfloat16 [2, 512, 1024], P('doc')
Inputs may be any that keep to these rules, and one draw needn't show every extreme that they name: `query_ids`: for each document and each c below the number of coarse groups, entries c * 16 to (c + 1) * 16 - 1 are distinct block numbers among blocks c * 16 to (c + 1) * 16 - 1 (so every block of the group is listed), and entry c * 16 + f is the block assigned to the f-th device of that group. `key_ids`: for each document and each c below the number of coarse groups, entries c * 8 to (c + 1) * 8 - 1 are distinct block numbers among blocks c * 16 * 1 to (c + 1) * 16 - 1.
All inputs are finite; a program needn't handle non-finite values.
Results may differ from a plain program's by a relative error of at most 0.009.
Values may be sent and summed in bfloat16 or wider, within the bound.
No kernel may reach another device: no remote copies, remote signals or barrier semaphores. Data moves between devices by JAX's collectives and lax.ppermute only.
A program may use at most 384 MiB of HBM per device.

v0:
```python
import jax
import jax.numpy as jnp
from jax import lax
from jax.sharding import Mesh
from jax.sharding import PartitionSpec as P

HEAD = 64
ROUTED_BLOCK = 128
KGRP = 8
COARSE_FINE = ("coarse", "fine_0", "fine_1")
FINE = ("fine_0", "fine_1")


def extended(value, sides, width):
    edges = {}
    for axis, dim in sides:
        size, length = (lax.axis_size(axis), value.shape[dim])
        up = [(i, (i + 1) % size) for i in range(size - 1)]
        last = lax.slice_in_dim(value, length - width, length, axis=dim)
        first = lax.slice_in_dim(value, 0, width, axis=dim)
        edges[dim] = (
            lax.ppermute(last, axis, up),
            lax.ppermute(first, axis, [(b, a) for a, b in up]),
        )
    done = []
    for _, dim in sides:
        low, high = edges[dim]
        around = [(width, width) if d in done else (0, 0) for d in range(value.ndim)]
        value = jnp.concatenate([jnp.pad(low, around), value, jnp.pad(high, around)], axis=dim)
        done.append(dim)
    return value


def split_up(value, dim, length):
    lengths = value.shape
    pieces = value.reshape(*lengths[:dim], length, lengths[dim] // length, *lengths[dim + 1 :])
    return jnp.moveaxis(pieces, dim, 0)


def sum_at_owner(value, axis, dim):
    pieces = split_up(value, dim, lax.axis_size(axis))
    arrived = lax.all_to_all(pieces, axis, split_axis=0, concat_axis=0, tiled=True)
    return arrived.astype(jnp.float32).sum(axis=0)


def joined_all(value, axes, combine):
    for axis in axes:
        pieces = jax.tree.map(lambda part: lax.all_gather(part, axis), value)
        value = jax.tree.map(lambda part: part[0], pieces)
        for k in range(1, lax.axis_size(axis)):
            value = combine(value, jax.tree.map(lambda part: part[k], pieces))
    return value


def attend(query, keys, value_rows, mask):
    rows = query.shape[0]
    count = keys.shape[0]
    heads = query.shape[1] // HEAD
    qh = query.reshape(rows, heads, HEAD).transpose(1, 0, 2)
    kh = keys.reshape(count, heads, HEAD).transpose(1, 0, 2)
    vh = value_rows.reshape(count, heads, HEAD).transpose(1, 0, 2)

    def one_head(triple):
        qa, ka, va = triple
        scores = jnp.dot(qa, ka.T, preferred_element_type=jnp.float32) * HEAD ** (-0.5)
        if mask is not None:
            scores = jnp.where(mask, scores, jnp.float32(-1e30))
        peak = jnp.max(scores, axis=1, keepdims=True)
        weights = jnp.exp(scores - peak)
        weights = (weights / jnp.sum(weights, axis=1, keepdims=True)).astype(jnp.bfloat16)
        return jnp.dot(weights, va, preferred_element_type=jnp.float32)

    out = lax.map(one_head, (qh, kh, vh))
    return out.transpose(1, 0, 2).reshape(rows, heads * HEAD)


def combine(leading_entry, second):
    peak = jnp.maximum(leading_entry[0], second[0])
    scale_a = jnp.exp(leading_entry[0] - peak)
    scale_b = jnp.exp(second[0] - peak)
    total = leading_entry[1] * scale_a + second[1] * scale_b
    value_rows = leading_entry[2] * scale_a[..., None] + second[2] * scale_b[..., None]
    return (peak, total, value_rows)


def local(
    q_light, k_light, v_light, q_heavy, k_heavy, v_heavy, enc_kv, dec_queries, query_ids, key_ids
):
    query = q_light[0]
    tokens, width = query.shape
    n_seq = lax.axis_size(COARSE_FINE)
    n_fine = lax.axis_size(FINE)
    here = lax.axis_index(COARSE_FINE)
    group = lax.axis_index("coarse")
    start = here * tokens
    light_kv = jnp.concatenate([k_light[0], v_light[0]], axis=1)
    padded = extended(light_kv, ((COARSE_FINE, 0),), ROUTED_BLOCK)
    key_pos = start - ROUTED_BLOCK + jnp.arange(tokens + 2 * ROUTED_BLOCK, dtype=jnp.int32)
    inside = (key_pos >= 0) & (key_pos < tokens * n_seq)
    rows = min(512, tokens)
    qpos = start + 0 + jnp.arange(rows, dtype=jnp.int32)
    mask = (jnp.abs(qpos[:, None] - key_pos[None, :]) <= ROUTED_BLOCK - 1) & inside[None, :]
    pieces = attend(query, padded[:, :width], padded[:, width:], mask)
    blocks = tokens // ROUTED_BLOCK
    mine = here * blocks + jnp.arange(blocks, dtype=jnp.int32)
    key_group = lax.dynamic_slice_in_dim(key_ids[0], group * KGRP, KGRP)
    pick_keys = (key_group[:, None] == mine[None, :]).astype(jnp.bfloat16)
    heavy_kv = jnp.concatenate([k_heavy[0], v_heavy[0]], axis=1).reshape(
        blocks, ROUTED_BLOCK, 2 * width
    )
    slots = jnp.einsum(
        "sb,bre->sre", pick_keys, heavy_kv, preferred_element_type=jnp.float32
    ).reshape(KGRP * ROUTED_BLOCK, 2 * width)
    share = sum_at_owner(slots.astype(jnp.bfloat16), FINE, 0).astype(jnp.bfloat16)
    keys_all = lax.all_gather(share, COARSE_FINE, axis=0, tiled=True)
    query_group = lax.dynamic_slice_in_dim(query_ids[0], group * n_fine, n_fine)
    pick_rows = (query_group[:, None] == mine[None, :]).astype(jnp.bfloat16)
    heavy_query = q_heavy[0]
    result = attend(heavy_query, keys_all[:, :width], keys_all[:, width:], None).astype(
        jnp.bfloat16
    )
    chosen = jnp.sum(pick_rows.astype(jnp.float32), axis=0)
    heavy = (
        result.reshape(blocks, ROUTED_BLOCK, width).astype(jnp.float32) * chosen[:, None, None]
    ).reshape(tokens, width)
    encoded = (pieces + heavy).astype(jnp.bfloat16)[None]
    decoder_query_rows = dec_queries[0]
    count = decoder_query_rows.shape[0]
    heads = width // HEAD
    enc_keys = enc_kv[0][:, :HEAD]
    enc_values = enc_kv[0][:, HEAD:]
    heads_query = decoder_query_rows.reshape(count, heads, HEAD).transpose(1, 0, 2)

    def partial_head(qa):
        scores = jnp.dot(qa, enc_keys.T, preferred_element_type=jnp.float32) * HEAD ** (-0.5)
        peak = jnp.max(scores, axis=1)
        weights = jnp.exp(scores - peak[:, None])
        total = jnp.sum(weights, axis=1)
        value_rows = jnp.dot(
            weights.astype(jnp.bfloat16), enc_values, preferred_element_type=jnp.float32
        )
        return (peak, total, value_rows)

    peak, total, value_rows = lax.map(partial_head, heads_query)
    peak, total, value_rows = joined_all((peak, total, value_rows), COARSE_FINE, combine)
    decoded = (
        (value_rows / total[..., None])
        .transpose(1, 0, 2)
        .reshape(count, width)
        .astype(jnp.bfloat16)[None]
    )
    return (encoded, decoded)


def solution(mesh):
    torus = Mesh(
        mesh.devices.reshape(mesh.shape["doc"], mesh.shape["coarse"], 4, 4),
        ("doc", "coarse", "fine_0", "fine_1"),
    )
    return jax.shard_map(
        local,
        mesh=torus,
        in_specs=(
            P("doc", COARSE_FINE, None),
            P("doc", COARSE_FINE, None),
            P("doc", COARSE_FINE, None),
            P("doc", COARSE_FINE, None),
            P("doc", COARSE_FINE, None),
            P("doc", COARSE_FINE, None),
            P("doc", COARSE_FINE, None),
            P("doc", None, None),
            P("doc", None),
            P("doc", None),
        ),
        out_specs=(P("doc", COARSE_FINE, None), P("doc", None, None)),
        check_vma=False,
    )
```

profile of v0, /device:TPU:0, one launch (start us, length us, event | category | flops | bytes accessed | tf_op | source)
XLA Modules:
  0.0 474.6 jit_solution(11982831535126823827)
XLA Ops:
  8.8 19.9 %while.39 = (s32[]{:T(128)}, f32[16,512]{1,0:T(8,128)S(1)}, f32[16,512]{1,0:T(8,128)S(1)}, f32[16,512,64]{1,2,0:T(8,128)}, bf16[16,512,64]{1,2,0:T(8,128)(2,1)S(...) while((s32[]{:T(128)}, f32[16,512]{1,0:T(8,128)S(1)}, ...), condition=%wide.region_13.14_spmd.clone, body=%wide.region_10.13_spmd.sunk.clone | while | flops 17169408 | bytes 1048677 | solution.py:144
  28.9 13.3 %all-gather.1 = f32[64,512]{1,0:T(8,128)S(1)} all-gather(f32[16,512]{1,0:T(8,128)S(1)} %get-tuple-element.103), channel_id=3, replica_groups=mesh['doc'=2,'coarse'=4,'fine_0'=4,'fine_1'=4] {'coarse'}, dimensions={0}, use_global_device_ids=true | all-gather | bytes 163840 | tf_op jit(solution)/shard_map/all_gather | solution.py:48
  42.2 72.6 %all-gather.14.cloned.1.call-done = f32[64,512,64]{1,2,0:T(8,128)} async-done(((f32[16,512,64]{1,2,0:T(8,128)}), f32[64,512,64]{1,2,0:T(8,128)}) %all-gather.14.cloned.1.call-update) | async-done | bytes 8388624 | tf_op jit(solution)/shard_map/all_gather | solution.py:48
  114.8 6.3 %fusion.50 = f32[1,16,512,64]{2,3,1,0:T(8,128)} fusion(f32[64,512,64]{1,2,0:T(8,128)} %all-gather.14.cloned.1.call-done, f32[16,512]{1,0:T(8,128)S(1)} %get-tuple-element.266, f32[16,512]{1,0:T(8,128)S(1)} %get-tuple-element.263, f32[16,512]{1,0:T(8,128)S(1)} %get-tuple-element.265, f32[16,512]{1,0:T(8,128)S(1)} %get-tuple-element.264, ...), kind=kLoop, calls=%fused_computation.70 | loop fusion | flops 4718592 | bytes 10682368 | tf_op jit(solution)/shard_map/add | solution.py:82
  123.5 66.0 %all_to_all.5 = bf16[16,64,2048]{2,1,0:T(8,128)(2,1)} all-to-all(bf16[16,64,2048]{2,1,0:T(8,128)(2,1)S(1)} %bitcast.387), channel_id=1, replica_groups=mesh['doc'=2,'coarse'=4,'fine_0'=4,'fine_1'=4] {'fine_0','fine_1'}, dimensions={0} | all-to-all | bytes 8388608 | tf_op jit(solution)/shard_map/all_to_all | solution.py:42
  189.5 3.9 reduce_sum.48
  195.1 4.6 collective-permute-start
  199.7 20.4 %all-gather.2 = f32[64,512]{1,0:T(8,128)S(1)} all-gather(f32[16,512]{1,0:T(8,128)S(1)} %get-tuple-element.104), channel_id=4, replica_groups=mesh['doc'=2,'coarse'=4,'fine_0'=4,'fine_1'=4] {'coarse'}, dimensions={0}, use_global_device_ids=true | all-gather | bytes 163840 | tf_op jit(solution)/shard_map/all_gather | solution.py:48
  220.1 12.5 %all_gather.51 = f32[4,16,512]{2,1,0:T(8,128)S(1)} all-gather(f32[1,16,512]{2,1,0:T(8,128)S(1)} %get-tuple-element.242), channel_id=1, replica_groups=mesh['doc'=2,'coarse'=4,'fine_0'=4,'fine_1'=4] {'fine_0'}, dimensions={0}, use_global_device_ids=true | all-gather | bytes 163840 | tf_op jit(solution)/shard_map/all_gather | solution.py:48
  232.7 12.4 %all_gather.56 = f32[4,16,512]{2,1,0:T(8,128)S(1)} all-gather(f32[1,16,512]{2,1,0:T(8,128)S(1)} %get-tuple-element.241), channel_id=1, replica_groups=mesh['doc'=2,'coarse'=4,'fine_0'=4,'fine_1'=4] {'fine_0'}, dimensions={0}, use_global_device_ids=true | all-gather | bytes 163840 | tf_op jit(solution)/shard_map/all_gather | solution.py:48
  245.9 12.0 %all_gather.57 = f32[4,16,512]{2,1,0:T(8,128)S(1)} all-gather(f32[1,16,512]{2,1,0:T(8,128)S(1)} %get-tuple-element.239), channel_id=1, replica_groups=mesh['doc'=2,'coarse'=4,'fine_0'=4,'fine_1'=4] {'fine_1'}, dimensions={0}, use_global_device_ids=true | all-gather | bytes 163840 | tf_op jit(solution)/shard_map/all_gather | solution.py:48
  258.7 1.8 copy.50
  261.1 12.2 %all_gather.53 = f32[4,16,512]{2,1,0:T(8,128)S(1)} all-gather(f32[1,16,512]{2,1,0:T(8,128)S(1)} %get-tuple-element.240), channel_id=1, replica_groups=mesh['doc'=2,'coarse'=4,'fine_0'=4,'fine_1'=4] {'fine_1'}, dimensions={0}, use_global_device_ids=true | all-gather | bytes 163840 | tf_op jit(solution)/shard_map/all_gather | solution.py:48
  275.1 23.9 %while.40 = (s32[]{:T(128)}, f32[16,128,64]{1,2,0:T(8,128)S(1)}, bf16[16,128,64]{1,2,0:T(8,128)(2,1)}, bf16[16,384,64]{1,2,0:T(8,128)(2,1)S(1)}, bf16[16,384,64]...) while((s32[]{:T(128)}, f32[16,128,64]{1,2,0:T(8,128)S(1)}, ...), condition=%wide.region_3.4_spmd.clone.clone, body=%wide.region_0.3_spmd.clone.sunk.clone | while | flops 13172482 | bytes 745053 | solution.py:73
  299.2 6.5 %fusion.44 = f32[1,16,512,64]{2,3,1,0:T(8,128)} fusion(f32[4,16,512,64]{2,3,1,0:T(8,128)} %all-gather.10.cloned.1.call-done, f32[16,512]{1,0:T(8,128)S(1)} %copy-done.9, f32[16,512]{1,0:T(8,128)S(1)} %copy-done.6, f32[16,512]{1,0:T(8,128)S(1)} %copy-done.8, f32[16,512]{1,0:T(8,128)S(1)} %copy-done.7, f32[16,512]{1,0:T(8,128)S(1)} %copy-done.5, ...), kind=kLoop, calls=%fused_computation.60 | loop fusion | flops 4718592 | bytes 10682368 | tf_op jit(solution)/shard_map/add | solution.py:82
  305.7 60.2 %all-gather.8.cloned.1.call-done = bf16[4096,2048]{1,0:T(8,128)(2,1)} async-done(((bf16[64,2048]{1,0:T(8,128)(2,1)}), bf16[4096,2048]{1,0:T(8,128)(2,1)}) %all-gather.8.cloned.1.call-update) | async-done | bytes 16777232 | tf_op jit(solution)/shard_map/all_gather | solution.py:115
  365.9 12.2 %fusion.107 = (bf16[4096,1024]{1,0:T(8,128)(2,1)}, bf16[4096,1024]{1,0:T(8,128)(2,1)}) fusion(bf16[4096,2048]{1,0:T(8,128)(2,1)} %all-gather.8.cloned.1.call-done), kind=kLoop, calls=%fused_computation.185 | loop fusion | bytes 33554432 | tf_op jit(solution)/shard_map/slice | solution.py:119
  378.1 11.4 %copy.67 = bf16[4096,1024]{0,1:T(8,128)(2,1)} copy(bf16[4096,1024]{1,0:T(8,128)(2,1)} %get-tuple-element.254) | data formatting | bytes 16777216
  389.5 11.4 %copy.68 = bf16[4096,1024]{0,1:T(8,128)(2,1)} copy(bf16[4096,1024]{1,0:T(8,128)(2,1)} %get-tuple-element.253) | data formatting | bytes 16777216
  401.0 59.2 %while.38 = (s32[]{:T(128)}, bf16[16,128,64]{1,2,0:T(8,128)(2,1)S(1)}, bf16[16,128,64]{1,2,0:T(8,128)(2,1)}, bf16[16,4096,64]{1,2,0:T(8,128)(2,1)}, bf16[16,4096,64]{1,2,0:T(8,128)(2,1)}) while((s32[]{:T(128)}, bf16[16,128,64]{1,2,0:T(8,128)(2,1)S(1)}, bf16[16,128,64]{1,2,0:T(8,128)(2,1)}, bf16[16,4096,64]{1,2,0:T(8,128)(2,1)}, ...), condition=%wide.region_8.9_spmd.clone, body=%wide.region_5.8_spmd.sunk.clone | while | flops 137887488 | bytes 7393861 | solution.py:73
  401.0 1.7 fusion.141
  403.1 1.6 fusion.143
  406.8 1.6 fusion.143
  417.9 1.6 fusion.143
  429.0 1.6 fusion.143
  432.7 1.6 fusion.143
  436.4 1.6 fusion.143
  440.1 1.6 fusion.143
  443.8 1.6 fusion.143
  447.4 1.6 fusion.143
  451.1 1.6 fusion.143
  461.7 5.0 %fusion.58 = bf16[16,512,64]{1,2,0:T(8,128)(2,1)S(1)} fusion(f32[4,16,512,64]{2,3,1,0:T(8,128)} %all-gather.12.cloned.1.call-done, f32[16,512]{1,0:T(8,128)S(1)} %copy-done.11, f32[16,512]{1,0:T(8,128)S(1)} %copy-done.17, f32[16,512]{1,0:T(8,128)S(1)} %copy-done.16, f32[16,512]{1,0:T(8,128)S(1)} %copy-done.15, f32[16,512]{1,0:T(8,128)S(1)} %copy-done.14, ...), kind=kLoop, calls=%fused_computation.81 | loop fusion | flops 5767168 | bytes 9666560 | tf_op jit(solution)/shard_map/convert_element_type | solution.py:150
  (250 shorter events, 96.7 us)
Async XLA Ops:
  7.2 1.6 copy-start.18
  7.2 107.6 %all-gather.14.cloned.1.call-start = ((), (), s32[]{:S(2)}) async-start(), calls=%async_computation.4 | async-start | bytes 10485760 | tf_op jit(solution)/shard_map/all_gather | solution.py:48
  28.8 270.3 %all-gather.10.cloned.1.call-start = ((), (), s32[]{:S(2)}) async-start(), calls=%async_computation.2 | async-start | bytes 10485760 | tf_op jit(solution)/shard_map/all_gather | solution.py:48
  121.1 0.7 copy-start.19
  121.1 1.0 copy-start.3
  121.1 1.0 copy-start.4
  121.1 244.8 %all-gather.8.cloned.1.call-start = ((), (), s32[]{:S(2)}) async-start(), calls=%async_computation.1 | async-start | bytes 17039360 | tf_op jit(solution)/shard_map/all_gather | solution.py:115
  189.5 3.9 copy-start
  189.5 4.1 copy-start.1
  193.3 64.5 %copy-start.2 = (bf16[1,128,1024]{2,1,0:T(8,128)(2,1)S(1)}, bf16[1,128,1024]{2,1,0:T(8,128)(2,1)}, u32[]{:S(2)}) copy-start(bf16[1,128,1024]{2,1,0:T(8,128)(2,1)} %param.16) | copy-start | bytes 786436
  193.4 268.3 %all-gather.12.cloned.1.call-start = ((), (), s32[]{:S(2)}) async-start(), calls=%async_computation.3 | async-start | bytes 10485760 | tf_op jit(solution)/shard_map/all_gather | solution.py:48
  193.6 66.9 %copy-start.20 = (s32[1,64]{1,0:T(1,128)S(1)}, s32[1,64]{1,0:T(1,128)}, u32[]{:S(2)}) copy-start(s32[1,64]{1,0:T(1,128)} %param.24) | copy-start | bytes 772
  193.8 80.8 %collective-permute-start.1 = (bf16[128,2048]{0,1:T(8,128)(2,1)S(1)}, bf16[128,2048]{0,1:T(8,128)(2,1)S(1)}, u32[]{:S(2)}, u32[]{:S(2)}) collective-permute-start(bf16[128,2048]{0,1:T(8,128)(2,1)S(1)} %pad_maximum_fusion.1), channel_id=1, source_target_pairs={{1,0},{2,1},{3,2},{4,3},{5,4},{6,5},{7,6},{8,7},{9,8},{10,9},{11,1... | collective-permute-start | bytes 1572872 | tf_op jit(solution)/shard_map/ppermute | solution.py:23
  195.1 79.5 %collective-permute-start = (bf16[128,2048]{0,1:T(8,128)(2,1)S(1)}, bf16[128,2048]{0,1:T(8,128)(2,1)S(1)}, u32[]{:S(2)}, u32[]{:S(2)}) collective-permute-start(bf16[128,2048]{0,1:T(8,128)(2,1)S(1)} %pad_maximum_fusion.1), channel_id=1, source_target_pairs={{0,1},{1,2},{2,3},{3,4},{4,5},{5,6},{6,7},{7,8},{8,9},{9,10},{10,1... | collective-permute-start | bytes 1572872 | tf_op jit(solution)/shard_map/ppermute | solution.py:22
  275.1 24.0 %copy-start.5 = (f32[16,512]{1,0:T(8,128)S(1)}, f32[16,512]{1,0:T(8,128)}, u32[]{:S(2)}) copy-start(f32[16,512]{1,0:T(8,128)} %get-tuple-element.257) | copy-start | bytes 98308
  275.1 24.0 %copy-start.6 = (f32[16,512]{1,0:T(8,128)S(1)}, f32[16,512]{1,0:T(8,128)}, u32[]{:S(2)}) copy-start(f32[16,512]{1,0:T(8,128)} %get-tuple-element.258) | copy-start | bytes 98308
  275.1 24.0 %copy-start.7 = (f32[16,512]{1,0:T(8,128)S(1)}, f32[16,512]{1,0:T(8,128)}, u32[]{:S(2)}) copy-start(f32[16,512]{1,0:T(8,128)} %get-tuple-element.259) | copy-start | bytes 98308
  275.1 24.0 %copy-start.8 = (f32[16,512]{1,0:T(8,128)S(1)}, f32[16,512]{1,0:T(8,128)}, u32[]{:S(2)}) copy-start(f32[16,512]{1,0:T(8,128)} %get-tuple-element.260) | copy-start | bytes 98308
  275.1 24.0 %copy-start.9 = (f32[16,512]{1,0:T(8,128)S(1)}, f32[16,512]{1,0:T(8,128)}, u32[]{:S(2)}) copy-start(f32[16,512]{1,0:T(8,128)} %get-tuple-element.261) | copy-start | bytes 98308
  275.1 24.0 %copy-start.10 = (f32[16,512]{1,0:T(8,128)S(1)}, f32[16,512]{1,0:T(8,128)}, u32[]{:S(2)}) copy-start(f32[16,512]{1,0:T(8,128)} %get-tuple-element.243) | copy-start | bytes 98308
  400.9 60.7 %copy-start.11 = (f32[16,512]{1,0:T(8,128)S(1)}, f32[16,512]{1,0:T(8,128)}, u32[]{:S(2)}) copy-start(f32[16,512]{1,0:T(8,128)} %get-tuple-element.232) | copy-start | bytes 98308
  400.9 60.7 %copy-start.12 = (f32[16,512]{1,0:T(8,128)S(1)}, f32[16,512]{1,0:T(8,128)}, u32[]{:S(2)}) copy-start(f32[16,512]{1,0:T(8,128)} %get-tuple-element.233) | copy-start | bytes 98308
  400.9 60.7 %copy-start.13 = (f32[16,512]{1,0:T(8,128)S(1)}, f32[16,512]{1,0:T(8,128)}, u32[]{:S(2)}) copy-start(f32[16,512]{1,0:T(8,128)} %get-tuple-element.234) | copy-start | bytes 98308
  400.9 60.7 %copy-start.14 = (f32[16,512]{1,0:T(8,128)S(1)}, f32[16,512]{1,0:T(8,128)}, u32[]{:S(2)}) copy-start(f32[16,512]{1,0:T(8,128)} %get-tuple-element.235) | copy-start | bytes 98308
  401.0 60.7 %copy-start.15 = (f32[16,512]{1,0:T(8,128)S(1)}, f32[16,512]{1,0:T(8,128)}, u32[]{:S(2)}) copy-start(f32[16,512]{1,0:T(8,128)} %get-tuple-element.236) | copy-start | bytes 98308
  401.0 60.7 %copy-start.16 = (f32[16,512]{1,0:T(8,128)S(1)}, f32[16,512]{1,0:T(8,128)}, u32[]{:S(2)}) copy-start(f32[16,512]{1,0:T(8,128)} %get-tuple-element.237) | copy-start | bytes 98308
  401.0 60.7 %copy-start.17 = (f32[16,512]{1,0:T(8,128)S(1)}, f32[16,512]{1,0:T(8,128)}, u32[]{:S(2)}) copy-start(f32[16,512]{1,0:T(8,128)} %get-tuple-element.238) | copy-start | bytes 98308
Sparse Core Ops, SparseCore 0:
  28.9 85.8 all-gather.13
  121.3 138.2 all-gather.9
  262.4 103.4 all-gather.7
  367.5 82.6 all-gather.11
where the time goes:
time: 478 us; the launch traced here: 475 us
  blocking collectives  149 us (31%)
  waiting for transfers between devices  133 us (28%)
  matrix products  88.8 us (19%)
  local copies, waits for them, and re-layouts  44.8 us (9%)
  other arithmetic  38.1 us (8%)
  between operations  14.2 us (3%)
  starting transfers between devices  6.03 us (1%)
    all_gather x6, blocking collectives, joined_all(): pieces = jax.tree.map(lambda part: lax.all_gather(part, axis), value)  82.8 us
    all_gather x3, waiting for transfers between devices, joined_all(): pieces = jax.tree.map(lambda part: lax.all_gather(part, axis), value)  72.6 us
    all_to_all x1, blocking collectives, sum_at_owner(): lax.all_to_all(pieces, axis, split_axis=0, concat_axis=0, tiled=True)  66 us
    all_gather x1, waiting for transfers between devices, local(): keys_all = lax.all_gather(share, COARSE_FINE, axis=0, tiled=True)  60.2 us
    dot_general x32, matrix products, one_head(): jnp.dot(qa, ka.T, preferred_element_type=jnp.float32) * HEAD ** (-0.5)  42.1 us
    unnamed x51, local copies, waits for them, and re-layouts  30.4 us
    dot_general x32, matrix products, one_head(): return jnp.dot(weights, va, preferred_element_type=jnp.float32)  30 us
    dot_general x16, matrix products, partial_head(): jnp.dot(weights.astype(jnp.bfloat16), enc_values, preferred_element_type=...  13.8 us
  transfers between devices with their start and end apart: 6, of which 2 were waited for; matrix products, arithmetic and copies ran while one was open for 29% of the time, Pallas kernels for 0%

commit v1 on v0

v1 whole, which is shorter than its diff:
```python
import jax
import jax.numpy as jnp
from jax import lax
from jax.experimental import pallas as pl
from jax.experimental.pallas import tpu as pltpu
from jax.sharding import PartitionSpec as P

HEAD = 64
LANES = 2 * HEAD
BLOCK = 128
KGRP = 8
HALF = BLOCK // 2
SCALE = HEAD**-0.5
LOG2E = 1.4426950408889634
TOKENS = ("coarse", "fine")
VMEM = 48 * 1024 * 1024

f32 = jnp.float32
bf16 = jnp.bfloat16


def params(**kw):
    return pltpu.CompilerParams(vmem_limit_bytes=VMEM, **kw)


def lane_ids(shape):
    return lax.broadcasted_iota(jnp.int32, shape, len(shape) - 1)


def nt(a, b):
    return lax.dot_general(a, b, (((1,), (1,)), ((), ())), preferred_element_type=f32)


def nn(a, b):
    return jnp.dot(a, b, preferred_element_type=f32)


def pack_kernel(q, k, v, enc, kv_out, q_out):
    heads = kv_out.shape[0]
    for h in range(heads):
        cols = slice(h * HEAD, (h + 1) * HEAD)
        kv_out[h] = jnp.concatenate([k[:, cols], v[:, cols]], axis=1)
        qh = q[:, cols]
        q_out[h, :HALF] = jnp.concatenate([qh[:HALF], qh[HALF:]], axis=1)
        q_out[h, HALF:] = enc[...]


def pack(q, k, v, enc):
    heads = q.shape[1] // HEAD
    return pl.pallas_call(
        pack_kernel,
        out_shape=(
            jax.ShapeDtypeStruct((heads, BLOCK, LANES), bf16),
            jax.ShapeDtypeStruct((heads, HALF + BLOCK, LANES), bf16),
        ),
        compiler_params=params(),
        name="pack",
    )(q, k, v, enc)


def pick_kernel(ids, kv, out):
    for s in range(KGRP):
        out[s] = kv[ids[s]]


def pick(ids, kv):
    return pl.pallas_call(
        pick_kernel,
        out_shape=jax.ShapeDtypeStruct((KGRP, BLOCK, LANES), bf16),
        in_specs=[pl.BlockSpec(memory_space=pltpu.SMEM), pl.BlockSpec(memory_space=pltpu.VMEM)],
        compiler_params=params(),
        name="pick",
    )(ids, kv)


def probs(q, keys, m=None):
    scores = [nt(q, k) for k in keys]
    peak = scores[0].max(axis=1, keepdims=True)
    for s in scores[1:]:
        peak = jnp.maximum(peak, s.max(axis=1, keepdims=True))
    return [jnp.exp2((s - peak) * (SCALE * LOG2E)).astype(bf16) for s in scores], peak


def with_ones(kv):
    return jnp.where(lane_ids(kv.shape) < HEAD, jnp.ones_like(kv), kv)


def summed(q, keys, values):
    p, peak = probs(q, keys)
    total = nn(p[0], values[0])
    for a, b in zip(p[1:], values[1:]):
        total = total + nn(a, b)
    return total, peak


def heavy_kernel(q, kv0, kv1, kv2, kv3, out, values):
    kvs = (kv0, kv1, kv2, kv3)

    @pl.when(pl.program_id(0) == 0)
    def _():
        for n, kv in enumerate(kvs):
            values[n] = with_ones(kv[...])

    rows = q.shape[0] * q.shape[1]
    both = q[...].reshape(rows, LANES)
    zero = jnp.zeros((rows, HEAD), bf16)
    keys = [kv[...] for kv in kvs]
    vals = [values[n] for n in range(len(kvs))]
    a, _ = summed(jnp.concatenate([both[:, :HEAD], zero], axis=1), keys, vals)
    b, _ = summed(jnp.concatenate([both[:, HEAD:], zero], axis=1), keys, vals)
    low = lane_ids(a.shape) < HEAD
    top = jnp.where(low, pltpu.roll(a, HEAD, 1), b)
    sums = jnp.where(low, a, pltpu.roll(b, HEAD, 1))
    out[...] = (top / sums).astype(bf16).reshape(out.shape)


def heavy_attend(q, kvs, step):
    blocks = q.shape[0]
    full = pl.BlockSpec(kvs[0].shape, lambda i: (0, 0))
    return pl.pallas_call(
        heavy_kernel,
        grid=(blocks // step,),
        in_specs=[pl.BlockSpec((step, HALF, LANES), lambda i: (i, 0, 0))] + [full] * len(kvs),
        out_specs=pl.BlockSpec((step, HALF, LANES), lambda i: (i, 0, 0)),
        out_shape=jax.ShapeDtypeStruct((blocks, HALF, LANES), bf16),
        scratch_shapes=[pltpu.VMEM((len(kvs),) + kvs[0].shape, bf16)],
        compiler_params=params(),
        name="heavy",
    )(q, *kvs)


def light_kernel(edge, q, k, v, pk, pv, nk, nv, out):
    qq = q[...]
    low = lane_ids(qq.shape) < HEAD
    zero = jnp.zeros_like(qq)
    rows = qq.shape[0]
    two = jnp.concatenate([jnp.where(low, qq, zero), jnp.where(low, zero, qq)], axis=0)
    i = lax.broadcasted_iota(jnp.int32, (2 * rows, BLOCK), 0) % rows
    j = lax.broadcasted_iota(jnp.int32, (2 * rows, BLOCK), 1)
    here = nt(two, k[...]) * SCALE
    prev = jnp.where((j > i) & (edge[0] > 0), nt(two, pk[...]) * SCALE, f32(-1e30))
    after = jnp.where((j < i) & (edge[1] > 0), nt(two, nk[...]) * SCALE, f32(-1e30))
    peak = jnp.maximum(jnp.maximum(here, prev), after).max(axis=1, keepdims=True)
    ph, pp, pn = (jnp.exp(s - peak) for s in (here, prev, after))
    total = (ph + pp + pn).sum(axis=1, keepdims=True)
    o = nn(ph.astype(bf16), v[...]) + nn(pp.astype(bf16), pv[...]) + nn(pn.astype(bf16), nv[...])
    o = o / total
    out[...] = jnp.where(low, o[:rows], o[rows:])


def light_attend(edge, q, k, v, prev, after):
    rows, width = q.shape
    pairs = width // LANES
    col = pl.BlockSpec((rows, LANES), lambda p: (0, p))
    col_v = pl.BlockSpec((rows, LANES), lambda p: (0, p + pairs))
    return pl.pallas_call(
        light_kernel,
        grid=(pairs,),
        in_specs=[pl.BlockSpec(memory_space=pltpu.SMEM), col, col, col, col, col_v, col, col_v],
        out_specs=col,
        out_shape=jax.ShapeDtypeStruct((rows, width), f32),
        compiler_params=params(),
        name="light",
    )(edge, q, k, v, prev, prev, after, after)


def join_kernel(chosen, light, heavy, out):
    scale = chosen[0].astype(f32)
    for p in range(heavy.shape[0] // 2):
        e, o = heavy[2 * p], heavy[2 * p + 1]
        for n in range(2):
            rows, lanes = slice(n * HALF, (n + 1) * HALF), slice(n * HEAD, (n + 1) * HEAD)
            cols = slice(p * LANES, (p + 1) * LANES)
            both = jnp.concatenate([e[:, lanes], o[:, lanes]], axis=1)
            out[rows, cols] = (light[rows, cols] + both.astype(f32) * scale).astype(bf16)


def join(chosen, light, heavy):
    vmem = pl.BlockSpec(memory_space=pltpu.VMEM)
    return pl.pallas_call(
        join_kernel,
        in_specs=[pl.BlockSpec(memory_space=pltpu.SMEM), vmem, vmem],
        out_shape=jax.ShapeDtypeStruct(light.shape, bf16),
        compiler_params=params(),
        name="join",
    )(chosen, light, heavy)


def decode_kernel(at, q, enc_a, enc_b, out):
    del at
    heads = q.shape[1] // HEAD
    rows = q.shape[0]
    zero = jnp.zeros((rows, HEAD), bf16)
    stack = jnp.concatenate(
        [
            jnp.concatenate([q[:, h * HEAD : (h + 1) * HEAD], zero], axis=1)
            for h in range(heads)
        ],
        axis=0,
    )
    keys = [e[...].reshape(-1, LANES) for e in (enc_a, enc_b)]
    vals = [with_ones(k) for k in keys]
    half = stack.shape[0] // 2
    for n in range(2):
        total, peak = summed(stack[n * half : (n + 1) * half], keys, vals)
        low = lane_ids(total.shape) < HEAD
        level = peak * SCALE + jnp.log(total)
        hi = level.astype(bf16).astype(f32)
        mid = (level - hi).astype(bf16).astype(f32)
        least = level - hi - mid
        lane = lane_ids(total.shape)
        parts = jnp.where(lane < 16, hi, jnp.where(lane < 32, mid, least))
        ratio = total / pltpu.roll(total, HEAD, 1)
        out[n * half : (n + 1) * half] = jnp.where(low, parts, ratio).astype(bf16)


def decode(at, q, enc, rows):
    blocks = enc.shape[0]
    width = q.shape[1]
    spec = lambda n: pl.BlockSpec((blocks, HALF, LANES), lambda i, at: (0, n, 0))
    out = (rows * (width // HEAD), LANES)
    return pl.pallas_call(
        decode_kernel,
        grid_spec=pltpu.PrefetchScalarGridSpec(
            num_scalar_prefetch=1,
            grid=(1,),
            in_specs=[pl.BlockSpec((rows, width), lambda i, at: (at[0], 0)), spec(1), spec(2)],
            out_specs=pl.BlockSpec(out, lambda i, at: (0, 0)),
        ),
        out_shape=jax.ShapeDtypeStruct(out, bf16),
        compiler_params=params(),
        name="decode",
    )(at, q, enc, enc)


def meet_kernel(a, b, c, d, out):
    parts = [x[...].astype(f32) for x in (a, b, c, d)]
    levels = [x[:, 0:1] + x[:, 16:17] + x[:, 32:33] for x in parts]
    peak = jnp.maximum(jnp.maximum(levels[0], levels[1]), jnp.maximum(levels[2], levels[3]))
    scales = [jnp.exp(n - peak) for n in levels]
    total = scales[0] + scales[1] + scales[2] + scales[3]
    value = parts[0] * scales[0]
    for x, s in zip(parts[1:], scales[1:]):
        value = value + x * s
    value = (value / total).astype(bf16)
    copies, rows, width = out.shape
    for p in range(width // LANES):
        e = value[2 * p * rows : (2 * p + 1) * rows, HEAD:]
        o = value[(2 * p + 1) * rows : (2 * p + 2) * rows, HEAD:]
        both = jnp.concatenate([e, o], axis=1)
        for n in range(copies):
            out[n, :, p * LANES : (p + 1) * LANES] = both


def meet(parts, copies, rows, width):
    return pl.pallas_call(
        meet_kernel,
        out_shape=jax.ShapeDtypeStruct((copies, rows, width), bf16),
        compiler_params=params(),
        name="meet",
    )(*parts)


def around(value, axis):
    size = lax.axis_size(axis)
    return [lax.ppermute(value, axis, [(i, (i + d) % size) for i in range(size)]) for d in range(1, size)]


def local(
    q_light, k_light, v_light, q_heavy, k_heavy, v_heavy, enc_kv, dec_queries, query_ids, key_ids
):
    n_seq = lax.axis_size(TOKENS)
    n_fine = lax.axis_size("fine")
    here = lax.axis_index(TOKENS)
    group = lax.axis_index("coarse")
    place = lax.axis_index("fine")
    width = q_light.shape[2]

    kv_chunks, q_chunks = pack(q_heavy[0], k_heavy[0], v_heavy[0], enc_kv[0])
    kv_group = lax.all_to_all(kv_chunks, "fine", 0, 0, tiled=True)
    q_enc = lax.all_to_all(q_chunks, "fine", 0, 0, tiled=True)

    light_kv = jnp.concatenate([k_light[0], v_light[0]], axis=1)
    up = [(i, i + 1) for i in range(n_seq - 1)]
    prev = lax.ppermute(light_kv, TOKENS, up)
    after = lax.ppermute(light_kv, TOKENS, [(b, a) for a, b in up])

    ids = lax.dynamic_slice_in_dim(key_ids[0], group * KGRP, KGRP) - group * n_fine
    own = pick(ids, kv_group).reshape(KGRP * BLOCK, LANES)
    routed = [own] + around(own, "coarse")

    dec_rows = dec_queries.shape[1] // n_fine
    part = decode(place[None], dec_queries[0], q_enc, dec_rows)
    parts = [part] + around(part, "coarse")
    shares = meet(parts, n_fine, dec_rows, width)
    decoded = lax.all_to_all(shares, "fine", 0, 0, tiled=True).reshape(1, -1, width)

    heavy = heavy_attend(q_enc, routed, 4)
    heavy = lax.all_to_all(heavy, "fine", 0, 0, tiled=True)

    edge = jnp.stack([here > 0, here < n_seq - 1]).astype(jnp.int32)
    light = light_attend(edge, q_light[0], k_light[0], v_light[0], prev, after)
    query_group = lax.dynamic_slice_in_dim(query_ids[0], group * n_fine, n_fine)
    chosen = jnp.sum((query_group == here).astype(jnp.int32))[None]
    encoded = join(chosen, light, heavy)[None]
    return (encoded, decoded)


def solution(mesh):
    seq = P("doc", TOKENS, None)
    whole = P("doc", None, None)
    return jax.shard_map(
        local,
        mesh=mesh,
        in_specs=(seq,) * 7 + (whole, P("doc", None), P("doc", None)),
        out_specs=(seq, whole),
        check_vma=False,
    )
```

time: 478 us -> 121 us (0.25)
  the two profiles are of different devices: /device:TPU:0 before, /device:TPU:32 now
where the time goes in v1:
time: 121 us; the launch traced here: 120 us
  starting transfers between devices  37.8 us (31%)
  Pallas kernels  28.7 us (24%)
  waiting for transfers between devices  27 us (22%)
  blocking collectives  18.4 us (15%)
  local copies, waits for them, and re-layouts  5.89 us (5%)
  other arithmetic  1.76 us (1%)
    all_to_all x1, blocking collectives, local(): kv_group = lax.all_to_all(kv_chunks, 'fine', 0, 0, tiled=True)  18.4 us
    pallas_call x1, Pallas kernels, heavy_attend(): pl.pallas_call(heavy_kernel, grid=(blocks // step,), in_specs=[pl.BlockSp...  16 us
    ppermute x1, waiting for transfers between devices, local(): prev = lax.ppermute(light_kv, TOKENS, up)  12.8 us
    ppermute x6, starting transfers between devices, around(): lax.ppermute(value, axis, [(i, (i + d) % size) for i in range(size)])  10.2 us
    ppermute x6, waiting for transfers between devices, around(): lax.ppermute(value, axis, [(i, (i + d) % size) for i in range(size)])  7.87 us
    all_to_all x1, starting transfers between devices, local(): lax.all_to_all(shares, 'fine', 0, 0, tiled=True).reshape(1, -1, width)  7.13 us
    all_to_all x1, starting transfers between devices, local(): heavy = lax.all_to_all(heavy, 'fine', 0, 0, tiled=True)  6.87 us
    all_to_all x1, waiting for transfers between devices, local(): q_enc = lax.all_to_all(q_chunks, 'fine', 0, 0, tiled=True)  6.32 us
  transfers between devices with their start and end apart: 11, of which 7 were waited for; matrix products, arithmetic and copies ran while one was open for 1% of the time, Pallas kernels for 10%

profile of v1, /device:TPU:32, one launch (start us, length us, event | category | flops | bytes accessed | tf_op | source)
XLA Modules:
  0.0 120.3 jit_solution(15473184616288583538)
XLA Ops:
  0.6 0.9 copy-done.3
  1.6 0.9 copy-done.4
  2.5 0.9 copy-done.5
  3.5 0.8 copy-done.7
  4.2 1.2 pack.1
  5.4 18.4 %all_to_all.20.kv = bf16[16,128,128]{2,1,0:T(8,128)(2,1)S(1)} all-to-all(bf16[16,128,128]{2,1,0:T(8,128)(2,1)S(1)} %get-tuple-element.5), channel_id=1, replica_groups=mesh['doc'=2,'coarse'=4,'fine'=16] {'fine'}, dimensions={0} | all-to-all | bytes 1048576 | tf_op jit(solution)/shard_map/all_to_all | solution.py:280
  23.8 3.6 %all-to-all-start = ((bf16[16,192,128]{2,1,0:T(8,128)(2,1)}), bf16[16,192,128]{2,1,0:T(8,128)(2,1)S(1)}, u32[]{:S(2)}, u32[]{:S(2)}) async-start(bf16[16,192,128]{2,1,0:T(8,128)(2,1)} %get-tuple-element.4), calls=%async_computation | async-start | bytes 1572864 | tf_op jit(solution)/shard_map/all_to_all | solution.py:281
  28.7 2.0 %collective-permute-start.2 = (bf16[1024,128]{1,0:T(8,128)(2,1)S(1)}, bf16[1024,128]{1,0:T(8,128)(2,1)S(1)}, u32[]{:S(2)}, u32[]{:S(2)}) collective-permute-start(bf16[1024,128]{1,0:T(8,128)(2,1)S(1)} %bitcast.22), channel_id=1, source_target_pairs={{0,16},{16,32},{32,48},{48,0},{1,17},{17,33},{33,49},{49,1},{2,18}... | collective-permute-start | bytes 786440 | tf_op jit(solution)/shard_map/ppermute | solution.py:266
  30.7 1.2 collective-permute-start.3
  31.9 2.5 %collective-permute-start.4 = (bf16[1024,128]{1,0:T(8,128)(2,1)S(1)}, bf16[1024,128]{1,0:T(8,128)(2,1)S(1)}, u32[]{:S(2)}, u32[]{:S(2)}) collective-permute-start(bf16[1024,128]{1,0:T(8,128)(2,1)S(1)} %bitcast.24), channel_id=1, source_target_pairs={{0,48},{16,0},{32,16},{48,32},{1,49},{17,1},{33,17},{49,33},{2,50}... | collective-permute-start | bytes 786440 | tf_op jit(solution)/shard_map/ppermute | solution.py:266
  34.4 6.3 %all-to-all-done.q.enc_a.enc_b = bf16[16,192,128]{2,1,0:T(8,128)(2,1)S(1)} async-done(((bf16[16,192,128]{2,1,0:T(8,128)(2,1)}), bf16[16,192,128]{2,1,0:T(8,128)(2,1)S(1)}, u32[]{:S(2)}, u32[]{:S(2)}) %all-to-all-start) | async-done | bytes 786464 | tf_op jit(solution)/shard_map/all_to_all | solution.py:281
  40.7 0.7 collective-permute-done.3.kv2
  41.5 2.5 %collective-permute-done.4.kv3 = bf16[1024,128]{1,0:T(8,128)(2,1)S(1)} collective-permute-done((bf16[1024,128]{1,0:T(8,128)(2,1)S(1)}, bf16[1024,128]{1,0:T(8,128)(2,1)S(1)}, u32[]{:S(2)}, u32[]{:S(2)}) %collective-permute-start.4) | collective-permute-done | bytes 262176 | tf_op jit(solution)/shard_map/ppermute | solution.py:266
  44.0 16.0 %heavy.1 = bf16[16,64,128]{2,1,0:T(8,128)(2,1)} custom-call(bf16[16,192,128]{2,1,0:T(8,128)(2,1)S(1)} %all-to-all-done.q.enc_a.enc_b, bf16[1024,128]{1,0:T(8,128)(2,1)S(1)} %bitcast.25, bf16[1024,128]{1,0:T(8,128)(2,1)S(1)} %collective-permute-done.2.kv1, bf16[1024,128]{1,0:T(8,128)(2,1)S(1)} %collective-permute-done.3.kv2, ...), custom_call_target="tpu_custom_call" | custom-call | tf_op jit(solution)/shard_map/heavy/pallas_call | solution.py:120
  59.9 6.9 %all-to-all-start.2 = ((bf16[16,64,128]{2,1,0:T(8,128)(2,1)}), bf16[16,64,128]{2,1,0:T(8,128)(2,1)S(1)}, u32[]{:S(2)}, u32[]{:S(2)}) async-start(bf16[16,64,128]{2,1,0:T(8,128)(2,1)} %heavy.1), calls=%async_computation.2 | async-start | bytes 524288 | tf_op jit(solution)/shard_map/all_to_all | solution.py:299
  66.8 1.8 %decode.1.a = bf16[512,128]{1,0:T(8,128)(2,1)S(1)} custom-call(s32[1]{0:T(128)} %bitcast.13.at, bf16[512,1024]{1,0:T(8,128)(2,1)S(1)} %bitcast.17, bf16[16,192,128]{2,1,0:T(8,128)(2,1)S(1)} %all-to-all-done.q.enc_a.enc_b, bf16[16,192,128]{2,1,0:T(8,128)(2,1)S(1)} %all-to-all-done.q.enc_a.enc_b), custom_call_target="tpu_custom_call" | custom-call | tf_op jit(solution)/shard_map/decode/pallas_call | solution.py:222
  68.6 1.0 collective-permute-start.5
  69.6 1.9 %collective-permute-start.6 = (bf16[512,128]{1,0:T(8,128)(2,1)S(1)}, bf16[512,128]{1,0:T(8,128)(2,1)S(1)}, u32[]{:S(2)}, u32[]{:S(2)}) collective-permute-start(bf16[512,128]{1,0:T(8,128)(2,1)S(1)} %decode.1.a), channel_id=1, source_target_pairs={{0,32},{16,48},{32,0},{48,16},{1,33},{17,49},{33,1},{49,17},{2,34}... | collective-permute-start | bytes 393224 | tf_op jit(solution)/shard_map/ppermute | solution.py:266
  71.5 1.6 %collective-permute-start.7 = (bf16[512,128]{1,0:T(8,128)(2,1)S(1)}, bf16[512,128]{1,0:T(8,128)(2,1)S(1)}, u32[]{:S(2)}, u32[]{:S(2)}) collective-permute-start(bf16[512,128]{1,0:T(8,128)(2,1)S(1)} %decode.1.a), channel_id=1, source_target_pairs={{0,48},{16,0},{32,16},{48,32},{1,49},{17,1},{33,17},{49,33},{2,50}... | collective-permute-start | bytes 393224 | tf_op jit(solution)/shard_map/ppermute | solution.py:266
  73.1 1.9 %collective-permute-done.5.b = bf16[512,128]{1,0:T(8,128)(2,1)S(1)} collective-permute-done((bf16[512,128]{1,0:T(8,128)(2,1)S(1)}, bf16[512,128]{1,0:T(8,128)(2,1)S(1)}, u32[]{:S(2)}, u32[]{:S(2)}) %collective-permute-start.5) | collective-permute-done | bytes 131104 | tf_op jit(solution)/shard_map/ppermute | solution.py:266
  74.9 1.6 %collective-permute-done.6.c = bf16[512,128]{1,0:T(8,128)(2,1)S(1)} collective-permute-done((bf16[512,128]{1,0:T(8,128)(2,1)S(1)}, bf16[512,128]{1,0:T(8,128)(2,1)S(1)}, u32[]{:S(2)}, u32[]{:S(2)}) %collective-permute-start.6) | collective-permute-done | bytes 131104 | tf_op jit(solution)/shard_map/ppermute | solution.py:266
  76.5 1.2 %collective-permute-done.7.d = bf16[512,128]{1,0:T(8,128)(2,1)S(1)} collective-permute-done((bf16[512,128]{1,0:T(8,128)(2,1)S(1)}, bf16[512,128]{1,0:T(8,128)(2,1)S(1)}, u32[]{:S(2)}, u32[]{:S(2)}) %collective-permute-start.7) | collective-permute-done | bytes 131104 | tf_op jit(solution)/shard_map/ppermute | solution.py:266
  77.7 2.0 %meet.1 = bf16[16,32,1024]{2,1,0:T(8,128)(2,1)} custom-call(bf16[512,128]{1,0:T(8,128)(2,1)S(1)} %decode.1.a, bf16[512,128]{1,0:T(8,128)(2,1)S(1)} %collective-permute-done.5.b, bf16[512,128]{1,0:T(8,128)(2,1)S(1)} %collective-permute-done.6.c, bf16[512,128]{1,0:T(8,128)(2,1)S(1)} %collective-permute-done.7.d), custom_call_target="tpu_custom_call" | custom-call | tf_op jit(solution)/shard_map/meet/pallas_call | solution.py:256
  79.7 7.1 %all-to-all-start.3 = ((bf16[16,32,1024]{2,1,0:T(8,128)(2,1)}), bf16[16,32,1024]{2,1,0:T(8,128)(2,1)S(1)}, u32[]{:S(2)}, u32[]{:S(2)}) async-start(bf16[16,32,1024]{2,1,0:T(8,128)(2,1)} %meet.1), calls=%async_computation.3 | async-start | bytes 2097152 | tf_op jit(solution)/shard_map/all_to_all | solution.py:296
  86.9 0.8 pad_maximum_fusion
  87.8 3.8 %collective-permute-start = (bf16[128,2048]{1,0:T(8,128)(2,1)}, bf16[128,2048]{1,0:T(8,128)(2,1)S(1)}, u32[]{:S(2)}, u32[]{:S(2)}) collective-permute-start(bf16[128,2048]{1,0:T(8,128)(2,1)} %pad_maximum_fusion), channel_id=1, source_target_pairs={{0,1},{1,2},{2,3},{3,4},{4,5},{5,6},{6,7},{7,8},{8,9},{9,10},{10,1... | collective-permute-start | bytes 1572872 | tf_op jit(solution)/shard_map/ppermute | solution.py:285
  91.6 6.2 %collective-permute-start.1 = (bf16[128,2048]{1,0:T(8,128)(2,1)}, bf16[128,2048]{1,0:T(8,128)(2,1)S(1)}, u32[]{:S(2)}, u32[]{:S(2)}) collective-permute-start(bf16[128,2048]{1,0:T(8,128)(2,1)} %pad_maximum_fusion), channel_id=1, source_target_pairs={{1,0},{2,1},{3,2},{4,3},{5,4},{6,5},{7,6},{8,7},{9,8},{10,9},{11,1... | collective-permute-start | bytes 1572872 | tf_op jit(solution)/shard_map/ppermute | solution.py:286
  98.5 0.8 fusion
  99.3 12.8 %collective-permute-done.pk.pv = bf16[128,2048]{1,0:T(8,128)(2,1)S(1)} collective-permute-done((bf16[128,2048]{1,0:T(8,128)(2,1)}, bf16[128,2048]{1,0:T(8,128)(2,1)S(1)}, u32[]{:S(2)}, u32[]{:S(2)}) %collective-permute-start) | collective-permute-done | bytes 524320 | tf_op jit(solution)/shard_map/ppermute | solution.py:285
  112.2 5.6 %light.1 = f32[128,1024]{1,0:T(8,128)S(1)} custom-call(s32[2]{0:T(128)S(1)} %add_convert_fusion.edge, bf16[128,1024]{1,0:T(8,128)(2,1)S(1)} %bitcast.29, bf16[128,1024]{1,0:T(8,128)(2,1)S(1)} %bitcast.19, bf16[128,1024]{1,0:T(8,128)(2,1)S(1)} %bitcast.21, bf16[128,2048]{1,0:T(8,128)(2,1)S(1)} %collective-permute-done.pk.pv, ...), custom_call_target="tpu_custom_call" | custom-call | tf_op jit(solution)/shard_map/light/pallas_call | solution.py:156
  117.8 1.5 %join.1 = bf16[128,1024]{1,0:T(8,128)(2,1)} custom-call(s32[1]{0:T(128)} %bitcast.chosen, f32[128,1024]{1,0:T(8,128)S(1)} %light.1, bf16[16,64,128]{2,1,0:T(8,128)(2,1)S(1)} %all-to-all-done.2.heavy), custom_call_target="tpu_custom_call" | custom-call | tf_op jit(solution)/shard_map/join/pallas_call | solution.py:180
  119.3 1.0 copy.13
  (23 shorter events, 2.0 us)
Async XLA Ops:
  0.6 1.0 copy-start.3
  1.6 0.9 copy-start.4
  2.5 0.9 copy-start.5
  3.5 0.8 copy-start.7
  23.8 16.9 %all-to-all-start = ((bf16[16,192,128]{2,1,0:T(8,128)(2,1)}), bf16[16,192,128]{2,1,0:T(8,128)(2,1)S(1)}, u32[]{:S(2)}, u32[]{:S(2)}) async-start(bf16[16,192,128]{2,1,0:T(8,128)(2,1)} %get-tuple-element.4), calls=%async_computation | async-start | bytes 1572864 | tf_op jit(solution)/shard_map/all_to_all | solution.py:281
  27.4 0.7 copy-start.8
  28.7 38.1 %copy-start = (bf16[1,512,1024]{2,1,0:T(8,128)(2,1)S(1)}, bf16[1,512,1024]{2,1,0:T(8,128)(2,1)}, u32[]{:S(2)}) copy-start(bf16[1,512,1024]{2,1,0:T(8,128)(2,1)} %param.17) | copy-start | bytes 3145732
  28.7 12.0 %collective-permute-start.2 = (bf16[1024,128]{1,0:T(8,128)(2,1)S(1)}, bf16[1024,128]{1,0:T(8,128)(2,1)S(1)}, u32[]{:S(2)}, u32[]{:S(2)}) collective-permute-start(bf16[1024,128]{1,0:T(8,128)(2,1)S(1)} %bitcast.22), channel_id=1, source_target_pairs={{0,16},{16,32},{32,48},{48,0},{1,17},{17,33},{33,49},{49,1},{2,18}... | collective-permute-start | bytes 786440 | tf_op jit(solution)/shard_map/ppermute | solution.py:266
  30.7 10.7 %collective-permute-start.3 = (bf16[1024,128]{1,0:T(8,128)(2,1)S(1)}, bf16[1024,128]{1,0:T(8,128)(2,1)S(1)}, u32[]{:S(2)}, u32[]{:S(2)}) collective-permute-start(bf16[1024,128]{1,0:T(8,128)(2,1)S(1)} %bitcast.23), channel_id=1, source_target_pairs={{0,32},{16,48},{32,0},{48,16},{1,33},{17,49},{33,1},{49,17},{2,34}... | collective-permute-start | bytes 786440 | tf_op jit(solution)/shard_map/ppermute | solution.py:266
  31.9 12.1 %collective-permute-start.4 = (bf16[1024,128]{1,0:T(8,128)(2,1)S(1)}, bf16[1024,128]{1,0:T(8,128)(2,1)S(1)}, u32[]{:S(2)}, u32[]{:S(2)}) collective-permute-start(bf16[1024,128]{1,0:T(8,128)(2,1)S(1)} %bitcast.24), channel_id=1, source_target_pairs={{0,48},{16,0},{32,16},{48,32},{1,49},{17,1},{33,17},{49,33},{2,50}... | collective-permute-start | bytes 786440 | tf_op jit(solution)/shard_map/ppermute | solution.py:266
  59.9 19.8 %all-to-all-start.2 = ((bf16[16,64,128]{2,1,0:T(8,128)(2,1)}), bf16[16,64,128]{2,1,0:T(8,128)(2,1)S(1)}, u32[]{:S(2)}, u32[]{:S(2)}) async-start(bf16[16,64,128]{2,1,0:T(8,128)(2,1)} %heavy.1), calls=%async_computation.2 | async-start | bytes 524288 | tf_op jit(solution)/shard_map/all_to_all | solution.py:299
  68.6 6.4 %collective-permute-start.5 = (bf16[512,128]{1,0:T(8,128)(2,1)S(1)}, bf16[512,128]{1,0:T(8,128)(2,1)S(1)}, u32[]{:S(2)}, u32[]{:S(2)}) collective-permute-start(bf16[512,128]{1,0:T(8,128)(2,1)S(1)} %decode.1.a), channel_id=1, source_target_pairs={{0,16},{16,32},{32,48},{48,0},{1,17},{17,33},{33,49},{49,1},{2,18}... | collective-permute-start | bytes 393224 | tf_op jit(solution)/shard_map/ppermute | solution.py:266
  69.6 6.9 %collective-permute-start.6 = (bf16[512,128]{1,0:T(8,128)(2,1)S(1)}, bf16[512,128]{1,0:T(8,128)(2,1)S(1)}, u32[]{:S(2)}, u32[]{:S(2)}) collective-permute-start(bf16[512,128]{1,0:T(8,128)(2,1)S(1)} %decode.1.a), channel_id=1, source_target_pairs={{0,32},{16,48},{32,0},{48,16},{1,33},{17,49},{33,1},{49,17},{2,34}... | collective-permute-start | bytes 393224 | tf_op jit(solution)/shard_map/ppermute | solution.py:266
  71.5 6.2 %collective-permute-start.7 = (bf16[512,128]{1,0:T(8,128)(2,1)S(1)}, bf16[512,128]{1,0:T(8,128)(2,1)S(1)}, u32[]{:S(2)}, u32[]{:S(2)}) collective-permute-start(bf16[512,128]{1,0:T(8,128)(2,1)S(1)} %decode.1.a), channel_id=1, source_target_pairs={{0,48},{16,0},{32,16},{48,32},{1,49},{17,1},{33,17},{49,33},{2,50}... | collective-permute-start | bytes 393224 | tf_op jit(solution)/shard_map/ppermute | solution.py:266
  79.7 7.2 %copy-start.1 = (bf16[1,128,1024]{2,1,0:T(8,128)(2,1)S(1)}, bf16[1,128,1024]{2,1,0:T(8,128)(2,1)}, u32[]{:S(2)}) copy-start(bf16[1,128,1024]{2,1,0:T(8,128)(2,1)} %param.11) | copy-start | bytes 786436
  79.7 7.2 %copy-start.2 = (bf16[1,128,1024]{2,1,0:T(8,128)(2,1)S(1)}, bf16[1,128,1024]{2,1,0:T(8,128)(2,1)}, u32[]{:S(2)}) copy-start(bf16[1,128,1024]{2,1,0:T(8,128)(2,1)} %param.12) | copy-start | bytes 786436
  79.7 39.6 %all-to-all-start.3 = ((bf16[16,32,1024]{2,1,0:T(8,128)(2,1)}), bf16[16,32,1024]{2,1,0:T(8,128)(2,1)S(1)}, u32[]{:S(2)}, u32[]{:S(2)}) async-start(bf16[16,32,1024]{2,1,0:T(8,128)(2,1)} %meet.1), calls=%async_computation.3 | async-start | bytes 2097152 | tf_op jit(solution)/shard_map/all_to_all | solution.py:296
  86.9 25.2 %copy-start.6 = (bf16[1,128,1024]{2,1,0:T(8,128)(2,1)S(1)}, bf16[1,128,1024]{2,1,0:T(8,128)(2,1)}, u32[]{:S(2)}) copy-start(bf16[1,128,1024]{2,1,0:T(8,128)(2,1)} %param.10) | copy-start | bytes 786436
  87.8 24.4 %collective-permute-start = (bf16[128,2048]{1,0:T(8,128)(2,1)}, bf16[128,2048]{1,0:T(8,128)(2,1)S(1)}, u32[]{:S(2)}, u32[]{:S(2)}) collective-permute-start(bf16[128,2048]{1,0:T(8,128)(2,1)} %pad_maximum_fusion), channel_id=1, source_target_pairs={{0,1},{1,2},{2,3},{3,4},{4,5},{5,6},{6,7},{7,8},{8,9},{9,10},{10,1... | collective-permute-start | bytes 1572872 | tf_op jit(solution)/shard_map/ppermute | solution.py:285
  91.6 20.6 %collective-permute-start.1 = (bf16[128,2048]{1,0:T(8,128)(2,1)}, bf16[128,2048]{1,0:T(8,128)(2,1)S(1)}, u32[]{:S(2)}, u32[]{:S(2)}) collective-permute-start(bf16[128,2048]{1,0:T(8,128)(2,1)} %pad_maximum_fusion), channel_id=1, source_target_pairs={{1,0},{2,1},{3,2},{4,3},{5,4},{6,5},{7,6},{8,7},{9,8},{10,9},{11,1... | collective-permute-start | bytes 1572872 | tf_op jit(solution)/shard_map/ppermute | solution.py:286
  97.8 0.7 copy-start.9

commit v2 on v1

v2 whole, which is shorter than its diff:
```python
import jax
import jax.numpy as jnp
from jax import lax
from jax.experimental import pallas as pl
from jax.experimental.pallas import tpu as pltpu
from jax.sharding import PartitionSpec as P

HEAD = 64
LANES = 2 * HEAD
BLOCK = 128
KGRP = 8
HALF = BLOCK // 2
SCALE = HEAD**-0.5
LOG2E = 1.4426950408889634
TOKENS = ("coarse", "fine")
VMEM = 48 * 1024 * 1024

f32 = jnp.float32
bf16 = jnp.bfloat16


def params(**kw):
    return pltpu.CompilerParams(vmem_limit_bytes=VMEM, **kw)


def lane_ids(shape):
    return lax.broadcasted_iota(jnp.int32, shape, len(shape) - 1)


def nt(a, b):
    return lax.dot_general(a, b, (((1,), (1,)), ((), ())), preferred_element_type=f32)


def nn(a, b):
    return jnp.dot(a, b, preferred_element_type=f32)


def pack_kernel(q_hbm, k_hbm, v_hbm, out, q, k, v, sem):
    copies = [
        pltpu.make_async_copy(src, dst, sem.at[n])
        for n, (src, dst) in enumerate(((k_hbm, k), (v_hbm, v), (q_hbm, q)))
    ]
    for c in copies:
        c.start()
    heads = out.shape[0]
    copies[0].wait()
    copies[1].wait()
    for h in range(heads):
        cols = slice(h * HEAD, (h + 1) * HEAD)
        out[h, :BLOCK] = jnp.concatenate([k[:, cols], v[:, cols]], axis=1)
    copies[2].wait()
    for h in range(heads):
        qh = q[:, h * HEAD : (h + 1) * HEAD]
        out[h, BLOCK:] = jnp.concatenate([qh[:HALF], qh[HALF:]], axis=1)


def pack(q, k, v):
    heads = q.shape[1] // HEAD
    hbm = pl.BlockSpec(memory_space=pltpu.HBM)
    return pl.pallas_call(
        pack_kernel,
        in_specs=[hbm] * 3,
        out_shape=jax.ShapeDtypeStruct((heads, BLOCK + HALF, LANES), bf16),
        scratch_shapes=[pltpu.VMEM(x.shape, bf16) for x in (q, k, v)]
        + [pltpu.SemaphoreType.DMA((3,))],
        compiler_params=params(),
        name="pack",
    )(q, k, v)


def pick_kernel(ids, kv, out):
    group = lax.axis_index("coarse")
    for s in range(KGRP):
        out[s] = kv[ids[0, group * KGRP + s] - group * kv.shape[0], :BLOCK]


def pick(ids, kv):
    return pl.pallas_call(
        pick_kernel,
        out_shape=jax.ShapeDtypeStruct((KGRP, BLOCK, LANES), bf16),
        in_specs=[pl.BlockSpec(memory_space=pltpu.SMEM), pl.BlockSpec(memory_space=pltpu.VMEM)],
        compiler_params=params(),
        name="pick",
    )(ids, kv)


def with_ones(kv):
    return jnp.where(lane_ids(kv.shape) < HEAD, jnp.ones_like(kv), kv)


def summed(q, keys, values):
    peak = total = None
    for k, v in zip(keys, values):
        s = nt(q, k)
        top = s.max(axis=1, keepdims=True)
        top = top if peak is None else jnp.maximum(peak, top)
        o = nn(jnp.exp2((s - top) * (SCALE * LOG2E)).astype(bf16), v)
        total = o if peak is None else total * jnp.exp2((peak - top) * (SCALE * LOG2E)) + o
        peak = top
    return total, peak


def heavy_kernel(part, q, kv0, kv1, kv2, kv3, *rest):
    out = rest[-1]
    rows = q.shape[0] * HALF
    both = q[:, BLOCK:].reshape(rows, LANES)
    zero = jnp.zeros((rows, HEAD), bf16)
    keys = [kv[...] for kv in (kv0, kv1, kv2, kv3)]
    vals = [with_ones(k) for k in keys]
    mine = jnp.concatenate([both[:, part * HEAD : (part + 1) * HEAD], zero], axis=1)
    o, _ = summed(mine, keys, vals)
    ratio = (o / pltpu.roll(o, HEAD, 1))[:, HEAD:].astype(bf16)
    if part == 0:
        out[...] = ratio.reshape(out.shape)
    else:
        out[...] = jnp.concatenate([rest[0][...].reshape(rows, HEAD), ratio], axis=1).reshape(out.shape)


def heavy_attend(part, q_kv, kvs, *first):
    blocks = q_kv.shape[0]
    lanes = (part + 1) * HEAD
    return pl.pallas_call(
        lambda *refs: heavy_kernel(part, *refs),
        out_shape=jax.ShapeDtypeStruct((blocks, HALF, lanes), bf16),
        compiler_params=params(),
        cost_estimate=pl.CostEstimate(flops=5_000_000_000, transcendentals=4_000_000, bytes_accessed=2_000_000),
        name=f"heavy{part}",
    )(q_kv, *kvs, *first)


def light_kernel(q, k, v, prev, after, out):
    here = lax.axis_index(TOKENS)
    last = lax.axis_size(TOKENS) - 1
    rows, width = q.shape
    low = lane_ids((rows, LANES)) < HEAD
    i = lax.broadcasted_iota(jnp.int32, (2 * rows, BLOCK), 0) % rows
    j = lax.broadcasted_iota(jnp.int32, (2 * rows, BLOCK), 1)
    sees_prev = (j > i) & (here > 0)
    sees_next = (j < i) & (here < last)
    for p in range(width // LANES):
        c = slice(p * LANES, (p + 1) * LANES)
        cv = slice(width + p * LANES, width + (p + 1) * LANES)
        qq = q[:, c]
        zero = jnp.zeros_like(qq)
        two = jnp.concatenate([jnp.where(low, qq, zero), jnp.where(low, zero, qq)], axis=0)
        own = nt(two, k[:, c])
        left = jnp.where(sees_prev, nt(two, prev[:, c]), f32(-1e30))
        right = jnp.where(sees_next, nt(two, after[:, c]), f32(-1e30))
        peak = jnp.maximum(jnp.maximum(own, left), right).max(axis=1, keepdims=True)
        po, pp, pn = (jnp.exp2((s - peak) * (SCALE * LOG2E)) for s in (own, left, right))
        total = (po + pp + pn).sum(axis=1, keepdims=True)
        o = nn(po.astype(bf16), v[:, c]) + nn(pp.astype(bf16), prev[:, cv]) + nn(pn.astype(bf16), after[:, cv])
        o = o / total
        out[:, c] = jnp.where(low, o[:rows], o[rows:])


def light_attend(q, k, v, prev, after):
    return pl.pallas_call(
        light_kernel,
        out_shape=jax.ShapeDtypeStruct(q.shape, f32),
        compiler_params=params(),
        cost_estimate=pl.CostEstimate(flops=3_000_000_000, transcendentals=800_000, bytes_accessed=2_000_000),
        name="light",
    )(q, k, v, prev, after)


def join_kernel(ids, light, heavy, out):
    here = lax.axis_index(TOKENS)
    count = jnp.int32(0)
    for n in range(ids.shape[1]):
        count = count + jnp.where(ids[0, n] == here, 1, 0)
    scale = count.astype(f32)
    for p in range(heavy.shape[0] // 2):
        e, o = heavy[2 * p], heavy[2 * p + 1]
        for n in range(2):
            rows, lanes = slice(n * HALF, (n + 1) * HALF), slice(n * HEAD, (n + 1) * HEAD)
            cols = slice(p * LANES, (p + 1) * LANES)
            both = jnp.concatenate([e[:, lanes], o[:, lanes]], axis=1)
            out[rows, cols] = (light[rows, cols] + both.astype(f32) * scale).astype(bf16)


def join(ids, light, heavy):
    vmem = pl.BlockSpec(memory_space=pltpu.VMEM)
    return pl.pallas_call(
        join_kernel,
        in_specs=[pl.BlockSpec(memory_space=pltpu.SMEM), vmem, vmem],
        out_shape=jax.ShapeDtypeStruct(light.shape, bf16),
        compiler_params=params(),
        name="join",
    )(ids, light, heavy)


def decode_kernel(q_hbm, e0, e1, e2, e3, out, q, sem):
    rows, width = q.shape
    at = pl.multiple_of(lax.axis_index("fine") * rows, rows)
    copy = pltpu.make_async_copy(q_hbm.at[pl.ds(at, rows)], q, sem)
    copy.start()
    copy.wait()
    zero = jnp.zeros((rows, HEAD), bf16)
    stack = jnp.concatenate(
        [
            jnp.concatenate([q[:, h * HEAD : (h + 1) * HEAD], zero], axis=1)
            for h in range(width // HEAD)
        ],
        axis=0,
    )
    keys = [e[...] for e in (e0, e1, e2, e3)]
    vals = [with_ones(k) for k in keys]
    total, peak = summed(stack, keys, vals)
    lane = lane_ids(total.shape)
    level = peak * SCALE + jnp.log(total)
    hi = level.astype(bf16).astype(f32)
    mid = (level - hi).astype(bf16).astype(f32)
    least = level - hi - mid
    parts = jnp.where(lane < 16, hi, jnp.where(lane < 32, mid, least))
    ratio = total / pltpu.roll(total, HEAD, 1)
    out[...] = jnp.where(lane < HEAD, parts, ratio).astype(bf16)


def decode(q, enc, rows):
    width = q.shape[1]
    vmem = pl.BlockSpec(memory_space=pltpu.VMEM)
    return pl.pallas_call(
        decode_kernel,
        in_specs=[pl.BlockSpec(memory_space=pltpu.HBM)] + [vmem] * len(enc),
        out_shape=jax.ShapeDtypeStruct((rows * (width // HEAD), LANES), bf16),
        scratch_shapes=[pltpu.VMEM((rows, width), bf16), pltpu.SemaphoreType.DMA(())],
        compiler_params=params(),
        cost_estimate=pl.CostEstimate(flops=1_000_000_000, transcendentals=1_000_000, bytes_accessed=1_000_000),
        name="decode",
    )(q, *enc)


def meet_kernel(a, b, c, d, out):
    parts = [x[...].astype(f32) for x in (a, b, c, d)]
    levels = [x[:, 0:1] + x[:, 16:17] + x[:, 32:33] for x in parts]
    peak = jnp.maximum(jnp.maximum(levels[0], levels[1]), jnp.maximum(levels[2], levels[3]))
    scales = [jnp.exp(n - peak) for n in levels]
    total = scales[0] + scales[1] + scales[2] + scales[3]
    value = parts[0] * scales[0]
    for x, s in zip(parts[1:], scales[1:]):
        value = value + x * s
    value = (value / total).astype(bf16)
    copies, rows, width = out.shape
    for p in range(width // LANES):
        e = value[2 * p * rows : (2 * p + 1) * rows, HEAD:]
        o = value[(2 * p + 1) * rows : (2 * p + 2) * rows, HEAD:]
        both = jnp.concatenate([e, o], axis=1)
        for n in range(copies):
            out[n, :, p * LANES : (p + 1) * LANES] = both


def meet(parts, copies, rows, width):
    return pl.pallas_call(
        meet_kernel,
        out_shape=jax.ShapeDtypeStruct((copies, rows, width), bf16),
        compiler_params=params(),
        name="meet",
    )(*parts)


def around(value, axis, stride=1, ring=None):
    size = lax.axis_size(axis)
    ring = ring or size

    def to(i, d):
        at = i // stride % ring
        return i + ((at + d) % ring - at) * stride

    return [lax.ppermute(value, axis, [(i, to(i, d)) for i in range(size)]) for d in range(1, ring)]


def after_all(value, *others):
    return lax.optimization_barrier((value, others))[0]


def local(
    q_light, k_light, v_light, q_heavy, k_heavy, v_heavy, enc_kv, dec_queries, query_ids, key_ids
):
    n_seq = lax.axis_size(TOKENS)
    n_fine = lax.axis_size("fine")
    side = 4
    width = q_light.shape[2]

    chunks = pack(q_heavy[0], k_heavy[0], v_heavy[0])
    group = lax.all_to_all(chunks, "fine", 0, 0, tiled=True)

    row = jnp.concatenate([enc_kv[0]] + around(enc_kv[0], "fine", 1, side), axis=0)
    enc = [row] + around(row, "fine", side, n_fine // side)
    dec_rows = dec_queries.shape[1] // n_fine
    part = decode(dec_queries[0], enc, dec_rows)
    parts = around(part, "coarse")

    own = pick(key_ids, after_all(group, part)).reshape(KGRP * BLOCK, LANES)
    routed = [own] + around(own, "coarse")

    shares = meet([after_all(part, own)] + parts, n_fine, dec_rows, width)
    decoded = lax.all_to_all(shares, "fine", 0, 0, tiled=True)

    light_kv = jnp.concatenate([k_light[0], v_light[0]], axis=1)
    light_kv = after_all(light_kv, own)
    up = [(i, i + 1) for i in range(n_seq - 1)]
    prev = lax.ppermute(light_kv, TOKENS, up)
    after = lax.ppermute(light_kv, TOKENS, [(b, a) for a, b in up])

    first = heavy_attend(0, after_all(group, shares), routed)
    heavy = heavy_attend(1, after_all(group, prev, after), routed, first)
    q_light = after_all(q_light, heavy)
    heavy, decoded = lax.optimization_barrier((heavy, decoded))
    heavy = lax.all_to_all(heavy, "fine", 0, 0, tiled=True)

    light = light_attend(q_light[0], k_light[0], v_light[0], prev, after)
    encoded = join(query_ids, light, heavy)[None]
    return (encoded, decoded.reshape(1, -1, width))


def solution(mesh):
    seq = P("doc", TOKENS, None)
    whole = P("doc", None, None)
    return jax.shard_map(
        local,
        mesh=mesh,
        in_specs=(seq,) * 7 + (whole, P("doc", None), P("doc", None)),
        out_specs=(seq, whole),
        check_vma=False,
    )
```

time: 121 us -> 104 us (0.86)
  the two profiles are of different devices: /device:TPU:32 before, /device:TPU:0 now
where the time goes in v2:
time: 104 us; the launch traced here: 103 us
  starting transfers between devices  49.3 us (47%)
  waiting for transfers between devices  25.5 us (25%)
  Pallas kernels  21.4 us (21%)
  local copies, waits for them, and re-layouts  5.14 us (5%)
    ppermute x12, starting transfers between devices, around(): lax.ppermute(value, axis, [(i, to(i, d)) for i in range(size)])  21 us
    ppermute x12, waiting for transfers between devices, around(): lax.ppermute(value, axis, [(i, to(i, d)) for i in range(size)])  18.4 us
    pallas_call x2, Pallas kernels, heavy_attend(): pl.pallas_call(lambda *refs: heavy_kernel(part, *refs), out_shape=jax.Sha...  12.8 us
    all_to_all x1, starting transfers between devices, local(): heavy = lax.all_to_all(heavy, 'fine', 0, 0, tiled=True)  8.98 us
    all_to_all x1, starting transfers between devices, local(): decoded = lax.all_to_all(shares, 'fine', 0, 0, tiled=True)  8.02 us
    all_to_all x1, starting transfers between devices, local(): group = lax.all_to_all(chunks, 'fine', 0, 0, tiled=True)  7.26 us
    all_to_all x1, waiting for transfers between devices, local(): heavy = lax.all_to_all(heavy, 'fine', 0, 0, tiled=True)  7.13 us
    unnamed x21, local copies, waits for them, and re-layouts  5.14 us
  transfers between devices with their start and end apart: 17, of which 8 were waited for; matrix products, arithmetic and copies ran while one was open for 1% of the time, Pallas kernels for 18%

profile of v2, /device:TPU:0, one launch (start us, length us, event | category | flops | bytes accessed | tf_op | source)
XLA Modules:
  0.0 103.1 jit_solution(16634393405445940419)
XLA Ops:
  0.6 0.9 copy-done
  1.6 0.9 copy-done.1
  2.5 0.9 copy-done.2
  3.5 1.3 %pack.1 = bf16[16,192,128]{2,1,0:T(8,128)(2,1)} custom-call(bf16[128,1024]{1,0:T(8,128)(2,1)S(1)} %bitcast.11, bf16[128,1024]{1,0:T(8,128)(2,1)S(1)} %bitcast.12, bf16[128,1024]{1,0:T(8,128)(2,1)S(1)} %bitcast.13), custom_call_target="tpu_custom_call" | custom-call | tf_op jit(solution)/shard_map/pack/pallas_call | solution.py:60
  4.8 7.3 %all-to-all-start = ((bf16[16,192,128]{2,1,0:T(8,128)(2,1)}), bf16[16,192,128]{2,1,0:T(8,128)(2,1)S(1)}, u32[]{:S(2)}, u32[]{:S(2)}) async-start(bf16[16,192,128]{2,1,0:T(8,128)(2,1)} %pack.1), calls=%async_computation | async-start | bytes 1572864 | tf_op jit(solution)/shard_map/all_to_all | solution.py:286
  12.1 3.2 %collective-permute-start.2 = (bf16[128,128]{1,0:T(8,128)(2,1)S(1)}, bf16[128,128]{1,0:T(8,128)(2,1)S(1)}, u32[]{:S(2)}, u32[]{:S(2)}) collective-permute-start(bf16[128,128]{1,0:T(8,128)(2,1)S(1)} %bitcast.26), channel_id=1, source_target_pairs={{0,3},{1,0},{2,1},{3,2},{4,7},{5,4},{6,5},{7,6},{8,11},{9,8},{10,9... | collective-permute-start | bytes 98312 | tf_op jit(solution)/shard_map/ppermute | solution.py:270
  17.0 6.9 %collective-permute-done.2 = bf16[128,128]{1,0:T(8,128)(2,1)S(1)} collective-permute-done((bf16[128,128]{1,0:T(8,128)(2,1)S(1)}, bf16[128,128]{1,0:T(8,128)(2,1)S(1)}, u32[]{:S(2)}, u32[]{:S(2)}) %collective-permute-start.2) | collective-permute-done | bytes 32800 | tf_op jit(solution)/shard_map/ppermute | solution.py:270
  23.9 1.5 %collective-permute-done.1 = bf16[128,128]{1,0:T(8,128)(2,1)S(1)} collective-permute-done((bf16[128,128]{1,0:T(8,128)(2,1)S(1)}, bf16[128,128]{1,0:T(8,128)(2,1)S(1)}, u32[]{:S(2)}, u32[]{:S(2)}) %collective-permute-start.1) | collective-permute-done | bytes 32800 | tf_op jit(solution)/shard_map/ppermute | solution.py:270
  25.4 1.5 %collective-permute-start.3 = (bf16[512,128]{1,0:T(8,128)(2,1)S(1)}, bf16[512,128]{1,0:T(8,128)(2,1)S(1)}, u32[]{:S(2)}, u32[]{:S(2)}) collective-permute-start(bf16[512,128]{1,0:T(8,128)(2,1)S(1)} %pad_maximum_fusion.1.e0), channel_id=1, source_target_pairs={{0,4},{1,5},{2,6},{3,7},{4,8},{5,9},{6,10},{7,11},{8,12},{9,13},{1... | collective-permute-start | bytes 393224 | tf_op jit(solution)/shard_map/ppermute | solution.py:270
  26.9 2.7 %collective-permute-start.4 = (bf16[512,128]{1,0:T(8,128)(2,1)S(1)}, bf16[512,128]{1,0:T(8,128)(2,1)S(1)}, u32[]{:S(2)}, u32[]{:S(2)}) collective-permute-start(bf16[512,128]{1,0:T(8,128)(2,1)S(1)} %pad_maximum_fusion.1.e0), channel_id=1, source_target_pairs={{0,8},{1,9},{2,10},{3,11},{4,12},{5,13},{6,14},{7,15},{8,0},{9,1},... | collective-permute-start | bytes 393224 | tf_op jit(solution)/shard_map/ppermute | solution.py:270
  29.6 1.5 %collective-permute-start.5 = (bf16[512,128]{1,0:T(8,128)(2,1)S(1)}, bf16[512,128]{1,0:T(8,128)(2,1)S(1)}, u32[]{:S(2)}, u32[]{:S(2)}) collective-permute-start(bf16[512,128]{1,0:T(8,128)(2,1)S(1)} %pad_maximum_fusion.1.e0), channel_id=1, source_target_pairs={{0,12},{1,13},{2,14},{3,15},{4,0},{5,1},{6,2},{7,3},{8,4},{9,5},{1... | collective-permute-start | bytes 393224 | tf_op jit(solution)/shard_map/ppermute | solution.py:270
  31.1 2.0 %collective-permute-done.3.e1 = bf16[512,128]{1,0:T(8,128)(2,1)S(1)} collective-permute-done((bf16[512,128]{1,0:T(8,128)(2,1)S(1)}, bf16[512,128]{1,0:T(8,128)(2,1)S(1)}, u32[]{:S(2)}, u32[]{:S(2)}) %collective-permute-start.3) | collective-permute-done | bytes 131104 | tf_op jit(solution)/shard_map/ppermute | solution.py:270
  33.1 1.5 %collective-permute-done.4.e2 = bf16[512,128]{1,0:T(8,128)(2,1)S(1)} collective-permute-done((bf16[512,128]{1,0:T(8,128)(2,1)S(1)}, bf16[512,128]{1,0:T(8,128)(2,1)S(1)}, u32[]{:S(2)}, u32[]{:S(2)}) %collective-permute-start.4) | collective-permute-done | bytes 131104 | tf_op jit(solution)/shard_map/ppermute | solution.py:270
  34.7 1.8 %decode.1.a = bf16[512,128]{1,0:T(8,128)(2,1)S(1)} custom-call(bf16[512,1024]{1,0:T(8,128)(2,1)S(1)} %bitcast.23, bf16[512,128]{1,0:T(8,128)(2,1)S(1)} %pad_maximum_fusion.1.e0, bf16[512,128]{1,0:T(8,128)(2,1)S(1)} %collective-permute-done.3.e1, bf16[512,128]{1,0:T(8,128)(2,1)S(1)} %collective-permute-done.4.e2, bf16[512,128]{1,0:T(8,128)(2,1)S(1)} %collective-permute-done.5.e3), custom_call_target="tpu_custom_call" | custom-call | flops 1000000000 | bytes 1000000 | tf_op jit(solution)/shard_map/decode/pallas_call | solution.py:223
  36.5 2.0 %collective-permute-start.11 = (bf16[512,128]{1,0:T(8,128)(2,1)S(1)}, bf16[512,128]{1,0:T(8,128)(2,1)S(1)}, u32[]{:S(2)}, u32[]{:S(2)}) collective-permute-start(bf16[512,128]{1,0:T(8,128)(2,1)S(1)} %decode.1.a), channel_id=1, source_target_pairs={{0,16},{16,32},{32,48},{48,0},{1,17},{17,33},{33,49},{49,1},{2,18}... | collective-permute-start | bytes 393224 | tf_op jit(solution)/shard_map/ppermute | solution.py:270
  38.4 3.6 %collective-permute-start.12 = (bf16[512,128]{1,0:T(8,128)(2,1)S(1)}, bf16[512,128]{1,0:T(8,128)(2,1)S(1)}, u32[]{:S(2)}, u32[]{:S(2)}) collective-permute-start(bf16[512,128]{1,0:T(8,128)(2,1)S(1)} %decode.1.a), channel_id=1, source_target_pairs={{0,32},{16,48},{32,0},{48,16},{1,33},{17,49},{33,1},{49,17},{2,34}... | collective-permute-start | bytes 393224 | tf_op jit(solution)/shard_map/ppermute | solution.py:270
  42.0 1.0 collective-permute-start.13
  43.6 1.1 %collective-permute-start.8 = (bf16[1024,128]{1,0:T(8,128)(2,1)S(1)}, bf16[1024,128]{1,0:T(8,128)(2,1)S(1)}, u32[]{:S(2)}, u32[]{:S(2)}) collective-permute-start(bf16[1024,128]{1,0:T(8,128)(2,1)S(1)} %bitcast.18), channel_id=1, source_target_pairs={{0,16},{16,32},{32,48},{48,0},{1,17},{17,33},{33,49},{49,1},{2,18}... | collective-permute-start | bytes 786440 | tf_op jit(solution)/shard_map/ppermute | solution.py:270
  45.2 2.3 %collective-permute-start.10 = (bf16[1024,128]{1,0:T(8,128)(2,1)S(1)}, bf16[1024,128]{1,0:T(8,128)(2,1)}, u32[]{:S(2)}, u32[]{:S(2)}) collective-permute-start(bf16[1024,128]{1,0:T(8,128)(2,1)S(1)} %bitcast.20), channel_id=1, source_target_pairs={{0,48},{16,0},{32,16},{48,32},{1,49},{17,1},{33,17},{49,33},{2,50}... | collective-permute-start | bytes 786440 | tf_op jit(solution)/shard_map/ppermute | solution.py:270
  48.3 1.0 collective-permute-done.12.c
  49.3 2.7 %collective-permute-start.6 = (bf16[128,2048]{1,0:T(8,128)(2,1)}, bf16[128,2048]{1,0:T(8,128)(2,1)S(1)}, u32[]{:S(2)}, u32[]{:S(2)}) collective-permute-start(bf16[128,2048]{1,0:T(8,128)(2,1)} %pad_maximum_fusion), channel_id=1, source_target_pairs={{0,1},{1,2},{2,3},{3,4},{4,5},{5,6},{6,7},{7,8},{8,9},{9,10},{10,1... | collective-permute-start | bytes 1572872 | tf_op jit(solution)/shard_map/ppermute | solution.py:303
  52.1 1.3 %collective-permute-start.7 = (bf16[128,2048]{1,0:T(8,128)(2,1)}, bf16[128,2048]{1,0:T(8,128)(2,1)S(1)}, u32[]{:S(2)}, u32[]{:S(2)}) collective-permute-start(bf16[128,2048]{1,0:T(8,128)(2,1)} %pad_maximum_fusion), channel_id=1, source_target_pairs={{1,0},{2,1},{3,2},{4,3},{5,4},{6,5},{7,6},{8,7},{9,8},{10,9},{11,1... | collective-permute-start | bytes 1572872 | tf_op jit(solution)/shard_map/ppermute | solution.py:304
  53.4 2.0 %meet.1 = bf16[16,32,1024]{2,1,0:T(8,128)(2,1)} custom-call(bf16[512,128]{1,0:T(8,128)(2,1)S(1)} %decode.1.a, bf16[512,128]{1,0:T(8,128)(2,1)S(1)} %collective-permute-done.11.b, bf16[512,128]{1,0:T(8,128)(2,1)S(1)} %collective-permute-done.12.c, bf16[512,128]{1,0:T(8,128)(2,1)S(1)} %collective-permute-done.13.d), custom_call_target="tpu_custom_call" | custom-call | tf_op jit(solution)/shard_map/meet/pallas_call | solution.py:254
  55.4 8.0 %all-to-all-start.1 = ((bf16[16,32,1024]{2,1,0:T(8,128)(2,1)}), bf16[16,32,1024]{2,1,0:T(8,128)(2,1)}, u32[]{:S(2)}, u32[]{:S(2)}) async-start(bf16[16,32,1024]{2,1,0:T(8,128)(2,1)} %meet.1), calls=%async_computation.1 | async-start | bytes 2097152 | tf_op jit(solution)/shard_map/all_to_all | solution.py:298
  63.5 5.4 %collective-permute-done.9.refs_3_ = bf16[1024,128]{1,0:T(8,128)(2,1)} collective-permute-done((bf16[1024,128]{1,0:T(8,128)(2,1)S(1)}, bf16[1024,128]{1,0:T(8,128)(2,1)}, u32[]{:S(2)}, u32[]{:S(2)}) %collective-permute-start.9) | collective-permute-done | bytes 262176 | tf_op jit(solution)/shard_map/ppermute | solution.py:270
  68.9 6.1 %heavy0.1.refs_5_ = bf16[16,64,64]{2,1,0:T(8,128)(2,1)S(1)} custom-call(bf16[16,192,128]{2,1,0:T(8,128)(2,1)S(1)} %all-to-all-done.kv.refs_0_, bf16[1024,128]{1,0:T(8,128)(2,1)S(1)} %bitcast.21, bf16[1024,128]{1,0:T(8,128)(2,1)S(1)} %collective-permute-done.8.refs_2_, bf16[1024,128]{1,0:T(8,128)(2,1)} %collective-permute-done.9.refs_3_, ...), custom_call_target="tpu_custom_call" | custom-call | flops 5000000000 | bytes 2000000 | tf_op jit(solution)/shard_map/heavy0/pallas_call | solution.py:122
  75.0 6.7 %heavy1.1 = bf16[16,64,128]{2,1,0:T(8,128)(2,1)} custom-call(bf16[16,192,128]{2,1,0:T(8,128)(2,1)S(1)} %all-to-all-done.kv.refs_0_, bf16[1024,128]{1,0:T(8,128)(2,1)S(1)} %bitcast.22, bf16[1024,128]{1,0:T(8,128)(2,1)S(1)} %collective-permute-done.8.refs_2_, bf16[1024,128]{1,0:T(8,128)(2,1)} %collective-permute-done.9.refs_3_, ...), custom_call_target="tpu_custom_call" | custom-call | flops 5000000000 | bytes 2000000 | tf_op jit(solution)/shard_map/heavy1/pallas_call | solution.py:122
  81.7 9.0 %all-to-all-start.2 = ((bf16[16,64,128]{2,1,0:T(8,128)(2,1)}), bf16[16,64,128]{2,1,0:T(8,128)(2,1)S(1)}, u32[]{:S(2)}, u32[]{:S(2)}) async-start(bf16[16,64,128]{2,1,0:T(8,128)(2,1)} %heavy1.1), calls=%async_computation.2 | async-start | bytes 524288 | tf_op jit(solution)/shard_map/all_to_all | solution.py:310
  90.7 1.5 %light.1 = f32[128,1024]{1,0:T(8,128)S(1)} custom-call(bf16[128,1024]{1,0:T(8,128)(2,1)S(1)} %bitcast.24, bf16[128,1024]{1,0:T(8,128)(2,1)S(1)} %bitcast.15, bf16[128,1024]{1,0:T(8,128)(2,1)S(1)} %bitcast.17, bf16[128,2048]{1,0:T(8,128)(2,1)S(1)} %collective-permute-done.6.prev, bf16[128,2048]{1,0:T(8,128)(2,1)S(1)} %collective-permute-done.7.after), custom_call_target="tpu_custom_call" | custom-call | flops 3000000000 | bytes 2000000 | tf_op jit(solution)/shard_map/light/pallas_call | solution.py:158
  92.2 7.1 %all-to-all-done.2.heavy = bf16[16,64,128]{2,1,0:T(8,128)(2,1)S(1)} async-done(((bf16[16,64,128]{2,1,0:T(8,128)(2,1)}), bf16[16,64,128]{2,1,0:T(8,128)(2,1)S(1)}, u32[]{:S(2)}, u32[]{:S(2)}) %all-to-all-start.2) | async-done | bytes 262176 | tf_op jit(solution)/shard_map/all_to_all | solution.py:310
  99.4 1.5 %join.1 = bf16[128,1024]{1,0:T(8,128)(2,1)} custom-call(s32[1,64]{1,0:T(1,128)S(1)} %copy-done.6, f32[128,1024]{1,0:T(8,128)S(1)} %light.1, bf16[16,64,128]{2,1,0:T(8,128)(2,1)S(1)} %all-to-all-done.2.heavy), custom_call_target="tpu_custom_call" | custom-call | tf_op jit(solution)/shard_map/join/pallas_call | solution.py:184
  100.8 2.3 %copy.13 = bf16[1,512,1024]{2,1,0:T(8,128)(2,1)} copy(bf16[1,512,1024]{2,1,0:T(8,128)(2,1)} %bitcast.10) | data formatting | bytes 2097152
  (33 shorter events, 3.7 us)
Async XLA Ops:
  0.6 1.0 copy-start
  1.6 0.9 copy-start.1
  2.5 0.9 copy-start.2
  4.8 7.3 %copy-start.9 = (bf16[1,128,128]{2,1,0:T(8,128)(2,1)S(1)}, bf16[1,128,128]{2,1,0:T(8,128)(2,1)}, u32[]{:S(2)}) copy-start(bf16[1,128,128]{2,1,0:T(8,128)(2,1)} %param.16) | copy-start | bytes 98308
  4.8 29.8 %copy-start.7 = (bf16[1,512,1024]{2,1,0:T(8,128)(2,1)S(1)}, bf16[1,512,1024]{2,1,0:T(8,128)(2,1)}, u32[]{:S(2)}) copy-start(bf16[1,512,1024]{2,1,0:T(8,128)(2,1)} %param.17) | copy-start | bytes 3145732
  4.8 38.2 %all-to-all-start = ((bf16[16,192,128]{2,1,0:T(8,128)(2,1)}), bf16[16,192,128]{2,1,0:T(8,128)(2,1)S(1)}, u32[]{:S(2)}, u32[]{:S(2)}) async-start(bf16[16,192,128]{2,1,0:T(8,128)(2,1)} %pack.1), calls=%async_computation | async-start | bytes 1572864 | tf_op jit(solution)/shard_map/all_to_all | solution.py:286
  12.1 11.8 %collective-permute-start.2 = (bf16[128,128]{1,0:T(8,128)(2,1)S(1)}, bf16[128,128]{1,0:T(8,128)(2,1)S(1)}, u32[]{:S(2)}, u32[]{:S(2)}) collective-permute-start(bf16[128,128]{1,0:T(8,128)(2,1)S(1)} %bitcast.26), channel_id=1, source_target_pairs={{0,3},{1,0},{2,1},{3,2},{4,7},{5,4},{6,5},{7,6},{8,11},{9,8},{10,9... | collective-permute-start | bytes 98312 | tf_op jit(solution)/shard_map/ppermute | solution.py:270
  15.3 10.1 %collective-permute-start.1 = (bf16[128,128]{1,0:T(8,128)(2,1)S(1)}, bf16[128,128]{1,0:T(8,128)(2,1)S(1)}, u32[]{:S(2)}, u32[]{:S(2)}) collective-permute-start(bf16[128,128]{1,0:T(8,128)(2,1)S(1)} %bitcast.27), channel_id=1, source_target_pairs={{0,2},{1,3},{2,0},{3,1},{4,6},{5,7},{6,4},{7,5},{8,10},{9,11},{10,... | collective-permute-start | bytes 98312 | tf_op jit(solution)/shard_map/ppermute | solution.py:270
  16.2 9.2 %collective-permute-start = (bf16[128,128]{1,0:T(8,128)(2,1)S(1)}, bf16[128,128]{1,0:T(8,128)(2,1)S(1)}, u32[]{:S(2)}, u32[]{:S(2)}) collective-permute-start(bf16[128,128]{1,0:T(8,128)(2,1)S(1)} %bitcast.28), channel_id=1, source_target_pairs={{0,1},{1,2},{2,3},{3,0},{4,5},{5,6},{6,7},{7,4},{8,9},{9,10},{10,1... | collective-permute-start | bytes 98312 | tf_op jit(solution)/shard_map/ppermute | solution.py:270
  25.4 7.7 %collective-permute-start.3 = (bf16[512,128]{1,0:T(8,128)(2,1)S(1)}, bf16[512,128]{1,0:T(8,128)(2,1)S(1)}, u32[]{:S(2)}, u32[]{:S(2)}) collective-permute-start(bf16[512,128]{1,0:T(8,128)(2,1)S(1)} %pad_maximum_fusion.1.e0), channel_id=1, source_target_pairs={{0,4},{1,5},{2,6},{3,7},{4,8},{5,9},{6,10},{7,11},{8,12},{9,13},{1... | collective-permute-start | bytes 393224 | tf_op jit(solution)/shard_map/ppermute | solution.py:270
  26.9 7.7 %collective-permute-start.4 = (bf16[512,128]{1,0:T(8,128)(2,1)S(1)}, bf16[512,128]{1,0:T(8,128)(2,1)S(1)}, u32[]{:S(2)}, u32[]{:S(2)}) collective-permute-start(bf16[512,128]{1,0:T(8,128)(2,1)S(1)} %pad_maximum_fusion.1.e0), channel_id=1, source_target_pairs={{0,8},{1,9},{2,10},{3,11},{4,12},{5,13},{6,14},{7,15},{8,0},{9,1},... | collective-permute-start | bytes 393224 | tf_op jit(solution)/shard_map/ppermute | solution.py:270
  29.6 5.0 %collective-permute-start.5 = (bf16[512,128]{1,0:T(8,128)(2,1)S(1)}, bf16[512,128]{1,0:T(8,128)(2,1)S(1)}, u32[]{:S(2)}, u32[]{:S(2)}) collective-permute-start(bf16[512,128]{1,0:T(8,128)(2,1)S(1)} %pad_maximum_fusion.1.e0), channel_id=1, source_target_pairs={{0,12},{1,13},{2,14},{3,15},{4,0},{5,1},{6,2},{7,3},{8,4},{9,5},{1... | collective-permute-start | bytes 393224 | tf_op jit(solution)/shard_map/ppermute | solution.py:270
  34.7 8.4 %copy-start.5 = (s32[1,32]{1,0:T(1,128)S(1)}, s32[1,32]{1,0:T(1,128)}, u32[]{:S(2)}) copy-start(s32[1,32]{1,0:T(1,128)} %ids.2) | copy-start | bytes 388
  36.4 11.1 %copy-start.3 = (bf16[1,128,1024]{2,1,0:T(8,128)(2,1)S(1)}, bf16[1,128,1024]{2,1,0:T(8,128)(2,1)}, u32[]{:S(2)}) copy-start(bf16[1,128,1024]{2,1,0:T(8,128)(2,1)} %param.11) | copy-start | bytes 786436
  36.4 11.1 %copy-start.4 = (bf16[1,128,1024]{2,1,0:T(8,128)(2,1)S(1)}, bf16[1,128,1024]{2,1,0:T(8,128)(2,1)}, u32[]{:S(2)}) copy-start(bf16[1,128,1024]{2,1,0:T(8,128)(2,1)} %param.12) | copy-start | bytes 786436
  36.5 8.7 %collective-permute-start.11 = (bf16[512,128]{1,0:T(8,128)(2,1)S(1)}, bf16[512,128]{1,0:T(8,128)(2,1)S(1)}, u32[]{:S(2)}, u32[]{:S(2)}) collective-permute-start(bf16[512,128]{1,0:T(8,128)(2,1)S(1)} %decode.1.a), channel_id=1, source_target_pairs={{0,16},{16,32},{32,48},{48,0},{1,17},{17,33},{33,49},{49,1},{2,18}... | collective-permute-start | bytes 393224 | tf_op jit(solution)/shard_map/ppermute | solution.py:270
  38.4 10.9 %collective-permute-start.12 = (bf16[512,128]{1,0:T(8,128)(2,1)S(1)}, bf16[512,128]{1,0:T(8,128)(2,1)S(1)}, u32[]{:S(2)}, u32[]{:S(2)}) collective-permute-start(bf16[512,128]{1,0:T(8,128)(2,1)S(1)} %decode.1.a), channel_id=1, source_target_pairs={{0,32},{16,48},{32,0},{48,16},{1,33},{17,49},{33,1},{49,17},{2,34}... | collective-permute-start | bytes 393224 | tf_op jit(solution)/shard_map/ppermute | solution.py:270
  42.0 10.0 %collective-permute-start.13 = (bf16[512,128]{1,0:T(8,128)(2,1)S(1)}, bf16[512,128]{1,0:T(8,128)(2,1)S(1)}, u32[]{:S(2)}, u32[]{:S(2)}) collective-permute-start(bf16[512,128]{1,0:T(8,128)(2,1)S(1)} %decode.1.a), channel_id=1, source_target_pairs={{0,48},{16,0},{32,16},{48,32},{1,49},{17,1},{33,17},{49,33},{2,50}... | collective-permute-start | bytes 393224 | tf_op jit(solution)/shard_map/ppermute | solution.py:270
  43.6 19.8 %collective-permute-start.8 = (bf16[1024,128]{1,0:T(8,128)(2,1)S(1)}, bf16[1024,128]{1,0:T(8,128)(2,1)S(1)}, u32[]{:S(2)}, u32[]{:S(2)}) collective-permute-start(bf16[1024,128]{1,0:T(8,128)(2,1)S(1)} %bitcast.18), channel_id=1, source_target_pairs={{0,16},{16,32},{32,48},{48,0},{1,17},{17,33},{33,49},{49,1},{2,18}... | collective-permute-start | bytes 786440 | tf_op jit(solution)/shard_map/ppermute | solution.py:270
  44.7 24.1 %collective-permute-start.9 = (bf16[1024,128]{1,0:T(8,128)(2,1)S(1)}, bf16[1024,128]{1,0:T(8,128)(2,1)}, u32[]{:S(2)}, u32[]{:S(2)}) collective-permute-start(bf16[1024,128]{1,0:T(8,128)(2,1)S(1)} %bitcast.19), channel_id=1, source_target_pairs={{0,32},{16,48},{32,0},{48,16},{1,33},{17,49},{33,1},{49,17},{2,34}... | collective-permute-start | bytes 786440 | tf_op jit(solution)/shard_map/ppermute | solution.py:270
  45.2 23.7 %collective-permute-start.10 = (bf16[1024,128]{1,0:T(8,128)(2,1)S(1)}, bf16[1024,128]{1,0:T(8,128)(2,1)}, u32[]{:S(2)}, u32[]{:S(2)}) collective-permute-start(bf16[1024,128]{1,0:T(8,128)(2,1)S(1)} %bitcast.20), channel_id=1, source_target_pairs={{0,48},{16,0},{32,16},{48,32},{1,49},{17,1},{33,17},{49,33},{2,50}... | collective-permute-start | bytes 786440 | tf_op jit(solution)/shard_map/ppermute | solution.py:270
  49.3 25.6 %collective-permute-start.6 = (bf16[128,2048]{1,0:T(8,128)(2,1)}, bf16[128,2048]{1,0:T(8,128)(2,1)S(1)}, u32[]{:S(2)}, u32[]{:S(2)}) collective-permute-start(bf16[128,2048]{1,0:T(8,128)(2,1)} %pad_maximum_fusion), channel_id=1, source_target_pairs={{0,1},{1,2},{2,3},{3,4},{4,5},{5,6},{6,7},{7,8},{8,9},{9,10},{10,1... | collective-permute-start | bytes 1572872 | tf_op jit(solution)/shard_map/ppermute | solution.py:303
  52.1 22.8 %collective-permute-start.7 = (bf16[128,2048]{1,0:T(8,128)(2,1)}, bf16[128,2048]{1,0:T(8,128)(2,1)S(1)}, u32[]{:S(2)}, u32[]{:S(2)}) collective-permute-start(bf16[128,2048]{1,0:T(8,128)(2,1)} %pad_maximum_fusion), channel_id=1, source_target_pairs={{1,0},{2,1},{3,2},{4,3},{5,4},{6,5},{7,6},{8,7},{9,8},{10,9},{11,1... | collective-permute-start | bytes 1572872 | tf_op jit(solution)/shard_map/ppermute | solution.py:304
  55.4 26.3 %all-to-all-start.1 = ((bf16[16,32,1024]{2,1,0:T(8,128)(2,1)}), bf16[16,32,1024]{2,1,0:T(8,128)(2,1)}, u32[]{:S(2)}, u32[]{:S(2)}) async-start(bf16[16,32,1024]{2,1,0:T(8,128)(2,1)} %meet.1), calls=%async_computation.1 | async-start | bytes 2097152 | tf_op jit(solution)/shard_map/all_to_all | solution.py:298
  81.7 9.0 %copy-start.8 = (bf16[1,128,1024]{2,1,0:T(8,128)(2,1)S(1)}, bf16[1,128,1024]{2,1,0:T(8,128)(2,1)}, u32[]{:S(2)}) copy-start(bf16[1,128,1024]{2,1,0:T(8,128)(2,1)} %param.10) | copy-start | bytes 786436
  81.7 17.7 %all-to-all-start.2 = ((bf16[16,64,128]{2,1,0:T(8,128)(2,1)}), bf16[16,64,128]{2,1,0:T(8,128)(2,1)S(1)}, u32[]{:S(2)}, u32[]{:S(2)}) async-start(bf16[16,64,128]{2,1,0:T(8,128)(2,1)} %heavy1.1), calls=%async_computation.2 | async-start | bytes 524288 | tf_op jit(solution)/shard_map/all_to_all | solution.py:310
  92.2 7.1 %copy-start.6 = (s32[1,64]{1,0:T(1,128)S(1)}, s32[1,64]{1,0:T(1,128)}, u32[]{:S(2)}) copy-start(s32[1,64]{1,0:T(1,128)} %ids.3) | copy-start | bytes 772

commit v3 on v2

--- a/solution.py
+++ b/solution.py
@@ -65,7 +65,7 @@
         + [pltpu.SemaphoreType.DMA((3,))],
         compiler_params=params(),
         name="pack",
-    )(q, k, v)
+    )(*(pltpu.with_memory_space_constraint(x, pltpu.HBM) for x in (q, k, v)))
 
 
 def pick_kernel(ids, kv, out):
@@ -100,32 +100,29 @@
     return total, peak
 
 
-def heavy_kernel(part, q, kv0, kv1, kv2, kv3, *rest):
-    out = rest[-1]
+def heavy_kernel(q, kv0, kv1, kv2, kv3, out):
     rows = q.shape[0] * HALF
     both = q[:, BLOCK:].reshape(rows, LANES)
     zero = jnp.zeros((rows, HEAD), bf16)
     keys = [kv[...] for kv in (kv0, kv1, kv2, kv3)]
     vals = [with_ones(k) for k in keys]
-    mine = jnp.concatenate([both[:, part * HEAD : (part + 1) * HEAD], zero], axis=1)
-    o, _ = summed(mine, keys, vals)
-    ratio = (o / pltpu.roll(o, HEAD, 1))[:, HEAD:].astype(bf16)
-    if part == 0:
-        out[...] = ratio.reshape(out.shape)
-    else:
-        out[...] = jnp.concatenate([rest[0][...].reshape(rows, HEAD), ratio], axis=1).reshape(out.shape)
-
-
-def heavy_attend(part, q_kv, kvs, *first):
+    a, _ = summed(jnp.concatenate([both[:, :HEAD], zero], axis=1), keys, vals)
+    b, _ = summed(jnp.concatenate([both[:, HEAD:], zero], axis=1), keys, vals)
+    low = lane_ids(a.shape) < HEAD
+    top = jnp.where(low, pltpu.roll(a, HEAD, 1), b)
+    sums = jnp.where(low, a, pltpu.roll(b, HEAD, 1))
+    out[...] = (top / sums).astype(bf16).reshape(out.shape)
+
+
+def heavy_attend(q_kv, kvs):
     blocks = q_kv.shape[0]
-    lanes = (part + 1) * HEAD
-    return pl.pallas_call(
-        lambda *refs: heavy_kernel(part, *refs),
-        out_shape=jax.ShapeDtypeStruct((blocks, HALF, lanes), bf16),
-        compiler_params=params(),
-        cost_estimate=pl.CostEstimate(flops=5_000_000_000, transcendentals=4_000_000, bytes_accessed=2_000_000),
-        name=f"heavy{part}",
-    )(q_kv, *kvs, *first)
+    return pl.pallas_call(
+        heavy_kernel,
+        out_shape=jax.ShapeDtypeStruct((blocks, HALF, LANES), bf16),
+        compiler_params=params(),
+        cost_estimate=pl.CostEstimate(flops=10_000_000_000, transcendentals=8_000_000, bytes_accessed=2_000_000),
+        name="heavy",
+    )(q_kv, *kvs)
 
 
 def light_kernel(q, k, v, prev, after, out):
@@ -241,19 +238,17 @@
     for x, s in zip(parts[1:], scales[1:]):
         value = value + x * s
     value = (value / total).astype(bf16)
-    copies, rows, width = out.shape
+    rows, width = out.shape
     for p in range(width // LANES):
         e = value[2 * p * rows : (2 * p + 1) * rows, HEAD:]
         o = value[(2 * p + 1) * rows : (2 * p + 2) * rows, HEAD:]
-        both = jnp.concatenate([e, o], axis=1)
-        for n in range(copies):
-            out[n, :, p * LANES : (p + 1) * LANES] = both
-
-
-def meet(parts, copies, rows, width):
+        out[:, p * LANES : (p + 1) * LANES] = jnp.concatenate([e, o], axis=1)
+
+
+def meet(parts, rows, width):
     return pl.pallas_call(
         meet_kernel,
-        out_shape=jax.ShapeDtypeStruct((copies, rows, width), bf16),
+        out_shape=jax.ShapeDtypeStruct((rows, width), bf16),
         compiler_params=params(),
         name="meet",
     )(*parts)
@@ -282,20 +277,18 @@
     side = 4
     width = q_light.shape[2]
 
-    chunks = pack(q_heavy[0], k_heavy[0], v_heavy[0])
-    group = lax.all_to_all(chunks, "fine", 0, 0, tiled=True)
-
     row = jnp.concatenate([enc_kv[0]] + around(enc_kv[0], "fine", 1, side), axis=0)
     enc = [row] + around(row, "fine", side, n_fine // side)
+    chunks = pack(q_heavy[0], k_heavy[0], v_heavy[0])
+    group = lax.all_to_all(after_all(chunks, row), "fine", 0, 0, tiled=True)
+
     dec_rows = dec_queries.shape[1] // n_fine
     part = decode(dec_queries[0], enc, dec_rows)
-    parts = around(part, "coarse")
-
-    own = pick(key_ids, after_all(group, part)).reshape(KGRP * BLOCK, LANES)
+    share = meet([part] + around(part, "coarse"), dec_rows, width)
+    decoded = lax.all_gather(share, "fine", axis=0, tiled=True)[None]
+
+    own = pick(key_ids, after_all(group, share)).reshape(KGRP * BLOCK, LANES)
     routed = [own] + around(own, "coarse")
-
-    shares = meet([after_all(part, own)] + parts, n_fine, dec_rows, width)
-    decoded = lax.all_to_all(shares, "fine", 0, 0, tiled=True)
 
     light_kv = jnp.concatenate([k_light[0], v_light[0]], axis=1)
     light_kv = after_all(light_kv, own)
@@ -303,15 +296,13 @@
     prev = lax.ppermute(light_kv, TOKENS, up)
     after = lax.ppermute(light_kv, TOKENS, [(b, a) for a, b in up])
 
-    first = heavy_attend(0, after_all(group, shares), routed)
-    heavy = heavy_attend(1, after_all(group, prev, after), routed, first)
+    heavy = heavy_attend(group, routed)
     q_light = after_all(q_light, heavy)
-    heavy, decoded = lax.optimization_barrier((heavy, decoded))
     heavy = lax.all_to_all(heavy, "fine", 0, 0, tiled=True)
 
     light = light_attend(q_light[0], k_light[0], v_light[0], prev, after)
     encoded = join(query_ids, light, heavy)[None]
-    return (encoded, decoded.reshape(1, -1, width))
+    return (encoded, decoded)
 
 
 def solution(mesh):

time: 104 us -> 102 us (0.981)
  the two profiles are of different devices: /device:TPU:0 before, /device:TPU:32 now
where the time goes in v3:
time: 102 us
  starting transfers between devices  42.6 us (42%)
  waiting for transfers between devices  21.6 us (21%)
  Pallas kernels  19.6 us (19%)
  between operations  14.2 us (14%)
  local copies, waits for them, and re-layouts  2.89 us (3%)
    ppermute x12, starting transfers between devices, around(): lax.ppermute(value, axis, [(i, to(i, d)) for i in range(size)])  21.6 us
    ppermute x12, waiting for transfers between devices, around(): lax.ppermute(value, axis, [(i, to(i, d)) for i in range(size)])  14.5 us
    pallas_call x1, Pallas kernels, heavy_attend(): pl.pallas_call(heavy_kernel, out_shape=jax.ShapeDtypeStruct((blocks, HALF...  10.4 us
    all_to_all x1, waiting for transfers between devices, local(): heavy = lax.all_to_all(heavy, 'fine', 0, 0, tiled=True)  7.03 us
    all_to_all x1, starting transfers between devices, local(): heavy = lax.all_to_all(heavy, 'fine', 0, 0, tiled=True)  6.44 us
    ppermute x1, starting transfers between devices, local(): after = lax.ppermute(light_kv, TOKENS, [(b, a) for a, b in up])  6.41 us
    all_to_all x1, starting transfers between devices, local(): group = lax.all_to_all(after_all(chunks, row), 'fine', 0, 0, tiled=True)  4.28 us
    ppermute x1, starting transfers between devices, local(): prev = lax.ppermute(light_kv, TOKENS, up)  3.84 us
  transfers between devices with their start and end apart: 17, of which 7 were waited for; matrix products, arithmetic and copies ran while one was open for 0% of the time, Pallas kernels for 19%

profile of v3, /device:TPU:32, one launch (start us, length us, event | category | flops | bytes accessed | tf_op | source)
XLA Modules:
  0.0 101.7 jit_solution(1142329961961896621)
XLA Ops:
  7.2 1.6 %collective-permute-start = (bf16[128,128]{1,0:T(8,128)(2,1)}, bf16[128,128]{1,0:T(8,128)(2,1)S(1)}, u32[]{:S(2)}, u32[]{:S(2)}) collective-permute-start(bf16[128,128]{1,0:T(8,128)(2,1)} %bitcast.26), channel_id=1, source_target_pairs={{0,1},{1,2},{2,3},{3,0},{4,5},{5,6},{6,7},{7,4},{8,9},{9,10},{10,1... | collective-permute-start | bytes 98312 | tf_op jit(solution)/shard_map/ppermute | solution.py:265
  8.7 2.7 %collective-permute-start.1 = (bf16[128,128]{1,0:T(8,128)(2,1)}, bf16[128,128]{1,0:T(8,128)(2,1)S(1)}, u32[]{:S(2)}, u32[]{:S(2)}) collective-permute-start(bf16[128,128]{1,0:T(8,128)(2,1)} %bitcast.27), channel_id=1, source_target_pairs={{0,2},{1,3},{2,0},{3,1},{4,6},{5,7},{6,4},{7,5},{8,10},{9,11},{10,... | collective-permute-start | bytes 98312 | tf_op jit(solution)/shard_map/ppermute | solution.py:265
  11.5 1.4 %collective-permute-start.2 = (bf16[128,128]{1,0:T(8,128)(2,1)}, bf16[128,128]{1,0:T(8,128)(2,1)S(1)}, u32[]{:S(2)}, u32[]{:S(2)}) collective-permute-start(bf16[128,128]{1,0:T(8,128)(2,1)} %bitcast.28), channel_id=1, source_target_pairs={{0,3},{1,0},{2,1},{3,2},{4,7},{5,4},{6,5},{7,6},{8,11},{9,8},{10,9... | collective-permute-start | bytes 98312 | tf_op jit(solution)/shard_map/ppermute | solution.py:265
  12.9 1.5 %collective-permute-done.1 = bf16[128,128]{1,0:T(8,128)(2,1)S(1)} collective-permute-done((bf16[128,128]{1,0:T(8,128)(2,1)}, bf16[128,128]{1,0:T(8,128)(2,1)S(1)}, u32[]{:S(2)}, u32[]{:S(2)}) %collective-permute-start.1) | collective-permute-done | bytes 32800 | tf_op jit(solution)/shard_map/ppermute | solution.py:265
  14.4 1.2 %collective-permute-done.2 = bf16[128,128]{1,0:T(8,128)(2,1)S(1)} collective-permute-done((bf16[128,128]{1,0:T(8,128)(2,1)}, bf16[128,128]{1,0:T(8,128)(2,1)S(1)}, u32[]{:S(2)}, u32[]{:S(2)}) %collective-permute-start.2) | collective-permute-done | bytes 32800 | tf_op jit(solution)/shard_map/ppermute | solution.py:265
  15.6 0.8 pad_maximum_fusion.1.e0
  16.4 1.6 %collective-permute-start.3 = (bf16[512,128]{1,0:T(8,128)(2,1)S(1)}, bf16[512,128]{1,0:T(8,128)(2,1)S(1)}, u32[]{:S(2)}, u32[]{:S(2)}) collective-permute-start(bf16[512,128]{1,0:T(8,128)(2,1)S(1)} %pad_maximum_fusion.1.e0), channel_id=1, source_target_pairs={{0,4},{1,5},{2,6},{3,7},{4,8},{5,9},{6,10},{7,11},{8,12},{9,13},{1... | collective-permute-start | bytes 393224 | tf_op jit(solution)/shard_map/ppermute | solution.py:265
  18.0 2.9 %collective-permute-start.4 = (bf16[512,128]{1,0:T(8,128)(2,1)S(1)}, bf16[512,128]{1,0:T(8,128)(2,1)S(1)}, u32[]{:S(2)}, u32[]{:S(2)}) collective-permute-start(bf16[512,128]{1,0:T(8,128)(2,1)S(1)} %pad_maximum_fusion.1.e0), channel_id=1, source_target_pairs={{0,8},{1,9},{2,10},{3,11},{4,12},{5,13},{6,14},{7,15},{8,0},{9,1},... | collective-permute-start | bytes 393224 | tf_op jit(solution)/shard_map/ppermute | solution.py:265
  20.9 1.3 %collective-permute-start.5 = (bf16[512,128]{1,0:T(8,128)(2,1)S(1)}, bf16[512,128]{1,0:T(8,128)(2,1)S(1)}, u32[]{:S(2)}, u32[]{:S(2)}) collective-permute-start(bf16[512,128]{1,0:T(8,128)(2,1)S(1)} %pad_maximum_fusion.1.e0), channel_id=1, source_target_pairs={{0,12},{1,13},{2,14},{3,15},{4,0},{5,1},{6,2},{7,3},{8,4},{9,5},{1... | collective-permute-start | bytes 393224 | tf_op jit(solution)/shard_map/ppermute | solution.py:265
  22.2 2.3 %pack.1 = bf16[16,192,128]{2,1,0:T(8,128)(2,1)} custom-call(bf16[128,1024]{1,0:T(8,128)(2,1)} %bitcast.22, bf16[128,1024]{1,0:T(8,128)(2,1)} %bitcast.23, bf16[128,1024]{1,0:T(8,128)(2,1)} %bitcast.24), custom_call_target="tpu_custom_call" | custom-call | tf_op jit(solution)/shard_map/pack/pallas_call | solution.py:60
  24.5 4.3 %all-to-all-start = ((bf16[16,192,128]{2,1,0:T(8,128)(2,1)}), bf16[16,192,128]{2,1,0:T(8,128)(2,1)S(1)}, u32[]{:S(2)}, u32[]{:S(2)}) async-start(bf16[16,192,128]{2,1,0:T(8,128)(2,1)} %pack.1), calls=%async_computation | async-start | bytes 1572864 | tf_op jit(solution)/shard_map/all_to_all | solution.py:283
  28.9 1.8 %decode.1.a = bf16[512,128]{1,0:T(8,128)(2,1)S(1)} custom-call(bf16[512,1024]{1,0:T(8,128)(2,1)S(1)} %bitcast.19, bf16[512,128]{1,0:T(8,128)(2,1)S(1)} %pad_maximum_fusion.1.e0, bf16[512,128]{1,0:T(8,128)(2,1)S(1)} %collective-permute-done.3.e1, bf16[512,128]{1,0:T(8,128)(2,1)S(1)} %collective-permute-done.4.e2, bf16[512,128]{1,0:T(8,128)(2,1)S(1)} %collective-permute-done.5.e3), custom_call_target="tpu_custom_call" | custom-call | flops 1000000000 | bytes 1000000 | tf_op jit(solution)/shard_map/decode/pallas_call | solution.py:220
  30.7 2.0 %collective-permute-start.6 = (bf16[512,128]{1,0:T(8,128)(2,1)S(1)}, bf16[512,128]{1,0:T(8,128)(2,1)S(1)}, u32[]{:S(2)}, u32[]{:S(2)}) collective-permute-start(bf16[512,128]{1,0:T(8,128)(2,1)S(1)} %decode.1.a), channel_id=1, source_target_pairs={{0,16},{16,32},{32,48},{48,0},{1,17},{17,33},{33,49},{49,1},{2,18}... | collective-permute-start | bytes 393224 | tf_op jit(solution)/shard_map/ppermute | solution.py:265
  32.7 1.2 %collective-permute-start.7 = (bf16[512,128]{1,0:T(8,128)(2,1)S(1)}, bf16[512,128]{1,0:T(8,128)(2,1)S(1)}, u32[]{:S(2)}, u32[]{:S(2)}) collective-permute-start(bf16[512,128]{1,0:T(8,128)(2,1)S(1)} %decode.1.a), channel_id=1, source_target_pairs={{0,32},{16,48},{32,0},{48,16},{1,33},{17,49},{33,1},{49,17},{2,34}... | collective-permute-start | bytes 393224 | tf_op jit(solution)/shard_map/ppermute | solution.py:265
  33.9 2.5 %collective-permute-start.8 = (bf16[512,128]{1,0:T(8,128)(2,1)S(1)}, bf16[512,128]{1,0:T(8,128)(2,1)S(1)}, u32[]{:S(2)}, u32[]{:S(2)}) collective-permute-start(bf16[512,128]{1,0:T(8,128)(2,1)S(1)} %decode.1.a), channel_id=1, source_target_pairs={{0,48},{16,0},{32,16},{48,32},{1,49},{17,1},{33,17},{49,33},{2,50}... | collective-permute-start | bytes 393224 | tf_op jit(solution)/shard_map/ppermute | solution.py:265
  36.5 2.7 %collective-permute-done.7.c = bf16[512,128]{1,0:T(8,128)(2,1)S(1)} collective-permute-done((bf16[512,128]{1,0:T(8,128)(2,1)S(1)}, bf16[512,128]{1,0:T(8,128)(2,1)S(1)}, u32[]{:S(2)}, u32[]{:S(2)}) %collective-permute-start.7) | collective-permute-done | bytes 131104 | tf_op jit(solution)/shard_map/ppermute | solution.py:265
  39.3 0.9 collective-permute-done.8.d
  40.2 1.5 %meet.1 = bf16[32,1024]{1,0:T(8,128)(2,1)} custom-call(bf16[512,128]{1,0:T(8,128)(2,1)S(1)} %decode.1.a, bf16[512,128]{1,0:T(8,128)(2,1)S(1)} %collective-permute-done.6.b, bf16[512,128]{1,0:T(8,128)(2,1)S(1)} %collective-permute-done.7.c, bf16[512,128]{1,0:T(8,128)(2,1)S(1)} %collective-permute-done.8.d), custom_call_target="tpu_custom_call" | custom-call | tf_op jit(solution)/shard_map/meet/pallas_call | solution.py:249
  41.8 0.6 copy-done.2
  42.4 0.6 pick.1
  42.9 2.3 %collective-permute-start.10 = (bf16[1024,128]{1,0:T(8,128)(2,1)S(1)}, bf16[1024,128]{1,0:T(8,128)(2,1)S(1)}, u32[]{:S(2)}, u32[]{:S(2)}) collective-permute-start(bf16[1024,128]{1,0:T(8,128)(2,1)S(1)} %bitcast.15), channel_id=1, source_target_pairs={{0,32},{16,48},{32,0},{48,16},{1,33},{17,49},{33,1},{49,17},{2,34}... | collective-permute-start | bytes 786440 | tf_op jit(solution)/shard_map/ppermute | solution.py:265
  45.2 0.9 collective-permute-start.11
  46.1 1.2 %collective-permute-start.9 = (bf16[1024,128]{1,0:T(8,128)(2,1)S(1)}, bf16[1024,128]{1,0:T(8,128)(2,1)S(1)}, u32[]{:S(2)}, u32[]{:S(2)}) collective-permute-start(bf16[1024,128]{1,0:T(8,128)(2,1)S(1)} %bitcast.17), channel_id=1, source_target_pairs={{0,16},{16,32},{32,48},{48,0},{1,17},{17,33},{33,49},{49,1},{2,18}... | collective-permute-start | bytes 786440 | tf_op jit(solution)/shard_map/ppermute | solution.py:265
  47.3 3.8 %collective-permute-start.12 = (bf16[128,2048]{1,0:T(8,128)(2,1)S(1)}, bf16[128,2048]{1,0:T(8,128)(2,1)S(1)}, u32[]{:S(2)}, u32[]{:S(2)}) collective-permute-start(bf16[128,2048]{1,0:T(8,128)(2,1)S(1)} %pad_maximum_fusion), channel_id=1, source_target_pairs={{0,1},{1,2},{2,3},{3,4},{4,5},{5,6},{6,7},{7,8},{8,9},{9,10},{10,1... | collective-permute-start | bytes 1572872 | tf_op jit(solution)/shard_map/ppermute | solution.py:296
  51.1 6.4 %collective-permute-start.13 = (bf16[128,2048]{1,0:T(8,128)(2,1)S(1)}, bf16[128,2048]{1,0:T(8,128)(2,1)S(1)}, u32[]{:S(2)}, u32[]{:S(2)}) collective-permute-start(bf16[128,2048]{1,0:T(8,128)(2,1)S(1)} %pad_maximum_fusion), channel_id=1, source_target_pairs={{1,0},{2,1},{3,2},{4,3},{5,4},{6,5},{7,6},{8,7},{9,8},{10,9},{11,1... | collective-permute-start | bytes 1572872 | tf_op jit(solution)/shard_map/ppermute | solution.py:297
  57.6 8.0 %collective-permute-done.9.kv1 = bf16[1024,128]{1,0:T(8,128)(2,1)S(1)} collective-permute-done((bf16[1024,128]{1,0:T(8,128)(2,1)S(1)}, bf16[1024,128]{1,0:T(8,128)(2,1)S(1)}, u32[]{:S(2)}, u32[]{:S(2)}) %collective-permute-start.9) | collective-permute-done | bytes 262176 | tf_op jit(solution)/shard_map/ppermute | solution.py:265
  65.6 10.4 %heavy.1 = bf16[16,64,128]{2,1,0:T(8,128)(2,1)} custom-call(bf16[16,192,128]{2,1,0:T(8,128)(2,1)S(1)} %all-to-all-done.kv.q, bf16[1024,128]{1,0:T(8,128)(2,1)S(1)} %bitcast.18, bf16[1024,128]{1,0:T(8,128)(2,1)S(1)} %collective-permute-done.9.kv1, bf16[1024,128]{1,0:T(8,128)(2,1)S(1)} %collective-permute-done.10.kv2, ...), custom_call_target="tpu_custom_call" | custom-call | flops 10000000000 | bytes 2000000 | tf_op jit(solution)/shard_map/heavy/pallas_call | solution.py:119
  76.0 6.4 %all-to-all-start.1 = ((bf16[16,64,128]{2,1,0:T(8,128)(2,1)}), bf16[16,64,128]{2,1,0:T(8,128)(2,1)S(1)}, u32[]{:S(2)}, u32[]{:S(2)}) async-start(bf16[16,64,128]{2,1,0:T(8,128)(2,1)} %heavy.1), calls=%async_computation.1 | async-start | bytes 524288 | tf_op jit(solution)/shard_map/all_to_all | solution.py:301
  82.5 1.6 %light.1 = f32[128,1024]{1,0:T(8,128)S(1)} custom-call(bf16[128,1024]{1,0:T(8,128)(2,1)S(1)} %bitcast.20, bf16[128,1024]{1,0:T(8,128)(2,1)S(1)} %bitcast.12, bf16[128,1024]{1,0:T(8,128)(2,1)S(1)} %bitcast.14, bf16[128,2048]{1,0:T(8,128)(2,1)S(1)} %collective-permute-done.12.prev, bf16[128,2048]{1,0:T(8,128)(2,1)S(1)} %collective-permute-done.13.after), custom_call_target="tpu_custom_call" | custom-call | flops 3000000000 | bytes 2000000 | tf_op jit(solution)/shard_map/light/pallas_call | solution.py:155
  84.1 7.0 %all-to-all-done.1.heavy = bf16[16,64,128]{2,1,0:T(8,128)(2,1)S(1)} async-done(((bf16[16,64,128]{2,1,0:T(8,128)(2,1)}), bf16[16,64,128]{2,1,0:T(8,128)(2,1)S(1)}, u32[]{:S(2)}, u32[]{:S(2)}) %all-to-all-start.1) | async-done | bytes 262176 | tf_op jit(solution)/shard_map/all_to_all | solution.py:301
  91.1 1.5 %join.1 = bf16[128,1024]{1,0:T(8,128)(2,1)} custom-call(s32[1,64]{1,0:T(1,128)S(1)} %copy-done.3, f32[128,1024]{1,0:T(8,128)S(1)} %light.1, bf16[16,64,128]{2,1,0:T(8,128)(2,1)S(1)} %all-to-all-done.1.heavy), custom_call_target="tpu_custom_call" | custom-call | tf_op jit(solution)/shard_map/join/pallas_call | solution.py:181
  92.6 2.3 %copy.13 = bf16[1,512,1024]{2,1,0:T(8,128)(2,1)} copy(bf16[1,512,1024]{2,1,0:T(8,128)(2,1)} %bitcast.21) | data formatting | bytes 2097152
  (25 shorter events, 0.3 us)
Async XLA Ops:
  7.2 5.7 %collective-permute-start = (bf16[128,128]{1,0:T(8,128)(2,1)}, bf16[128,128]{1,0:T(8,128)(2,1)S(1)}, u32[]{:S(2)}, u32[]{:S(2)}) collective-permute-start(bf16[128,128]{1,0:T(8,128)(2,1)} %bitcast.26), channel_id=1, source_target_pairs={{0,1},{1,2},{2,3},{3,0},{4,5},{5,6},{6,7},{7,4},{8,9},{9,10},{10,1... | collective-permute-start | bytes 98312 | tf_op jit(solution)/shard_map/ppermute | solution.py:265
  8.7 5.6 %collective-permute-start.1 = (bf16[128,128]{1,0:T(8,128)(2,1)}, bf16[128,128]{1,0:T(8,128)(2,1)S(1)}, u32[]{:S(2)}, u32[]{:S(2)}) collective-permute-start(bf16[128,128]{1,0:T(8,128)(2,1)} %bitcast.27), channel_id=1, source_target_pairs={{0,2},{1,3},{2,0},{3,1},{4,6},{5,7},{6,4},{7,5},{8,10},{9,11},{10,... | collective-permute-start | bytes 98312 | tf_op jit(solution)/shard_map/ppermute | solution.py:265
  11.5 4.1 %collective-permute-start.2 = (bf16[128,128]{1,0:T(8,128)(2,1)}, bf16[128,128]{1,0:T(8,128)(2,1)S(1)}, u32[]{:S(2)}, u32[]{:S(2)}) collective-permute-start(bf16[128,128]{1,0:T(8,128)(2,1)} %bitcast.28), channel_id=1, source_target_pairs={{0,3},{1,0},{2,1},{3,2},{4,7},{5,4},{6,5},{7,6},{8,11},{9,8},{10,9... | collective-permute-start | bytes 98312 | tf_op jit(solution)/shard_map/ppermute | solution.py:265
  16.4 12.5 %collective-permute-start.3 = (bf16[512,128]{1,0:T(8,128)(2,1)S(1)}, bf16[512,128]{1,0:T(8,128)(2,1)S(1)}, u32[]{:S(2)}, u32[]{:S(2)}) collective-permute-start(bf16[512,128]{1,0:T(8,128)(2,1)S(1)} %pad_maximum_fusion.1.e0), channel_id=1, source_target_pairs={{0,4},{1,5},{2,6},{3,7},{4,8},{5,9},{6,10},{7,11},{8,12},{9,13},{1... | collective-permute-start | bytes 393224 | tf_op jit(solution)/shard_map/ppermute | solution.py:265
  18.0 10.9 %collective-permute-start.4 = (bf16[512,128]{1,0:T(8,128)(2,1)S(1)}, bf16[512,128]{1,0:T(8,128)(2,1)S(1)}, u32[]{:S(2)}, u32[]{:S(2)}) collective-permute-start(bf16[512,128]{1,0:T(8,128)(2,1)S(1)} %pad_maximum_fusion.1.e0), channel_id=1, source_target_pairs={{0,8},{1,9},{2,10},{3,11},{4,12},{5,13},{6,14},{7,15},{8,0},{9,1},... | collective-permute-start | bytes 393224 | tf_op jit(solution)/shard_map/ppermute | solution.py:265
  20.9 8.0 %collective-permute-start.5 = (bf16[512,128]{1,0:T(8,128)(2,1)S(1)}, bf16[512,128]{1,0:T(8,128)(2,1)S(1)}, u32[]{:S(2)}, u32[]{:S(2)}) collective-permute-start(bf16[512,128]{1,0:T(8,128)(2,1)S(1)} %pad_maximum_fusion.1.e0), channel_id=1, source_target_pairs={{0,12},{1,13},{2,14},{3,15},{4,0},{5,1},{6,2},{7,3},{8,4},{9,5},{1... | collective-permute-start | bytes 393224 | tf_op jit(solution)/shard_map/ppermute | solution.py:265
  24.5 4.4 %copy-start.4 = (bf16[1,512,1024]{2,1,0:T(8,128)(2,1)S(1)}, bf16[1,512,1024]{2,1,0:T(8,128)(2,1)}, u32[]{:S(2)}) copy-start(bf16[1,512,1024]{2,1,0:T(8,128)(2,1)} %param.17) | copy-start | bytes 3145732
  24.5 17.2 %all-to-all-start = ((bf16[16,192,128]{2,1,0:T(8,128)(2,1)}), bf16[16,192,128]{2,1,0:T(8,128)(2,1)S(1)}, u32[]{:S(2)}, u32[]{:S(2)}) async-start(bf16[16,192,128]{2,1,0:T(8,128)(2,1)} %pack.1), calls=%async_computation | async-start | bytes 1572864 | tf_op jit(solution)/shard_map/all_to_all | solution.py:283
  28.8 63.8 %all-gather.2.cloned.1.call-start = ((), (), s32[]{:S(2)}) async-start(), calls=%async_computation.2 | async-start | bytes 1114112 | tf_op jit(solution)/shard_map/all_gather | solution.py:288
  30.7 5.8 %collective-permute-start.6 = (bf16[512,128]{1,0:T(8,128)(2,1)S(1)}, bf16[512,128]{1,0:T(8,128)(2,1)S(1)}, u32[]{:S(2)}, u32[]{:S(2)}) collective-permute-start(bf16[512,128]{1,0:T(8,128)(2,1)S(1)} %decode.1.a), channel_id=1, source_target_pairs={{0,16},{16,32},{32,48},{48,0},{1,17},{17,33},{33,49},{49,1},{2,18}... | collective-permute-start | bytes 393224 | tf_op jit(solution)/shard_map/ppermute | solution.py:265
  32.7 6.6 %collective-permute-start.7 = (bf16[512,128]{1,0:T(8,128)(2,1)S(1)}, bf16[512,128]{1,0:T(8,128)(2,1)S(1)}, u32[]{:S(2)}, u32[]{:S(2)}) collective-permute-start(bf16[512,128]{1,0:T(8,128)(2,1)S(1)} %decode.1.a), channel_id=1, source_target_pairs={{0,32},{16,48},{32,0},{48,16},{1,33},{17,49},{33,1},{49,17},{2,34}... | collective-permute-start | bytes 393224 | tf_op jit(solution)/shard_map/ppermute | solution.py:265
  33.9 6.4 %collective-permute-start.8 = (bf16[512,128]{1,0:T(8,128)(2,1)S(1)}, bf16[512,128]{1,0:T(8,128)(2,1)S(1)}, u32[]{:S(2)}, u32[]{:S(2)}) collective-permute-start(bf16[512,128]{1,0:T(8,128)(2,1)S(1)} %decode.1.a), channel_id=1, source_target_pairs={{0,48},{16,0},{32,16},{48,32},{1,49},{17,1},{33,17},{49,33},{2,50}... | collective-permute-start | bytes 393224 | tf_op jit(solution)/shard_map/ppermute | solution.py:265
  41.7 0.7 copy-start.2
  41.7 5.5 %copy-start = (bf16[1,128,1024]{2,1,0:T(8,128)(2,1)S(1)}, bf16[1,128,1024]{2,1,0:T(8,128)(2,1)}, u32[]{:S(2)}) copy-start(bf16[1,128,1024]{2,1,0:T(8,128)(2,1)} %param.11) | copy-start | bytes 786436
  41.7 5.5 %copy-start.1 = (bf16[1,128,1024]{2,1,0:T(8,128)(2,1)S(1)}, bf16[1,128,1024]{2,1,0:T(8,128)(2,1)}, u32[]{:S(2)}) copy-start(bf16[1,128,1024]{2,1,0:T(8,128)(2,1)} %param.12) | copy-start | bytes 786436
  42.9 14.6 %collective-permute-start.10 = (bf16[1024,128]{1,0:T(8,128)(2,1)S(1)}, bf16[1024,128]{1,0:T(8,128)(2,1)S(1)}, u32[]{:S(2)}, u32[]{:S(2)}) collective-permute-start(bf16[1024,128]{1,0:T(8,128)(2,1)S(1)} %bitcast.15), channel_id=1, source_target_pairs={{0,32},{16,48},{32,0},{48,16},{1,33},{17,49},{33,1},{49,17},{2,34}... | collective-permute-start | bytes 786440 | tf_op jit(solution)/shard_map/ppermute | solution.py:265
  45.2 12.3 %collective-permute-start.11 = (bf16[1024,128]{1,0:T(8,128)(2,1)S(1)}, bf16[1024,128]{1,0:T(8,128)(2,1)S(1)}, u32[]{:S(2)}, u32[]{:S(2)}) collective-permute-start(bf16[1024,128]{1,0:T(8,128)(2,1)S(1)} %bitcast.16), channel_id=1, source_target_pairs={{0,48},{16,0},{32,16},{48,32},{1,49},{17,1},{33,17},{49,33},{2,50}... | collective-permute-start | bytes 786440 | tf_op jit(solution)/shard_map/ppermute | solution.py:265
  46.1 19.5 %collective-permute-start.9 = (bf16[1024,128]{1,0:T(8,128)(2,1)S(1)}, bf16[1024,128]{1,0:T(8,128)(2,1)S(1)}, u32[]{:S(2)}, u32[]{:S(2)}) collective-permute-start(bf16[1024,128]{1,0:T(8,128)(2,1)S(1)} %bitcast.17), channel_id=1, source_target_pairs={{0,16},{16,32},{32,48},{48,0},{1,17},{17,33},{33,49},{49,1},{2,18}... | collective-permute-start | bytes 786440 | tf_op jit(solution)/shard_map/ppermute | solution.py:265
  47.3 35.2 %collective-permute-start.12 = (bf16[128,2048]{1,0:T(8,128)(2,1)S(1)}, bf16[128,2048]{1,0:T(8,128)(2,1)S(1)}, u32[]{:S(2)}, u32[]{:S(2)}) collective-permute-start(bf16[128,2048]{1,0:T(8,128)(2,1)S(1)} %pad_maximum_fusion), channel_id=1, source_target_pairs={{0,1},{1,2},{2,3},{3,4},{4,5},{5,6},{6,7},{7,8},{8,9},{9,10},{10,1... | collective-permute-start | bytes 1572872 | tf_op jit(solution)/shard_map/ppermute | solution.py:296
  51.1 31.3 %collective-permute-start.13 = (bf16[128,2048]{1,0:T(8,128)(2,1)S(1)}, bf16[128,2048]{1,0:T(8,128)(2,1)S(1)}, u32[]{:S(2)}, u32[]{:S(2)}) collective-permute-start(bf16[128,2048]{1,0:T(8,128)(2,1)S(1)} %pad_maximum_fusion), channel_id=1, source_target_pairs={{1,0},{2,1},{3,2},{4,3},{5,4},{6,5},{7,6},{8,7},{9,8},{10,9},{11,1... | collective-permute-start | bytes 1572872 | tf_op jit(solution)/shard_map/ppermute | solution.py:297
  76.0 6.5 %copy-start.5 = (bf16[1,128,1024]{2,1,0:T(8,128)(2,1)S(1)}, bf16[1,128,1024]{2,1,0:T(8,128)(2,1)}, u32[]{:S(2)}) copy-start(bf16[1,128,1024]{2,1,0:T(8,128)(2,1)} %param.10) | copy-start | bytes 786436
  76.0 15.1 %all-to-all-start.1 = ((bf16[16,64,128]{2,1,0:T(8,128)(2,1)}), bf16[16,64,128]{2,1,0:T(8,128)(2,1)S(1)}, u32[]{:S(2)}, u32[]{:S(2)}) async-start(bf16[16,64,128]{2,1,0:T(8,128)(2,1)} %heavy.1), calls=%async_computation.1 | async-start | bytes 524288 | tf_op jit(solution)/shard_map/all_to_all | solution.py:301
  82.5 8.7 %copy-start.3 = (s32[1,64]{1,0:T(1,128)S(1)}, s32[1,64]{1,0:T(1,128)}, u32[]{:S(2)}) copy-start(s32[1,64]{1,0:T(1,128)} %ids.3) | copy-start | bytes 772
Sparse Core Ops, SparseCore 0:
  41.9 45.8 all-gather.1

commit v4 on v3

--- a/solution.py
+++ b/solution.py
@@ -254,6 +254,26 @@
     )(*parts)
 
 
+def spread_kernel(own, down1, down2, down3, out):
+    place = lax.axis_index("fine")
+    side = own.shape[0]
+    row, col = place // side, place % side
+    for dr, got in enumerate((own, down1, down2, down3)):
+        at = (row + side - dr) % side * side
+        for dc in range(side):
+            out[at + (col + side - dc) % side] = got[dc]
+
+
+def spread(rows):
+    side, count, width = rows[0].shape
+    return pl.pallas_call(
+        spread_kernel,
+        out_shape=jax.ShapeDtypeStruct((len(rows) * side, count, width), bf16),
+        compiler_params=params(),
+        name="spread",
+    )(*rows)
+
+
 def around(value, axis, stride=1, ring=None):
     size = lax.axis_size(axis)
     ring = ring or size
@@ -277,30 +297,35 @@
     side = 4
     width = q_light.shape[2]
 
-    row = jnp.concatenate([enc_kv[0]] + around(enc_kv[0], "fine", 1, side), axis=0)
-    enc = [row] + around(row, "fine", side, n_fine // side)
-    chunks = pack(q_heavy[0], k_heavy[0], v_heavy[0])
-    group = lax.all_to_all(after_all(chunks, row), "fine", 0, 0, tiled=True)
-
-    dec_rows = dec_queries.shape[1] // n_fine
-    part = decode(dec_queries[0], enc, dec_rows)
-    share = meet([part] + around(part, "coarse"), dec_rows, width)
-    decoded = lax.all_gather(share, "fine", axis=0, tiled=True)[None]
-
-    own = pick(key_ids, after_all(group, share)).reshape(KGRP * BLOCK, LANES)
-    routed = [own] + around(own, "coarse")
-
     light_kv = jnp.concatenate([k_light[0], v_light[0]], axis=1)
-    light_kv = after_all(light_kv, own)
     up = [(i, i + 1) for i in range(n_seq - 1)]
     prev = lax.ppermute(light_kv, TOKENS, up)
     after = lax.ppermute(light_kv, TOKENS, [(b, a) for a, b in up])
 
+    def rows_of(value):
+        return jnp.concatenate([value] + around(value, "fine", 1, side), axis=0)
+
+    def square(row):
+        return [row] + around(row, "fine", side, n_fine // side)
+
+    row = rows_of(enc_kv[0])
+    enc = square(row)
+    chunks = pack(q_heavy[0], k_heavy[0], v_heavy[0])
+    group = lax.all_to_all(after_all(chunks, enc[1]), "fine", 0, 0, tiled=True)
+
+    dec_rows = dec_queries.shape[1] // n_fine
+    part = decode(dec_queries[0], enc, dec_rows)
+    light = light_attend(after_all(q_light[0], part), k_light[0], v_light[0], prev, after)
+    share = meet([after_all(part, light)] + around(part, "coarse"), dec_rows, width)
+
+    own = pick(key_ids, after_all(group, share)).reshape(KGRP * BLOCK, LANES)
+    routed = [own] + around(own, "coarse")
+    shares = square(rows_of(after_all(share, own)[None]))
+
     heavy = heavy_attend(group, routed)
-    q_light = after_all(q_light, heavy)
+    shares = after_all(shares, heavy)
     heavy = lax.all_to_all(heavy, "fine", 0, 0, tiled=True)
-
-    light = light_attend(q_light[0], k_light[0], v_light[0], prev, after)
+    decoded = spread(shares).reshape(1, -1, width)
     encoded = join(query_ids, light, heavy)[None]
     return (encoded, decoded)
 

time: 102 us -> 109 us (1.069)
  the two profiles are of different devices: /device:TPU:32 before, /device:TPU:0 now
where the time goes in v4:
time: 109 us
  starting transfers between devices  51.8 us (48%)
  waiting for transfers between devices  33.4 us (31%)
  Pallas kernels  20 us (18%)
  other arithmetic  2.6 us (2%)
    ppermute x18, starting transfers between devices, around(): lax.ppermute(value, axis, [(i, to(i, d)) for i in range(size)])  34.6 us
    ppermute x18, waiting for transfers between devices, around(): lax.ppermute(value, axis, [(i, to(i, d)) for i in range(size)])  25.8 us
    pallas_call x1, Pallas kernels, heavy_attend(): pl.pallas_call(heavy_kernel, out_shape=jax.ShapeDtypeStruct((blocks, HALF...  10.5 us
    all_to_all x1, starting transfers between devices, local(): group = lax.all_to_all(after_all(chunks, enc[1]), 'fine', 0, 0, tiled=True)  9.5 us
    all_to_all x1, waiting for transfers between devices, local(): heavy = lax.all_to_all(heavy, 'fine', 0, 0, tiled=True)  7.58 us
    all_to_all x1, starting transfers between devices, local(): heavy = lax.all_to_all(heavy, 'fine', 0, 0, tiled=True)  4.85 us
    pallas_call x1, Pallas kernels, pack(): pl.pallas_call(pack_kernel, in_specs=[hbm] * 3, out_shape=jax.ShapeDtypeS...  2.28 us
  transfers between devices with their start and end apart: 22, of which 12 were waited for; matrix products, arithmetic and copies ran while one was open for 2% of the time, Pallas kernels for 17%

profile of v4, /device:TPU:0, one launch (start us, length us, event | category | flops | bytes accessed | tf_op | source)
XLA Modules:
  0.0 108.6 jit_solution(5211812486187436510)
XLA Ops:
  0.6 2.9 %collective-permute-start.2 = (bf16[128,128]{1,0:T(8,128)(2,1)}, bf16[128,128]{1,0:T(8,128)(2,1)S(1)}, u32[]{:S(2)}, u32[]{:S(2)}) collective-permute-start(bf16[128,128]{1,0:T(8,128)(2,1)} %bitcast.31), channel_id=1, source_target_pairs={{0,3},{1,0},{2,1},{3,2},{4,7},{5,4},{6,5},{7,6},{8,11},{9,8},{10,9... | collective-permute-start | bytes 98312 | tf_op jit(solution)/shard_map/ppermute | solution.py:285
  4.4 0.9 collective-permute-start
  5.5 3.7 %collective-permute-done.1 = bf16[128,128]{1,0:T(8,128)(2,1)S(1)} collective-permute-done((bf16[128,128]{1,0:T(8,128)(2,1)}, bf16[128,128]{1,0:T(8,128)(2,1)S(1)}, u32[]{:S(2)}, u32[]{:S(2)}) %collective-permute-start.1) | collective-permute-done | bytes 32800 | tf_op jit(solution)/shard_map/ppermute | solution.py:285
  10.5 1.6 %collective-permute-start.3 = (bf16[512,128]{1,0:T(8,128)(2,1)S(1)}, bf16[512,128]{1,0:T(8,128)(2,1)S(1)}, u32[]{:S(2)}, u32[]{:S(2)}) collective-permute-start(bf16[512,128]{1,0:T(8,128)(2,1)S(1)} %pad_maximum_fusion.2.e0), channel_id=1, source_target_pairs={{0,4},{1,5},{2,6},{3,7},{4,8},{5,9},{6,10},{7,11},{8,12},{9,13},{1... | collective-permute-start | bytes 393224 | tf_op jit(solution)/shard_map/ppermute | solution.py:285
  12.1 1.8 %pad_maximum_fusion = bf16[128,2048]{1,0:T(8,128)(2,1)} fusion(bf16[128,1024]{1,0:T(8,128)(2,1)} %bitcast.14, bf16[128,1024]{1,0:T(8,128)(2,1)S(1)} %bitcast.12), kind=kLoop, calls=%fused_computation | loop fusion | flops 1048576 | bytes 1048576 | tf_op jit(solution)/shard_map/concatenate | solution.py:300
  13.9 1.6 %collective-permute-start.6 = (bf16[128,2048]{1,0:T(8,128)(2,1)}, bf16[128,2048]{1,0:T(8,128)(2,1)S(1)}, u32[]{:S(2)}, u32[]{:S(2)}) collective-permute-start(bf16[128,2048]{1,0:T(8,128)(2,1)} %pad_maximum_fusion), channel_id=1, source_target_pairs={{0,1},{1,2},{2,3},{3,4},{4,5},{5,6},{6,7},{7,8},{8,9},{9,10},{10,1... | collective-permute-start | bytes 1572872 | tf_op jit(solution)/shard_map/ppermute | solution.py:302
  15.5 1.3 %collective-permute-start.7 = (bf16[128,2048]{1,0:T(8,128)(2,1)}, bf16[128,2048]{1,0:T(8,128)(2,1)S(1)}, u32[]{:S(2)}, u32[]{:S(2)}) collective-permute-start(bf16[128,2048]{1,0:T(8,128)(2,1)} %pad_maximum_fusion), channel_id=1, source_target_pairs={{1,0},{2,1},{3,2},{4,3},{5,4},{6,5},{7,6},{8,7},{9,8},{10,9},{11,1... | collective-permute-start | bytes 1572872 | tf_op jit(solution)/shard_map/ppermute | solution.py:303
  16.8 2.3 %pack.1 = bf16[16,192,128]{2,1,0:T(8,128)(2,1)} custom-call(bf16[128,1024]{1,0:T(8,128)(2,1)} %bitcast.27, bf16[128,1024]{1,0:T(8,128)(2,1)} %bitcast.28, bf16[128,1024]{1,0:T(8,128)(2,1)} %bitcast.29), custom_call_target="tpu_custom_call" | custom-call | tf_op jit(solution)/shard_map/pack/pallas_call | solution.py:60
  19.1 9.5 %all-to-all-start = ((bf16[16,192,128]{2,1,0:T(8,128)(2,1)}), bf16[16,192,128]{2,1,0:T(8,128)(2,1)S(1)}, u32[]{:S(2)}, u32[]{:S(2)}) async-start(bf16[16,192,128]{2,1,0:T(8,128)(2,1)} %pack.1), calls=%async_computation | async-start | bytes 1572864 | tf_op jit(solution)/shard_map/all_to_all | solution.py:314
  28.6 3.4 %collective-permute-start.4 = (bf16[512,128]{1,0:T(8,128)(2,1)S(1)}, bf16[512,128]{1,0:T(8,128)(2,1)S(1)}, u32[]{:S(2)}, u32[]{:S(2)}) collective-permute-start(bf16[512,128]{1,0:T(8,128)(2,1)S(1)} %pad_maximum_fusion.2.e0), channel_id=1, source_target_pairs={{0,8},{1,9},{2,10},{3,11},{4,12},{5,13},{6,14},{7,15},{8,0},{9,1},... | collective-permute-start | bytes 393224 | tf_op jit(solution)/shard_map/ppermute | solution.py:285
  32.1 1.2 %collective-permute-start.5 = (bf16[512,128]{1,0:T(8,128)(2,1)S(1)}, bf16[512,128]{1,0:T(8,128)(2,1)S(1)}, u32[]{:S(2)}, u32[]{:S(2)}) collective-permute-start(bf16[512,128]{1,0:T(8,128)(2,1)S(1)} %pad_maximum_fusion.2.e0), channel_id=1, source_target_pairs={{0,12},{1,13},{2,14},{3,15},{4,0},{5,1},{6,2},{7,3},{8,4},{9,5},{1... | collective-permute-start | bytes 393224 | tf_op jit(solution)/shard_map/ppermute | solution.py:285
  33.2 9.8 %collective-permute-done.4.e2 = bf16[512,128]{1,0:T(8,128)(2,1)S(1)} collective-permute-done((bf16[512,128]{1,0:T(8,128)(2,1)S(1)}, bf16[512,128]{1,0:T(8,128)(2,1)S(1)}, u32[]{:S(2)}, u32[]{:S(2)}) %collective-permute-start.4) | collective-permute-done | bytes 131104 | tf_op jit(solution)/shard_map/ppermute | solution.py:285
  43.8 1.8 %decode.1.a = bf16[512,128]{1,0:T(8,128)(2,1)S(1)} custom-call(bf16[512,1024]{1,0:T(8,128)(2,1)S(1)} %bitcast.24, bf16[512,128]{1,0:T(8,128)(2,1)S(1)} %pad_maximum_fusion.2.e0, bf16[512,128]{1,0:T(8,128)(2,1)S(1)} %collective-permute-done.3.e1, bf16[512,128]{1,0:T(8,128)(2,1)S(1)} %collective-permute-done.4.e2, bf16[512,128]{1,0:T(8,128)(2,1)S(1)} %collective-permute-done.5.e3), custom_call_target="tpu_custom_call" | custom-call | flops 1000000000 | bytes 1000000 | tf_op jit(solution)/shard_map/decode/pallas_call | solution.py:220
  45.5 3.0 %collective-permute-start.8 = (bf16[512,128]{1,0:T(8,128)(2,1)S(1)}, bf16[512,128]{1,0:T(8,128)(2,1)S(1)}, u32[]{:S(2)}, u32[]{:S(2)}) collective-permute-start(bf16[512,128]{1,0:T(8,128)(2,1)S(1)} %decode.1.a), channel_id=1, source_target_pairs={{0,16},{16,32},{32,48},{48,0},{1,17},{17,33},{33,49},{49,1},{2,18}... | collective-permute-start | bytes 393224 | tf_op jit(solution)/shard_map/ppermute | solution.py:285
  48.5 3.6 %collective-permute-start.9 = (bf16[512,128]{1,0:T(8,128)(2,1)S(1)}, bf16[512,128]{1,0:T(8,128)(2,1)S(1)}, u32[]{:S(2)}, u32[]{:S(2)}) collective-permute-start(bf16[512,128]{1,0:T(8,128)(2,1)S(1)} %decode.1.a), channel_id=1, source_target_pairs={{0,32},{16,48},{32,0},{48,16},{1,33},{17,49},{33,1},{49,17},{2,34}... | collective-permute-start | bytes 393224 | tf_op jit(solution)/shard_map/ppermute | solution.py:285
  52.1 1.0 collective-permute-start.10
  53.1 1.5 %light.1 = f32[128,1024]{1,0:T(8,128)S(1)} custom-call(bf16[128,1024]{1,0:T(8,128)(2,1)S(1)} %bitcast.25, bf16[128,1024]{1,0:T(8,128)(2,1)S(1)} %bitcast.13, bf16[128,1024]{1,0:T(8,128)(2,1)S(1)} %bitcast.15, bf16[128,2048]{1,0:T(8,128)(2,1)S(1)} %collective-permute-done.6.prev, bf16[128,2048]{1,0:T(8,128)(2,1)S(1)} %collective-permute-done.7.after), custom_call_target="tpu_custom_call" | custom-call | flops 3000000000 | bytes 2000000 | tf_op jit(solution)/shard_map/light/pallas_call | solution.py:155
  55.0 1.7 %collective-permute-done.9.c = bf16[512,128]{1,0:T(8,128)(2,1)S(1)} collective-permute-done((bf16[512,128]{1,0:T(8,128)(2,1)S(1)}, bf16[512,128]{1,0:T(8,128)(2,1)S(1)}, u32[]{:S(2)}, u32[]{:S(2)}) %collective-permute-start.9) | collective-permute-done | bytes 131104 | tf_op jit(solution)/shard_map/ppermute | solution.py:285
  57.1 0.8 meet.1
  58.5 1.0 collective-permute-start.11
  59.5 2.9 %collective-permute-start.12 = (bf16[1024,128]{1,0:T(8,128)(2,1)S(1)}, bf16[1024,128]{1,0:T(8,128)(2,1)S(1)}, u32[]{:S(2)}, u32[]{:S(2)}) collective-permute-start(bf16[1024,128]{1,0:T(8,128)(2,1)S(1)} %bitcast.17), channel_id=1, source_target_pairs={{0,32},{16,48},{32,0},{48,16},{1,33},{17,49},{33,1},{49,17},{2,34}... | collective-permute-start | bytes 786440 | tf_op jit(solution)/shard_map/ppermute | solution.py:285
  63.1 6.3 %collective-permute-start.16 = (bf16[1,32,1024]{2,1,0:T(8,128)(2,1)S(1)}, bf16[1,32,1024]{2,1,0:T(8,128)(2,1)S(1)}, u32[]{:S(2)}, u32[]{:S(2)}) collective-permute-start(bf16[1,32,1024]{2,1,0:T(8,128)(2,1)S(1)} %bitcast.20), channel_id=1, source_target_pairs={{0,3},{1,0},{2,1},{3,2},{4,7},{5,4},{6,5},{7,6},{8,11},{9,8},{10,9... | collective-permute-start | bytes 196616 | tf_op jit(solution)/shard_map/ppermute | solution.py:285
  69.4 2.5 %collective-permute-done.16 = bf16[1,32,1024]{2,1,0:T(8,128)(2,1)S(1)} collective-permute-done((bf16[1,32,1024]{2,1,0:T(8,128)(2,1)S(1)}, bf16[1,32,1024]{2,1,0:T(8,128)(2,1)S(1)}, u32[]{:S(2)}, u32[]{:S(2)}) %collective-permute-start.16) | collective-permute-done | bytes 65568 | tf_op jit(solution)/shard_map/ppermute | solution.py:285
  72.0 3.2 %collective-permute-done.15 = bf16[1,32,1024]{2,1,0:T(8,128)(2,1)S(1)} collective-permute-done((bf16[1,32,1024]{2,1,0:T(8,128)(2,1)S(1)}, bf16[1,32,1024]{2,1,0:T(8,128)(2,1)S(1)}, u32[]{:S(2)}, u32[]{:S(2)}) %collective-permute-start.15) | collective-permute-done | bytes 65568 | tf_op jit(solution)/shard_map/ppermute | solution.py:285
  75.2 2.7 %collective-permute-done.14 = bf16[1,32,1024]{2,1,0:T(8,128)(2,1)S(1)} collective-permute-done((bf16[1,32,1024]{2,1,0:T(8,128)(2,1)S(1)}, bf16[1,32,1024]{2,1,0:T(8,128)(2,1)S(1)}, u32[]{:S(2)}, u32[]{:S(2)}) %collective-permute-start.14) | collective-permute-done | bytes 65568 | tf_op jit(solution)/shard_map/ppermute | solution.py:285
  77.9 1.4 %collective-permute-start.17 = (bf16[4,32,1024]{2,1,0:T(8,128)(2,1)S(1)}, bf16[4,32,1024]{2,1,0:T(8,128)(2,1)S(1)}, u32[]{:S(2)}, u32[]{:S(2)}) collective-permute-start(bf16[4,32,1024]{2,1,0:T(8,128)(2,1)S(1)} %pad_maximum_fusion.1.own), channel_id=1, source_target_pairs={{0,4},{1,5},{2,6},{3,7},{4,8},{5,9},{6,10},{7,11},{8,12},{9,13},{1... | collective-permute-start | bytes 786440 | tf_op jit(solution)/shard_map/ppermute | solution.py:285
  79.3 3.8 %collective-permute-start.18 = (bf16[4,32,1024]{2,1,0:T(8,128)(2,1)S(1)}, bf16[4,32,1024]{2,1,0:T(8,128)(2,1)S(1)}, u32[]{:S(2)}, u32[]{:S(2)}) collective-permute-start(bf16[4,32,1024]{2,1,0:T(8,128)(2,1)S(1)} %pad_maximum_fusion.1.own), channel_id=1, source_target_pairs={{0,8},{1,9},{2,10},{3,11},{4,12},{5,13},{6,14},{7,15},{8,0},{9,1},... | collective-permute-start | bytes 786440 | tf_op jit(solution)/shard_map/ppermute | solution.py:285
  83.1 10.5 %heavy.1 = bf16[16,64,128]{2,1,0:T(8,128)(2,1)} custom-call(bf16[16,192,128]{2,1,0:T(8,128)(2,1)S(1)} %all-to-all-done.kv.q, bf16[1024,128]{1,0:T(8,128)(2,1)S(1)} %bitcast.19, bf16[1024,128]{1,0:T(8,128)(2,1)S(1)} %collective-permute-done.11.kv1, bf16[1024,128]{1,0:T(8,128)(2,1)S(1)} %collective-permute-done.12.kv2, ...), custom_call_target="tpu_custom_call" | custom-call | flops 10000000000 | bytes 2000000 | tf_op jit(solution)/shard_map/heavy/pallas_call | solution.py:119
  93.6 4.9 %all-to-all-start.1 = ((bf16[16,64,128]{2,1,0:T(8,128)(2,1)}), bf16[16,64,128]{2,1,0:T(8,128)(2,1)S(1)}, u32[]{:S(2)}, u32[]{:S(2)}) async-start(bf16[16,64,128]{2,1,0:T(8,128)(2,1)} %heavy.1), calls=%async_computation.1 | async-start | bytes 524288 | tf_op jit(solution)/shard_map/all_to_all | solution.py:327
  98.5 1.1 spread.1
  99.6 7.6 %all-to-all-done.1.heavy = bf16[16,64,128]{2,1,0:T(8,128)(2,1)S(1)} async-done(((bf16[16,64,128]{2,1,0:T(8,128)(2,1)}), bf16[16,64,128]{2,1,0:T(8,128)(2,1)S(1)}, u32[]{:S(2)}, u32[]{:S(2)}) %all-to-all-start.1) | async-done | bytes 262176 | tf_op jit(solution)/shard_map/all_to_all | solution.py:327
  107.2 1.5 %join.1 = bf16[128,1024]{1,0:T(8,128)(2,1)} custom-call(s32[1,64]{1,0:T(1,128)S(1)} %copy-done.3, f32[128,1024]{1,0:T(8,128)S(1)} %light.1, bf16[16,64,128]{2,1,0:T(8,128)(2,1)S(1)} %all-to-all-done.1.heavy), custom_call_target="tpu_custom_call" | custom-call | tf_op jit(solution)/shard_map/join/pallas_call | solution.py:181
  (35 shorter events, 5.1 us)
Async XLA Ops:
  0.6 11.5 %copy-start = (bf16[1,128,1024]{2,1,0:T(8,128)(2,1)S(1)}, bf16[1,128,1024]{2,1,0:T(8,128)(2,1)}, u32[]{:S(2)}) copy-start(bf16[1,128,1024]{2,1,0:T(8,128)(2,1)} %param.11) | copy-start | bytes 786436
  0.6 4.8 %collective-permute-start.2 = (bf16[128,128]{1,0:T(8,128)(2,1)}, bf16[128,128]{1,0:T(8,128)(2,1)S(1)}, u32[]{:S(2)}, u32[]{:S(2)}) collective-permute-start(bf16[128,128]{1,0:T(8,128)(2,1)} %bitcast.31), channel_id=1, source_target_pairs={{0,3},{1,0},{2,1},{3,2},{4,7},{5,4},{6,5},{7,6},{8,11},{9,8},{10,9... | collective-permute-start | bytes 98312 | tf_op jit(solution)/shard_map/ppermute | solution.py:285
  3.6 5.6 %collective-permute-start.1 = (bf16[128,128]{1,0:T(8,128)(2,1)}, bf16[128,128]{1,0:T(8,128)(2,1)S(1)}, u32[]{:S(2)}, u32[]{:S(2)}) collective-permute-start(bf16[128,128]{1,0:T(8,128)(2,1)} %bitcast.32), channel_id=1, source_target_pairs={{0,2},{1,3},{2,0},{3,1},{4,6},{5,7},{6,4},{7,5},{8,10},{9,11},{10,... | collective-permute-start | bytes 98312 | tf_op jit(solution)/shard_map/ppermute | solution.py:285
  4.4 5.3 %collective-permute-start = (bf16[128,128]{1,0:T(8,128)(2,1)}, bf16[128,128]{1,0:T(8,128)(2,1)S(1)}, u32[]{:S(2)}, u32[]{:S(2)}) collective-permute-start(bf16[128,128]{1,0:T(8,128)(2,1)} %bitcast.33), channel_id=1, source_target_pairs={{0,1},{1,2},{2,3},{3,0},{4,5},{5,6},{6,7},{7,4},{8,9},{9,10},{10,1... | collective-permute-start | bytes 98312 | tf_op jit(solution)/shard_map/ppermute | solution.py:285
  10.5 8.7 %collective-permute-start.3 = (bf16[512,128]{1,0:T(8,128)(2,1)S(1)}, bf16[512,128]{1,0:T(8,128)(2,1)S(1)}, u32[]{:S(2)}, u32[]{:S(2)}) collective-permute-start(bf16[512,128]{1,0:T(8,128)(2,1)S(1)} %pad_maximum_fusion.2.e0), channel_id=1, source_target_pairs={{0,4},{1,5},{2,6},{3,7},{4,8},{5,9},{6,10},{7,11},{8,12},{9,13},{1... | collective-permute-start | bytes 393224 | tf_op jit(solution)/shard_map/ppermute | solution.py:285
  13.9 39.2 %collective-permute-start.6 = (bf16[128,2048]{1,0:T(8,128)(2,1)}, bf16[128,2048]{1,0:T(8,128)(2,1)S(1)}, u32[]{:S(2)}, u32[]{:S(2)}) collective-permute-start(bf16[128,2048]{1,0:T(8,128)(2,1)} %pad_maximum_fusion), channel_id=1, source_target_pairs={{0,1},{1,2},{2,3},{3,4},{4,5},{5,6},{6,7},{7,8},{8,9},{9,10},{10,1... | collective-permute-start | bytes 1572872 | tf_op jit(solution)/shard_map/ppermute | solution.py:302
  15.5 37.6 %collective-permute-start.7 = (bf16[128,2048]{1,0:T(8,128)(2,1)}, bf16[128,2048]{1,0:T(8,128)(2,1)S(1)}, u32[]{:S(2)}, u32[]{:S(2)}) collective-permute-start(bf16[128,2048]{1,0:T(8,128)(2,1)} %pad_maximum_fusion), channel_id=1, source_target_pairs={{1,0},{2,1},{3,2},{4,3},{5,4},{6,5},{7,6},{8,7},{9,8},{10,9},{11,1... | collective-permute-start | bytes 1572872 | tf_op jit(solution)/shard_map/ppermute | solution.py:303
  19.1 24.7 %copy-start.4 = (bf16[1,512,1024]{2,1,0:T(8,128)(2,1)S(1)}, bf16[1,512,1024]{2,1,0:T(8,128)(2,1)}, u32[]{:S(2)}) copy-start(bf16[1,512,1024]{2,1,0:T(8,128)(2,1)} %param.17) | copy-start | bytes 3145732
  19.1 38.8 %all-to-all-start = ((bf16[16,192,128]{2,1,0:T(8,128)(2,1)}), bf16[16,192,128]{2,1,0:T(8,128)(2,1)S(1)}, u32[]{:S(2)}, u32[]{:S(2)}) async-start(bf16[16,192,128]{2,1,0:T(8,128)(2,1)} %pack.1), calls=%async_computation | async-start | bytes 1572864 | tf_op jit(solution)/shard_map/all_to_all | solution.py:314
  28.6 14.4 %collective-permute-start.4 = (bf16[512,128]{1,0:T(8,128)(2,1)S(1)}, bf16[512,128]{1,0:T(8,128)(2,1)S(1)}, u32[]{:S(2)}, u32[]{:S(2)}) collective-permute-start(bf16[512,128]{1,0:T(8,128)(2,1)S(1)} %pad_maximum_fusion.2.e0), channel_id=1, source_target_pairs={{0,8},{1,9},{2,10},{3,11},{4,12},{5,13},{6,14},{7,15},{8,0},{9,1},... | collective-permute-start | bytes 393224 | tf_op jit(solution)/shard_map/ppermute | solution.py:285
  32.1 11.7 %collective-permute-start.5 = (bf16[512,128]{1,0:T(8,128)(2,1)S(1)}, bf16[512,128]{1,0:T(8,128)(2,1)S(1)}, u32[]{:S(2)}, u32[]{:S(2)}) collective-permute-start(bf16[512,128]{1,0:T(8,128)(2,1)S(1)} %pad_maximum_fusion.2.e0), channel_id=1, source_target_pairs={{0,12},{1,13},{2,14},{3,15},{4,0},{5,1},{6,2},{7,3},{8,4},{9,5},{1... | collective-permute-start | bytes 393224 | tf_op jit(solution)/shard_map/ppermute | solution.py:285
  43.8 9.4 %copy-start.1 = (bf16[1,128,1024]{2,1,0:T(8,128)(2,1)S(1)}, bf16[1,128,1024]{2,1,0:T(8,128)(2,1)}, u32[]{:S(2)}) copy-start(bf16[1,128,1024]{2,1,0:T(8,128)(2,1)} %param.12) | copy-start | bytes 786436
  43.8 9.4 %copy-start.5 = (bf16[1,128,1024]{2,1,0:T(8,128)(2,1)S(1)}, bf16[1,128,1024]{2,1,0:T(8,128)(2,1)}, u32[]{:S(2)}) copy-start(bf16[1,128,1024]{2,1,0:T(8,128)(2,1)} %param.10) | copy-start | bytes 786436
  45.5 9.4 %collective-permute-start.8 = (bf16[512,128]{1,0:T(8,128)(2,1)S(1)}, bf16[512,128]{1,0:T(8,128)(2,1)S(1)}, u32[]{:S(2)}, u32[]{:S(2)}) collective-permute-start(bf16[512,128]{1,0:T(8,128)(2,1)S(1)} %decode.1.a), channel_id=1, source_target_pairs={{0,16},{16,32},{32,48},{48,0},{1,17},{17,33},{33,49},{49,1},{2,18}... | collective-permute-start | bytes 393224 | tf_op jit(solution)/shard_map/ppermute | solution.py:285
  48.5 8.2 %collective-permute-start.9 = (bf16[512,128]{1,0:T(8,128)(2,1)S(1)}, bf16[512,128]{1,0:T(8,128)(2,1)S(1)}, u32[]{:S(2)}, u32[]{:S(2)}) collective-permute-start(bf16[512,128]{1,0:T(8,128)(2,1)S(1)} %decode.1.a), channel_id=1, source_target_pairs={{0,32},{16,48},{32,0},{48,16},{1,33},{17,49},{33,1},{49,17},{2,34}... | collective-permute-start | bytes 393224 | tf_op jit(solution)/shard_map/ppermute | solution.py:285
  52.1 5.0 %collective-permute-start.10 = (bf16[512,128]{1,0:T(8,128)(2,1)S(1)}, bf16[512,128]{1,0:T(8,128)(2,1)S(1)}, u32[]{:S(2)}, u32[]{:S(2)}) collective-permute-start(bf16[512,128]{1,0:T(8,128)(2,1)S(1)} %decode.1.a), channel_id=1, source_target_pairs={{0,48},{16,0},{32,16},{48,32},{1,49},{17,1},{33,17},{49,33},{2,50}... | collective-permute-start | bytes 393224 | tf_op jit(solution)/shard_map/ppermute | solution.py:285
  54.7 3.3 %copy-start.2 = (s32[1,32]{1,0:T(1,128)S(1)}, s32[1,32]{1,0:T(1,128)}, u32[]{:S(2)}) copy-start(s32[1,32]{1,0:T(1,128)} %ids.2) | copy-start | bytes 388
  58.5 24.6 %collective-permute-start.11 = (bf16[1024,128]{1,0:T(8,128)(2,1)S(1)}, bf16[1024,128]{1,0:T(8,128)(2,1)S(1)}, u32[]{:S(2)}, u32[]{:S(2)}) collective-permute-start(bf16[1024,128]{1,0:T(8,128)(2,1)S(1)} %bitcast.16), channel_id=1, source_target_pairs={{0,16},{16,32},{32,48},{48,0},{1,17},{17,33},{33,49},{49,1},{2,18}... | collective-permute-start | bytes 786440 | tf_op jit(solution)/shard_map/ppermute | solution.py:285
  59.5 23.7 %collective-permute-start.12 = (bf16[1024,128]{1,0:T(8,128)(2,1)S(1)}, bf16[1024,128]{1,0:T(8,128)(2,1)S(1)}, u32[]{:S(2)}, u32[]{:S(2)}) collective-permute-start(bf16[1024,128]{1,0:T(8,128)(2,1)S(1)} %bitcast.17), channel_id=1, source_target_pairs={{0,32},{16,48},{32,0},{48,16},{1,33},{17,49},{33,1},{49,17},{2,34}... | collective-permute-start | bytes 786440 | tf_op jit(solution)/shard_map/ppermute | solution.py:285
  62.4 20.7 %collective-permute-start.13 = (bf16[1024,128]{1,0:T(8,128)(2,1)S(1)}, bf16[1024,128]{1,0:T(8,128)(2,1)S(1)}, u32[]{:S(2)}, u32[]{:S(2)}) collective-permute-start(bf16[1024,128]{1,0:T(8,128)(2,1)S(1)} %bitcast.18), channel_id=1, source_target_pairs={{0,48},{16,0},{32,16},{48,32},{1,49},{17,1},{33,17},{49,33},{2,50}... | collective-permute-start | bytes 786440 | tf_op jit(solution)/shard_map/ppermute | solution.py:285
  63.1 8.8 %collective-permute-start.16 = (bf16[1,32,1024]{2,1,0:T(8,128)(2,1)S(1)}, bf16[1,32,1024]{2,1,0:T(8,128)(2,1)S(1)}, u32[]{:S(2)}, u32[]{:S(2)}) collective-permute-start(bf16[1,32,1024]{2,1,0:T(8,128)(2,1)S(1)} %bitcast.20), channel_id=1, source_target_pairs={{0,3},{1,0},{2,1},{3,2},{4,7},{5,4},{6,5},{7,6},{8,11},{9,8},{10,9... | collective-permute-start | bytes 196616 | tf_op jit(solution)/shard_map/ppermute | solution.py:285
  69.4 5.8 %collective-permute-start.15 = (bf16[1,32,1024]{2,1,0:T(8,128)(2,1)S(1)}, bf16[1,32,1024]{2,1,0:T(8,128)(2,1)S(1)}, u32[]{:S(2)}, u32[]{:S(2)}) collective-permute-start(bf16[1,32,1024]{2,1,0:T(8,128)(2,1)S(1)} %bitcast.21), channel_id=1, source_target_pairs={{0,2},{1,3},{2,0},{3,1},{4,6},{5,7},{6,4},{7,5},{8,10},{9,11},{10,... | collective-permute-start | bytes 196616 | tf_op jit(solution)/shard_map/ppermute | solution.py:285
  72.0 5.9 %collective-permute-start.14 = (bf16[1,32,1024]{2,1,0:T(8,128)(2,1)S(1)}, bf16[1,32,1024]{2,1,0:T(8,128)(2,1)S(1)}, u32[]{:S(2)}, u32[]{:S(2)}) collective-permute-start(bf16[1,32,1024]{2,1,0:T(8,128)(2,1)S(1)} %bitcast.22), channel_id=1, source_target_pairs={{0,1},{1,2},{2,3},{3,0},{4,5},{5,6},{6,7},{7,4},{8,9},{9,10},{10,1... | collective-permute-start | bytes 196616 | tf_op jit(solution)/shard_map/ppermute | solution.py:285
  77.9 20.6 %collective-permute-start.17 = (bf16[4,32,1024]{2,1,0:T(8,128)(2,1)S(1)}, bf16[4,32,1024]{2,1,0:T(8,128)(2,1)S(1)}, u32[]{:S(2)}, u32[]{:S(2)}) collective-permute-start(bf16[4,32,1024]{2,1,0:T(8,128)(2,1)S(1)} %pad_maximum_fusion.1.own), channel_id=1, source_target_pairs={{0,4},{1,5},{2,6},{3,7},{4,8},{5,9},{6,10},{7,11},{8,12},{9,13},{1... | collective-permute-start | bytes 786440 | tf_op jit(solution)/shard_map/ppermute | solution.py:285
  79.3 19.2 %collective-permute-start.18 = (bf16[4,32,1024]{2,1,0:T(8,128)(2,1)S(1)}, bf16[4,32,1024]{2,1,0:T(8,128)(2,1)S(1)}, u32[]{:S(2)}, u32[]{:S(2)}) collective-permute-start(bf16[4,32,1024]{2,1,0:T(8,128)(2,1)S(1)} %pad_maximum_fusion.1.own), channel_id=1, source_target_pairs={{0,8},{1,9},{2,10},{3,11},{4,12},{5,13},{6,14},{7,15},{8,0},{9,1},... | collective-permute-start | bytes 786440 | tf_op jit(solution)/shard_map/ppermute | solution.py:285
  83.1 15.4 %collective-permute-start.19 = (bf16[4,32,1024]{2,1,0:T(8,128)(2,1)S(1)}, bf16[4,32,1024]{2,1,0:T(8,128)(2,1)S(1)}, u32[]{:S(2)}, u32[]{:S(2)}) collective-permute-start(bf16[4,32,1024]{2,1,0:T(8,128)(2,1)S(1)} %pad_maximum_fusion.1.own), channel_id=1, source_target_pairs={{0,12},{1,13},{2,14},{3,15},{4,0},{5,1},{6,2},{7,3},{8,4},{9,5},{1... | collective-permute-start | bytes 786440 | tf_op jit(solution)/shard_map/ppermute | solution.py:285
  93.6 13.6 %all-to-all-start.1 = ((bf16[16,64,128]{2,1,0:T(8,128)(2,1)}), bf16[16,64,128]{2,1,0:T(8,128)(2,1)S(1)}, u32[]{:S(2)}, u32[]{:S(2)}) async-start(bf16[16,64,128]{2,1,0:T(8,128)(2,1)} %heavy.1), calls=%async_computation.1 | async-start | bytes 524288 | tf_op jit(solution)/shard_map/all_to_all | solution.py:327
  98.5 8.7 %copy-start.3 = (s32[1,64]{1,0:T(1,128)S(1)}, s32[1,64]{1,0:T(1,128)}, u32[]{:S(2)}) copy-start(s32[1,64]{1,0:T(1,128)} %ids.3) | copy-start | bytes 772

commit v5 on v4

--- a/solution.py
+++ b/solution.py
@@ -254,6 +254,25 @@
     )(*parts)
 
 
+def stack_kernel(*refs):
+    parts, out = refs[:4], refs[-1]
+    size = parts[0].shape[0]
+    for n, part in enumerate(parts):
+        out[n * size : (n + 1) * size] = part[...]
+
+
+def stack(parts, *others):
+    first = parts[0]
+    specs = [pl.BlockSpec(memory_space=pltpu.VMEM)] * len(parts)
+    return pl.pallas_call(
+        stack_kernel,
+        in_specs=specs + [pl.BlockSpec(memory_space=pl.ANY)] * len(others),
+        out_shape=jax.ShapeDtypeStruct((len(parts) * first.shape[0],) + first.shape[1:], first.dtype),
+        compiler_params=params(),
+        name="stack",
+    )(*parts, *others)
+
+
 def spread_kernel(own, down1, down2, down3, out):
     place = lax.axis_index("fine")
     side = own.shape[0]
@@ -298,33 +317,34 @@
     width = q_light.shape[2]
 
     light_kv = jnp.concatenate([k_light[0], v_light[0]], axis=1)
+
+    def rows_of(value):
+        return [value] + around(value, "fine", 1, side)
+
+    def square(row):
+        return [row] + around(row, "fine", side, n_fine // side)
+
+    enc = square(stack(rows_of(enc_kv[0]), light_kv))
+    chunks = pack(q_heavy[0], k_heavy[0], v_heavy[0])
+    group = lax.all_to_all(after_all(chunks, enc[1], enc[2], enc[3]), "fine", 0, 0, tiled=True)
+
+    dec_rows = dec_queries.shape[1] // n_fine
+    part = decode(dec_queries[0], enc, dec_rows)
+    share = meet([part] + around(part, "coarse"), dec_rows, width)
+
+    own = pick(key_ids, after_all(group, share)).reshape(KGRP * BLOCK, LANES)
+    routed = [own] + around(own, "coarse")
+    shares = square(stack(rows_of(after_all(share, own)[None])))
+
+    light_kv = after_all(light_kv, routed)
     up = [(i, i + 1) for i in range(n_seq - 1)]
     prev = lax.ppermute(light_kv, TOKENS, up)
     after = lax.ppermute(light_kv, TOKENS, [(b, a) for a, b in up])
 
-    def rows_of(value):
-        return jnp.concatenate([value] + around(value, "fine", 1, side), axis=0)
-
-    def square(row):
-        return [row] + around(row, "fine", side, n_fine // side)
-
-    row = rows_of(enc_kv[0])
-    enc = square(row)
-    chunks = pack(q_heavy[0], k_heavy[0], v_heavy[0])
-    group = lax.all_to_all(after_all(chunks, enc[1]), "fine", 0, 0, tiled=True)
-
-    dec_rows = dec_queries.shape[1] // n_fine
-    part = decode(dec_queries[0], enc, dec_rows)
-    light = light_attend(after_all(q_light[0], part), k_light[0], v_light[0], prev, after)
-    share = meet([after_all(part, light)] + around(part, "coarse"), dec_rows, width)
-
-    own = pick(key_ids, after_all(group, share)).reshape(KGRP * BLOCK, LANES)
-    routed = [own] + around(own, "coarse")
-    shares = square(rows_of(after_all(share, own)[None]))
-
     heavy = heavy_attend(group, routed)
-    shares = after_all(shares, heavy)
+    shares, q_light = after_all((shares, q_light), heavy)
     heavy = lax.all_to_all(heavy, "fine", 0, 0, tiled=True)
+    light = light_attend(q_light[0], k_light[0], v_light[0], prev, after)
     decoded = spread(shares).reshape(1, -1, width)
     encoded = join(query_ids, light, heavy)[None]
     return (encoded, decoded)

time: 109 us -> 93.3 us (0.86)
  waiting for transfers between devices: 33.4 us -> 25.3 us
  starting transfers between devices: 51.8 us -> 45.6 us
  other arithmetic: 2.6 us -> 1.07 us
    ppermute x18, starting transfers between devices: 34.6 us -> 26.6 us  [around(): lax.ppermute(value, axis, [(i, to(i, d)) for i in range(size)])]
    ppermute x18, waiting for transfers between devices: 25.8 us -> 19.4 us  [around(): lax.ppermute(value, axis, [(i, to(i, d)) for i in range(size)])]
    all_to_all x1, starting transfers between devices: 9.5 us -> 3.61 us  [local(): lax.all_to_all(after_all(chunks, enc[1], enc[2], enc[3]), 'fine', 0, 0, t...]
    all_to_all x1, starting transfers between devices: 4.85 us -> 9.39 us  [local(): heavy = lax.all_to_all(heavy, 'fine', 0, 0, tiled=True)]
    ppermute x1, starting transfers between devices: 1.6 us -> 4.76 us  [local(): prev = lax.ppermute(light_kv, TOKENS, up)]
    all_to_all x1, waiting for transfers between devices: 7.58 us -> 5.9 us  [local(): heavy = lax.all_to_all(heavy, 'fine', 0, 0, tiled=True)]
  transfers between devices with their start and end apart: 22 -> 22, of which waited for: 12 -> 12; matrix products, arithmetic and copies ran while one was open for 2% -> 1% of each run, Pallas kernels for 17% -> 19%
where the time goes in v5:
time: 93.3 us; the launch traced here: 92.9 us
  starting transfers between devices  45.6 us (49%)
  waiting for transfers between devices  25.3 us (27%)
  Pallas kernels  19.9 us (21%)
  other arithmetic  1.07 us (1%)
    ppermute x18, starting transfers between devices, around(): lax.ppermute(value, axis, [(i, to(i, d)) for i in range(size)])  26.6 us
    ppermute x18, waiting for transfers between devices, around(): lax.ppermute(value, axis, [(i, to(i, d)) for i in range(size)])  19.4 us
    pallas_call x1, Pallas kernels, heavy_attend(): pl.pallas_call(heavy_kernel, out_shape=jax.ShapeDtypeStruct((blocks, HALF...  10.4 us
    all_to_all x1, starting transfers between devices, local(): heavy = lax.all_to_all(heavy, 'fine', 0, 0, tiled=True)  9.39 us
    all_to_all x1, waiting for transfers between devices, local(): heavy = lax.all_to_all(heavy, 'fine', 0, 0, tiled=True)  5.9 us
    ppermute x1, starting transfers between devices, local(): prev = lax.ppermute(light_kv, TOKENS, up)  4.76 us
    all_to_all x1, starting transfers between devices, local(): lax.all_to_all(after_all(chunks, enc[1], enc[2], enc[3]), 'fine', 0, 0, t...  3.61 us
    pallas_call x1, Pallas kernels, pack(): pl.pallas_call(pack_kernel, in_specs=[hbm] * 3, out_shape=jax.ShapeDtypeS...  2.28 us
  transfers between devices with their start and end apart: 22, of which 12 were waited for; matrix products, arithmetic and copies ran while one was open for 1% of the time, Pallas kernels for 19%

profile of v5, /device:TPU:0, one launch (start us, length us, event | category | flops | bytes accessed | tf_op | source)
XLA Modules:
  0.0 92.9 jit_solution(5391798425485560800)
XLA Ops:
  0.6 2.9 %collective-permute-start.2 = (bf16[128,128]{1,0:T(8,128)(2,1)}, bf16[128,128]{1,0:T(8,128)(2,1)S(1)}, u32[]{:S(2)}, u32[]{:S(2)}) collective-permute-start(bf16[128,128]{1,0:T(8,128)(2,1)} %bitcast.24), channel_id=1, source_target_pairs={{0,3},{1,0},{2,1},{3,2},{4,7},{5,4},{6,5},{7,6},{8,11},{9,8},{10,9... | collective-permute-start | bytes 98312 | tf_op jit(solution)/shard_map/ppermute | solution.py:304
  4.3 0.9 collective-permute-start
  5.2 1.1 %pad_maximum_fusion.refs_4_ = bf16[128,2048]{1,0:T(8,128)(2,1)S(1)} fusion(bf16[128,1024]{1,0:T(8,128)(2,1)} %bitcast.14, bf16[128,1024]{1,0:T(8,128)(2,1)} %bitcast.12), kind=kLoop, calls=%fused_computation | loop fusion | flops 1048576 | bytes 1048576 | tf_op jit(solution)/shard_map/concatenate | solution.py:319
  6.3 2.9 %collective-permute-done.1.refs_2_ = bf16[128,128]{1,0:T(8,128)(2,1)S(1)} collective-permute-done((bf16[128,128]{1,0:T(8,128)(2,1)}, bf16[128,128]{1,0:T(8,128)(2,1)S(1)}, u32[]{:S(2)}, u32[]{:S(2)}) %collective-permute-start.1) | collective-permute-done | bytes 32800 | tf_op jit(solution)/shard_map/ppermute | solution.py:304
  9.7 3.1 %collective-permute-start.5 = (bf16[512,128]{1,0:T(8,128)(2,1)S(1)}, bf16[512,128]{1,0:T(8,128)(2,1)S(1)}, u32[]{:S(2)}, u32[]{:S(2)}) collective-permute-start(bf16[512,128]{1,0:T(8,128)(2,1)S(1)} %stack.2.e0), channel_id=1, source_target_pairs={{0,12},{1,13},{2,14},{3,15},{4,0},{5,1},{6,2},{7,3},{8,4},{9,5},{1... | collective-permute-start | bytes 393224 | tf_op jit(solution)/shard_map/ppermute | solution.py:304
  13.4 1.0 %collective-permute-start.3 = (bf16[512,128]{1,0:T(8,128)(2,1)S(1)}, bf16[512,128]{1,0:T(8,128)(2,1)S(1)}, u32[]{:S(2)}, u32[]{:S(2)}) collective-permute-start(bf16[512,128]{1,0:T(8,128)(2,1)S(1)} %stack.2.e0), channel_id=1, source_target_pairs={{0,4},{1,5},{2,6},{3,7},{4,8},{5,9},{6,10},{7,11},{8,12},{9,13},{1... | collective-permute-start | bytes 393224 | tf_op jit(solution)/shard_map/ppermute | solution.py:304
  14.4 2.3 %pack.1 = bf16[16,192,128]{2,1,0:T(8,128)(2,1)} custom-call(bf16[128,1024]{1,0:T(8,128)(2,1)} %bitcast.31, bf16[128,1024]{1,0:T(8,128)(2,1)} %bitcast.32, bf16[128,1024]{1,0:T(8,128)(2,1)} %bitcast.33), custom_call_target="tpu_custom_call" | custom-call | tf_op jit(solution)/shard_map/pack/pallas_call | solution.py:60
  17.0 2.4 %collective-permute-done.4.e2 = bf16[512,128]{1,0:T(8,128)(2,1)S(1)} collective-permute-done((bf16[512,128]{1,0:T(8,128)(2,1)S(1)}, bf16[512,128]{1,0:T(8,128)(2,1)S(1)}, u32[]{:S(2)}, u32[]{:S(2)}) %collective-permute-start.4) | collective-permute-done | bytes 131104 | tf_op jit(solution)/shard_map/ppermute | solution.py:304
  19.4 1.3 %collective-permute-done.3.e1 = bf16[512,128]{1,0:T(8,128)(2,1)S(1)} collective-permute-done((bf16[512,128]{1,0:T(8,128)(2,1)S(1)}, bf16[512,128]{1,0:T(8,128)(2,1)S(1)}, u32[]{:S(2)}, u32[]{:S(2)}) %collective-permute-start.3) | collective-permute-done | bytes 131104 | tf_op jit(solution)/shard_map/ppermute | solution.py:304
  20.7 3.6 %all-to-all-start = ((bf16[16,192,128]{2,1,0:T(8,128)(2,1)}), bf16[16,192,128]{2,1,0:T(8,128)(2,1)S(1)}, u32[]{:S(2)}, u32[]{:S(2)}) async-start(bf16[16,192,128]{2,1,0:T(8,128)(2,1)} %pack.1), calls=%async_computation | async-start | bytes 1572864 | tf_op jit(solution)/shard_map/all_to_all | solution.py:329
  24.3 1.8 %decode.1.a = bf16[512,128]{1,0:T(8,128)(2,1)S(1)} custom-call(bf16[512,1024]{1,0:T(8,128)(2,1)S(1)} %bitcast.28, bf16[512,128]{1,0:T(8,128)(2,1)S(1)} %stack.2.e0, bf16[512,128]{1,0:T(8,128)(2,1)S(1)} %collective-permute-done.3.e1, bf16[512,128]{1,0:T(8,128)(2,1)S(1)} %collective-permute-done.4.e2, bf16[512,128]{1,0:T(8,128)(2,1)S(1)} %collective-permute-done.5.e3), custom_call_target="tpu_custom_call" | custom-call | flops 1000000000 | bytes 1000000 | tf_op jit(solution)/shard_map/decode/pallas_call | solution.py:220
  26.1 4.1 %collective-permute-start.8 = (bf16[512,128]{1,0:T(8,128)(2,1)S(1)}, bf16[512,128]{1,0:T(8,128)(2,1)S(1)}, u32[]{:S(2)}, u32[]{:S(2)}) collective-permute-start(bf16[512,128]{1,0:T(8,128)(2,1)S(1)} %decode.1.a), channel_id=1, source_target_pairs={{0,48},{16,0},{32,16},{48,32},{1,49},{17,1},{33,17},{49,33},{2,50}... | collective-permute-start | bytes 393224 | tf_op jit(solution)/shard_map/ppermute | solution.py:304
  30.2 1.3 %collective-permute-start.6 = (bf16[512,128]{1,0:T(8,128)(2,1)S(1)}, bf16[512,128]{1,0:T(8,128)(2,1)S(1)}, u32[]{:S(2)}, u32[]{:S(2)}) collective-permute-start(bf16[512,128]{1,0:T(8,128)(2,1)S(1)} %decode.1.a), channel_id=1, source_target_pairs={{0,16},{16,32},{32,48},{48,0},{1,17},{17,33},{33,49},{49,1},{2,18}... | collective-permute-start | bytes 393224 | tf_op jit(solution)/shard_map/ppermute | solution.py:304
  31.5 2.7 %collective-permute-done.8.d = bf16[512,128]{1,0:T(8,128)(2,1)S(1)} collective-permute-done((bf16[512,128]{1,0:T(8,128)(2,1)S(1)}, bf16[512,128]{1,0:T(8,128)(2,1)S(1)}, u32[]{:S(2)}, u32[]{:S(2)}) %collective-permute-start.8) | collective-permute-done | bytes 131104 | tf_op jit(solution)/shard_map/ppermute | solution.py:304
  34.1 2.7 %collective-permute-done.7.c = bf16[512,128]{1,0:T(8,128)(2,1)S(1)} collective-permute-done((bf16[512,128]{1,0:T(8,128)(2,1)S(1)}, bf16[512,128]{1,0:T(8,128)(2,1)S(1)}, u32[]{:S(2)}, u32[]{:S(2)}) %collective-permute-start.7) | collective-permute-done | bytes 131104 | tf_op jit(solution)/shard_map/ppermute | solution.py:304
  36.8 1.0 %collective-permute-done.6.b = bf16[512,128]{1,0:T(8,128)(2,1)S(1)} collective-permute-done((bf16[512,128]{1,0:T(8,128)(2,1)S(1)}, bf16[512,128]{1,0:T(8,128)(2,1)S(1)}, u32[]{:S(2)}, u32[]{:S(2)}) %collective-permute-start.6) | collective-permute-done | bytes 131104 | tf_op jit(solution)/shard_map/ppermute | solution.py:304
  39.2 1.4 %collective-permute-start.17 = (bf16[1024,128]{1,0:T(8,128)(2,1)S(1)}, bf16[1024,128]{1,0:T(8,128)(2,1)S(1)}, u32[]{:S(2)}, u32[]{:S(2)}) collective-permute-start(bf16[1024,128]{1,0:T(8,128)(2,1)S(1)} %bitcast.16), channel_id=1, source_target_pairs={{0,48},{16,0},{32,16},{48,32},{1,49},{17,1},{33,17},{49,33},{2,50}... | collective-permute-start | bytes 786440 | tf_op jit(solution)/shard_map/ppermute | solution.py:304
  40.6 1.3 %collective-permute-start.15 = (bf16[1024,128]{1,0:T(8,128)(2,1)S(1)}, bf16[1024,128]{1,0:T(8,128)(2,1)S(1)}, u32[]{:S(2)}, u32[]{:S(2)}) collective-permute-start(bf16[1024,128]{1,0:T(8,128)(2,1)S(1)} %bitcast.18), channel_id=1, source_target_pairs={{0,16},{16,32},{32,48},{48,0},{1,17},{17,33},{33,49},{49,1},{2,18}... | collective-permute-start | bytes 786440 | tf_op jit(solution)/shard_map/ppermute | solution.py:304
  41.9 2.8 %collective-permute-start.11 = (bf16[1,32,1024]{2,1,0:T(8,128)(2,1)S(1)}, bf16[1,32,1024]{2,1,0:T(8,128)(2,1)S(1)}, u32[]{:S(2)}, u32[]{:S(2)}) collective-permute-start(bf16[1,32,1024]{2,1,0:T(8,128)(2,1)S(1)} %bitcast.20), channel_id=1, source_target_pairs={{0,3},{1,0},{2,1},{3,2},{4,7},{5,4},{6,5},{7,6},{8,11},{9,8},{10,9... | collective-permute-start | bytes 196616 | tf_op jit(solution)/shard_map/ppermute | solution.py:304
  45.5 1.1 %collective-permute-done.11.refs_3_ = bf16[1,32,1024]{2,1,0:T(8,128)(2,1)S(1)} collective-permute-done((bf16[1,32,1024]{2,1,0:T(8,128)(2,1)S(1)}, bf16[1,32,1024]{2,1,0:T(8,128)(2,1)S(1)}, u32[]{:S(2)}, u32[]{:S(2)}) %collective-permute-start.11) | collective-permute-done | bytes 65568 | tf_op jit(solution)/shard_map/ppermute | solution.py:304
  46.6 1.1 %collective-permute-start.9 = (bf16[1,32,1024]{2,1,0:T(8,128)(2,1)S(1)}, bf16[1,32,1024]{2,1,0:T(8,128)(2,1)S(1)}, u32[]{:S(2)}, u32[]{:S(2)}) collective-permute-start(bf16[1,32,1024]{2,1,0:T(8,128)(2,1)S(1)} %bitcast.22), channel_id=1, source_target_pairs={{0,1},{1,2},{2,3},{3,0},{4,5},{5,6},{6,7},{7,4},{8,9},{9,10},{10,1... | collective-permute-start | bytes 196616 | tf_op jit(solution)/shard_map/ppermute | solution.py:304
  47.7 2.7 %collective-permute-done.10.refs_2_ = bf16[1,32,1024]{2,1,0:T(8,128)(2,1)S(1)} collective-permute-done((bf16[1,32,1024]{2,1,0:T(8,128)(2,1)S(1)}, bf16[1,32,1024]{2,1,0:T(8,128)(2,1)S(1)}, u32[]{:S(2)}, u32[]{:S(2)}) %collective-permute-start.10) | collective-permute-done | bytes 65568 | tf_op jit(solution)/shard_map/ppermute | solution.py:304
  50.4 1.9 %collective-permute-done.9.refs_1_ = bf16[1,32,1024]{2,1,0:T(8,128)(2,1)S(1)} collective-permute-done((bf16[1,32,1024]{2,1,0:T(8,128)(2,1)S(1)}, bf16[1,32,1024]{2,1,0:T(8,128)(2,1)S(1)}, u32[]{:S(2)}, u32[]{:S(2)}) %collective-permute-start.9) | collective-permute-done | bytes 65568 | tf_op jit(solution)/shard_map/ppermute | solution.py:304
  52.4 2.8 %collective-permute-start.14 = (bf16[4,32,1024]{2,1,0:T(8,128)(2,1)S(1)}, bf16[4,32,1024]{2,1,0:T(8,128)(2,1)S(1)}, u32[]{:S(2)}, u32[]{:S(2)}) collective-permute-start(bf16[4,32,1024]{2,1,0:T(8,128)(2,1)S(1)} %stack.3.own), channel_id=1, source_target_pairs={{0,12},{1,13},{2,14},{3,15},{4,0},{5,1},{6,2},{7,3},{8,4},{9,5},{1... | collective-permute-start | bytes 786440 | tf_op jit(solution)/shard_map/ppermute | solution.py:304
  56.9 1.3 %collective-permute-start.19 = (bf16[128,2048]{1,0:T(8,128)(2,1)S(1)}, bf16[128,2048]{1,0:T(8,128)(2,1)S(1)}, u32[]{:S(2)}, u32[]{:S(2)}) collective-permute-start(bf16[128,2048]{1,0:T(8,128)(2,1)S(1)} %pad_maximum_fusion.refs_4_), channel_id=1, source_target_pairs={{1,0},{2,1},{3,2},{4,3},{5,4},{6,5},{7,6},{8,7},{9,8},{10,9},{11,1... | collective-permute-start | bytes 1572872 | tf_op jit(solution)/shard_map/ppermute | solution.py:342
  58.2 4.8 %collective-permute-start.18 = (bf16[128,2048]{1,0:T(8,128)(2,1)S(1)}, bf16[128,2048]{1,0:T(8,128)(2,1)S(1)}, u32[]{:S(2)}, u32[]{:S(2)}) collective-permute-start(bf16[128,2048]{1,0:T(8,128)(2,1)S(1)} %pad_maximum_fusion.refs_4_), channel_id=1, source_target_pairs={{0,1},{1,2},{2,3},{3,4},{4,5},{5,6},{6,7},{7,8},{8,9},{9,10},{10,1... | collective-permute-start | bytes 1572872 | tf_op jit(solution)/shard_map/ppermute | solution.py:341
  63.0 10.4 %heavy.1 = bf16[16,64,128]{2,1,0:T(8,128)(2,1)} custom-call(bf16[16,192,128]{2,1,0:T(8,128)(2,1)S(1)} %all-to-all-done.kv.q, bf16[1024,128]{1,0:T(8,128)(2,1)S(1)} %bitcast.19, bf16[1024,128]{1,0:T(8,128)(2,1)S(1)} %collective-permute-done.15.kv1, bf16[1024,128]{1,0:T(8,128)(2,1)S(1)} %collective-permute-done.16.kv2, ...), custom_call_target="tpu_custom_call" | custom-call | flops 10000000000 | bytes 2000000 | tf_op jit(solution)/shard_map/heavy/pallas_call | solution.py:119
  73.4 9.4 %all-to-all-start.1 = ((bf16[16,64,128]{2,1,0:T(8,128)(2,1)}), bf16[16,64,128]{2,1,0:T(8,128)(2,1)S(1)}, u32[]{:S(2)}, u32[]{:S(2)}) async-start(bf16[16,64,128]{2,1,0:T(8,128)(2,1)} %heavy.1), calls=%async_computation.1 | async-start | bytes 524288 | tf_op jit(solution)/shard_map/all_to_all | solution.py:346
  82.8 1.1 %spread.1 = bf16[16,32,1024]{2,1,0:T(8,128)(2,1)} custom-call(bf16[4,32,1024]{2,1,0:T(8,128)(2,1)S(1)} %stack.3.own, bf16[4,32,1024]{2,1,0:T(8,128)(2,1)S(1)} %collective-permute-done.12.down1, bf16[4,32,1024]{2,1,0:T(8,128)(2,1)S(1)} %collective-permute-done.13.down2, bf16[4,32,1024]{2,1,0:T(8,128)(2,1)S(1)} %collective-permute-done.14.down3), custom_call_target="tpu_custom_call" | custom-call | tf_op jit(solution)/shard_map/spread/pallas_call | solution.py:288
  84.0 1.5 %light.1 = f32[128,1024]{1,0:T(8,128)S(1)} custom-call(bf16[128,1024]{1,0:T(8,128)(2,1)S(1)} %bitcast.29, bf16[128,1024]{1,0:T(8,128)(2,1)S(1)} %bitcast.13, bf16[128,1024]{1,0:T(8,128)(2,1)S(1)} %bitcast.15, bf16[128,2048]{1,0:T(8,128)(2,1)S(1)} %collective-permute-done.18.prev, bf16[128,2048]{1,0:T(8,128)(2,1)S(1)} %collective-permute-done.19.after), custom_call_target="tpu_custom_call" | custom-call | flops 3000000000 | bytes 2000000 | tf_op jit(solution)/shard_map/light/pallas_call | solution.py:155
  85.5 5.9 %all-to-all-done.1.heavy = bf16[16,64,128]{2,1,0:T(8,128)(2,1)S(1)} async-done(((bf16[16,64,128]{2,1,0:T(8,128)(2,1)}), bf16[16,64,128]{2,1,0:T(8,128)(2,1)S(1)}, u32[]{:S(2)}, u32[]{:S(2)}) %all-to-all-start.1) | async-done | bytes 262176 | tf_op jit(solution)/shard_map/all_to_all | solution.py:346
  91.4 1.5 %join.1 = bf16[128,1024]{1,0:T(8,128)(2,1)} custom-call(s32[1,64]{1,0:T(1,128)S(1)} %copy-done.4, f32[128,1024]{1,0:T(8,128)S(1)} %light.1, bf16[16,64,128]{2,1,0:T(8,128)(2,1)S(1)} %all-to-all-done.1.heavy), custom_call_target="tpu_custom_call" | custom-call | tf_op jit(solution)/shard_map/join/pallas_call | solution.py:181
  (37 shorter events, 6.4 us)
Async XLA Ops:
  0.6 5.7 %collective-permute-start.2 = (bf16[128,128]{1,0:T(8,128)(2,1)}, bf16[128,128]{1,0:T(8,128)(2,1)S(1)}, u32[]{:S(2)}, u32[]{:S(2)}) collective-permute-start(bf16[128,128]{1,0:T(8,128)(2,1)} %bitcast.24), channel_id=1, source_target_pairs={{0,3},{1,0},{2,1},{3,2},{4,7},{5,4},{6,5},{7,6},{8,11},{9,8},{10,9... | collective-permute-start | bytes 98312 | tf_op jit(solution)/shard_map/ppermute | solution.py:304
  3.5 5.6 %collective-permute-start.1 = (bf16[128,128]{1,0:T(8,128)(2,1)}, bf16[128,128]{1,0:T(8,128)(2,1)S(1)}, u32[]{:S(2)}, u32[]{:S(2)}) collective-permute-start(bf16[128,128]{1,0:T(8,128)(2,1)} %bitcast.25), channel_id=1, source_target_pairs={{0,2},{1,3},{2,0},{3,1},{4,6},{5,7},{6,4},{7,5},{8,10},{9,11},{10,... | collective-permute-start | bytes 98312 | tf_op jit(solution)/shard_map/ppermute | solution.py:304
  4.3 5.3 %collective-permute-start = (bf16[128,128]{1,0:T(8,128)(2,1)}, bf16[128,128]{1,0:T(8,128)(2,1)S(1)}, u32[]{:S(2)}, u32[]{:S(2)}) collective-permute-start(bf16[128,128]{1,0:T(8,128)(2,1)} %bitcast.26), channel_id=1, source_target_pairs={{0,1},{1,2},{2,3},{3,0},{4,5},{5,6},{6,7},{7,4},{8,9},{9,10},{10,1... | collective-permute-start | bytes 98312 | tf_op jit(solution)/shard_map/ppermute | solution.py:304
  5.2 4.5 %copy-start.2 = (bf16[1,128,128]{2,1,0:T(8,128)(2,1)S(1)}, bf16[1,128,128]{2,1,0:T(8,128)(2,1)}, u32[]{:S(2)}) copy-start(bf16[1,128,128]{2,1,0:T(8,128)(2,1)} %param.16) | copy-start | bytes 98308
  9.7 7.3 %collective-permute-start.5 = (bf16[512,128]{1,0:T(8,128)(2,1)S(1)}, bf16[512,128]{1,0:T(8,128)(2,1)S(1)}, u32[]{:S(2)}, u32[]{:S(2)}) collective-permute-start(bf16[512,128]{1,0:T(8,128)(2,1)S(1)} %stack.2.e0), channel_id=1, source_target_pairs={{0,12},{1,13},{2,14},{3,15},{4,0},{5,1},{6,2},{7,3},{8,4},{9,5},{1... | collective-permute-start | bytes 393224 | tf_op jit(solution)/shard_map/ppermute | solution.py:304
  12.8 6.6 %collective-permute-start.4 = (bf16[512,128]{1,0:T(8,128)(2,1)S(1)}, bf16[512,128]{1,0:T(8,128)(2,1)S(1)}, u32[]{:S(2)}, u32[]{:S(2)}) collective-permute-start(bf16[512,128]{1,0:T(8,128)(2,1)S(1)} %stack.2.e0), channel_id=1, source_target_pairs={{0,8},{1,9},{2,10},{3,11},{4,12},{5,13},{6,14},{7,15},{8,0},{9,1},... | collective-permute-start | bytes 393224 | tf_op jit(solution)/shard_map/ppermute | solution.py:304
  13.4 7.2 %collective-permute-start.3 = (bf16[512,128]{1,0:T(8,128)(2,1)S(1)}, bf16[512,128]{1,0:T(8,128)(2,1)S(1)}, u32[]{:S(2)}, u32[]{:S(2)}) collective-permute-start(bf16[512,128]{1,0:T(8,128)(2,1)S(1)} %stack.2.e0), channel_id=1, source_target_pairs={{0,4},{1,5},{2,6},{3,7},{4,8},{5,9},{6,10},{7,11},{8,12},{9,13},{1... | collective-permute-start | bytes 393224 | tf_op jit(solution)/shard_map/ppermute | solution.py:304
  16.7 7.6 %copy-start.5 = (bf16[1,512,1024]{2,1,0:T(8,128)(2,1)S(1)}, bf16[1,512,1024]{2,1,0:T(8,128)(2,1)}, u32[]{:S(2)}) copy-start(bf16[1,512,1024]{2,1,0:T(8,128)(2,1)} %param.17) | copy-start | bytes 3145732
  20.7 18.0 %all-to-all-start = ((bf16[16,192,128]{2,1,0:T(8,128)(2,1)}), bf16[16,192,128]{2,1,0:T(8,128)(2,1)S(1)}, u32[]{:S(2)}, u32[]{:S(2)}) async-start(bf16[16,192,128]{2,1,0:T(8,128)(2,1)} %pack.1), calls=%async_computation | async-start | bytes 1572864 | tf_op jit(solution)/shard_map/all_to_all | solution.py:329
  26.1 12.6 %copy-start.3 = (s32[1,32]{1,0:T(1,128)S(1)}, s32[1,32]{1,0:T(1,128)}, u32[]{:S(2)}) copy-start(s32[1,32]{1,0:T(1,128)} %ids.2) | copy-start | bytes 388
  26.1 8.0 %collective-permute-start.8 = (bf16[512,128]{1,0:T(8,128)(2,1)S(1)}, bf16[512,128]{1,0:T(8,128)(2,1)S(1)}, u32[]{:S(2)}, u32[]{:S(2)}) collective-permute-start(bf16[512,128]{1,0:T(8,128)(2,1)S(1)} %decode.1.a), channel_id=1, source_target_pairs={{0,48},{16,0},{32,16},{48,32},{1,49},{17,1},{33,17},{49,33},{2,50}... | collective-permute-start | bytes 393224 | tf_op jit(solution)/shard_map/ppermute | solution.py:304
  30.2 6.6 %collective-permute-start.7 = (bf16[512,128]{1,0:T(8,128)(2,1)S(1)}, bf16[512,128]{1,0:T(8,128)(2,1)S(1)}, u32[]{:S(2)}, u32[]{:S(2)}) collective-permute-start(bf16[512,128]{1,0:T(8,128)(2,1)S(1)} %decode.1.a), channel_id=1, source_target_pairs={{0,32},{16,48},{32,0},{48,16},{1,33},{17,49},{33,1},{49,17},{2,34}... | collective-permute-start | bytes 393224 | tf_op jit(solution)/shard_map/ppermute | solution.py:304
  30.2 7.6 %collective-permute-start.6 = (bf16[512,128]{1,0:T(8,128)(2,1)S(1)}, bf16[512,128]{1,0:T(8,128)(2,1)S(1)}, u32[]{:S(2)}, u32[]{:S(2)}) collective-permute-start(bf16[512,128]{1,0:T(8,128)(2,1)S(1)} %decode.1.a), channel_id=1, source_target_pairs={{0,16},{16,32},{32,48},{48,0},{1,17},{17,33},{33,49},{49,1},{2,18}... | collective-permute-start | bytes 393224 | tf_op jit(solution)/shard_map/ppermute | solution.py:304
  39.2 16.8 %collective-permute-start.17 = (bf16[1024,128]{1,0:T(8,128)(2,1)S(1)}, bf16[1024,128]{1,0:T(8,128)(2,1)S(1)}, u32[]{:S(2)}, u32[]{:S(2)}) collective-permute-start(bf16[1024,128]{1,0:T(8,128)(2,1)S(1)} %bitcast.16), channel_id=1, source_target_pairs={{0,48},{16,0},{32,16},{48,32},{1,49},{17,1},{33,17},{49,33},{2,50}... | collective-permute-start | bytes 786440 | tf_op jit(solution)/shard_map/ppermute | solution.py:304
  40.6 16.3 %collective-permute-start.16 = (bf16[1024,128]{1,0:T(8,128)(2,1)S(1)}, bf16[1024,128]{1,0:T(8,128)(2,1)S(1)}, u32[]{:S(2)}, u32[]{:S(2)}) collective-permute-start(bf16[1024,128]{1,0:T(8,128)(2,1)S(1)} %bitcast.17), channel_id=1, source_target_pairs={{0,32},{16,48},{32,0},{48,16},{1,33},{17,49},{33,1},{49,17},{2,34}... | collective-permute-start | bytes 786440 | tf_op jit(solution)/shard_map/ppermute | solution.py:304
  40.6 16.3 %collective-permute-start.15 = (bf16[1024,128]{1,0:T(8,128)(2,1)S(1)}, bf16[1024,128]{1,0:T(8,128)(2,1)S(1)}, u32[]{:S(2)}, u32[]{:S(2)}) collective-permute-start(bf16[1024,128]{1,0:T(8,128)(2,1)S(1)} %bitcast.18), channel_id=1, source_target_pairs={{0,16},{16,32},{32,48},{48,0},{1,17},{17,33},{33,49},{49,1},{2,18}... | collective-permute-start | bytes 786440 | tf_op jit(solution)/shard_map/ppermute | solution.py:304
  41.9 4.7 %collective-permute-start.11 = (bf16[1,32,1024]{2,1,0:T(8,128)(2,1)S(1)}, bf16[1,32,1024]{2,1,0:T(8,128)(2,1)S(1)}, u32[]{:S(2)}, u32[]{:S(2)}) collective-permute-start(bf16[1,32,1024]{2,1,0:T(8,128)(2,1)S(1)} %bitcast.20), channel_id=1, source_target_pairs={{0,3},{1,0},{2,1},{3,2},{4,7},{5,4},{6,5},{7,6},{8,11},{9,8},{10,9... | collective-permute-start | bytes 196616 | tf_op jit(solution)/shard_map/ppermute | solution.py:304
  44.7 5.8 %collective-permute-start.10 = (bf16[1,32,1024]{2,1,0:T(8,128)(2,1)S(1)}, bf16[1,32,1024]{2,1,0:T(8,128)(2,1)S(1)}, u32[]{:S(2)}, u32[]{:S(2)}) collective-permute-start(bf16[1,32,1024]{2,1,0:T(8,128)(2,1)S(1)} %bitcast.21), channel_id=1, source_target_pairs={{0,2},{1,3},{2,0},{3,1},{4,6},{5,7},{6,4},{7,5},{8,10},{9,11},{10,... | collective-permute-start | bytes 196616 | tf_op jit(solution)/shard_map/ppermute | solution.py:304
  46.6 5.8 %collective-permute-start.9 = (bf16[1,32,1024]{2,1,0:T(8,128)(2,1)S(1)}, bf16[1,32,1024]{2,1,0:T(8,128)(2,1)S(1)}, u32[]{:S(2)}, u32[]{:S(2)}) collective-permute-start(bf16[1,32,1024]{2,1,0:T(8,128)(2,1)S(1)} %bitcast.22), channel_id=1, source_target_pairs={{0,1},{1,2},{2,3},{3,0},{4,5},{5,6},{6,7},{7,4},{8,9},{9,10},{10,1... | collective-permute-start | bytes 196616 | tf_op jit(solution)/shard_map/ppermute | solution.py:304
  52.4 30.4 %collective-permute-start.14 = (bf16[4,32,1024]{2,1,0:T(8,128)(2,1)S(1)}, bf16[4,32,1024]{2,1,0:T(8,128)(2,1)S(1)}, u32[]{:S(2)}, u32[]{:S(2)}) collective-permute-start(bf16[4,32,1024]{2,1,0:T(8,128)(2,1)S(1)} %stack.3.own), channel_id=1, source_target_pairs={{0,12},{1,13},{2,14},{3,15},{4,0},{5,1},{6,2},{7,3},{8,4},{9,5},{1... | collective-permute-start | bytes 786440 | tf_op jit(solution)/shard_map/ppermute | solution.py:304
  55.2 27.6 %collective-permute-start.13 = (bf16[4,32,1024]{2,1,0:T(8,128)(2,1)S(1)}, bf16[4,32,1024]{2,1,0:T(8,128)(2,1)S(1)}, u32[]{:S(2)}, u32[]{:S(2)}) collective-permute-start(bf16[4,32,1024]{2,1,0:T(8,128)(2,1)S(1)} %stack.3.own), channel_id=1, source_target_pairs={{0,8},{1,9},{2,10},{3,11},{4,12},{5,13},{6,14},{7,15},{8,0},{9,1},... | collective-permute-start | bytes 786440 | tf_op jit(solution)/shard_map/ppermute | solution.py:304
  56.0 26.8 %collective-permute-start.12 = (bf16[4,32,1024]{2,1,0:T(8,128)(2,1)S(1)}, bf16[4,32,1024]{2,1,0:T(8,128)(2,1)S(1)}, u32[]{:S(2)}, u32[]{:S(2)}) collective-permute-start(bf16[4,32,1024]{2,1,0:T(8,128)(2,1)S(1)} %stack.3.own), channel_id=1, source_target_pairs={{0,4},{1,5},{2,6},{3,7},{4,8},{5,9},{6,10},{7,11},{8,12},{9,13},{1... | collective-permute-start | bytes 786440 | tf_op jit(solution)/shard_map/ppermute | solution.py:304
  56.9 27.0 %collective-permute-start.19 = (bf16[128,2048]{1,0:T(8,128)(2,1)S(1)}, bf16[128,2048]{1,0:T(8,128)(2,1)S(1)}, u32[]{:S(2)}, u32[]{:S(2)}) collective-permute-start(bf16[128,2048]{1,0:T(8,128)(2,1)S(1)} %pad_maximum_fusion.refs_4_), channel_id=1, source_target_pairs={{1,0},{2,1},{3,2},{4,3},{5,4},{6,5},{7,6},{8,7},{9,8},{10,9},{11,1... | collective-permute-start | bytes 1572872 | tf_op jit(solution)/shard_map/ppermute | solution.py:342
  58.2 25.7 %collective-permute-start.18 = (bf16[128,2048]{1,0:T(8,128)(2,1)S(1)}, bf16[128,2048]{1,0:T(8,128)(2,1)S(1)}, u32[]{:S(2)}, u32[]{:S(2)}) collective-permute-start(bf16[128,2048]{1,0:T(8,128)(2,1)S(1)} %pad_maximum_fusion.refs_4_), channel_id=1, source_target_pairs={{0,1},{1,2},{2,3},{3,4},{4,5},{5,6},{6,7},{7,8},{8,9},{9,10},{10,1... | collective-permute-start | bytes 1572872 | tf_op jit(solution)/shard_map/ppermute | solution.py:341
  73.4 18.1 %all-to-all-start.1 = ((bf16[16,64,128]{2,1,0:T(8,128)(2,1)}), bf16[16,64,128]{2,1,0:T(8,128)(2,1)S(1)}, u32[]{:S(2)}, u32[]{:S(2)}) async-start(bf16[16,64,128]{2,1,0:T(8,128)(2,1)} %heavy.1), calls=%async_computation.1 | async-start | bytes 524288 | tf_op jit(solution)/shard_map/all_to_all | solution.py:346
  82.8 1.1 %copy-start = (bf16[1,128,1024]{2,1,0:T(8,128)(2,1)S(1)}, bf16[1,128,1024]{2,1,0:T(8,128)(2,1)}, u32[]{:S(2)}) copy-start(bf16[1,128,1024]{2,1,0:T(8,128)(2,1)} %param.11) | copy-start | bytes 786436
  82.8 1.1 %copy-start.1 = (bf16[1,128,1024]{2,1,0:T(8,128)(2,1)S(1)}, bf16[1,128,1024]{2,1,0:T(8,128)(2,1)}, u32[]{:S(2)}) copy-start(bf16[1,128,1024]{2,1,0:T(8,128)(2,1)} %param.12) | copy-start | bytes 786436
  82.8 1.2 %copy-start.6 = (bf16[1,128,1024]{2,1,0:T(8,128)(2,1)S(1)}, bf16[1,128,1024]{2,1,0:T(8,128)(2,1)}, u32[]{:S(2)}) copy-start(bf16[1,128,1024]{2,1,0:T(8,128)(2,1)} %param.10) | copy-start | bytes 786436
  84.0 7.4 %copy-start.4 = (s32[1,64]{1,0:T(1,128)S(1)}, s32[1,64]{1,0:T(1,128)}, u32[]{:S(2)}) copy-start(s32[1,64]{1,0:T(1,128)} %ids.3) | copy-start | bytes 772

commit v6 on v5

--- a/solution.py
+++ b/solution.py
@@ -125,15 +125,16 @@
     )(q_kv, *kvs)
 
 
-def light_kernel(q, k, v, prev, after, out):
+def light_kernel(q, k, v, even, odd, out):
     here = lax.axis_index(TOKENS)
     last = lax.axis_size(TOKENS) - 1
     rows, width = q.shape
     low = lane_ids((rows, LANES)) < HEAD
     i = lax.broadcasted_iota(jnp.int32, (2 * rows, BLOCK), 0) % rows
     j = lax.broadcasted_iota(jnp.int32, (2 * rows, BLOCK), 1)
-    sees_prev = (j > i) & (here > 0)
-    sees_next = (j < i) & (here < last)
+    ahead = (j - i) * (1 - 2 * (here % 2))
+    sees_even = ahead < 0
+    sees_odd = (ahead > 0) & (here > 0) & (here < last)
     for p in range(width // LANES):
         c = slice(p * LANES, (p + 1) * LANES)
         cv = slice(width + p * LANES, width + (p + 1) * LANES)
@@ -141,24 +142,24 @@
         zero = jnp.zeros_like(qq)
         two = jnp.concatenate([jnp.where(low, qq, zero), jnp.where(low, zero, qq)], axis=0)
         own = nt(two, k[:, c])
-        left = jnp.where(sees_prev, nt(two, prev[:, c]), f32(-1e30))
-        right = jnp.where(sees_next, nt(two, after[:, c]), f32(-1e30))
-        peak = jnp.maximum(jnp.maximum(own, left), right).max(axis=1, keepdims=True)
-        po, pp, pn = (jnp.exp2((s - peak) * (SCALE * LOG2E)) for s in (own, left, right))
-        total = (po + pp + pn).sum(axis=1, keepdims=True)
-        o = nn(po.astype(bf16), v[:, c]) + nn(pp.astype(bf16), prev[:, cv]) + nn(pn.astype(bf16), after[:, cv])
+        first = jnp.where(sees_even, nt(two, even[:, c]), f32(-1e30))
+        second = jnp.where(sees_odd, nt(two, odd[:, c]), f32(-1e30))
+        peak = jnp.maximum(jnp.maximum(own, first), second).max(axis=1, keepdims=True)
+        po, pe, pd = (jnp.exp2((s - peak) * (SCALE * LOG2E)) for s in (own, first, second))
+        total = (po + pe + pd).sum(axis=1, keepdims=True)
+        o = nn(po.astype(bf16), v[:, c]) + nn(pe.astype(bf16), even[:, cv]) + nn(pd.astype(bf16), odd[:, cv])
         o = o / total
         out[:, c] = jnp.where(low, o[:rows], o[rows:])
 
 
-def light_attend(q, k, v, prev, after):
+def light_attend(q, k, v, even, odd):
     return pl.pallas_call(
         light_kernel,
         out_shape=jax.ShapeDtypeStruct(q.shape, f32),
         compiler_params=params(),
         cost_estimate=pl.CostEstimate(flops=3_000_000_000, transcendentals=800_000, bytes_accessed=2_000_000),
         name="light",
-    )(q, k, v, prev, after)
+    )(q, k, v, even, odd)
 
 
 def join_kernel(ids, light, heavy, out):
@@ -273,14 +274,12 @@
     )(*parts, *others)
 
 
-def spread_kernel(own, down1, down2, down3, out):
+def spread_kernel(own, other1, other2, other3, out):
     place = lax.axis_index("fine")
     side = own.shape[0]
-    row, col = place // side, place % side
-    for dr, got in enumerate((own, down1, down2, down3)):
-        at = (row + side - dr) % side * side
+    for dr, got in enumerate((own, other1, other2, other3)):
         for dc in range(side):
-            out[at + (col + side - dc) % side] = got[dc]
+            out[place ^ (dr * side + dc)] = got[dc]
 
 
 def spread(rows):
@@ -297,11 +296,10 @@
     size = lax.axis_size(axis)
     ring = ring or size
 
-    def to(i, d):
-        at = i // stride % ring
-        return i + ((at + d) % ring - at) * stride
-
-    return [lax.ppermute(value, axis, [(i, to(i, d)) for i in range(size)]) for d in range(1, ring)]
+    def pairs(d):
+        return [(i, i + ((i // stride % ring ^ d) - i // stride % ring) * stride) for i in range(size)]
+
+    return [lax.ppermute(value, axis, pairs(d)) for d in range(1, ring)]
 
 
 def after_all(value, *others):
@@ -337,14 +335,13 @@
     shares = square(stack(rows_of(after_all(share, own)[None])))
 
     light_kv = after_all(light_kv, routed)
-    up = [(i, i + 1) for i in range(n_seq - 1)]
-    prev = lax.ppermute(light_kv, TOKENS, up)
-    after = lax.ppermute(light_kv, TOKENS, [(b, a) for a, b in up])
+    even = lax.ppermute(light_kv, TOKENS, [(i, i ^ 1) for i in range(n_seq)])
+    odd = lax.ppermute(light_kv, TOKENS, [(i, (i - 1 ^ 1) + 1) for i in range(1, n_seq - 1)])
 
     heavy = heavy_attend(group, routed)
     shares, q_light = after_all((shares, q_light), heavy)
     heavy = lax.all_to_all(heavy, "fine", 0, 0, tiled=True)
-    light = light_attend(q_light[0], k_light[0], v_light[0], prev, after)
+    light = light_attend(q_light[0], k_light[0], v_light[0], even, odd)
     decoded = spread(shares).reshape(1, -1, width)
     encoded = join(query_ids, light, heavy)[None]
     return (encoded, decoded)

time: 93.3 us -> 88.4 us (0.947)
  starting transfers between devices: 45.6 us -> 42.8 us
  waiting for transfers between devices: 25.3 us -> 23.2 us
    all_to_all x1, starting transfers between devices: 9.39 us -> 6.32 us  [local(): heavy = lax.all_to_all(heavy, 'fine', 0, 0, tiled=True)]
    ppermute x20, waiting for transfers between devices: 19.4 us -> 17.3 us  [the longest x18 17.3 us: around(): return [lax.ppermute(value, axis, pairs(d)) for d in range(1, ring)]]
    all_to_all x1, starting transfers between devices: 3.61 us -> 4.97 us  [local(): lax.all_to_all(after_all(chunks, enc[1], enc[2], enc[3]), 'fine', 0, 0, t...]
    ppermute x20, starting transfers between devices: 32.6 us -> 31.5 us  [the longest x18 26.3 us: around(): return [lax.ppermute(value, axis, pairs(d)) for d in range(1, ring)]]
  transfers between devices with their start and end apart: 22 -> 22, of which waited for: 12 -> 10; matrix products, arithmetic and copies ran while one was open for 1% -> 1% of each run, Pallas kernels for 19% -> 20%
where the time goes in v6:
time: 88.4 us; the launch traced here: 88 us
  starting transfers between devices  42.8 us (48%)
  waiting for transfers between devices  23.2 us (26%)
  Pallas kernels  19.9 us (23%)
  other arithmetic  1.07 us (1%)
    ppermute x18, starting transfers between devices, around(): return [lax.ppermute(value, axis, pairs(d)) for d in range(1, ring)]  26.3 us
    ppermute x18, waiting for transfers between devices, around(): return [lax.ppermute(value, axis, pairs(d)) for d in range(1, ring)]  17.3 us
    pallas_call x1, Pallas kernels, heavy_attend(): pl.pallas_call(heavy_kernel, out_shape=jax.ShapeDtypeStruct((blocks, HALF...  10.4 us
    all_to_all x1, starting transfers between devices, local(): heavy = lax.all_to_all(heavy, 'fine', 0, 0, tiled=True)  6.32 us
    all_to_all x1, waiting for transfers between devices, local(): heavy = lax.all_to_all(heavy, 'fine', 0, 0, tiled=True)  5.86 us
    all_to_all x1, starting transfers between devices, local(): lax.all_to_all(after_all(chunks, enc[1], enc[2], enc[3]), 'fine', 0, 0, t...  4.97 us
    ppermute x1, starting transfers between devices, local(): even = lax.ppermute(light_kv, TOKENS, [(i, i ^ 1) for i in range(n_seq)])  4.53 us
    pallas_call x1, Pallas kernels, pack(): pl.pallas_call(pack_kernel, in_specs=[hbm] * 3, out_shape=jax.ShapeDtypeS...  2.28 us
  transfers between devices with their start and end apart: 22, of which 10 were waited for; matrix products, arithmetic and copies ran while one was open for 1% of the time, Pallas kernels for 20%

profile of v6, /device:TPU:0, one launch (start us, length us, event | category | flops | bytes accessed | tf_op | source)
XLA Modules:
  0.0 88.0 jit_solution(1222560674660600947)
XLA Ops:
  0.6 2.9 %collective-permute-start.2 = (bf16[128,128]{1,0:T(8,128)(2,1)}, bf16[128,128]{1,0:T(8,128)(2,1)S(1)}, u32[]{:S(2)}, u32[]{:S(2)}) collective-permute-start(bf16[128,128]{1,0:T(8,128)(2,1)} %bitcast.24), channel_id=1, source_target_pairs={{0,3},{1,2},{2,1},{3,0},{4,7},{5,6},{6,5},{7,4},{8,11},{9,10},{10,... | collective-permute-start | bytes 98312 | tf_op jit(solution)/shard_map/ppermute | solution.py:302
  3.6 0.8 collective-permute-start.1
  4.8 1.1 %pad_maximum_fusion.refs_4_ = bf16[128,2048]{1,0:T(8,128)(2,1)S(1)} fusion(bf16[128,1024]{1,0:T(8,128)(2,1)} %bitcast.14, bf16[128,1024]{1,0:T(8,128)(2,1)} %bitcast.12), kind=kLoop, calls=%fused_computation | loop fusion | flops 1048576 | bytes 1048576 | tf_op jit(solution)/shard_map/concatenate | solution.py:317
  6.0 3.1 %collective-permute-done.1.refs_2_ = bf16[128,128]{1,0:T(8,128)(2,1)S(1)} collective-permute-done((bf16[128,128]{1,0:T(8,128)(2,1)}, bf16[128,128]{1,0:T(8,128)(2,1)S(1)}, u32[]{:S(2)}, u32[]{:S(2)}) %collective-permute-start.1) | collective-permute-done | bytes 32800 | tf_op jit(solution)/shard_map/ppermute | solution.py:302
  9.2 3.1 %collective-permute-start.5 = (bf16[512,128]{1,0:T(8,128)(2,1)S(1)}, bf16[512,128]{1,0:T(8,128)(2,1)S(1)}, u32[]{:S(2)}, u32[]{:S(2)}) collective-permute-start(bf16[512,128]{1,0:T(8,128)(2,1)S(1)} %stack.2.e0), channel_id=1, source_target_pairs={{0,12},{1,13},{2,14},{3,15},{4,8},{5,9},{6,10},{7,11},{8,4},{9,5},... | collective-permute-start | bytes 393224 | tf_op jit(solution)/shard_map/ppermute | solution.py:302
  13.4 2.3 %pack.1 = bf16[16,192,128]{2,1,0:T(8,128)(2,1)} custom-call(bf16[128,1024]{1,0:T(8,128)(2,1)} %bitcast.31, bf16[128,1024]{1,0:T(8,128)(2,1)} %bitcast.32, bf16[128,1024]{1,0:T(8,128)(2,1)} %bitcast.33), custom_call_target="tpu_custom_call" | custom-call | tf_op jit(solution)/shard_map/pack/pallas_call | solution.py:60
  15.7 1.2 %collective-permute-done.5.e3 = bf16[512,128]{1,0:T(8,128)(2,1)S(1)} collective-permute-done((bf16[512,128]{1,0:T(8,128)(2,1)S(1)}, bf16[512,128]{1,0:T(8,128)(2,1)S(1)}, u32[]{:S(2)}, u32[]{:S(2)}) %collective-permute-start.5) | collective-permute-done | bytes 131104 | tf_op jit(solution)/shard_map/ppermute | solution.py:302
  16.9 1.9 %collective-permute-done.4.e2 = bf16[512,128]{1,0:T(8,128)(2,1)S(1)} collective-permute-done((bf16[512,128]{1,0:T(8,128)(2,1)S(1)}, bf16[512,128]{1,0:T(8,128)(2,1)S(1)}, u32[]{:S(2)}, u32[]{:S(2)}) %collective-permute-start.4) | collective-permute-done | bytes 131104 | tf_op jit(solution)/shard_map/ppermute | solution.py:302
  18.8 5.0 %all-to-all-start = ((bf16[16,192,128]{2,1,0:T(8,128)(2,1)}), bf16[16,192,128]{2,1,0:T(8,128)(2,1)S(1)}, u32[]{:S(2)}, u32[]{:S(2)}) async-start(bf16[16,192,128]{2,1,0:T(8,128)(2,1)} %pack.1), calls=%async_computation | async-start | bytes 1572864 | tf_op jit(solution)/shard_map/all_to_all | solution.py:327
  23.8 1.8 %decode.1.a = bf16[512,128]{1,0:T(8,128)(2,1)S(1)} custom-call(bf16[512,1024]{1,0:T(8,128)(2,1)S(1)} %bitcast.28, bf16[512,128]{1,0:T(8,128)(2,1)S(1)} %stack.2.e0, bf16[512,128]{1,0:T(8,128)(2,1)S(1)} %collective-permute-done.3.e1, bf16[512,128]{1,0:T(8,128)(2,1)S(1)} %collective-permute-done.4.e2, bf16[512,128]{1,0:T(8,128)(2,1)S(1)} %collective-permute-done.5.e3), custom_call_target="tpu_custom_call" | custom-call | flops 1000000000 | bytes 1000000 | tf_op jit(solution)/shard_map/decode/pallas_call | solution.py:221
  25.6 4.1 %collective-permute-start.8 = (bf16[512,128]{1,0:T(8,128)(2,1)S(1)}, bf16[512,128]{1,0:T(8,128)(2,1)S(1)}, u32[]{:S(2)}, u32[]{:S(2)}) collective-permute-start(bf16[512,128]{1,0:T(8,128)(2,1)S(1)} %decode.1.a), channel_id=1, source_target_pairs={{0,48},{16,32},{32,16},{48,0},{1,49},{17,33},{33,17},{49,1},{2,50}... | collective-permute-start | bytes 393224 | tf_op jit(solution)/shard_map/ppermute | solution.py:302
  29.7 0.9 %collective-permute-start.6 = (bf16[512,128]{1,0:T(8,128)(2,1)S(1)}, bf16[512,128]{1,0:T(8,128)(2,1)S(1)}, u32[]{:S(2)}, u32[]{:S(2)}) collective-permute-start(bf16[512,128]{1,0:T(8,128)(2,1)S(1)} %decode.1.a), channel_id=1, source_target_pairs={{0,16},{16,0},{32,48},{48,32},{1,17},{17,1},{33,49},{49,33},{2,18}... | collective-permute-start | bytes 393224 | tf_op jit(solution)/shard_map/ppermute | solution.py:302
  30.7 3.0 %collective-permute-done.8.d = bf16[512,128]{1,0:T(8,128)(2,1)S(1)} collective-permute-done((bf16[512,128]{1,0:T(8,128)(2,1)S(1)}, bf16[512,128]{1,0:T(8,128)(2,1)S(1)}, u32[]{:S(2)}, u32[]{:S(2)}) %collective-permute-start.8) | collective-permute-done | bytes 131104 | tf_op jit(solution)/shard_map/ppermute | solution.py:302
  33.6 2.5 %collective-permute-done.7.c = bf16[512,128]{1,0:T(8,128)(2,1)S(1)} collective-permute-done((bf16[512,128]{1,0:T(8,128)(2,1)S(1)}, bf16[512,128]{1,0:T(8,128)(2,1)S(1)}, u32[]{:S(2)}, u32[]{:S(2)}) %collective-permute-start.7) | collective-permute-done | bytes 131104 | tf_op jit(solution)/shard_map/ppermute | solution.py:302
  36.2 0.8 meet.1
  37.6 2.3 %collective-permute-start.17 = (bf16[1024,128]{1,0:T(8,128)(2,1)S(1)}, bf16[1024,128]{1,0:T(8,128)(2,1)S(1)}, u32[]{:S(2)}, u32[]{:S(2)}) collective-permute-start(bf16[1024,128]{1,0:T(8,128)(2,1)S(1)} %bitcast.16), channel_id=1, source_target_pairs={{0,48},{16,32},{32,16},{48,0},{1,49},{17,33},{33,17},{49,1},{2,50}... | collective-permute-start | bytes 786440 | tf_op jit(solution)/shard_map/ppermute | solution.py:302
  40.0 1.8 %collective-permute-start.15 = (bf16[1024,128]{1,0:T(8,128)(2,1)S(1)}, bf16[1024,128]{1,0:T(8,128)(2,1)S(1)}, u32[]{:S(2)}, u32[]{:S(2)}) collective-permute-start(bf16[1024,128]{1,0:T(8,128)(2,1)S(1)} %bitcast.18), channel_id=1, source_target_pairs={{0,16},{16,0},{32,48},{48,32},{1,17},{17,1},{33,49},{49,33},{2,18}... | collective-permute-start | bytes 786440 | tf_op jit(solution)/shard_map/ppermute | solution.py:302
  41.8 3.1 %collective-permute-start.11 = (bf16[1,32,1024]{2,1,0:T(8,128)(2,1)S(1)}, bf16[1,32,1024]{2,1,0:T(8,128)(2,1)S(1)}, u32[]{:S(2)}, u32[]{:S(2)}) collective-permute-start(bf16[1,32,1024]{2,1,0:T(8,128)(2,1)S(1)} %bitcast.20), channel_id=1, source_target_pairs={{0,3},{1,2},{2,1},{3,0},{4,7},{5,6},{6,5},{7,4},{8,11},{9,10},{10,... | collective-permute-start | bytes 196616 | tf_op jit(solution)/shard_map/ppermute | solution.py:302
  44.9 0.9 collective-permute-start.10
  45.8 1.7 %collective-permute-done.11.refs_3_ = bf16[1,32,1024]{2,1,0:T(8,128)(2,1)S(1)} collective-permute-done((bf16[1,32,1024]{2,1,0:T(8,128)(2,1)S(1)}, bf16[1,32,1024]{2,1,0:T(8,128)(2,1)S(1)}, u32[]{:S(2)}, u32[]{:S(2)}) %collective-permute-start.11) | collective-permute-done | bytes 65568 | tf_op jit(solution)/shard_map/ppermute | solution.py:302
  48.0 2.7 %collective-permute-done.10.refs_2_ = bf16[1,32,1024]{2,1,0:T(8,128)(2,1)S(1)} collective-permute-done((bf16[1,32,1024]{2,1,0:T(8,128)(2,1)S(1)}, bf16[1,32,1024]{2,1,0:T(8,128)(2,1)S(1)}, u32[]{:S(2)}, u32[]{:S(2)}) %collective-permute-start.10) | collective-permute-done | bytes 65568 | tf_op jit(solution)/shard_map/ppermute | solution.py:302
  50.7 1.0 %collective-permute-done.9.refs_1_ = bf16[1,32,1024]{2,1,0:T(8,128)(2,1)S(1)} collective-permute-done((bf16[1,32,1024]{2,1,0:T(8,128)(2,1)S(1)}, bf16[1,32,1024]{2,1,0:T(8,128)(2,1)S(1)}, u32[]{:S(2)}, u32[]{:S(2)}) %collective-permute-start.9) | collective-permute-done | bytes 65568 | tf_op jit(solution)/shard_map/ppermute | solution.py:302
  51.7 3.0 %collective-permute-start.14 = (bf16[4,32,1024]{2,1,0:T(8,128)(2,1)S(1)}, bf16[4,32,1024]{2,1,0:T(8,128)(2,1)S(1)}, u32[]{:S(2)}, u32[]{:S(2)}) collective-permute-start(bf16[4,32,1024]{2,1,0:T(8,128)(2,1)S(1)} %stack.3.own), channel_id=1, source_target_pairs={{0,12},{1,13},{2,14},{3,15},{4,8},{5,9},{6,10},{7,11},{8,4},{9,5},... | collective-permute-start | bytes 786440 | tf_op jit(solution)/shard_map/ppermute | solution.py:302
  54.8 0.9 collective-permute-start.13
  55.9 0.7 collective-permute-start.19
  56.6 4.5 %collective-permute-start.18 = (bf16[128,2048]{1,0:T(8,128)(2,1)S(1)}, bf16[128,2048]{1,0:T(8,128)(2,1)S(1)}, u32[]{:S(2)}, u32[]{:S(2)}) collective-permute-start(bf16[128,2048]{1,0:T(8,128)(2,1)S(1)} %pad_maximum_fusion.refs_4_), channel_id=1, source_target_pairs={{0,1},{1,0},{2,3},{3,2},{4,5},{5,4},{6,7},{7,6},{8,9},{9,8},{10,11... | collective-permute-start | bytes 1572872 | tf_op jit(solution)/shard_map/ppermute | solution.py:338
  61.2 10.4 %heavy.1 = bf16[16,64,128]{2,1,0:T(8,128)(2,1)} custom-call(bf16[16,192,128]{2,1,0:T(8,128)(2,1)S(1)} %all-to-all-done.kv.q, bf16[1024,128]{1,0:T(8,128)(2,1)S(1)} %bitcast.19, bf16[1024,128]{1,0:T(8,128)(2,1)S(1)} %collective-permute-done.15.kv1, bf16[1024,128]{1,0:T(8,128)(2,1)S(1)} %collective-permute-done.16.kv2, ...), custom_call_target="tpu_custom_call" | custom-call | flops 10000000000 | bytes 2000000 | tf_op jit(solution)/shard_map/heavy/pallas_call | solution.py:119
  71.5 6.3 %all-to-all-start.1 = ((bf16[16,64,128]{2,1,0:T(8,128)(2,1)}), bf16[16,64,128]{2,1,0:T(8,128)(2,1)S(1)}, u32[]{:S(2)}, u32[]{:S(2)}) async-start(bf16[16,64,128]{2,1,0:T(8,128)(2,1)} %heavy.1), calls=%async_computation.1 | async-start | bytes 524288 | tf_op jit(solution)/shard_map/all_to_all | solution.py:343
  77.9 1.1 %spread.1 = bf16[16,32,1024]{2,1,0:T(8,128)(2,1)} custom-call(bf16[4,32,1024]{2,1,0:T(8,128)(2,1)S(1)} %stack.3.own, bf16[4,32,1024]{2,1,0:T(8,128)(2,1)S(1)} %collective-permute-done.12.other1, bf16[4,32,1024]{2,1,0:T(8,128)(2,1)S(1)} %collective-permute-done.13.other2, bf16[4,32,1024]{2,1,0:T(8,128)(2,1)S(1)} %collective-permute-done.14.other3), custom_call_target="tpu_custom_call" | custom-call | tf_op jit(solution)/shard_map/spread/pallas_call | solution.py:287
  79.1 1.5 %light.1 = f32[128,1024]{1,0:T(8,128)S(1)} custom-call(bf16[128,1024]{1,0:T(8,128)(2,1)S(1)} %bitcast.29, bf16[128,1024]{1,0:T(8,128)(2,1)S(1)} %bitcast.13, bf16[128,1024]{1,0:T(8,128)(2,1)S(1)} %bitcast.15, bf16[128,2048]{1,0:T(8,128)(2,1)S(1)} %collective-permute-done.18.even, bf16[128,2048]{1,0:T(8,128)(2,1)S(1)} %collective-permute-done.19.odd), custom_call_target="tpu_custom_call" | custom-call | flops 3000000000 | bytes 2000000 | tf_op jit(solution)/shard_map/light/pallas_call | solution.py:156
  80.7 5.9 %all-to-all-done.1.heavy = bf16[16,64,128]{2,1,0:T(8,128)(2,1)S(1)} async-done(((bf16[16,64,128]{2,1,0:T(8,128)(2,1)}), bf16[16,64,128]{2,1,0:T(8,128)(2,1)S(1)}, u32[]{:S(2)}, u32[]{:S(2)}) %all-to-all-start.1) | async-done | bytes 262176 | tf_op jit(solution)/shard_map/all_to_all | solution.py:343
  86.5 1.5 %join.1 = bf16[128,1024]{1,0:T(8,128)(2,1)} custom-call(s32[1,64]{1,0:T(1,128)S(1)} %copy-done.4, f32[128,1024]{1,0:T(8,128)S(1)} %light.1, bf16[16,64,128]{2,1,0:T(8,128)(2,1)S(1)} %all-to-all-done.1.heavy), custom_call_target="tpu_custom_call" | custom-call | tf_op jit(solution)/shard_map/join/pallas_call | solution.py:182
  (37 shorter events, 3.3 us)
Async XLA Ops:
  0.6 5.4 %collective-permute-start.2 = (bf16[128,128]{1,0:T(8,128)(2,1)}, bf16[128,128]{1,0:T(8,128)(2,1)S(1)}, u32[]{:S(2)}, u32[]{:S(2)}) collective-permute-start(bf16[128,128]{1,0:T(8,128)(2,1)} %bitcast.24), channel_id=1, source_target_pairs={{0,3},{1,2},{2,1},{3,0},{4,7},{5,6},{6,5},{7,4},{8,11},{9,10},{10,... | collective-permute-start | bytes 98312 | tf_op jit(solution)/shard_map/ppermute | solution.py:302
  3.6 5.6 %collective-permute-start.1 = (bf16[128,128]{1,0:T(8,128)(2,1)}, bf16[128,128]{1,0:T(8,128)(2,1)S(1)}, u32[]{:S(2)}, u32[]{:S(2)}) collective-permute-start(bf16[128,128]{1,0:T(8,128)(2,1)} %bitcast.25), channel_id=1, source_target_pairs={{0,2},{1,3},{2,0},{3,1},{4,6},{5,7},{6,4},{7,5},{8,10},{9,11},{10,... | collective-permute-start | bytes 98312 | tf_op jit(solution)/shard_map/ppermute | solution.py:302
  4.4 4.8 %collective-permute-start = (bf16[128,128]{1,0:T(8,128)(2,1)}, bf16[128,128]{1,0:T(8,128)(2,1)S(1)}, u32[]{:S(2)}, u32[]{:S(2)}) collective-permute-start(bf16[128,128]{1,0:T(8,128)(2,1)} %bitcast.26), channel_id=1, source_target_pairs={{0,1},{1,0},{2,3},{3,2},{4,5},{5,4},{6,7},{7,6},{8,9},{9,8},{10,11... | collective-permute-start | bytes 98312 | tf_op jit(solution)/shard_map/ppermute | solution.py:302
  4.8 4.4 %copy-start.2 = (bf16[1,128,128]{2,1,0:T(8,128)(2,1)S(1)}, bf16[1,128,128]{2,1,0:T(8,128)(2,1)}, u32[]{:S(2)}) copy-start(bf16[1,128,128]{2,1,0:T(8,128)(2,1)} %param.16) | copy-start | bytes 98308
  9.2 7.7 %collective-permute-start.5 = (bf16[512,128]{1,0:T(8,128)(2,1)S(1)}, bf16[512,128]{1,0:T(8,128)(2,1)S(1)}, u32[]{:S(2)}, u32[]{:S(2)}) collective-permute-start(bf16[512,128]{1,0:T(8,128)(2,1)S(1)} %stack.2.e0), channel_id=1, source_target_pairs={{0,12},{1,13},{2,14},{3,15},{4,8},{5,9},{6,10},{7,11},{8,4},{9,5},... | collective-permute-start | bytes 393224 | tf_op jit(solution)/shard_map/ppermute | solution.py:302
  12.3 6.5 %collective-permute-start.4 = (bf16[512,128]{1,0:T(8,128)(2,1)S(1)}, bf16[512,128]{1,0:T(8,128)(2,1)S(1)}, u32[]{:S(2)}, u32[]{:S(2)}) collective-permute-start(bf16[512,128]{1,0:T(8,128)(2,1)S(1)} %stack.2.e0), channel_id=1, source_target_pairs={{0,8},{1,9},{2,10},{3,11},{4,12},{5,13},{6,14},{7,15},{8,0},{9,1},... | collective-permute-start | bytes 393224 | tf_op jit(solution)/shard_map/ppermute | solution.py:302
  12.9 5.9 %collective-permute-start.3 = (bf16[512,128]{1,0:T(8,128)(2,1)S(1)}, bf16[512,128]{1,0:T(8,128)(2,1)S(1)}, u32[]{:S(2)}, u32[]{:S(2)}) collective-permute-start(bf16[512,128]{1,0:T(8,128)(2,1)S(1)} %stack.2.e0), channel_id=1, source_target_pairs={{0,4},{1,5},{2,6},{3,7},{4,0},{5,1},{6,2},{7,3},{8,12},{9,13},{10,... | collective-permute-start | bytes 393224 | tf_op jit(solution)/shard_map/ppermute | solution.py:302
  15.7 8.1 %copy-start.5 = (bf16[1,512,1024]{2,1,0:T(8,128)(2,1)S(1)}, bf16[1,512,1024]{2,1,0:T(8,128)(2,1)}, u32[]{:S(2)}) copy-start(bf16[1,512,1024]{2,1,0:T(8,128)(2,1)} %param.17) | copy-start | bytes 3145732
  18.8 18.2 %all-to-all-start = ((bf16[16,192,128]{2,1,0:T(8,128)(2,1)}), bf16[16,192,128]{2,1,0:T(8,128)(2,1)S(1)}, u32[]{:S(2)}, u32[]{:S(2)}) async-start(bf16[16,192,128]{2,1,0:T(8,128)(2,1)} %pack.1), calls=%async_computation | async-start | bytes 1572864 | tf_op jit(solution)/shard_map/all_to_all | solution.py:327
  25.6 11.5 %copy-start.3 = (s32[1,32]{1,0:T(1,128)S(1)}, s32[1,32]{1,0:T(1,128)}, u32[]{:S(2)}) copy-start(s32[1,32]{1,0:T(1,128)} %ids.2) | copy-start | bytes 388
  25.6 8.0 %collective-permute-start.8 = (bf16[512,128]{1,0:T(8,128)(2,1)S(1)}, bf16[512,128]{1,0:T(8,128)(2,1)S(1)}, u32[]{:S(2)}, u32[]{:S(2)}) collective-permute-start(bf16[512,128]{1,0:T(8,128)(2,1)S(1)} %decode.1.a), channel_id=1, source_target_pairs={{0,48},{16,32},{32,16},{48,0},{1,49},{17,33},{33,17},{49,1},{2,50}... | collective-permute-start | bytes 393224 | tf_op jit(solution)/shard_map/ppermute | solution.py:302
  29.7 6.5 %collective-permute-start.7 = (bf16[512,128]{1,0:T(8,128)(2,1)S(1)}, bf16[512,128]{1,0:T(8,128)(2,1)S(1)}, u32[]{:S(2)}, u32[]{:S(2)}) collective-permute-start(bf16[512,128]{1,0:T(8,128)(2,1)S(1)} %decode.1.a), channel_id=1, source_target_pairs={{0,32},{16,48},{32,0},{48,16},{1,33},{17,49},{33,1},{49,17},{2,34}... | collective-permute-start | bytes 393224 | tf_op jit(solution)/shard_map/ppermute | solution.py:302
  29.7 6.5 %collective-permute-start.6 = (bf16[512,128]{1,0:T(8,128)(2,1)S(1)}, bf16[512,128]{1,0:T(8,128)(2,1)S(1)}, u32[]{:S(2)}, u32[]{:S(2)}) collective-permute-start(bf16[512,128]{1,0:T(8,128)(2,1)S(1)} %decode.1.a), channel_id=1, source_target_pairs={{0,16},{16,0},{32,48},{48,32},{1,17},{17,1},{33,49},{49,33},{2,18}... | collective-permute-start | bytes 393224 | tf_op jit(solution)/shard_map/ppermute | solution.py:302
  37.6 18.0 %collective-permute-start.17 = (bf16[1024,128]{1,0:T(8,128)(2,1)S(1)}, bf16[1024,128]{1,0:T(8,128)(2,1)S(1)}, u32[]{:S(2)}, u32[]{:S(2)}) collective-permute-start(bf16[1024,128]{1,0:T(8,128)(2,1)S(1)} %bitcast.16), channel_id=1, source_target_pairs={{0,48},{16,32},{32,16},{48,0},{1,49},{17,33},{33,17},{49,1},{2,50}... | collective-permute-start | bytes 786440 | tf_op jit(solution)/shard_map/ppermute | solution.py:302
  40.0 16.0 %collective-permute-start.16 = (bf16[1024,128]{1,0:T(8,128)(2,1)S(1)}, bf16[1024,128]{1,0:T(8,128)(2,1)S(1)}, u32[]{:S(2)}, u32[]{:S(2)}) collective-permute-start(bf16[1024,128]{1,0:T(8,128)(2,1)S(1)} %bitcast.17), channel_id=1, source_target_pairs={{0,32},{16,48},{32,0},{48,16},{1,33},{17,49},{33,1},{49,17},{2,34}... | collective-permute-start | bytes 786440 | tf_op jit(solution)/shard_map/ppermute | solution.py:302
  40.0 16.0 %collective-permute-start.15 = (bf16[1024,128]{1,0:T(8,128)(2,1)S(1)}, bf16[1024,128]{1,0:T(8,128)(2,1)S(1)}, u32[]{:S(2)}, u32[]{:S(2)}) collective-permute-start(bf16[1024,128]{1,0:T(8,128)(2,1)S(1)} %bitcast.18), channel_id=1, source_target_pairs={{0,16},{16,0},{32,48},{48,32},{1,17},{17,1},{33,49},{49,33},{2,18}... | collective-permute-start | bytes 786440 | tf_op jit(solution)/shard_map/ppermute | solution.py:302
  41.8 5.6 %collective-permute-start.11 = (bf16[1,32,1024]{2,1,0:T(8,128)(2,1)S(1)}, bf16[1,32,1024]{2,1,0:T(8,128)(2,1)S(1)}, u32[]{:S(2)}, u32[]{:S(2)}) collective-permute-start(bf16[1,32,1024]{2,1,0:T(8,128)(2,1)S(1)} %bitcast.20), channel_id=1, source_target_pairs={{0,3},{1,2},{2,1},{3,0},{4,7},{5,6},{6,5},{7,4},{8,11},{9,10},{10,... | collective-permute-start | bytes 196616 | tf_op jit(solution)/shard_map/ppermute | solution.py:302
  44.9 5.8 %collective-permute-start.10 = (bf16[1,32,1024]{2,1,0:T(8,128)(2,1)S(1)}, bf16[1,32,1024]{2,1,0:T(8,128)(2,1)S(1)}, u32[]{:S(2)}, u32[]{:S(2)}) collective-permute-start(bf16[1,32,1024]{2,1,0:T(8,128)(2,1)S(1)} %bitcast.21), channel_id=1, source_target_pairs={{0,2},{1,3},{2,0},{3,1},{4,6},{5,7},{6,4},{7,5},{8,10},{9,11},{10,... | collective-permute-start | bytes 196616 | tf_op jit(solution)/shard_map/ppermute | solution.py:302
  47.5 4.3 %collective-permute-start.9 = (bf16[1,32,1024]{2,1,0:T(8,128)(2,1)S(1)}, bf16[1,32,1024]{2,1,0:T(8,128)(2,1)S(1)}, u32[]{:S(2)}, u32[]{:S(2)}) collective-permute-start(bf16[1,32,1024]{2,1,0:T(8,128)(2,1)S(1)} %bitcast.22), channel_id=1, source_target_pairs={{0,1},{1,0},{2,3},{3,2},{4,5},{5,4},{6,7},{7,6},{8,9},{9,8},{10,11... | collective-permute-start | bytes 196616 | tf_op jit(solution)/shard_map/ppermute | solution.py:302
  51.7 26.1 %collective-permute-start.14 = (bf16[4,32,1024]{2,1,0:T(8,128)(2,1)S(1)}, bf16[4,32,1024]{2,1,0:T(8,128)(2,1)S(1)}, u32[]{:S(2)}, u32[]{:S(2)}) collective-permute-start(bf16[4,32,1024]{2,1,0:T(8,128)(2,1)S(1)} %stack.3.own), channel_id=1, source_target_pairs={{0,12},{1,13},{2,14},{3,15},{4,8},{5,9},{6,10},{7,11},{8,4},{9,5},... | collective-permute-start | bytes 786440 | tf_op jit(solution)/shard_map/ppermute | solution.py:302
  54.8 23.1 %collective-permute-start.13 = (bf16[4,32,1024]{2,1,0:T(8,128)(2,1)S(1)}, bf16[4,32,1024]{2,1,0:T(8,128)(2,1)S(1)}, u32[]{:S(2)}, u32[]{:S(2)}) collective-permute-start(bf16[4,32,1024]{2,1,0:T(8,128)(2,1)S(1)} %stack.3.own), channel_id=1, source_target_pairs={{0,8},{1,9},{2,10},{3,11},{4,12},{5,13},{6,14},{7,15},{8,0},{9,1},... | collective-permute-start | bytes 786440 | tf_op jit(solution)/shard_map/ppermute | solution.py:302
  55.6 22.3 %collective-permute-start.12 = (bf16[4,32,1024]{2,1,0:T(8,128)(2,1)S(1)}, bf16[4,32,1024]{2,1,0:T(8,128)(2,1)S(1)}, u32[]{:S(2)}, u32[]{:S(2)}) collective-permute-start(bf16[4,32,1024]{2,1,0:T(8,128)(2,1)S(1)} %stack.3.own), channel_id=1, source_target_pairs={{0,4},{1,5},{2,6},{3,7},{4,0},{5,1},{6,2},{7,3},{8,12},{9,13},{10,... | collective-permute-start | bytes 786440 | tf_op jit(solution)/shard_map/ppermute | solution.py:302
  55.9 23.0 %collective-permute-start.19 = (bf16[128,2048]{1,0:T(8,128)(2,1)S(1)}, bf16[128,2048]{1,0:T(8,128)(2,1)S(1)}, u32[]{:S(2)}, u32[]{:S(2)}) collective-permute-start(bf16[128,2048]{1,0:T(8,128)(2,1)S(1)} %pad_maximum_fusion.refs_4_), channel_id=1, source_target_pairs={{1,2},{2,1},{3,4},{4,3},{5,6},{6,5},{7,8},{8,7},{9,10},{10,9},{11,... | collective-permute-start | bytes 1572872 | tf_op jit(solution)/shard_map/ppermute | solution.py:339
  56.6 22.4 %collective-permute-start.18 = (bf16[128,2048]{1,0:T(8,128)(2,1)S(1)}, bf16[128,2048]{1,0:T(8,128)(2,1)S(1)}, u32[]{:S(2)}, u32[]{:S(2)}) collective-permute-start(bf16[128,2048]{1,0:T(8,128)(2,1)S(1)} %pad_maximum_fusion.refs_4_), channel_id=1, source_target_pairs={{0,1},{1,0},{2,3},{3,2},{4,5},{5,4},{6,7},{7,6},{8,9},{9,8},{10,11... | collective-permute-start | bytes 1572872 | tf_op jit(solution)/shard_map/ppermute | solution.py:338
  71.5 15.0 %all-to-all-start.1 = ((bf16[16,64,128]{2,1,0:T(8,128)(2,1)}), bf16[16,64,128]{2,1,0:T(8,128)(2,1)S(1)}, u32[]{:S(2)}, u32[]{:S(2)}) async-start(bf16[16,64,128]{2,1,0:T(8,128)(2,1)} %heavy.1), calls=%async_computation.1 | async-start | bytes 524288 | tf_op jit(solution)/shard_map/all_to_all | solution.py:343
  77.8 1.1 %copy-start = (bf16[1,128,1024]{2,1,0:T(8,128)(2,1)S(1)}, bf16[1,128,1024]{2,1,0:T(8,128)(2,1)}, u32[]{:S(2)}) copy-start(bf16[1,128,1024]{2,1,0:T(8,128)(2,1)} %param.11) | copy-start | bytes 786436
  77.9 1.1 %copy-start.1 = (bf16[1,128,1024]{2,1,0:T(8,128)(2,1)S(1)}, bf16[1,128,1024]{2,1,0:T(8,128)(2,1)}, u32[]{:S(2)}) copy-start(bf16[1,128,1024]{2,1,0:T(8,128)(2,1)} %param.12) | copy-start | bytes 786436
  77.9 1.3 %copy-start.6 = (bf16[1,128,1024]{2,1,0:T(8,128)(2,1)S(1)}, bf16[1,128,1024]{2,1,0:T(8,128)(2,1)}, u32[]{:S(2)}) copy-start(bf16[1,128,1024]{2,1,0:T(8,128)(2,1)} %param.10) | copy-start | bytes 786436
  79.1 7.4 %copy-start.4 = (s32[1,64]{1,0:T(1,128)S(1)}, s32[1,64]{1,0:T(1,128)}, u32[]{:S(2)}) copy-start(s32[1,64]{1,0:T(1,128)} %ids.3) | copy-start | bytes 772

commit v7 on v6

--- a/solution.py
+++ b/solution.py
@@ -188,7 +188,16 @@
     )(ids, light, heavy)
 
 
-def decode_kernel(q_hbm, e0, e1, e2, e3, out, q, sem):
+def partial(level, ratio):
+    lane = lane_ids(ratio.shape)
+    hi = level.astype(bf16).astype(f32)
+    mid = (level - hi).astype(bf16).astype(f32)
+    least = level - hi - mid
+    parts = jnp.where(lane < 16, hi, jnp.where(lane < 32, mid, least))
+    return jnp.where(lane < HEAD, parts, ratio).astype(bf16)
+
+
+def decode_kernel(q_hbm, e0, e1, out, q, sem):
     rows, width = q.shape
     at = pl.multiple_of(lax.axis_index("fine") * rows, rows)
     copy = pltpu.make_async_copy(q_hbm.at[pl.ds(at, rows)], q, sem)
@@ -202,17 +211,10 @@
         ],
         axis=0,
     )
-    keys = [e[...] for e in (e0, e1, e2, e3)]
+    keys = [e[...] for e in (e0, e1)]
     vals = [with_ones(k) for k in keys]
     total, peak = summed(stack, keys, vals)
-    lane = lane_ids(total.shape)
-    level = peak * SCALE + jnp.log(total)
-    hi = level.astype(bf16).astype(f32)
-    mid = (level - hi).astype(bf16).astype(f32)
-    least = level - hi - mid
-    parts = jnp.where(lane < 16, hi, jnp.where(lane < 32, mid, least))
-    ratio = total / pltpu.roll(total, HEAD, 1)
-    out[...] = jnp.where(lane < HEAD, parts, ratio).astype(bf16)
+    out[...] = partial(peak * SCALE + jnp.log(total), total / pltpu.roll(total, HEAD, 1))
 
 
 def decode(q, enc, rows):
@@ -229,16 +231,17 @@
     )(q, *enc)
 
 
-def meet_kernel(a, b, c, d, out):
-    parts = [x[...].astype(f32) for x in (a, b, c, d)]
+def meet_kernel(a, b, out, *, last):
+    parts = [x[...].astype(f32) for x in (a, b)]
     levels = [x[:, 0:1] + x[:, 16:17] + x[:, 32:33] for x in parts]
-    peak = jnp.maximum(jnp.maximum(levels[0], levels[1]), jnp.maximum(levels[2], levels[3]))
+    peak = jnp.maximum(*levels)
     scales = [jnp.exp(n - peak) for n in levels]
-    total = scales[0] + scales[1] + scales[2] + scales[3]
-    value = parts[0] * scales[0]
-    for x, s in zip(parts[1:], scales[1:]):
-        value = value + x * s
-    value = (value / total).astype(bf16)
+    total = scales[0] + scales[1]
+    value = (parts[0] * scales[0] + parts[1] * scales[1]) / total
+    if not last:
+        out[...] = partial(jnp.broadcast_to(peak + jnp.log(total), value.shape), value)
+        return
+    value = value.astype(bf16)
     rows, width = out.shape
     for p in range(width // LANES):
         e = value[2 * p * rows : (2 * p + 1) * rows, HEAD:]
@@ -246,60 +249,56 @@
         out[:, p * LANES : (p + 1) * LANES] = jnp.concatenate([e, o], axis=1)
 
 
-def meet(parts, rows, width):
-    return pl.pallas_call(
-        meet_kernel,
-        out_shape=jax.ShapeDtypeStruct((rows, width), bf16),
+def meet(a, b, shape, last):
+    return pl.pallas_call(
+        lambda *refs: meet_kernel(*refs, last=last),
+        out_shape=jax.ShapeDtypeStruct(shape, bf16),
         compiler_params=params(),
         name="meet",
-    )(*parts)
-
-
-def stack_kernel(*refs):
-    parts, out = refs[:4], refs[-1]
-    size = parts[0].shape[0]
-    for n, part in enumerate(parts):
-        out[n * size : (n + 1) * size] = part[...]
-
-
-def stack(parts, *others):
-    first = parts[0]
-    specs = [pl.BlockSpec(memory_space=pltpu.VMEM)] * len(parts)
+    )(a, b)
+
+
+def stack_kernel(a, b, *rest):
+    out = rest[-1]
+    size = a.shape[0]
+    out[:size] = a[...]
+    out[size:] = b[...]
+
+
+def stack(a, b, *others):
     return pl.pallas_call(
         stack_kernel,
-        in_specs=specs + [pl.BlockSpec(memory_space=pl.ANY)] * len(others),
-        out_shape=jax.ShapeDtypeStruct((len(parts) * first.shape[0],) + first.shape[1:], first.dtype),
+        in_specs=[pl.BlockSpec(memory_space=pltpu.VMEM)] * 2
+        + [pl.BlockSpec(memory_space=pl.ANY)] * len(others),
+        out_shape=jax.ShapeDtypeStruct((2 * a.shape[0],) + a.shape[1:], a.dtype),
         compiler_params=params(),
         name="stack",
-    )(*parts, *others)
-
-
-def spread_kernel(own, other1, other2, other3, out):
+    )(a, b, *others)
+
+
+def spread_kernel(own, other, out):
     place = lax.axis_index("fine")
-    side = own.shape[0]
-    for dr, got in enumerate((own, other1, other2, other3)):
-        for dc in range(side):
-            out[place ^ (dr * side + dc)] = got[dc]
-
-
-def spread(rows):
-    side, count, width = rows[0].shape
+    order = (0, 1, 3, 2)
+    for r, dr in enumerate(order):
+        got = own if r < 2 else other
+        for c, dc in enumerate(order):
+            out[place ^ (dr * 4 + dc)] = got[r % 2 * 4 + c]
+
+
+def spread(own, other):
+    side, count, width = own.shape
     return pl.pallas_call(
         spread_kernel,
-        out_shape=jax.ShapeDtypeStruct((len(rows) * side, count, width), bf16),
+        out_shape=jax.ShapeDtypeStruct((2 * side, count, width), bf16),
         compiler_params=params(),
         name="spread",
-    )(*rows)
-
-
-def around(value, axis, stride=1, ring=None):
+    )(own, other)
+
+
+def swap(value, axis, d, stride=1, ring=4):
     size = lax.axis_size(axis)
-    ring = ring or size
-
-    def pairs(d):
-        return [(i, i + ((i // stride % ring ^ d) - i // stride % ring) * stride) for i in range(size)]
-
-    return [lax.ppermute(value, axis, pairs(d)) for d in range(1, ring)]
+    pairs = [(i, i + ((i // stride % ring ^ d) - i // stride % ring) * stride) for i in range(size)]
+    return lax.ppermute(value, axis, pairs)
 
 
 def after_all(value, *others):
@@ -311,28 +310,37 @@
 ):
     n_seq = lax.axis_size(TOKENS)
     n_fine = lax.axis_size("fine")
-    side = 4
     width = q_light.shape[2]
 
     light_kv = jnp.concatenate([k_light[0], v_light[0]], axis=1)
 
-    def rows_of(value):
-        return [value] + around(value, "fine", 1, side)
-
-    def square(row):
-        return [row] + around(row, "fine", side, n_fine // side)
-
-    enc = square(stack(rows_of(enc_kv[0]), light_kv))
+    def across(value, d):
+        return swap(value, "fine", d, 1)
+
+    def down(value, d):
+        return swap(value, "fine", d, 4)
+
+    enc = enc_kv[0]
+    enc = stack(enc, across(enc, 1), light_kv)
+    enc = stack(enc, across(enc, 3))
+    enc = stack(enc, down(enc, 1))
+    enc = (enc, down(enc, 3))
     chunks = pack(q_heavy[0], k_heavy[0], v_heavy[0])
-    group = lax.all_to_all(after_all(chunks, enc[1], enc[2], enc[3]), "fine", 0, 0, tiled=True)
+    group = lax.all_to_all(after_all(chunks, enc[1]), "fine", 0, 0, tiled=True)
 
     dec_rows = dec_queries.shape[1] // n_fine
     part = decode(dec_queries[0], enc, dec_rows)
-    share = meet([part] + around(part, "coarse"), dec_rows, width)
+    part = meet(part, swap(part, "coarse", 1), part.shape, False)
+    share = meet(part, swap(part, "coarse", 3), (dec_rows, width), True)
 
     own = pick(key_ids, after_all(group, share)).reshape(KGRP * BLOCK, LANES)
-    routed = [own] + around(own, "coarse")
-    shares = square(stack(rows_of(after_all(share, own)[None])))
+    near, far = swap(own, "coarse", 1), swap(own, "coarse", 3)
+    routed = [own, near, far, swap(near, "coarse", 3)]
+    share = share[None]
+    share = stack(share, across(share, 1), near, far)
+    share = stack(share, across(share, 3))
+    share = stack(share, down(share, 1))
+    shares = (share, down(share, 3))
 
     light_kv = after_all(light_kv, routed)
     even = lax.ppermute(light_kv, TOKENS, [(i, i ^ 1) for i in range(n_seq)])
@@ -342,7 +350,7 @@
     shares, q_light = after_all((shares, q_light), heavy)
     heavy = lax.all_to_all(heavy, "fine", 0, 0, tiled=True)
     light = light_attend(q_light[0], k_light[0], v_light[0], even, odd)
-    decoded = spread(shares).reshape(1, -1, width)
+    decoded = spread(*shares).reshape(1, -1, width)
     encoded = join(query_ids, light, heavy)[None]
     return (encoded, decoded)
 

time: 88.4 us -> 100 us (1.13)
  waiting for transfers between devices: 23.2 us -> 30.8 us
  starting transfers between devices: 42.8 us -> 47 us
    ppermute x18 -> x13, waiting for transfers between devices: 17.3 us -> 25 us  [swap(): return lax.ppermute(value, axis, pairs)]
    ppermute x18 -> x13, starting transfers between devices: 26.3 us -> 33 us  [swap(): return lax.ppermute(value, axis, pairs)]
    all_to_all x1, starting transfers between devices: 6.32 us -> 4.03 us  [local(): heavy = lax.all_to_all(heavy, 'fine', 0, 0, tiled=True)]
    ppermute x1, starting transfers between devices: 4.53 us -> 2.63 us  [local(): even = lax.ppermute(light_kv, TOKENS, [(i, i ^ 1) for i in range(n_seq)])]
    all_to_all x1, starting transfers between devices: 4.97 us -> 6.67 us  [local(): group = lax.all_to_all(after_all(chunks, enc[1]), 'fine', 0, 0, tiled=True)]
    pallas_call x4 -> x9, Pallas kernels: 1.92 us -> 2.23 us  [the longest x2 1.09 us: meet(): pl.pallas_call(lambda *refs: meet_kernel(*refs, last=last), out_shape=jax...]
  transfers between devices with their start and end apart: 22 -> 17, of which waited for: 10 -> 13; matrix products, arithmetic and copies ran while one was open for 1% -> 1% of each run, Pallas kernels for 20% -> 18%
where the time goes in v7:
time: 100 us
  starting transfers between devices  47 us (47%)
  waiting for transfers between devices  30.8 us (31%)
  Pallas kernels  20.1 us (20%)
  other arithmetic  1.07 us (1%)
    ppermute x13, starting transfers between devices, swap(): return lax.ppermute(value, axis, pairs)  33 us
    ppermute x13, waiting for transfers between devices, swap(): return lax.ppermute(value, axis, pairs)  25 us
    pallas_call x1, Pallas kernels, heavy_attend(): pl.pallas_call(heavy_kernel, out_shape=jax.ShapeDtypeStruct((blocks, HALF...  10.4 us
    all_to_all x1, starting transfers between devices, local(): group = lax.all_to_all(after_all(chunks, enc[1]), 'fine', 0, 0, tiled=True)  6.67 us
    all_to_all x1, waiting for transfers between devices, local(): heavy = lax.all_to_all(heavy, 'fine', 0, 0, tiled=True)  5.79 us
    all_to_all x1, starting transfers between devices, local(): heavy = lax.all_to_all(heavy, 'fine', 0, 0, tiled=True)  4.03 us
    ppermute x1, starting transfers between devices, local(): even = lax.ppermute(light_kv, TOKENS, [(i, i ^ 1) for i in range(n_seq)])  2.63 us
    pallas_call x1, Pallas kernels, pack(): pl.pallas_call(pack_kernel, in_specs=[hbm] * 3, out_shape=jax.ShapeDtypeS...  2.28 us
  transfers between devices with their start and end apart: 17, of which 13 were waited for; matrix products, arithmetic and copies ran while one was open for 1% of the time, Pallas kernels for 18%

profile of v7, /device:TPU:0, one launch (start us, length us, event | category | flops | bytes accessed | tf_op | source)
XLA Modules:
  0.0 100.0 jit_solution(13462341568380636307)
XLA Ops:
  0.6 1.7 %collective-permute-start = (bf16[128,128]{1,0:T(8,128)(2,1)}, bf16[128,128]{1,0:T(8,128)(2,1)S(1)}, u32[]{:S(2)}, u32[]{:S(2)}) collective-permute-start(bf16[128,128]{1,0:T(8,128)(2,1)} %bitcast.21), channel_id=1, source_target_pairs={{0,1},{1,0},{2,3},{3,2},{4,5},{5,4},{6,7},{7,6},{8,9},{9,8},{10,11... | collective-permute-start | bytes 98312 | tf_op jit(solution)/shard_map/ppermute | solution.py:301
  2.3 1.1 %pad_maximum_fusion.rest_0_ = bf16[128,2048]{1,0:T(8,128)(2,1)S(1)} fusion(bf16[128,1024]{1,0:T(8,128)(2,1)} %bitcast.16, bf16[128,1024]{1,0:T(8,128)(2,1)} %bitcast.14), kind=kLoop, calls=%fused_computation | loop fusion | flops 1048576 | bytes 1048576 | tf_op jit(solution)/shard_map/concatenate | solution.py:315
  3.4 1.5 %collective-permute-done.b = bf16[128,128]{1,0:T(8,128)(2,1)S(1)} collective-permute-done((bf16[128,128]{1,0:T(8,128)(2,1)}, bf16[128,128]{1,0:T(8,128)(2,1)S(1)}, u32[]{:S(2)}, u32[]{:S(2)}) %collective-permute-start) | collective-permute-done | bytes 32800 | tf_op jit(solution)/shard_map/ppermute | solution.py:301
  4.8 2.9 %collective-permute-start.1 = (bf16[256,128]{1,0:T(8,128)(2,1)S(1)}, bf16[256,128]{1,0:T(8,128)(2,1)S(1)}, u32[]{:S(2)}, u32[]{:S(2)}) collective-permute-start(bf16[256,128]{1,0:T(8,128)(2,1)S(1)} %stack.6.a), channel_id=1, source_target_pairs={{0,3},{1,2},{2,1},{3,0},{4,7},{5,6},{6,5},{7,4},{8,11},{9,10},{10,... | collective-permute-start | bytes 196616 | tf_op jit(solution)/shard_map/ppermute | solution.py:301
  7.8 2.6 %collective-permute-done.1.b = bf16[256,128]{1,0:T(8,128)(2,1)S(1)} collective-permute-done((bf16[256,128]{1,0:T(8,128)(2,1)S(1)}, bf16[256,128]{1,0:T(8,128)(2,1)S(1)}, u32[]{:S(2)}, u32[]{:S(2)}) %collective-permute-start.1) | collective-permute-done | bytes 65568 | tf_op jit(solution)/shard_map/ppermute | solution.py:301
  10.4 1.7 %collective-permute-start.2 = (bf16[512,128]{1,0:T(8,128)(2,1)S(1)}, bf16[512,128]{1,0:T(8,128)(2,1)S(1)}, u32[]{:S(2)}, u32[]{:S(2)}) collective-permute-start(bf16[512,128]{1,0:T(8,128)(2,1)S(1)} %stack.7.a), channel_id=1, source_target_pairs={{0,4},{1,5},{2,6},{3,7},{4,0},{5,1},{6,2},{7,3},{8,12},{9,13},{10,... | collective-permute-start | bytes 393224 | tf_op jit(solution)/shard_map/ppermute | solution.py:301
  12.2 3.3 %collective-permute-done.2.b = bf16[512,128]{1,0:T(8,128)(2,1)S(1)} collective-permute-done((bf16[512,128]{1,0:T(8,128)(2,1)S(1)}, bf16[512,128]{1,0:T(8,128)(2,1)S(1)}, u32[]{:S(2)}, u32[]{:S(2)}) %collective-permute-start.2) | collective-permute-done | bytes 131104 | tf_op jit(solution)/shard_map/ppermute | solution.py:301
  15.5 3.2 %collective-permute-start.3 = (bf16[1024,128]{1,0:T(8,128)(2,1)S(1)}, bf16[1024,128]{1,0:T(8,128)(2,1)S(1)}, u32[]{:S(2)}, u32[]{:S(2)}) collective-permute-start(bf16[1024,128]{1,0:T(8,128)(2,1)S(1)} %stack.8.e0), channel_id=1, source_target_pairs={{0,12},{1,13},{2,14},{3,15},{4,8},{5,9},{6,10},{7,11},{8,4},{9,5},... | collective-permute-start | bytes 786440 | tf_op jit(solution)/shard_map/ppermute | solution.py:301
  18.7 2.3 %pack.1 = bf16[16,192,128]{2,1,0:T(8,128)(2,1)} custom-call(bf16[128,1024]{1,0:T(8,128)(2,1)} %bitcast.26, bf16[128,1024]{1,0:T(8,128)(2,1)} %bitcast.27, bf16[128,1024]{1,0:T(8,128)(2,1)} %bitcast.28), custom_call_target="tpu_custom_call" | custom-call | tf_op jit(solution)/shard_map/pack/pallas_call | solution.py:60
  21.0 2.2 %collective-permute-done.3.e1 = bf16[1024,128]{1,0:T(8,128)(2,1)S(1)} collective-permute-done((bf16[1024,128]{1,0:T(8,128)(2,1)S(1)}, bf16[1024,128]{1,0:T(8,128)(2,1)S(1)}, u32[]{:S(2)}, u32[]{:S(2)}) %collective-permute-start.3) | collective-permute-done | bytes 262176 | tf_op jit(solution)/shard_map/ppermute | solution.py:301
  23.1 6.7 %all-to-all-start = ((bf16[16,192,128]{2,1,0:T(8,128)(2,1)}), bf16[16,192,128]{2,1,0:T(8,128)(2,1)S(1)}, u32[]{:S(2)}, u32[]{:S(2)}) async-start(bf16[16,192,128]{2,1,0:T(8,128)(2,1)} %pack.1), calls=%async_computation | async-start | bytes 1572864 | tf_op jit(solution)/shard_map/all_to_all | solution.py:329
  29.8 1.6 %decode.1.refs_0_ = bf16[512,128]{1,0:T(8,128)(2,1)S(1)} custom-call(bf16[512,1024]{1,0:T(8,128)(2,1)S(1)} %bitcast.23, bf16[1024,128]{1,0:T(8,128)(2,1)S(1)} %stack.8.e0, bf16[1024,128]{1,0:T(8,128)(2,1)S(1)} %collective-permute-done.3.e1), custom_call_target="tpu_custom_call" | custom-call | flops 1000000000 | bytes 1000000 | tf_op jit(solution)/shard_map/decode/pallas_call | solution.py:223
  31.4 2.0 %collective-permute-start.4 = (bf16[512,128]{1,0:T(8,128)(2,1)S(1)}, bf16[512,128]{1,0:T(8,128)(2,1)S(1)}, u32[]{:S(2)}, u32[]{:S(2)}) collective-permute-start(bf16[512,128]{1,0:T(8,128)(2,1)S(1)} %decode.1.refs_0_), channel_id=1, source_target_pairs={{0,16},{16,0},{32,48},{48,32},{1,17},{17,1},{33,49},{49,33},{2,18}... | collective-permute-start | bytes 393224 | tf_op jit(solution)/shard_map/ppermute | solution.py:301
  33.4 3.1 %collective-permute-done.4.refs_1_ = bf16[512,128]{1,0:T(8,128)(2,1)S(1)} collective-permute-done((bf16[512,128]{1,0:T(8,128)(2,1)S(1)}, bf16[512,128]{1,0:T(8,128)(2,1)S(1)}, u32[]{:S(2)}, u32[]{:S(2)}) %collective-permute-start.4) | collective-permute-done | bytes 131104 | tf_op jit(solution)/shard_map/ppermute | solution.py:301
  37.1 4.1 %collective-permute-start.5 = (bf16[512,128]{1,0:T(8,128)(2,1)S(1)}, bf16[512,128]{1,0:T(8,128)(2,1)S(1)}, u32[]{:S(2)}, u32[]{:S(2)}) collective-permute-start(bf16[512,128]{1,0:T(8,128)(2,1)S(1)} %meet.2.refs_0_), channel_id=1, source_target_pairs={{0,48},{16,32},{32,16},{48,0},{1,49},{17,33},{33,17},{49,1},{2,50}... | collective-permute-start | bytes 393224 | tf_op jit(solution)/shard_map/ppermute | solution.py:301
  41.2 4.3 %collective-permute-done.5.refs_1_ = bf16[512,128]{1,0:T(8,128)(2,1)S(1)} collective-permute-done((bf16[512,128]{1,0:T(8,128)(2,1)S(1)}, bf16[512,128]{1,0:T(8,128)(2,1)S(1)}, u32[]{:S(2)}, u32[]{:S(2)}) %collective-permute-start.5) | collective-permute-done | bytes 131104 | tf_op jit(solution)/shard_map/ppermute | solution.py:301
  46.6 3.3 %collective-permute-start.8 = (bf16[1024,128]{1,0:T(8,128)(2,1)S(1)}, bf16[1024,128]{1,0:T(8,128)(2,1)S(1)}, u32[]{:S(2)}, u32[]{:S(2)}) collective-permute-start(bf16[1024,128]{1,0:T(8,128)(2,1)S(1)} %bitcast.18), channel_id=1, source_target_pairs={{0,48},{16,32},{32,16},{48,0},{1,49},{17,33},{33,17},{49,1},{2,50}... | collective-permute-start | bytes 786440 | tf_op jit(solution)/shard_map/ppermute | solution.py:301
  49.9 2.0 %collective-permute-start.6 = (bf16[1,32,1024]{2,1,0:T(8,128)(2,1)S(1)}, bf16[1,32,1024]{2,1,0:T(8,128)(2,1)S(1)}, u32[]{:S(2)}, u32[]{:S(2)}) collective-permute-start(bf16[1,32,1024]{2,1,0:T(8,128)(2,1)S(1)} %bitcast.12), channel_id=1, source_target_pairs={{0,1},{1,0},{2,3},{3,2},{4,5},{5,4},{6,7},{7,6},{8,9},{9,8},{10,11... | collective-permute-start | bytes 196616 | tf_op jit(solution)/shard_map/ppermute | solution.py:301
  51.9 2.3 %collective-permute-done.6.b = bf16[1,32,1024]{2,1,0:T(8,128)(2,1)S(1)} collective-permute-done((bf16[1,32,1024]{2,1,0:T(8,128)(2,1)S(1)}, bf16[1,32,1024]{2,1,0:T(8,128)(2,1)S(1)}, u32[]{:S(2)}, u32[]{:S(2)}) %collective-permute-start.6) | collective-permute-done | bytes 65568 | tf_op jit(solution)/shard_map/ppermute | solution.py:301
  54.2 1.3 %collective-permute-done.8.rest_1_.kv2 = bf16[1024,128]{1,0:T(8,128)(2,1)S(1)} collective-permute-done((bf16[1024,128]{1,0:T(8,128)(2,1)S(1)}, bf16[1024,128]{1,0:T(8,128)(2,1)S(1)}, u32[]{:S(2)}, u32[]{:S(2)}) %collective-permute-start.8) | collective-permute-done | bytes 262176 | tf_op jit(solution)/shard_map/ppermute | solution.py:301
  56.3 3.2 %collective-permute-start.9 = (bf16[2,32,1024]{2,1,0:T(8,128)(2,1)S(1)}, bf16[2,32,1024]{2,1,0:T(8,128)(2,1)S(1)}, u32[]{:S(2)}, u32[]{:S(2)}) collective-permute-start(bf16[2,32,1024]{2,1,0:T(8,128)(2,1)S(1)} %stack.9.a), channel_id=1, source_target_pairs={{0,3},{1,2},{2,1},{3,0},{4,7},{5,6},{6,5},{7,4},{8,11},{9,10},{10,... | collective-permute-start | bytes 393224 | tf_op jit(solution)/shard_map/ppermute | solution.py:301
  59.6 2.4 %collective-permute-start.12 = (bf16[1024,128]{1,0:T(8,128)(2,1)S(1)}, bf16[1024,128]{1,0:T(8,128)(2,1)S(1)}, u32[]{:S(2)}, u32[]{:S(2)}) collective-permute-start(bf16[1024,128]{1,0:T(8,128)(2,1)S(1)} %collective-permute-done.7.rest_0_.kv1), channel_id=1, source_target_pairs={{0,48},{16,32},{32,16},{48,0},{1,49},{17,33},{33,17},{49,1},{2,50}... | collective-permute-start | bytes 786440 | tf_op jit(solution)/shard_map/ppermute | solution.py:301
  62.6 2.5 %collective-permute-start.10 = (bf16[4,32,1024]{2,1,0:T(8,128)(2,1)S(1)}, bf16[4,32,1024]{2,1,0:T(8,128)(2,1)S(1)}, u32[]{:S(2)}, u32[]{:S(2)}) collective-permute-start(bf16[4,32,1024]{2,1,0:T(8,128)(2,1)S(1)} %stack.10.a), channel_id=1, source_target_pairs={{0,4},{1,5},{2,6},{3,7},{4,0},{5,1},{6,2},{7,3},{8,12},{9,13},{10,... | collective-permute-start | bytes 786440 | tf_op jit(solution)/shard_map/ppermute | solution.py:301
  65.1 2.1 %collective-permute-done.12.kv3 = bf16[1024,128]{1,0:T(8,128)(2,1)S(1)} collective-permute-done((bf16[1024,128]{1,0:T(8,128)(2,1)S(1)}, bf16[1024,128]{1,0:T(8,128)(2,1)S(1)}, u32[]{:S(2)}, u32[]{:S(2)}) %collective-permute-start.12) | collective-permute-done | bytes 262176 | tf_op jit(solution)/shard_map/ppermute | solution.py:301
  67.8 2.6 %collective-permute-start.13 = (bf16[128,2048]{1,0:T(8,128)(2,1)S(1)}, bf16[128,2048]{1,0:T(8,128)(2,1)S(1)}, u32[]{:S(2)}, u32[]{:S(2)}) collective-permute-start(bf16[128,2048]{1,0:T(8,128)(2,1)S(1)} %pad_maximum_fusion.rest_0_), channel_id=1, source_target_pairs={{0,1},{1,0},{2,3},{3,2},{4,5},{5,4},{6,7},{7,6},{8,9},{9,8},{10,11... | collective-permute-start | bytes 1572872 | tf_op jit(solution)/shard_map/ppermute | solution.py:346
  71.4 4.0 %collective-permute-start.11 = (bf16[8,32,1024]{2,1,0:T(8,128)(2,1)S(1)}, bf16[8,32,1024]{2,1,0:T(8,128)(2,1)S(1)}, u32[]{:S(2)}, u32[]{:S(2)}) collective-permute-start(bf16[8,32,1024]{2,1,0:T(8,128)(2,1)S(1)} %stack.11.own), channel_id=1, source_target_pairs={{0,12},{1,13},{2,14},{3,15},{4,8},{5,9},{6,10},{7,11},{8,4},{9,5},... | collective-permute-start | bytes 1572872 | tf_op jit(solution)/shard_map/ppermute | solution.py:301
  75.4 10.4 %heavy.1 = bf16[16,64,128]{2,1,0:T(8,128)(2,1)} custom-call(bf16[16,192,128]{2,1,0:T(8,128)(2,1)S(1)} %all-to-all-done.kv.q, bf16[1024,128]{1,0:T(8,128)(2,1)S(1)} %bitcast.20, bf16[1024,128]{1,0:T(8,128)(2,1)S(1)} %collective-permute-done.7.rest_0_.kv1, bf16[1024,128]{1,0:T(8,128)(2,1)S(1)} %collective-permute-done.8.rest_1_.kv2, ...), custom_call_target="tpu_custom_call" | custom-call | flops 10000000000 | bytes 2000000 | tf_op jit(solution)/shard_map/heavy/pallas_call | solution.py:119
  85.8 4.0 %all-to-all-start.1 = ((bf16[16,64,128]{2,1,0:T(8,128)(2,1)}), bf16[16,64,128]{2,1,0:T(8,128)(2,1)S(1)}, u32[]{:S(2)}, u32[]{:S(2)}) async-start(bf16[16,64,128]{2,1,0:T(8,128)(2,1)} %heavy.1), calls=%async_computation.1 | async-start | bytes 524288 | tf_op jit(solution)/shard_map/all_to_all | solution.py:351
  89.9 1.1 %spread.1 = bf16[16,32,1024]{2,1,0:T(8,128)(2,1)} custom-call(bf16[8,32,1024]{2,1,0:T(8,128)(2,1)S(1)} %stack.11.own, bf16[8,32,1024]{2,1,0:T(8,128)(2,1)S(1)} %collective-permute-done.11.other), custom_call_target="tpu_custom_call" | custom-call | tf_op jit(solution)/shard_map/spread/pallas_call | solution.py:290
  91.2 1.5 %light.1 = f32[128,1024]{1,0:T(8,128)S(1)} custom-call(bf16[128,1024]{1,0:T(8,128)(2,1)S(1)} %bitcast.24, bf16[128,1024]{1,0:T(8,128)(2,1)S(1)} %bitcast.15, bf16[128,1024]{1,0:T(8,128)(2,1)S(1)} %bitcast.17, bf16[128,2048]{1,0:T(8,128)(2,1)S(1)} %collective-permute-done.13.even, bf16[128,2048]{1,0:T(8,128)(2,1)S(1)} %collective-permute-done.14.odd), custom_call_target="tpu_custom_call" | custom-call | flops 3000000000 | bytes 2000000 | tf_op jit(solution)/shard_map/light/pallas_call | solution.py:156
  92.7 5.8 %all-to-all-done.1.heavy = bf16[16,64,128]{2,1,0:T(8,128)(2,1)S(1)} async-done(((bf16[16,64,128]{2,1,0:T(8,128)(2,1)}), bf16[16,64,128]{2,1,0:T(8,128)(2,1)S(1)}, u32[]{:S(2)}, u32[]{:S(2)}) %all-to-all-start.1) | async-done | bytes 262176 | tf_op jit(solution)/shard_map/all_to_all | solution.py:351
  98.5 1.5 %join.1 = bf16[128,1024]{1,0:T(8,128)(2,1)} custom-call(s32[1,64]{1,0:T(1,128)S(1)} %copy-done.4, f32[128,1024]{1,0:T(8,128)S(1)} %light.1, bf16[16,64,128]{2,1,0:T(8,128)(2,1)S(1)} %all-to-all-done.1.heavy), custom_call_target="tpu_custom_call" | custom-call | tf_op jit(solution)/shard_map/join/pallas_call | solution.py:182
  (32 shorter events, 5.0 us)
Async XLA Ops:
  0.6 4.2 %collective-permute-start = (bf16[128,128]{1,0:T(8,128)(2,1)}, bf16[128,128]{1,0:T(8,128)(2,1)S(1)}, u32[]{:S(2)}, u32[]{:S(2)}) collective-permute-start(bf16[128,128]{1,0:T(8,128)(2,1)} %bitcast.21), channel_id=1, source_target_pairs={{0,1},{1,0},{2,3},{3,2},{4,5},{5,4},{6,7},{7,6},{8,9},{9,8},{10,11... | collective-permute-start | bytes 98312 | tf_op jit(solution)/shard_map/ppermute | solution.py:301
  2.3 2.6 %copy-start.2 = (bf16[1,128,128]{2,1,0:T(8,128)(2,1)S(1)}, bf16[1,128,128]{2,1,0:T(8,128)(2,1)}, u32[]{:S(2)}) copy-start(bf16[1,128,128]{2,1,0:T(8,128)(2,1)} %param.16) | copy-start | bytes 98308
  4.8 5.6 %collective-permute-start.1 = (bf16[256,128]{1,0:T(8,128)(2,1)S(1)}, bf16[256,128]{1,0:T(8,128)(2,1)S(1)}, u32[]{:S(2)}, u32[]{:S(2)}) collective-permute-start(bf16[256,128]{1,0:T(8,128)(2,1)S(1)} %stack.6.a), channel_id=1, source_target_pairs={{0,3},{1,2},{2,1},{3,0},{4,7},{5,6},{6,5},{7,4},{8,11},{9,10},{10,... | collective-permute-start | bytes 196616 | tf_op jit(solution)/shard_map/ppermute | solution.py:301
  10.4 5.0 %collective-permute-start.2 = (bf16[512,128]{1,0:T(8,128)(2,1)S(1)}, bf16[512,128]{1,0:T(8,128)(2,1)S(1)}, u32[]{:S(2)}, u32[]{:S(2)}) collective-permute-start(bf16[512,128]{1,0:T(8,128)(2,1)S(1)} %stack.7.a), channel_id=1, source_target_pairs={{0,4},{1,5},{2,6},{3,7},{4,0},{5,1},{6,2},{7,3},{8,12},{9,13},{10,... | collective-permute-start | bytes 393224 | tf_op jit(solution)/shard_map/ppermute | solution.py:301
  15.5 7.7 %collective-permute-start.3 = (bf16[1024,128]{1,0:T(8,128)(2,1)S(1)}, bf16[1024,128]{1,0:T(8,128)(2,1)S(1)}, u32[]{:S(2)}, u32[]{:S(2)}) collective-permute-start(bf16[1024,128]{1,0:T(8,128)(2,1)S(1)} %stack.8.e0), channel_id=1, source_target_pairs={{0,12},{1,13},{2,14},{3,15},{4,8},{5,9},{6,10},{7,11},{8,4},{9,5},... | collective-permute-start | bytes 786440 | tf_op jit(solution)/shard_map/ppermute | solution.py:301
  20.9 8.9 %copy-start.5 = (bf16[1,512,1024]{2,1,0:T(8,128)(2,1)S(1)}, bf16[1,512,1024]{2,1,0:T(8,128)(2,1)}, u32[]{:S(2)}) copy-start(bf16[1,512,1024]{2,1,0:T(8,128)(2,1)} %param.17) | copy-start | bytes 3145732
  23.1 22.8 %all-to-all-start = ((bf16[16,192,128]{2,1,0:T(8,128)(2,1)}), bf16[16,192,128]{2,1,0:T(8,128)(2,1)S(1)}, u32[]{:S(2)}, u32[]{:S(2)}) async-start(bf16[16,192,128]{2,1,0:T(8,128)(2,1)} %pack.1), calls=%async_computation | async-start | bytes 1572864 | tf_op jit(solution)/shard_map/all_to_all | solution.py:329
  31.4 5.0 %collective-permute-start.4 = (bf16[512,128]{1,0:T(8,128)(2,1)S(1)}, bf16[512,128]{1,0:T(8,128)(2,1)S(1)}, u32[]{:S(2)}, u32[]{:S(2)}) collective-permute-start(bf16[512,128]{1,0:T(8,128)(2,1)S(1)} %decode.1.refs_0_), channel_id=1, source_target_pairs={{0,16},{16,0},{32,48},{48,32},{1,17},{17,1},{33,49},{49,33},{2,18}... | collective-permute-start | bytes 393224 | tf_op jit(solution)/shard_map/ppermute | solution.py:301
  37.1 8.9 %copy-start.3 = (s32[1,32]{1,0:T(1,128)S(1)}, s32[1,32]{1,0:T(1,128)}, u32[]{:S(2)}) copy-start(s32[1,32]{1,0:T(1,128)} %ids.2) | copy-start | bytes 388
  37.1 8.4 %collective-permute-start.5 = (bf16[512,128]{1,0:T(8,128)(2,1)S(1)}, bf16[512,128]{1,0:T(8,128)(2,1)S(1)}, u32[]{:S(2)}, u32[]{:S(2)}) collective-permute-start(bf16[512,128]{1,0:T(8,128)(2,1)S(1)} %meet.2.refs_0_), channel_id=1, source_target_pairs={{0,48},{16,32},{32,16},{48,0},{1,49},{17,33},{33,17},{49,1},{2,50}... | collective-permute-start | bytes 393224 | tf_op jit(solution)/shard_map/ppermute | solution.py:301
  46.6 9.0 %collective-permute-start.8 = (bf16[1024,128]{1,0:T(8,128)(2,1)S(1)}, bf16[1024,128]{1,0:T(8,128)(2,1)S(1)}, u32[]{:S(2)}, u32[]{:S(2)}) collective-permute-start(bf16[1024,128]{1,0:T(8,128)(2,1)S(1)} %bitcast.18), channel_id=1, source_target_pairs={{0,48},{16,32},{32,16},{48,0},{1,49},{17,33},{33,17},{49,1},{2,50}... | collective-permute-start | bytes 786440 | tf_op jit(solution)/shard_map/ppermute | solution.py:301
  49.9 6.4 %collective-permute-start.7 = (bf16[1024,128]{1,0:T(8,128)(2,1)S(1)}, bf16[1024,128]{1,0:T(8,128)(2,1)S(1)}, u32[]{:S(2)}, u32[]{:S(2)}) collective-permute-start(bf16[1024,128]{1,0:T(8,128)(2,1)S(1)} %bitcast.19), channel_id=1, source_target_pairs={{0,16},{16,0},{32,48},{48,32},{1,17},{17,1},{33,49},{49,33},{2,18}... | collective-permute-start | bytes 786440 | tf_op jit(solution)/shard_map/ppermute | solution.py:301
  49.9 4.3 %collective-permute-start.6 = (bf16[1,32,1024]{2,1,0:T(8,128)(2,1)S(1)}, bf16[1,32,1024]{2,1,0:T(8,128)(2,1)S(1)}, u32[]{:S(2)}, u32[]{:S(2)}) collective-permute-start(bf16[1,32,1024]{2,1,0:T(8,128)(2,1)S(1)} %bitcast.12), channel_id=1, source_target_pairs={{0,1},{1,0},{2,3},{3,2},{4,5},{5,4},{6,7},{7,6},{8,9},{9,8},{10,11... | collective-permute-start | bytes 196616 | tf_op jit(solution)/shard_map/ppermute | solution.py:301
  56.3 6.3 %collective-permute-start.9 = (bf16[2,32,1024]{2,1,0:T(8,128)(2,1)S(1)}, bf16[2,32,1024]{2,1,0:T(8,128)(2,1)S(1)}, u32[]{:S(2)}, u32[]{:S(2)}) collective-permute-start(bf16[2,32,1024]{2,1,0:T(8,128)(2,1)S(1)} %stack.9.a), channel_id=1, source_target_pairs={{0,3},{1,2},{2,1},{3,0},{4,7},{5,6},{6,5},{7,4},{8,11},{9,10},{10,... | collective-permute-start | bytes 393224 | tf_op jit(solution)/shard_map/ppermute | solution.py:301
  59.6 7.6 %collective-permute-start.12 = (bf16[1024,128]{1,0:T(8,128)(2,1)S(1)}, bf16[1024,128]{1,0:T(8,128)(2,1)S(1)}, u32[]{:S(2)}, u32[]{:S(2)}) collective-permute-start(bf16[1024,128]{1,0:T(8,128)(2,1)S(1)} %collective-permute-done.7.rest_0_.kv1), channel_id=1, source_target_pairs={{0,48},{16,32},{32,16},{48,0},{1,49},{17,33},{33,17},{49,1},{2,50}... | collective-permute-start | bytes 786440 | tf_op jit(solution)/shard_map/ppermute | solution.py:301
  62.6 8.8 %collective-permute-start.10 = (bf16[4,32,1024]{2,1,0:T(8,128)(2,1)S(1)}, bf16[4,32,1024]{2,1,0:T(8,128)(2,1)S(1)}, u32[]{:S(2)}, u32[]{:S(2)}) collective-permute-start(bf16[4,32,1024]{2,1,0:T(8,128)(2,1)S(1)} %stack.10.a), channel_id=1, source_target_pairs={{0,4},{1,5},{2,6},{3,7},{4,0},{5,1},{6,2},{7,3},{8,12},{9,13},{10,... | collective-permute-start | bytes 786440 | tf_op jit(solution)/shard_map/ppermute | solution.py:301
  67.1 23.8 %collective-permute-start.14 = (bf16[128,2048]{1,0:T(8,128)(2,1)S(1)}, bf16[128,2048]{1,0:T(8,128)(2,1)S(1)}, u32[]{:S(2)}, u32[]{:S(2)}) collective-permute-start(bf16[128,2048]{1,0:T(8,128)(2,1)S(1)} %pad_maximum_fusion.rest_0_), channel_id=1, source_target_pairs={{1,2},{2,1},{3,4},{4,3},{5,6},{6,5},{7,8},{8,7},{9,10},{10,9},{11,... | collective-permute-start | bytes 1572872 | tf_op jit(solution)/shard_map/ppermute | solution.py:347
  67.8 23.1 %collective-permute-start.13 = (bf16[128,2048]{1,0:T(8,128)(2,1)S(1)}, bf16[128,2048]{1,0:T(8,128)(2,1)S(1)}, u32[]{:S(2)}, u32[]{:S(2)}) collective-permute-start(bf16[128,2048]{1,0:T(8,128)(2,1)S(1)} %pad_maximum_fusion.rest_0_), channel_id=1, source_target_pairs={{0,1},{1,0},{2,3},{3,2},{4,5},{5,4},{6,7},{7,6},{8,9},{9,8},{10,11... | collective-permute-start | bytes 1572872 | tf_op jit(solution)/shard_map/ppermute | solution.py:346
  71.4 18.4 %collective-permute-start.11 = (bf16[8,32,1024]{2,1,0:T(8,128)(2,1)S(1)}, bf16[8,32,1024]{2,1,0:T(8,128)(2,1)S(1)}, u32[]{:S(2)}, u32[]{:S(2)}) collective-permute-start(bf16[8,32,1024]{2,1,0:T(8,128)(2,1)S(1)} %stack.11.own), channel_id=1, source_target_pairs={{0,12},{1,13},{2,14},{3,15},{4,8},{5,9},{6,10},{7,11},{8,4},{9,5},... | collective-permute-start | bytes 1572872 | tf_op jit(solution)/shard_map/ppermute | solution.py:301
  85.8 12.7 %all-to-all-start.1 = ((bf16[16,64,128]{2,1,0:T(8,128)(2,1)}), bf16[16,64,128]{2,1,0:T(8,128)(2,1)S(1)}, u32[]{:S(2)}, u32[]{:S(2)}) async-start(bf16[16,64,128]{2,1,0:T(8,128)(2,1)} %heavy.1), calls=%async_computation.1 | async-start | bytes 524288 | tf_op jit(solution)/shard_map/all_to_all | solution.py:351
  89.8 1.1 %copy-start = (bf16[1,128,1024]{2,1,0:T(8,128)(2,1)S(1)}, bf16[1,128,1024]{2,1,0:T(8,128)(2,1)}, u32[]{:S(2)}) copy-start(bf16[1,128,1024]{2,1,0:T(8,128)(2,1)} %param.11) | copy-start | bytes 786436
  89.8 1.1 %copy-start.1 = (bf16[1,128,1024]{2,1,0:T(8,128)(2,1)S(1)}, bf16[1,128,1024]{2,1,0:T(8,128)(2,1)}, u32[]{:S(2)}) copy-start(bf16[1,128,1024]{2,1,0:T(8,128)(2,1)} %param.12) | copy-start | bytes 786436
  89.8 1.3 %copy-start.6 = (bf16[1,128,1024]{2,1,0:T(8,128)(2,1)S(1)}, bf16[1,128,1024]{2,1,0:T(8,128)(2,1)}, u32[]{:S(2)}) copy-start(bf16[1,128,1024]{2,1,0:T(8,128)(2,1)} %param.10) | copy-start | bytes 786436
  91.2 7.3 %copy-start.4 = (s32[1,64]{1,0:T(1,128)S(1)}, s32[1,64]{1,0:T(1,128)}, u32[]{:S(2)}) copy-start(s32[1,64]{1,0:T(1,128)} %ids.3) | copy-start | bytes 772

commit v8 on v6

--- a/solution.py
+++ b/solution.py
@@ -125,7 +125,9 @@
     )(q_kv, *kvs)
 
 
-def light_kernel(q, k, v, even, odd, out):
+def light_kernel(q, k, v, even, odd, rows_in, out, rows_out, sem):
+    copy = pltpu.make_async_copy(rows_in, rows_out, sem)
+    copy.start()
     here = lax.axis_index(TOKENS)
     last = lax.axis_size(TOKENS) - 1
     rows, width = q.shape
@@ -150,16 +152,22 @@
         o = nn(po.astype(bf16), v[:, c]) + nn(pe.astype(bf16), even[:, cv]) + nn(pd.astype(bf16), odd[:, cv])
         o = o / total
         out[:, c] = jnp.where(low, o[:rows], o[rows:])
-
-
-def light_attend(q, k, v, even, odd):
+    copy.wait()
+
+
+def light_attend(q, k, v, even, odd, decoded):
+    vmem = pl.BlockSpec(memory_space=pltpu.VMEM)
+    hbm = pl.BlockSpec(memory_space=pl.ANY)
     return pl.pallas_call(
         light_kernel,
-        out_shape=jax.ShapeDtypeStruct(q.shape, f32),
+        in_specs=[vmem] * 5 + [hbm],
+        out_specs=(vmem, hbm),
+        out_shape=(jax.ShapeDtypeStruct(q.shape, f32), jax.ShapeDtypeStruct(decoded.shape, bf16)),
+        scratch_shapes=[pltpu.SemaphoreType.DMA(())],
         compiler_params=params(),
         cost_estimate=pl.CostEstimate(flops=3_000_000_000, transcendentals=800_000, bytes_accessed=2_000_000),
         name="light",
-    )(q, k, v, even, odd)
+    )(q, k, v, even, odd, decoded)
 
 
 def join_kernel(ids, light, heavy, out):
@@ -224,7 +232,7 @@
         out_shape=jax.ShapeDtypeStruct((rows * (width // HEAD), LANES), bf16),
         scratch_shapes=[pltpu.VMEM((rows, width), bf16), pltpu.SemaphoreType.DMA(())],
         compiler_params=params(),
-        cost_estimate=pl.CostEstimate(flops=1_000_000_000, transcendentals=1_000_000, bytes_accessed=1_000_000),
+        cost_estimate=pl.CostEstimate(flops=30_000_000_000, transcendentals=1_000_000, bytes_accessed=1_000_000),
         name="decode",
     )(q, *enc)
 
@@ -239,17 +247,19 @@
     for x, s in zip(parts[1:], scales[1:]):
         value = value + x * s
     value = (value / total).astype(bf16)
-    rows, width = out.shape
+    copies, rows, width = out.shape
     for p in range(width // LANES):
         e = value[2 * p * rows : (2 * p + 1) * rows, HEAD:]
         o = value[(2 * p + 1) * rows : (2 * p + 2) * rows, HEAD:]
-        out[:, p * LANES : (p + 1) * LANES] = jnp.concatenate([e, o], axis=1)
-
-
-def meet(parts, rows, width):
+        both = jnp.concatenate([e, o], axis=1)
+        for n in range(copies):
+            out[n, :, p * LANES : (p + 1) * LANES] = both
+
+
+def meet(parts, copies, rows, width):
     return pl.pallas_call(
         meet_kernel,
-        out_shape=jax.ShapeDtypeStruct((rows, width), bf16),
+        out_shape=jax.ShapeDtypeStruct((copies, rows, width), bf16),
         compiler_params=params(),
         name="meet",
     )(*parts)
@@ -272,24 +282,6 @@
         compiler_params=params(),
         name="stack",
     )(*parts, *others)
-
-
-def spread_kernel(own, other1, other2, other3, out):
-    place = lax.axis_index("fine")
-    side = own.shape[0]
-    for dr, got in enumerate((own, other1, other2, other3)):
-        for dc in range(side):
-            out[place ^ (dr * side + dc)] = got[dc]
-
-
-def spread(rows):
-    side, count, width = rows[0].shape
-    return pl.pallas_call(
-        spread_kernel,
-        out_shape=jax.ShapeDtypeStruct((len(rows) * side, count, width), bf16),
-        compiler_params=params(),
-        name="spread",
-    )(*rows)
 
 
 def around(value, axis, stride=1, ring=None):
@@ -324,27 +316,29 @@
 
     enc = square(stack(rows_of(enc_kv[0]), light_kv))
     chunks = pack(q_heavy[0], k_heavy[0], v_heavy[0])
-    group = lax.all_to_all(after_all(chunks, enc[1], enc[2], enc[3]), "fine", 0, 0, tiled=True)
+    group = lax.all_to_all(after_all(chunks, enc[0]), "fine", 0, 0, tiled=True)
 
     dec_rows = dec_queries.shape[1] // n_fine
     part = decode(dec_queries[0], enc, dec_rows)
-    share = meet([part] + around(part, "coarse"), dec_rows, width)
+    share = meet([part] + around(part, "coarse"), n_fine, dec_rows, width)
 
     own = pick(key_ids, after_all(group, share)).reshape(KGRP * BLOCK, LANES)
     routed = [own] + around(own, "coarse")
-    shares = square(stack(rows_of(after_all(share, own)[None])))
+    decoded = lax.all_to_all(after_all(share, own), "fine", 0, 0, tiled=True)
 
     light_kv = after_all(light_kv, routed)
     even = lax.ppermute(light_kv, TOKENS, [(i, i ^ 1) for i in range(n_seq)])
     odd = lax.ppermute(light_kv, TOKENS, [(i, (i - 1 ^ 1) + 1) for i in range(1, n_seq - 1)])
 
     heavy = heavy_attend(group, routed)
-    shares, q_light = after_all((shares, q_light), heavy)
+    q_light = after_all(q_light, heavy)
+    heavy, decoded = lax.optimization_barrier((heavy, decoded))
     heavy = lax.all_to_all(heavy, "fine", 0, 0, tiled=True)
-    light = light_attend(q_light[0], k_light[0], v_light[0], even, odd)
-    decoded = spread(shares).reshape(1, -1, width)
+    light, decoded = light_attend(
+        q_light[0], k_light[0], v_light[0], even, odd, decoded.reshape(-1, width)
+    )
     encoded = join(query_ids, light, heavy)[None]
-    return (encoded, decoded)
+    return (encoded, decoded[None])
 
 
 def solution(mesh):

time: 88.4 us -> 84.6 us (0.957)
  waiting for transfers between devices: 23.2 us -> 13.6 us
  local copies, waits for them, and re-layouts: 0.17 us -> 4.29 us
  Pallas kernels: 19.9 us -> 21.5 us
    ppermute x18 -> x12, starting transfers between devices: 26.3 us -> 17.6 us  [around(): return [lax.ppermute(value, axis, pairs(d)) for d in range(1, ring)]]
    ppermute x18 -> x12, waiting for transfers between devices: 17.3 us -> 8.84 us  [around(): return [lax.ppermute(value, axis, pairs(d)) for d in range(1, ring)]]
    all_to_all x1 -> x2, starting transfers between devices: 4.97 us -> 13.4 us  [the longest x1 7.22 us: local(): decoded = lax.all_to_all(after_all(share, own), 'fine', 0, 0, tiled=True)]
    unnamed x14 -> x22, local copies, waits for them, and re-layouts: 0.17 us -> 4.29 us
    pallas_call x3 -> x2, Pallas kernels: 3.43 us -> 4.99 us  [the longest x1 2.97 us: light_attend(): pl.pallas_call(light_kernel, in_specs=[vmem] * 5 + [hbm], out_specs=(vmem...]
    all_to_all x1, waiting for transfers between devices: 5.86 us -> 4.7 us  [local(): heavy = lax.all_to_all(heavy, 'fine', 0, 0, tiled=True)]
  transfers between devices with their start and end apart: 22 -> 17, of which waited for: 10 -> 5; matrix products, arithmetic and copies ran while one was open for 1% -> 1% of each run, Pallas kernels for 20% -> 23%
where the time goes in v8:
time: 84.6 us; the launch traced here: 84.1 us
  starting transfers between devices  42.8 us (51%)
  Pallas kernels  21.5 us (25%)
  waiting for transfers between devices  13.6 us (16%)
  local copies, waits for them, and re-layouts  4.29 us (5%)
  other arithmetic  1.07 us (1%)
    ppermute x12, starting transfers between devices, around(): return [lax.ppermute(value, axis, pairs(d)) for d in range(1, ring)]  17.6 us
    pallas_call x1, Pallas kernels, heavy_attend(): pl.pallas_call(heavy_kernel, out_shape=jax.ShapeDtypeStruct((blocks, HALF...  10.4 us
    ppermute x12, waiting for transfers between devices, around(): return [lax.ppermute(value, axis, pairs(d)) for d in range(1, ring)]  8.84 us
    all_to_all x1, starting transfers between devices, local(): decoded = lax.all_to_all(after_all(share, own), 'fine', 0, 0, tiled=True)  7.22 us
    all_to_all x1, starting transfers between devices, local(): heavy = lax.all_to_all(heavy, 'fine', 0, 0, tiled=True)  6.3 us
    all_to_all x1, starting transfers between devices, local(): group = lax.all_to_all(after_all(chunks, enc[0]), 'fine', 0, 0, tiled=True)  6.18 us
    ppermute x1, starting transfers between devices, local(): even = lax.ppermute(light_kv, TOKENS, [(i, i ^ 1) for i in range(n_seq)])  4.86 us
    all_to_all x1, waiting for transfers between devices, local(): heavy = lax.all_to_all(heavy, 'fine', 0, 0, tiled=True)  4.7 us
  transfers between devices with their start and end apart: 17, of which 5 were waited for; matrix products, arithmetic and copies ran while one was open for 1% of the time, Pallas kernels for 23%

profile of v8, /device:TPU:0, one launch (start us, length us, event | category | flops | bytes accessed | tf_op | source)
XLA Modules:
  0.0 84.1 jit_solution(13795327372824551137)
XLA Ops:
  0.6 2.9 %collective-permute-start.2 = (bf16[128,128]{1,0:T(8,128)(2,1)}, bf16[128,128]{1,0:T(8,128)(2,1)S(1)}, u32[]{:S(2)}, u32[]{:S(2)}) collective-permute-start(bf16[128,128]{1,0:T(8,128)(2,1)} %bitcast.21), channel_id=1, source_target_pairs={{0,3},{1,2},{2,1},{3,0},{4,7},{5,6},{6,5},{7,4},{8,11},{9,10},{10,... | collective-permute-start | bytes 98312 | tf_op jit(solution)/shard_map/ppermute | solution.py:294
  3.6 0.8 collective-permute-start.1
  4.4 0.5 collective-permute-start
  4.8 1.1 %pad_maximum_fusion.refs_4_ = bf16[128,2048]{1,0:T(8,128)(2,1)S(1)} fusion(bf16[128,1024]{1,0:T(8,128)(2,1)} %bitcast.15, bf16[128,1024]{1,0:T(8,128)(2,1)} %bitcast.13), kind=kLoop, calls=%fused_computation | loop fusion | flops 1048576 | bytes 1048576 | tf_op jit(solution)/shard_map/concatenate | solution.py:309
  6.0 3.1 %collective-permute-done.1.refs_2_ = bf16[128,128]{1,0:T(8,128)(2,1)S(1)} collective-permute-done((bf16[128,128]{1,0:T(8,128)(2,1)}, bf16[128,128]{1,0:T(8,128)(2,1)S(1)}, u32[]{:S(2)}, u32[]{:S(2)}) %collective-permute-start.1) | collective-permute-done | bytes 32800 | tf_op jit(solution)/shard_map/ppermute | solution.py:294
  9.2 3.1 %collective-permute-start.5 = (bf16[512,128]{1,0:T(8,128)(2,1)S(1)}, bf16[512,128]{1,0:T(8,128)(2,1)S(1)}, u32[]{:S(2)}, u32[]{:S(2)}) collective-permute-start(bf16[512,128]{1,0:T(8,128)(2,1)S(1)} %stack.1.e0), channel_id=1, source_target_pairs={{0,12},{1,13},{2,14},{3,15},{4,8},{5,9},{6,10},{7,11},{8,4},{9,5},... | collective-permute-start | bytes 393224 | tf_op jit(solution)/shard_map/ppermute | solution.py:294
  12.3 0.6 collective-permute-start.4
  12.9 0.5 collective-permute-start.3
  13.4 2.3 %pack.1 = bf16[16,192,128]{2,1,0:T(8,128)(2,1)} custom-call(bf16[128,1024]{1,0:T(8,128)(2,1)} %bitcast.27, bf16[128,1024]{1,0:T(8,128)(2,1)} %bitcast.28, bf16[128,1024]{1,0:T(8,128)(2,1)} %bitcast.29), custom_call_target="tpu_custom_call" | custom-call | tf_op jit(solution)/shard_map/pack/pallas_call | solution.py:60
  15.7 6.2 %all-to-all-start = ((bf16[16,192,128]{2,1,0:T(8,128)(2,1)}), bf16[16,192,128]{2,1,0:T(8,128)(2,1)S(1)}, u32[]{:S(2)}, u32[]{:S(2)}) async-start(bf16[16,192,128]{2,1,0:T(8,128)(2,1)} %pack.1), calls=%async_computation | async-start | bytes 1572864 | tf_op jit(solution)/shard_map/all_to_all | solution.py:319
  21.9 1.8 %decode.1.a = bf16[512,128]{1,0:T(8,128)(2,1)S(1)} custom-call(bf16[512,1024]{1,0:T(8,128)(2,1)S(1)} %bitcast.25, bf16[512,128]{1,0:T(8,128)(2,1)S(1)} %stack.1.e0, bf16[512,128]{1,0:T(8,128)(2,1)S(1)} %collective-permute-done.3.e1, bf16[512,128]{1,0:T(8,128)(2,1)S(1)} %collective-permute-done.4.e2, bf16[512,128]{1,0:T(8,128)(2,1)S(1)} %collective-permute-done.5.e3), custom_call_target="tpu_custom_call" | custom-call | flops 30000001024 | bytes 1000000 | tf_op jit(solution)/shard_map/decode/pallas_call | solution.py:229
  23.7 4.1 %collective-permute-start.8 = (bf16[512,128]{1,0:T(8,128)(2,1)S(1)}, bf16[512,128]{1,0:T(8,128)(2,1)S(1)}, u32[]{:S(2)}, u32[]{:S(2)}) collective-permute-start(bf16[512,128]{1,0:T(8,128)(2,1)S(1)} %decode.1.a), channel_id=1, source_target_pairs={{0,48},{16,32},{32,16},{48,0},{1,49},{17,33},{33,17},{49,1},{2,50}... | collective-permute-start | bytes 393224 | tf_op jit(solution)/shard_map/ppermute | solution.py:294
  27.8 0.9 %collective-permute-start.6 = (bf16[512,128]{1,0:T(8,128)(2,1)S(1)}, bf16[512,128]{1,0:T(8,128)(2,1)S(1)}, u32[]{:S(2)}, u32[]{:S(2)}) collective-permute-start(bf16[512,128]{1,0:T(8,128)(2,1)S(1)} %decode.1.a), channel_id=1, source_target_pairs={{0,16},{16,0},{32,48},{48,32},{1,17},{17,1},{33,49},{49,33},{2,18}... | collective-permute-start | bytes 393224 | tf_op jit(solution)/shard_map/ppermute | solution.py:294
  28.8 3.0 %collective-permute-done.8.d = bf16[512,128]{1,0:T(8,128)(2,1)S(1)} collective-permute-done((bf16[512,128]{1,0:T(8,128)(2,1)S(1)}, bf16[512,128]{1,0:T(8,128)(2,1)S(1)}, u32[]{:S(2)}, u32[]{:S(2)}) %collective-permute-start.8) | collective-permute-done | bytes 131104 | tf_op jit(solution)/shard_map/ppermute | solution.py:294
  31.8 2.5 %collective-permute-done.7.c = bf16[512,128]{1,0:T(8,128)(2,1)S(1)} collective-permute-done((bf16[512,128]{1,0:T(8,128)(2,1)S(1)}, bf16[512,128]{1,0:T(8,128)(2,1)S(1)}, u32[]{:S(2)}, u32[]{:S(2)}) %collective-permute-start.7) | collective-permute-done | bytes 131104 | tf_op jit(solution)/shard_map/ppermute | solution.py:294
  34.3 2.0 %meet.1 = bf16[16,32,1024]{2,1,0:T(8,128)(2,1)} custom-call(bf16[512,128]{1,0:T(8,128)(2,1)S(1)} %decode.1.a, bf16[512,128]{1,0:T(8,128)(2,1)S(1)} %collective-permute-done.6.b, bf16[512,128]{1,0:T(8,128)(2,1)S(1)} %collective-permute-done.7.c, bf16[512,128]{1,0:T(8,128)(2,1)S(1)} %collective-permute-done.8.d), custom_call_target="tpu_custom_call" | custom-call | tf_op jit(solution)/shard_map/meet/pallas_call | solution.py:260
  36.3 0.6 pick.1
  36.9 2.0 %collective-permute-start.11 = (bf16[1024,128]{1,0:T(8,128)(2,1)S(1)}, bf16[1024,128]{1,0:T(8,128)(2,1)S(1)}, u32[]{:S(2)}, u32[]{:S(2)}) collective-permute-start(bf16[1024,128]{1,0:T(8,128)(2,1)S(1)} %bitcast.17), channel_id=1, source_target_pairs={{0,48},{16,32},{32,16},{48,0},{1,49},{17,33},{33,17},{49,1},{2,50}... | collective-permute-start | bytes 786440 | tf_op jit(solution)/shard_map/ppermute | solution.py:294
  39.1 2.0 %collective-permute-start.9 = (bf16[1024,128]{1,0:T(8,128)(2,1)S(1)}, bf16[1024,128]{1,0:T(8,128)(2,1)S(1)}, u32[]{:S(2)}, u32[]{:S(2)}) collective-permute-start(bf16[1024,128]{1,0:T(8,128)(2,1)S(1)} %bitcast.19), channel_id=1, source_target_pairs={{0,16},{16,0},{32,48},{48,32},{1,17},{17,1},{33,49},{49,33},{2,18}... | collective-permute-start | bytes 786440 | tf_op jit(solution)/shard_map/ppermute | solution.py:294
  41.1 7.2 %all-to-all-start.1 = ((bf16[16,32,1024]{2,1,0:T(8,128)(2,1)}), bf16[16,32,1024]{2,1,0:T(8,128)(2,1)S(1)}, u32[]{:S(2)}, u32[]{:S(2)}) async-start(bf16[16,32,1024]{2,1,0:T(8,128)(2,1)} %meet.1), calls=%async_computation.1 | async-start | bytes 2097152 | tf_op jit(solution)/shard_map/all_to_all | solution.py:327
  48.4 0.7 copy-done.7
  49.1 0.7 copy-done.9
  49.8 0.7 collective-permute-start.13
  50.5 4.9 %collective-permute-start.12 = (bf16[128,2048]{1,0:T(8,128)(2,1)S(1)}, bf16[128,2048]{1,0:T(8,128)(2,1)}, u32[]{:S(2)}, u32[]{:S(2)}) collective-permute-start(bf16[128,2048]{1,0:T(8,128)(2,1)S(1)} %pad_maximum_fusion.refs_4_), channel_id=1, source_target_pairs={{0,1},{1,0},{2,3},{3,2},{4,5},{5,4},{6,7},{7,6},{8,9},{9,8},{10,11... | collective-permute-start | bytes 1572872 | tf_op jit(solution)/shard_map/ppermute | solution.py:330
  55.3 0.9 %copy-done.8 = bf16[1024,128]{1,0:T(8,128)(2,1)S(1)} copy-done((bf16[1024,128]{1,0:T(8,128)(2,1)S(1)}, bf16[1024,128]{1,0:T(8,128)(2,1)}, u32[]{:S(2)}) %copy-start.8) | copy-done | bytes 262168
  56.3 0.9 %copy-done.10 = bf16[1024,128]{1,0:T(8,128)(2,1)S(1)} copy-done((bf16[1024,128]{1,0:T(8,128)(2,1)S(1)}, bf16[1024,128]{1,0:T(8,128)(2,1)}, u32[]{:S(2)}) %copy-start.10) | copy-done | bytes 262168
  57.2 10.4 %heavy.1 = bf16[16,64,128]{2,1,0:T(8,128)(2,1)} custom-call(bf16[16,192,128]{2,1,0:T(8,128)(2,1)S(1)} %all-to-all-done.kv.q, bf16[1024,128]{1,0:T(8,128)(2,1)S(1)} %bitcast.20, bf16[1024,128]{1,0:T(8,128)(2,1)S(1)} %copy-done.10, bf16[1024,128]{1,0:T(8,128)(2,1)S(1)} %copy-done.8, bf16[1024,128]{1,0:T(8,128)(2,1)S(1)} %collective-permute-done.11.kv3), custom_call_target="tpu_custom_call" | custom-call | flops 10000000000 | bytes 2000000 | tf_op jit(solution)/shard_map/heavy/pallas_call | solution.py:119
  67.6 6.3 %all-to-all-start.2 = ((bf16[16,64,128]{2,1,0:T(8,128)(2,1)}), bf16[16,64,128]{2,1,0:T(8,128)(2,1)S(1)}, u32[]{:S(2)}, u32[]{:S(2)}) async-start(bf16[16,64,128]{2,1,0:T(8,128)(2,1)} %heavy.1), calls=%async_computation.2 | async-start | bytes 524288 | tf_op jit(solution)/shard_map/all_to_all | solution.py:336
  74.0 0.9 %copy-done.6 = bf16[1,128,1024]{2,1,0:T(8,128)(2,1)S(1)} copy-done((bf16[1,128,1024]{2,1,0:T(8,128)(2,1)S(1)}, bf16[1,128,1024]{2,1,0:T(8,128)(2,1)}, u32[]{:S(2)}) %copy-start.6) | copy-done | bytes 262168
  74.9 3.0 %light.1 = (f32[128,1024]{1,0:T(8,128)S(1)}, bf16[512,1024]{1,0:T(8,128)(2,1)}) custom-call(bf16[128,1024]{1,0:T(8,128)(2,1)S(1)} %bitcast.26, bf16[128,1024]{1,0:T(8,128)(2,1)S(1)} %bitcast.14, bf16[128,1024]{1,0:T(8,128)(2,1)S(1)} %bitcast.16, bf16[128,2048]{1,0:T(8,128)(2,1)} %collective-permute-done.12.even, ...), custom_call_target="tpu_custom_call" | custom-call | flops 3000000000 | bytes 2000000 | tf_op jit(solution)/shard_map/light/pallas_call | solution.py:161
  77.9 4.7 %all-to-all-done.2.heavy = bf16[16,64,128]{2,1,0:T(8,128)(2,1)S(1)} async-done(((bf16[16,64,128]{2,1,0:T(8,128)(2,1)}), bf16[16,64,128]{2,1,0:T(8,128)(2,1)S(1)}, u32[]{:S(2)}, u32[]{:S(2)}) %all-to-all-start.2) | async-done | bytes 262176 | tf_op jit(solution)/shard_map/all_to_all | solution.py:336
  82.6 1.5 %join.1 = bf16[128,1024]{1,0:T(8,128)(2,1)} custom-call(s32[1,64]{1,0:T(1,128)S(1)} %copy-done.4, f32[128,1024]{1,0:T(8,128)S(1)} %get-tuple-element.17.light, bf16[16,64,128]{2,1,0:T(8,128)(2,1)S(1)} %all-to-all-done.2.heavy), custom_call_target="tpu_custom_call" | custom-call | tf_op jit(solution)/shard_map/join/pallas_call | solution.py:190
  (33 shorter events, 0.4 us)
Async XLA Ops:
  0.6 5.4 %collective-permute-start.2 = (bf16[128,128]{1,0:T(8,128)(2,1)}, bf16[128,128]{1,0:T(8,128)(2,1)S(1)}, u32[]{:S(2)}, u32[]{:S(2)}) collective-permute-start(bf16[128,128]{1,0:T(8,128)(2,1)} %bitcast.21), channel_id=1, source_target_pairs={{0,3},{1,2},{2,1},{3,0},{4,7},{5,6},{6,5},{7,4},{8,11},{9,10},{10,... | collective-permute-start | bytes 98312 | tf_op jit(solution)/shard_map/ppermute | solution.py:294
  3.6 5.6 %collective-permute-start.1 = (bf16[128,128]{1,0:T(8,128)(2,1)}, bf16[128,128]{1,0:T(8,128)(2,1)S(1)}, u32[]{:S(2)}, u32[]{:S(2)}) collective-permute-start(bf16[128,128]{1,0:T(8,128)(2,1)} %bitcast.22), channel_id=1, source_target_pairs={{0,2},{1,3},{2,0},{3,1},{4,6},{5,7},{6,4},{7,5},{8,10},{9,11},{10,... | collective-permute-start | bytes 98312 | tf_op jit(solution)/shard_map/ppermute | solution.py:294
  4.4 4.8 %collective-permute-start = (bf16[128,128]{1,0:T(8,128)(2,1)}, bf16[128,128]{1,0:T(8,128)(2,1)S(1)}, u32[]{:S(2)}, u32[]{:S(2)}) collective-permute-start(bf16[128,128]{1,0:T(8,128)(2,1)} %bitcast.23), channel_id=1, source_target_pairs={{0,1},{1,0},{2,3},{3,2},{4,5},{5,4},{6,7},{7,6},{8,9},{9,8},{10,11... | collective-permute-start | bytes 98312 | tf_op jit(solution)/shard_map/ppermute | solution.py:294
  4.8 4.4 %copy-start.2 = (bf16[1,128,128]{2,1,0:T(8,128)(2,1)S(1)}, bf16[1,128,128]{2,1,0:T(8,128)(2,1)}, u32[]{:S(2)}) copy-start(bf16[1,128,128]{2,1,0:T(8,128)(2,1)} %param.16) | copy-start | bytes 98308
  9.2 12.7 %collective-permute-start.5 = (bf16[512,128]{1,0:T(8,128)(2,1)S(1)}, bf16[512,128]{1,0:T(8,128)(2,1)S(1)}, u32[]{:S(2)}, u32[]{:S(2)}) collective-permute-start(bf16[512,128]{1,0:T(8,128)(2,1)S(1)} %stack.1.e0), channel_id=1, source_target_pairs={{0,12},{1,13},{2,14},{3,15},{4,8},{5,9},{6,10},{7,11},{8,4},{9,5},... | collective-permute-start | bytes 393224 | tf_op jit(solution)/shard_map/ppermute | solution.py:294
  12.3 9.6 %collective-permute-start.4 = (bf16[512,128]{1,0:T(8,128)(2,1)S(1)}, bf16[512,128]{1,0:T(8,128)(2,1)S(1)}, u32[]{:S(2)}, u32[]{:S(2)}) collective-permute-start(bf16[512,128]{1,0:T(8,128)(2,1)S(1)} %stack.1.e0), channel_id=1, source_target_pairs={{0,8},{1,9},{2,10},{3,11},{4,12},{5,13},{6,14},{7,15},{8,0},{9,1},... | collective-permute-start | bytes 393224 | tf_op jit(solution)/shard_map/ppermute | solution.py:294
  12.9 9.0 %collective-permute-start.3 = (bf16[512,128]{1,0:T(8,128)(2,1)S(1)}, bf16[512,128]{1,0:T(8,128)(2,1)S(1)}, u32[]{:S(2)}, u32[]{:S(2)}) collective-permute-start(bf16[512,128]{1,0:T(8,128)(2,1)S(1)} %stack.1.e0), channel_id=1, source_target_pairs={{0,4},{1,5},{2,6},{3,7},{4,0},{5,1},{6,2},{7,3},{8,12},{9,13},{10,... | collective-permute-start | bytes 393224 | tf_op jit(solution)/shard_map/ppermute | solution.py:294
  15.7 6.2 %copy-start.5 = (bf16[1,512,1024]{2,1,0:T(8,128)(2,1)S(1)}, bf16[1,512,1024]{2,1,0:T(8,128)(2,1)}, u32[]{:S(2)}) copy-start(bf16[1,512,1024]{2,1,0:T(8,128)(2,1)} %param.17) | copy-start | bytes 3145732
  15.7 20.6 %all-to-all-start = ((bf16[16,192,128]{2,1,0:T(8,128)(2,1)}), bf16[16,192,128]{2,1,0:T(8,128)(2,1)S(1)}, u32[]{:S(2)}, u32[]{:S(2)}) async-start(bf16[16,192,128]{2,1,0:T(8,128)(2,1)} %pack.1), calls=%async_computation | async-start | bytes 1572864 | tf_op jit(solution)/shard_map/all_to_all | solution.py:319
  23.7 12.6 %copy-start.3 = (s32[1,32]{1,0:T(1,128)S(1)}, s32[1,32]{1,0:T(1,128)}, u32[]{:S(2)}) copy-start(s32[1,32]{1,0:T(1,128)} %ids.2) | copy-start | bytes 388
  23.7 8.0 %collective-permute-start.8 = (bf16[512,128]{1,0:T(8,128)(2,1)S(1)}, bf16[512,128]{1,0:T(8,128)(2,1)S(1)}, u32[]{:S(2)}, u32[]{:S(2)}) collective-permute-start(bf16[512,128]{1,0:T(8,128)(2,1)S(1)} %decode.1.a), channel_id=1, source_target_pairs={{0,48},{16,32},{32,16},{48,0},{1,49},{17,33},{33,17},{49,1},{2,50}... | collective-permute-start | bytes 393224 | tf_op jit(solution)/shard_map/ppermute | solution.py:294
  27.8 6.5 %collective-permute-start.7 = (bf16[512,128]{1,0:T(8,128)(2,1)S(1)}, bf16[512,128]{1,0:T(8,128)(2,1)S(1)}, u32[]{:S(2)}, u32[]{:S(2)}) collective-permute-start(bf16[512,128]{1,0:T(8,128)(2,1)S(1)} %decode.1.a), channel_id=1, source_target_pairs={{0,32},{16,48},{32,0},{48,16},{1,33},{17,49},{33,1},{49,17},{2,34}... | collective-permute-start | bytes 393224 | tf_op jit(solution)/shard_map/ppermute | solution.py:294
  27.8 6.5 %collective-permute-start.6 = (bf16[512,128]{1,0:T(8,128)(2,1)S(1)}, bf16[512,128]{1,0:T(8,128)(2,1)S(1)}, u32[]{:S(2)}, u32[]{:S(2)}) collective-permute-start(bf16[512,128]{1,0:T(8,128)(2,1)S(1)} %decode.1.a), channel_id=1, source_target_pairs={{0,16},{16,0},{32,48},{48,32},{1,17},{17,1},{33,49},{49,33},{2,18}... | collective-permute-start | bytes 393224 | tf_op jit(solution)/shard_map/ppermute | solution.py:294
  36.9 11.4 %collective-permute-start.11 = (bf16[1024,128]{1,0:T(8,128)(2,1)S(1)}, bf16[1024,128]{1,0:T(8,128)(2,1)S(1)}, u32[]{:S(2)}, u32[]{:S(2)}) collective-permute-start(bf16[1024,128]{1,0:T(8,128)(2,1)S(1)} %bitcast.17), channel_id=1, source_target_pairs={{0,48},{16,32},{32,16},{48,0},{1,49},{17,33},{33,17},{49,1},{2,50}... | collective-permute-start | bytes 786440 | tf_op jit(solution)/shard_map/ppermute | solution.py:294
  39.0 9.4 %collective-permute-start.10 = (bf16[1024,128]{1,0:T(8,128)(2,1)S(1)}, bf16[1024,128]{1,0:T(8,128)(2,1)S(1)}, u32[]{:S(2)}, u32[]{:S(2)}) collective-permute-start(bf16[1024,128]{1,0:T(8,128)(2,1)S(1)} %bitcast.18), channel_id=1, source_target_pairs={{0,32},{16,48},{32,0},{48,16},{1,33},{17,49},{33,1},{49,17},{2,34}... | collective-permute-start | bytes 786440 | tf_op jit(solution)/shard_map/ppermute | solution.py:294
  39.1 9.9 %collective-permute-start.9 = (bf16[1024,128]{1,0:T(8,128)(2,1)S(1)}, bf16[1024,128]{1,0:T(8,128)(2,1)S(1)}, u32[]{:S(2)}, u32[]{:S(2)}) collective-permute-start(bf16[1024,128]{1,0:T(8,128)(2,1)S(1)} %bitcast.19), channel_id=1, source_target_pairs={{0,16},{16,0},{32,48},{48,32},{1,17},{17,1},{33,49},{49,33},{2,18}... | collective-permute-start | bytes 786440 | tf_op jit(solution)/shard_map/ppermute | solution.py:294
  41.1 26.5 %all-to-all-start.1 = ((bf16[16,32,1024]{2,1,0:T(8,128)(2,1)}), bf16[16,32,1024]{2,1,0:T(8,128)(2,1)S(1)}, u32[]{:S(2)}, u32[]{:S(2)}) async-start(bf16[16,32,1024]{2,1,0:T(8,128)(2,1)} %meet.1), calls=%async_computation.1 | async-start | bytes 2097152 | tf_op jit(solution)/shard_map/all_to_all | solution.py:327
  48.3 0.7 copy-start.7
  49.1 0.7 copy-start.9
  49.8 24.1 %collective-permute-start.13 = (bf16[128,2048]{1,0:T(8,128)(2,1)S(1)}, bf16[128,2048]{1,0:T(8,128)(2,1)S(1)}, u32[]{:S(2)}, u32[]{:S(2)}) collective-permute-start(bf16[128,2048]{1,0:T(8,128)(2,1)S(1)} %pad_maximum_fusion.refs_4_), channel_id=1, source_target_pairs={{1,2},{2,1},{3,4},{4,3},{5,6},{6,5},{7,8},{8,7},{9,10},{10,9},{11,... | collective-permute-start | bytes 1572872 | tf_op jit(solution)/shard_map/ppermute | solution.py:331
  50.5 23.5 %collective-permute-start.12 = (bf16[128,2048]{1,0:T(8,128)(2,1)S(1)}, bf16[128,2048]{1,0:T(8,128)(2,1)}, u32[]{:S(2)}, u32[]{:S(2)}) collective-permute-start(bf16[128,2048]{1,0:T(8,128)(2,1)S(1)} %pad_maximum_fusion.refs_4_), channel_id=1, source_target_pairs={{0,1},{1,0},{2,3},{3,2},{4,5},{5,4},{6,7},{7,6},{8,9},{9,8},{10,11... | collective-permute-start | bytes 1572872 | tf_op jit(solution)/shard_map/ppermute | solution.py:330
  55.3 0.9 %copy-start.8 = (bf16[1024,128]{1,0:T(8,128)(2,1)S(1)}, bf16[1024,128]{1,0:T(8,128)(2,1)}, u32[]{:S(2)}) copy-start(bf16[1024,128]{1,0:T(8,128)(2,1)} %copy-done.7) | copy-start | bytes 786436
  56.3 0.9 %copy-start.10 = (bf16[1024,128]{1,0:T(8,128)(2,1)S(1)}, bf16[1024,128]{1,0:T(8,128)(2,1)}, u32[]{:S(2)}) copy-start(bf16[1024,128]{1,0:T(8,128)(2,1)} %copy-done.9) | copy-start | bytes 786436
  67.6 6.3 %copy-start = (bf16[1,128,1024]{2,1,0:T(8,128)(2,1)S(1)}, bf16[1,128,1024]{2,1,0:T(8,128)(2,1)}, u32[]{:S(2)}) copy-start(bf16[1,128,1024]{2,1,0:T(8,128)(2,1)} %param.11) | copy-start | bytes 786436
  67.6 6.3 %copy-start.1 = (bf16[1,128,1024]{2,1,0:T(8,128)(2,1)S(1)}, bf16[1,128,1024]{2,1,0:T(8,128)(2,1)}, u32[]{:S(2)}) copy-start(bf16[1,128,1024]{2,1,0:T(8,128)(2,1)} %param.12) | copy-start | bytes 786436
  67.6 15.0 %all-to-all-start.2 = ((bf16[16,64,128]{2,1,0:T(8,128)(2,1)}), bf16[16,64,128]{2,1,0:T(8,128)(2,1)S(1)}, u32[]{:S(2)}, u32[]{:S(2)}) async-start(bf16[16,64,128]{2,1,0:T(8,128)(2,1)} %heavy.1), calls=%async_computation.2 | async-start | bytes 524288 | tf_op jit(solution)/shard_map/all_to_all | solution.py:336
  73.9 1.0 %copy-start.6 = (bf16[1,128,1024]{2,1,0:T(8,128)(2,1)S(1)}, bf16[1,128,1024]{2,1,0:T(8,128)(2,1)}, u32[]{:S(2)}) copy-start(bf16[1,128,1024]{2,1,0:T(8,128)(2,1)} %param.10) | copy-start | bytes 786436
  77.9 4.7 %copy-start.4 = (s32[1,64]{1,0:T(1,128)S(1)}, s32[1,64]{1,0:T(1,128)}, u32[]{:S(2)}) copy-start(s32[1,64]{1,0:T(1,128)} %ids.3) | copy-start | bytes 772

commit v9 on v8

--- a/solution.py
+++ b/solution.py
@@ -13,14 +13,14 @@
 SCALE = HEAD**-0.5
 LOG2E = 1.4426950408889634
 TOKENS = ("coarse", "fine")
-VMEM = 48 * 1024 * 1024
+MIB = 1024 * 1024
 
 f32 = jnp.float32
 bf16 = jnp.bfloat16
 
 
-def params(**kw):
-    return pltpu.CompilerParams(vmem_limit_bytes=VMEM, **kw)
+def params(mib):
+    return pltpu.CompilerParams(vmem_limit_bytes=mib * MIB)
 
 
 def lane_ids(shape):
@@ -63,7 +63,7 @@
         out_shape=jax.ShapeDtypeStruct((heads, BLOCK + HALF, LANES), bf16),
         scratch_shapes=[pltpu.VMEM(x.shape, bf16) for x in (q, k, v)]
         + [pltpu.SemaphoreType.DMA((3,))],
-        compiler_params=params(),
+        compiler_params=params(8),
         name="pack",
     )(*(pltpu.with_memory_space_constraint(x, pltpu.HBM) for x in (q, k, v)))
 
@@ -79,7 +79,7 @@
         pick_kernel,
         out_shape=jax.ShapeDtypeStruct((KGRP, BLOCK, LANES), bf16),
         in_specs=[pl.BlockSpec(memory_space=pltpu.SMEM), pl.BlockSpec(memory_space=pltpu.VMEM)],
-        compiler_params=params(),
+        compiler_params=params(4),
         name="pick",
     )(ids, kv)
 
@@ -88,26 +88,35 @@
     return jnp.where(lane_ids(kv.shape) < HEAD, jnp.ones_like(kv), kv)
 
 
-def summed(q, keys, values):
+def summed(q, keys):
     peak = total = None
-    for k, v in zip(keys, values):
+    for k in keys:
         s = nt(q, k)
         top = s.max(axis=1, keepdims=True)
         top = top if peak is None else jnp.maximum(peak, top)
-        o = nn(jnp.exp2((s - top) * (SCALE * LOG2E)).astype(bf16), v)
+        o = nn(jnp.exp2((s - top) * (SCALE * LOG2E)).astype(bf16), with_ones(k))
         total = o if peak is None else total * jnp.exp2((peak - top) * (SCALE * LOG2E)) + o
         peak = top
     return total, peak
 
 
-def heavy_kernel(q, kv0, kv1, kv2, kv3, out):
+def heavy_kernel(q, kv0, kv1, kv2, kv3, out, others, sem):
+    copies = [pltpu.make_async_copy(kv, others.at[n], sem.at[n]) for n, kv in enumerate((kv1, kv2, kv3))]
+    for copy in copies:
+        copy.start()
+
+    def arriving():
+        yield kv0[...]
+        for n, copy in enumerate(copies):
+            copy.wait()
+            yield others[n]
+
     rows = q.shape[0] * HALF
     both = q[:, BLOCK:].reshape(rows, LANES)
     zero = jnp.zeros((rows, HEAD), bf16)
-    keys = [kv[...] for kv in (kv0, kv1, kv2, kv3)]
-    vals = [with_ones(k) for k in keys]
-    a, _ = summed(jnp.concatenate([both[:, :HEAD], zero], axis=1), keys, vals)
-    b, _ = summed(jnp.concatenate([both[:, HEAD:], zero], axis=1), keys, vals)
+    a, _ = summed(jnp.concatenate([both[:, :HEAD], zero], axis=1), arriving())
+    keys = [kv0[...]] + [others[n] for n in range(len(copies))]
+    b, _ = summed(jnp.concatenate([both[:, HEAD:], zero], axis=1), keys)
     low = lane_ids(a.shape) < HEAD
     top = jnp.where(low, pltpu.roll(a, HEAD, 1), b)
     sums = jnp.where(low, a, pltpu.roll(b, HEAD, 1))
@@ -116,18 +125,31 @@
 
 def heavy_attend(q_kv, kvs):
     blocks = q_kv.shape[0]
+    vmem = pl.BlockSpec(memory_space=pltpu.VMEM)
+    hbm = pl.BlockSpec(memory_space=pl.ANY)
+    others = kvs[1:]
     return pl.pallas_call(
         heavy_kernel,
+        in_specs=[vmem] * 2 + [hbm] * len(others),
         out_shape=jax.ShapeDtypeStruct((blocks, HALF, LANES), bf16),
-        compiler_params=params(),
+        scratch_shapes=[
+            pltpu.VMEM((len(others),) + kvs[0].shape, bf16),
+            pltpu.SemaphoreType.DMA((len(others),)),
+        ],
+        compiler_params=params(28),
         cost_estimate=pl.CostEstimate(flops=10_000_000_000, transcendentals=8_000_000, bytes_accessed=2_000_000),
         name="heavy",
-    )(q_kv, *kvs)
+    )(q_kv, kvs[0], *others)
 
 
 def light_kernel(q, k, v, even, odd, rows_in, out, rows_out, sem):
-    copy = pltpu.make_async_copy(rows_in, rows_out, sem)
-    copy.start()
+    count = rows_in.shape[0] // 4
+    copies = [
+        pltpu.make_async_copy(rows_in.at[pl.ds(n * count, count)], rows_out.at[pl.ds(n * count, count)], sem.at[n])
+        for n in range(4)
+    ]
+    for copy in copies:
+        copy.start()
     here = lax.axis_index(TOKENS)
     last = lax.axis_size(TOKENS) - 1
     rows, width = q.shape
@@ -152,7 +174,8 @@
         o = nn(po.astype(bf16), v[:, c]) + nn(pe.astype(bf16), even[:, cv]) + nn(pd.astype(bf16), odd[:, cv])
         o = o / total
         out[:, c] = jnp.where(low, o[:rows], o[rows:])
-    copy.wait()
+    for copy in copies:
+        copy.wait()
 
 
 def light_attend(q, k, v, even, odd, decoded):
@@ -163,8 +186,8 @@
         in_specs=[vmem] * 5 + [hbm],
         out_specs=(vmem, hbm),
         out_shape=(jax.ShapeDtypeStruct(q.shape, f32), jax.ShapeDtypeStruct(decoded.shape, bf16)),
-        scratch_shapes=[pltpu.SemaphoreType.DMA(())],
-        compiler_params=params(),
+        scratch_shapes=[pltpu.SemaphoreType.DMA((4,))],
+        compiler_params=params(12),
         cost_estimate=pl.CostEstimate(flops=3_000_000_000, transcendentals=800_000, bytes_accessed=2_000_000),
         name="light",
     )(q, k, v, even, odd, decoded)
@@ -191,7 +214,7 @@
         join_kernel,
         in_specs=[pl.BlockSpec(memory_space=pltpu.SMEM), vmem, vmem],
         out_shape=jax.ShapeDtypeStruct(light.shape, bf16),
-        compiler_params=params(),
+        compiler_params=params(6),
         name="join",
     )(ids, light, heavy)
 
@@ -211,8 +234,7 @@
         axis=0,
     )
     keys = [e[...] for e in (e0, e1, e2, e3)]
-    vals = [with_ones(k) for k in keys]
-    total, peak = summed(stack, keys, vals)
+    total, peak = summed(stack, keys)
     lane = lane_ids(total.shape)
     level = peak * SCALE + jnp.log(total)
     hi = level.astype(bf16).astype(f32)
@@ -231,7 +253,7 @@
         in_specs=[pl.BlockSpec(memory_space=pltpu.HBM)] + [vmem] * len(enc),
         out_shape=jax.ShapeDtypeStruct((rows * (width // HEAD), LANES), bf16),
         scratch_shapes=[pltpu.VMEM((rows, width), bf16), pltpu.SemaphoreType.DMA(())],
-        compiler_params=params(),
+        compiler_params=params(16),
         cost_estimate=pl.CostEstimate(flops=30_000_000_000, transcendentals=1_000_000, bytes_accessed=1_000_000),
         name="decode",
     )(q, *enc)
@@ -260,7 +282,8 @@
     return pl.pallas_call(
         meet_kernel,
         out_shape=jax.ShapeDtypeStruct((copies, rows, width), bf16),
-        compiler_params=params(),
+        compiler_params=params(8),
+        cost_estimate=pl.CostEstimate(flops=30_000_000_000, transcendentals=0, bytes_accessed=2_000_000),
         name="meet",
     )(*parts)
 
@@ -279,7 +302,7 @@
         stack_kernel,
         in_specs=specs + [pl.BlockSpec(memory_space=pl.ANY)] * len(others),
         out_shape=jax.ShapeDtypeStruct((len(parts) * first.shape[0],) + first.shape[1:], first.dtype),
-        compiler_params=params(),
+        compiler_params=params(4),
         name="stack",
     )(*parts, *others)
 
@@ -314,24 +337,24 @@
     def square(row):
         return [row] + around(row, "fine", side, n_fine // side)
 
-    enc = square(stack(rows_of(enc_kv[0]), light_kv))
     chunks = pack(q_heavy[0], k_heavy[0], v_heavy[0])
+    enc = square(stack(rows_of(enc_kv[0]), chunks))
     group = lax.all_to_all(after_all(chunks, enc[0]), "fine", 0, 0, tiled=True)
 
     dec_rows = dec_queries.shape[1] // n_fine
     part = decode(dec_queries[0], enc, dec_rows)
-    share = meet([part] + around(part, "coarse"), n_fine, dec_rows, width)
-
-    own = pick(key_ids, after_all(group, share)).reshape(KGRP * BLOCK, LANES)
+
+    parts = around(part, "coarse")
+    own = pick(key_ids, after_all(group, part, light_kv)).reshape(KGRP * BLOCK, LANES)
     routed = [own] + around(own, "coarse")
-    decoded = lax.all_to_all(after_all(share, own), "fine", 0, 0, tiled=True)
-
-    light_kv = after_all(light_kv, routed)
+    share = meet([after_all(part, own)] + parts, n_fine, dec_rows, width)
+    decoded = lax.all_to_all(share, "fine", 0, 0, tiled=True)
+
+    light_kv = after_all(light_kv, share)
     even = lax.ppermute(light_kv, TOKENS, [(i, i ^ 1) for i in range(n_seq)])
     odd = lax.ppermute(light_kv, TOKENS, [(i, (i - 1 ^ 1) + 1) for i in range(1, n_seq - 1)])
 
     heavy = heavy_attend(group, routed)
-    q_light = after_all(q_light, heavy)
     heavy, decoded = lax.optimization_barrier((heavy, decoded))
     heavy = lax.all_to_all(heavy, "fine", 0, 0, tiled=True)
     light, decoded = light_attend(

time: 84.6 us -> 80.5 us (0.952)
  local copies, waits for them, and re-layouts: 4.29 us -> 0.04 us
  Pallas kernels: 21.5 us -> 23.2 us
    ppermute x12, waiting for transfers between devices: 8.84 us -> 2.1 us  [around(): return [lax.ppermute(value, axis, pairs(d)) for d in range(1, ring)]]
    unnamed x22 -> x14, local copies, waits for them, and re-layouts: 4.29 us -> 0.04 us
    all_to_all x1, waiting for transfers between devices: 0.01 us -> 4.13 us  [local(): group = lax.all_to_all(after_all(chunks, enc[0]), 'fine', 0, 0, tiled=True)]
    all_to_all x1, starting transfers between devices: 7.22 us -> 3.66 us  [local(): decoded = lax.all_to_all(share, 'fine', 0, 0, tiled=True)]
    all_to_all x1, starting transfers between devices: 6.3 us -> 8.6 us  [local(): heavy = lax.all_to_all(heavy, 'fine', 0, 0, tiled=True)]
    pallas_call x1, Pallas kernels: 10.4 us -> 12.1 us  [heavy_attend(): pl.pallas_call(heavy_kernel, in_specs=[vmem] * 2 + [hbm] * len(others), o...]
    all_to_all x1, waiting for transfers between devices: 0.01 us -> 1.05 us  [local(): decoded = lax.all_to_all(share, 'fine', 0, 0, tiled=True)]
    all_to_all x1, waiting for transfers between devices: 4.7 us -> 5.64 us  [local(): heavy = lax.all_to_all(heavy, 'fine', 0, 0, tiled=True)]
  transfers between devices with their start and end apart: 17 -> 17, of which waited for: 5 -> 4; matrix products, arithmetic and copies ran while one was open for 1% -> 1% of each run, Pallas kernels for 23% -> 27%
where the time goes in v9:
time: 80.5 us; the launch traced here: 80.1 us
  starting transfers between devices  42.2 us (52%)
  Pallas kernels  23.2 us (29%)
  waiting for transfers between devices  12.9 us (16%)
  other arithmetic  0.85 us (1%)
  between operations  0.83 us (1%)
    ppermute x12, starting transfers between devices, around(): return [lax.ppermute(value, axis, pairs(d)) for d in range(1, ring)]  18.5 us
    pallas_call x1, Pallas kernels, heavy_attend(): pl.pallas_call(heavy_kernel, in_specs=[vmem] * 2 + [hbm] * len(others), o...  12.1 us
    all_to_all x1, starting transfers between devices, local(): heavy = lax.all_to_all(heavy, 'fine', 0, 0, tiled=True)  8.6 us
    all_to_all x1, starting transfers between devices, local(): group = lax.all_to_all(after_all(chunks, enc[0]), 'fine', 0, 0, tiled=True)  6.03 us
    all_to_all x1, waiting for transfers between devices, local(): heavy = lax.all_to_all(heavy, 'fine', 0, 0, tiled=True)  5.64 us
    ppermute x1, starting transfers between devices, local(): even = lax.ppermute(light_kv, TOKENS, [(i, i ^ 1) for i in range(n_seq)])  4.74 us
    all_to_all x1, waiting for transfers between devices, local(): group = lax.all_to_all(after_all(chunks, enc[0]), 'fine', 0, 0, tiled=True)  4.13 us
    all_to_all x1, starting transfers between devices, local(): decoded = lax.all_to_all(share, 'fine', 0, 0, tiled=True)  3.66 us
  transfers between devices with their start and end apart: 17, of which 4 were waited for; matrix products, arithmetic and copies ran while one was open for 1% of the time, Pallas kernels for 27%

profile of v9, /device:TPU:0, one launch (start us, length us, event | category | flops | bytes accessed | tf_op | source)
XLA Modules:
  0.0 80.1 jit_solution(3337412050142437627)
XLA Ops:
  0.6 2.9 %collective-permute-start.2 = (bf16[128,128]{1,0:T(8,128)(2,1)}, bf16[128,128]{1,0:T(8,128)(2,1)S(1)}, u32[]{:S(2)}, u32[]{:S(2)}) collective-permute-start(bf16[128,128]{1,0:T(8,128)(2,1)} %bitcast.21), channel_id=1, source_target_pairs={{0,3},{1,2},{2,1},{3,0},{4,7},{5,6},{6,5},{7,4},{8,11},{9,10},{10,... | collective-permute-start | bytes 98312 | tf_op jit(solution)/shard_map/ppermute | solution.py:317
  3.6 0.8 collective-permute-start.1
  4.4 0.5 collective-permute-start
  4.8 2.3 %pack.1.refs_4_ = bf16[16,192,128]{2,1,0:T(8,128)(2,1)} custom-call(bf16[128,1024]{1,0:T(8,128)(2,1)} %bitcast.27, bf16[128,1024]{1,0:T(8,128)(2,1)} %bitcast.28, bf16[128,1024]{1,0:T(8,128)(2,1)} %bitcast.29), custom_call_target="tpu_custom_call" | custom-call | tf_op jit(solution)/shard_map/pack/pallas_call | solution.py:60
  7.1 2.1 %collective-permute-done.1.refs_2_ = bf16[128,128]{1,0:T(8,128)(2,1)S(1)} collective-permute-done((bf16[128,128]{1,0:T(8,128)(2,1)}, bf16[128,128]{1,0:T(8,128)(2,1)S(1)}, u32[]{:S(2)}, u32[]{:S(2)}) %collective-permute-start.1) | collective-permute-done | bytes 32800 | tf_op jit(solution)/shard_map/ppermute | solution.py:317
  9.2 0.0 copy-start.5
  9.2 3.1 %collective-permute-start.5 = (bf16[512,128]{1,0:T(8,128)(2,1)S(1)}, bf16[512,128]{1,0:T(8,128)(2,1)S(1)}, u32[]{:S(2)}, u32[]{:S(2)}) collective-permute-start(bf16[512,128]{1,0:T(8,128)(2,1)S(1)} %stack.1.e0), channel_id=1, source_target_pairs={{0,12},{1,13},{2,14},{3,15},{4,8},{5,9},{6,10},{7,11},{8,4},{9,5},... | collective-permute-start | bytes 393224 | tf_op jit(solution)/shard_map/ppermute | solution.py:317
  12.3 0.6 collective-permute-start.4
  12.9 0.5 collective-permute-start.3
  13.4 6.0 %all-to-all-start = ((bf16[16,192,128]{2,1,0:T(8,128)(2,1)}), bf16[16,192,128]{2,1,0:T(8,128)(2,1)S(1)}, u32[]{:S(2)}, u32[]{:S(2)}) async-start(bf16[16,192,128]{2,1,0:T(8,128)(2,1)} %pack.1.refs_4_), calls=%async_computation | async-start | bytes 1572864 | tf_op jit(solution)/shard_map/all_to_all | solution.py:342
  19.5 0.0 copy-start
  19.5 0.0 copy-start.1
  19.5 1.8 %decode.1.a = bf16[512,128]{1,0:T(8,128)(2,1)S(1)} custom-call(bf16[512,1024]{1,0:T(8,128)(2,1)S(1)} %bitcast.25, bf16[512,128]{1,0:T(8,128)(2,1)S(1)} %stack.1.e0, bf16[512,128]{1,0:T(8,128)(2,1)S(1)} %collective-permute-done.3.e1, bf16[512,128]{1,0:T(8,128)(2,1)S(1)} %collective-permute-done.4.e2, bf16[512,128]{1,0:T(8,128)(2,1)S(1)} %collective-permute-done.5.e3), custom_call_target="tpu_custom_call" | custom-call | flops 30000001024 | bytes 1000000 | tf_op jit(solution)/shard_map/decode/pallas_call | solution.py:251
  21.3 4.1 %collective-permute-start.8 = (bf16[512,128]{1,0:T(8,128)(2,1)S(1)}, bf16[512,128]{1,0:T(8,128)(2,1)S(1)}, u32[]{:S(2)}, u32[]{:S(2)}) collective-permute-start(bf16[512,128]{1,0:T(8,128)(2,1)S(1)} %decode.1.a), channel_id=1, source_target_pairs={{0,48},{16,32},{32,16},{48,0},{1,49},{17,33},{33,17},{49,1},{2,50}... | collective-permute-start | bytes 393224 | tf_op jit(solution)/shard_map/ppermute | solution.py:317
  25.4 0.9 %collective-permute-start.6 = (bf16[512,128]{1,0:T(8,128)(2,1)S(1)}, bf16[512,128]{1,0:T(8,128)(2,1)S(1)}, u32[]{:S(2)}, u32[]{:S(2)}) collective-permute-start(bf16[512,128]{1,0:T(8,128)(2,1)S(1)} %decode.1.a), channel_id=1, source_target_pairs={{0,16},{16,0},{32,48},{48,32},{1,17},{17,1},{33,49},{49,33},{2,18}... | collective-permute-start | bytes 393224 | tf_op jit(solution)/shard_map/ppermute | solution.py:317
  26.4 0.8 %pad_maximum_fusion = bf16[128,2048]{1,0:T(8,128)(2,1)} fusion(bf16[128,1024]{1,0:T(8,128)(2,1)S(1)} %bitcast.15, bf16[128,1024]{1,0:T(8,128)(2,1)S(1)} %bitcast.13), kind=kLoop, calls=%fused_computation | loop fusion | flops 1048576 | bytes 1048576 | tf_op jit(solution)/shard_map/concatenate | solution.py:332
  27.2 4.1 %all-to-all-done.kv.q = bf16[16,192,128]{2,1,0:T(8,128)(2,1)S(1)} async-done(((bf16[16,192,128]{2,1,0:T(8,128)(2,1)}), bf16[16,192,128]{2,1,0:T(8,128)(2,1)S(1)}, u32[]{:S(2)}, u32[]{:S(2)}) %all-to-all-start) | async-done | bytes 786464 | tf_op jit(solution)/shard_map/all_to_all | solution.py:342
  31.4 0.6 pick.1
  31.9 4.1 %collective-permute-start.13 = (bf16[1024,128]{1,0:T(8,128)(2,1)S(1)}, bf16[1024,128]{1,0:T(8,128)(2,1)S(1)}, u32[]{:S(2)}, u32[]{:S(2)}) collective-permute-start(bf16[1024,128]{1,0:T(8,128)(2,1)S(1)} %bitcast.17), channel_id=1, source_target_pairs={{0,48},{16,32},{32,16},{48,0},{1,49},{17,33},{33,17},{49,1},{2,50}... | collective-permute-start | bytes 786440 | tf_op jit(solution)/shard_map/ppermute | solution.py:317
  36.1 0.9 %collective-permute-start.11 = (bf16[1024,128]{1,0:T(8,128)(2,1)S(1)}, bf16[1024,128]{1,0:T(8,128)(2,1)}, u32[]{:S(2)}, u32[]{:S(2)}) collective-permute-start(bf16[1024,128]{1,0:T(8,128)(2,1)S(1)} %bitcast.19), channel_id=1, source_target_pairs={{0,16},{16,0},{32,48},{48,32},{1,17},{17,1},{33,49},{49,33},{2,18}... | collective-permute-start | bytes 786440 | tf_op jit(solution)/shard_map/ppermute | solution.py:317
  37.0 2.0 %meet.1 = bf16[16,32,1024]{2,1,0:T(8,128)(2,1)} custom-call(bf16[512,128]{1,0:T(8,128)(2,1)S(1)} %decode.1.a, bf16[512,128]{1,0:T(8,128)(2,1)S(1)} %collective-permute-done.6.b, bf16[512,128]{1,0:T(8,128)(2,1)S(1)} %collective-permute-done.7.c, bf16[512,128]{1,0:T(8,128)(2,1)S(1)} %collective-permute-done.8.d), custom_call_target="tpu_custom_call" | custom-call | flops 30000001024 | bytes 2000000 | tf_op jit(solution)/shard_map/meet/pallas_call | solution.py:282
  39.0 3.7 %all-to-all-start.1 = ((bf16[16,32,1024]{2,1,0:T(8,128)(2,1)}), bf16[16,32,1024]{2,1,0:T(8,128)(2,1)S(1)}, u32[]{:S(2)}, u32[]{:S(2)}) async-start(bf16[16,32,1024]{2,1,0:T(8,128)(2,1)} %meet.1), calls=%async_computation.1 | async-start | bytes 2097152 | tf_op jit(solution)/shard_map/all_to_all | solution.py:351
  42.7 0.7 collective-permute-start.10
  43.4 4.7 %collective-permute-start.9 = (bf16[128,2048]{1,0:T(8,128)(2,1)}, bf16[128,2048]{1,0:T(8,128)(2,1)}, u32[]{:S(2)}, u32[]{:S(2)}) collective-permute-start(bf16[128,2048]{1,0:T(8,128)(2,1)} %pad_maximum_fusion), channel_id=1, source_target_pairs={{0,1},{1,0},{2,3},{3,2},{4,5},{5,4},{6,7},{7,6},{8,9},{9,8},{10,11... | collective-permute-start | bytes 1572872 | tf_op jit(solution)/shard_map/ppermute | solution.py:354
  48.1 12.1 %heavy.1 = bf16[16,64,128]{2,1,0:T(8,128)(2,1)} custom-call(bf16[16,192,128]{2,1,0:T(8,128)(2,1)S(1)} %all-to-all-done.kv.q, bf16[1024,128]{1,0:T(8,128)(2,1)S(1)} %bitcast.20, bf16[1024,128]{1,0:T(8,128)(2,1)} %collective-permute-done.11.kv1, bf16[1024,128]{1,0:T(8,128)(2,1)} %collective-permute-done.12.kv2, bf16[1024,128]{1,0:T(8,128)(2,1)S(1)} %collective-permute-done.13.kv3), custom_call_target="tpu_custom_call" | custom-call | flops 10000000000 | bytes 2000000 | tf_op jit(solution)/shard_map/heavy/pallas_call | solution.py:131
  60.2 0.0 copy-start.6
  60.2 1.1 %all-to-all-done.1 = bf16[16,32,1024]{2,1,0:T(8,128)(2,1)S(1)} async-done(((bf16[16,32,1024]{2,1,0:T(8,128)(2,1)}), bf16[16,32,1024]{2,1,0:T(8,128)(2,1)S(1)}, u32[]{:S(2)}, u32[]{:S(2)}) %all-to-all-start.1) | async-done | bytes 1048608 | tf_op jit(solution)/shard_map/all_to_all | solution.py:351
  61.3 8.6 %all-to-all-start.2 = ((bf16[16,64,128]{2,1,0:T(8,128)(2,1)}), bf16[16,64,128]{2,1,0:T(8,128)(2,1)S(1)}, u32[]{:S(2)}, u32[]{:S(2)}) async-start(bf16[16,64,128]{2,1,0:T(8,128)(2,1)} %heavy.1), calls=%async_computation.2 | async-start | bytes 524288 | tf_op jit(solution)/shard_map/all_to_all | solution.py:359
  69.9 3.0 %light.1 = (f32[128,1024]{1,0:T(8,128)S(1)}, bf16[512,1024]{1,0:T(8,128)(2,1)}) custom-call(bf16[128,1024]{1,0:T(8,128)(2,1)S(1)} %bitcast.26, bf16[128,1024]{1,0:T(8,128)(2,1)S(1)} %bitcast.14, bf16[128,1024]{1,0:T(8,128)(2,1)S(1)} %bitcast.16, bf16[128,2048]{1,0:T(8,128)(2,1)} %collective-permute-done.9.even, ...), custom_call_target="tpu_custom_call" | custom-call | flops 3000000000 | bytes 2000000 | tf_op jit(solution)/shard_map/light/pallas_call | solution.py:184
  72.9 0.0 copy-start.4
  73.0 5.6 %all-to-all-done.2.heavy = bf16[16,64,128]{2,1,0:T(8,128)(2,1)S(1)} async-done(((bf16[16,64,128]{2,1,0:T(8,128)(2,1)}), bf16[16,64,128]{2,1,0:T(8,128)(2,1)S(1)}, u32[]{:S(2)}, u32[]{:S(2)}) %all-to-all-start.2) | async-done | bytes 262176 | tf_op jit(solution)/shard_map/all_to_all | solution.py:359
  78.6 1.5 %join.1 = bf16[128,1024]{1,0:T(8,128)(2,1)} custom-call(s32[1,64]{1,0:T(1,128)S(1)} %copy-done.4, f32[128,1024]{1,0:T(8,128)S(1)} %get-tuple-element.15.light, bf16[16,64,128]{2,1,0:T(8,128)(2,1)S(1)} %all-to-all-done.2.heavy), custom_call_target="tpu_custom_call" | custom-call | tf_op jit(solution)/shard_map/join/pallas_call | solution.py:213
  (25 shorter events, 0.1 us)
Async XLA Ops:
  0.6 6.5 %collective-permute-start.2 = (bf16[128,128]{1,0:T(8,128)(2,1)}, bf16[128,128]{1,0:T(8,128)(2,1)S(1)}, u32[]{:S(2)}, u32[]{:S(2)}) collective-permute-start(bf16[128,128]{1,0:T(8,128)(2,1)} %bitcast.21), channel_id=1, source_target_pairs={{0,3},{1,2},{2,1},{3,0},{4,7},{5,6},{6,5},{7,4},{8,11},{9,10},{10,... | collective-permute-start | bytes 98312 | tf_op jit(solution)/shard_map/ppermute | solution.py:317
  3.6 5.6 %collective-permute-start.1 = (bf16[128,128]{1,0:T(8,128)(2,1)}, bf16[128,128]{1,0:T(8,128)(2,1)S(1)}, u32[]{:S(2)}, u32[]{:S(2)}) collective-permute-start(bf16[128,128]{1,0:T(8,128)(2,1)} %bitcast.22), channel_id=1, source_target_pairs={{0,2},{1,3},{2,0},{3,1},{4,6},{5,7},{6,4},{7,5},{8,10},{9,11},{10,... | collective-permute-start | bytes 98312 | tf_op jit(solution)/shard_map/ppermute | solution.py:317
  4.4 4.8 %collective-permute-start = (bf16[128,128]{1,0:T(8,128)(2,1)}, bf16[128,128]{1,0:T(8,128)(2,1)S(1)}, u32[]{:S(2)}, u32[]{:S(2)}) collective-permute-start(bf16[128,128]{1,0:T(8,128)(2,1)} %bitcast.23), channel_id=1, source_target_pairs={{0,1},{1,0},{2,3},{3,2},{4,5},{5,4},{6,7},{7,6},{8,9},{9,8},{10,11... | collective-permute-start | bytes 98312 | tf_op jit(solution)/shard_map/ppermute | solution.py:317
  4.8 4.4 %copy-start.2 = (bf16[1,128,128]{2,1,0:T(8,128)(2,1)S(1)}, bf16[1,128,128]{2,1,0:T(8,128)(2,1)}, u32[]{:S(2)}) copy-start(bf16[1,128,128]{2,1,0:T(8,128)(2,1)} %param.16) | copy-start | bytes 98308
  9.2 10.3 %copy-start.5 = (bf16[1,512,1024]{2,1,0:T(8,128)(2,1)S(1)}, bf16[1,512,1024]{2,1,0:T(8,128)(2,1)}, u32[]{:S(2)}) copy-start(bf16[1,512,1024]{2,1,0:T(8,128)(2,1)} %param.17) | copy-start | bytes 3145732
  9.2 10.2 %collective-permute-start.5 = (bf16[512,128]{1,0:T(8,128)(2,1)S(1)}, bf16[512,128]{1,0:T(8,128)(2,1)S(1)}, u32[]{:S(2)}, u32[]{:S(2)}) collective-permute-start(bf16[512,128]{1,0:T(8,128)(2,1)S(1)} %stack.1.e0), channel_id=1, source_target_pairs={{0,12},{1,13},{2,14},{3,15},{4,8},{5,9},{6,10},{7,11},{8,4},{9,5},... | collective-permute-start | bytes 393224 | tf_op jit(solution)/shard_map/ppermute | solution.py:317
  12.3 7.1 %collective-permute-start.4 = (bf16[512,128]{1,0:T(8,128)(2,1)S(1)}, bf16[512,128]{1,0:T(8,128)(2,1)S(1)}, u32[]{:S(2)}, u32[]{:S(2)}) collective-permute-start(bf16[512,128]{1,0:T(8,128)(2,1)S(1)} %stack.1.e0), channel_id=1, source_target_pairs={{0,8},{1,9},{2,10},{3,11},{4,12},{5,13},{6,14},{7,15},{8,0},{9,1},... | collective-permute-start | bytes 393224 | tf_op jit(solution)/shard_map/ppermute | solution.py:317
  12.9 6.5 %collective-permute-start.3 = (bf16[512,128]{1,0:T(8,128)(2,1)S(1)}, bf16[512,128]{1,0:T(8,128)(2,1)S(1)}, u32[]{:S(2)}, u32[]{:S(2)}) collective-permute-start(bf16[512,128]{1,0:T(8,128)(2,1)S(1)} %stack.1.e0), channel_id=1, source_target_pairs={{0,4},{1,5},{2,6},{3,7},{4,0},{5,1},{6,2},{7,3},{8,12},{9,13},{10,... | collective-permute-start | bytes 393224 | tf_op jit(solution)/shard_map/ppermute | solution.py:317
  13.4 18.0 %all-to-all-start = ((bf16[16,192,128]{2,1,0:T(8,128)(2,1)}), bf16[16,192,128]{2,1,0:T(8,128)(2,1)S(1)}, u32[]{:S(2)}, u32[]{:S(2)}) async-start(bf16[16,192,128]{2,1,0:T(8,128)(2,1)} %pack.1.refs_4_), calls=%async_computation | async-start | bytes 1572864 | tf_op jit(solution)/shard_map/all_to_all | solution.py:342
  19.5 6.9 %copy-start = (bf16[1,128,1024]{2,1,0:T(8,128)(2,1)S(1)}, bf16[1,128,1024]{2,1,0:T(8,128)(2,1)}, u32[]{:S(2)}) copy-start(bf16[1,128,1024]{2,1,0:T(8,128)(2,1)} %param.11) | copy-start | bytes 786436
  19.5 6.9 %copy-start.1 = (bf16[1,128,1024]{2,1,0:T(8,128)(2,1)S(1)}, bf16[1,128,1024]{2,1,0:T(8,128)(2,1)}, u32[]{:S(2)}) copy-start(bf16[1,128,1024]{2,1,0:T(8,128)(2,1)} %param.12) | copy-start | bytes 786436
  21.3 14.8 %collective-permute-start.8 = (bf16[512,128]{1,0:T(8,128)(2,1)S(1)}, bf16[512,128]{1,0:T(8,128)(2,1)S(1)}, u32[]{:S(2)}, u32[]{:S(2)}) collective-permute-start(bf16[512,128]{1,0:T(8,128)(2,1)S(1)} %decode.1.a), channel_id=1, source_target_pairs={{0,48},{16,32},{32,16},{48,0},{1,49},{17,33},{33,17},{49,1},{2,50}... | collective-permute-start | bytes 393224 | tf_op jit(solution)/shard_map/ppermute | solution.py:317
  25.4 11.6 %collective-permute-start.7 = (bf16[512,128]{1,0:T(8,128)(2,1)S(1)}, bf16[512,128]{1,0:T(8,128)(2,1)S(1)}, u32[]{:S(2)}, u32[]{:S(2)}) collective-permute-start(bf16[512,128]{1,0:T(8,128)(2,1)S(1)} %decode.1.a), channel_id=1, source_target_pairs={{0,32},{16,48},{32,0},{48,16},{1,33},{17,49},{33,1},{49,17},{2,34}... | collective-permute-start | bytes 393224 | tf_op jit(solution)/shard_map/ppermute | solution.py:317
  25.4 11.6 %collective-permute-start.6 = (bf16[512,128]{1,0:T(8,128)(2,1)S(1)}, bf16[512,128]{1,0:T(8,128)(2,1)S(1)}, u32[]{:S(2)}, u32[]{:S(2)}) collective-permute-start(bf16[512,128]{1,0:T(8,128)(2,1)S(1)} %decode.1.a), channel_id=1, source_target_pairs={{0,16},{16,0},{32,48},{48,32},{1,17},{17,1},{33,49},{49,33},{2,18}... | collective-permute-start | bytes 393224 | tf_op jit(solution)/shard_map/ppermute | solution.py:317
  26.4 5.0 %copy-start.3 = (s32[1,32]{1,0:T(1,128)S(1)}, s32[1,32]{1,0:T(1,128)}, u32[]{:S(2)}) copy-start(s32[1,32]{1,0:T(1,128)} %ids.2) | copy-start | bytes 388
  31.9 16.2 %collective-permute-start.13 = (bf16[1024,128]{1,0:T(8,128)(2,1)S(1)}, bf16[1024,128]{1,0:T(8,128)(2,1)S(1)}, u32[]{:S(2)}, u32[]{:S(2)}) collective-permute-start(bf16[1024,128]{1,0:T(8,128)(2,1)S(1)} %bitcast.17), channel_id=1, source_target_pairs={{0,48},{16,32},{32,16},{48,0},{1,49},{17,33},{33,17},{49,1},{2,50}... | collective-permute-start | bytes 786440 | tf_op jit(solution)/shard_map/ppermute | solution.py:317
  36.1 12.1 %collective-permute-start.12 = (bf16[1024,128]{1,0:T(8,128)(2,1)S(1)}, bf16[1024,128]{1,0:T(8,128)(2,1)}, u32[]{:S(2)}, u32[]{:S(2)}) collective-permute-start(bf16[1024,128]{1,0:T(8,128)(2,1)S(1)} %bitcast.18), channel_id=1, source_target_pairs={{0,32},{16,48},{32,0},{48,16},{1,33},{17,49},{33,1},{49,17},{2,34}... | collective-permute-start | bytes 786440 | tf_op jit(solution)/shard_map/ppermute | solution.py:317
  36.1 12.1 %collective-permute-start.11 = (bf16[1024,128]{1,0:T(8,128)(2,1)S(1)}, bf16[1024,128]{1,0:T(8,128)(2,1)}, u32[]{:S(2)}, u32[]{:S(2)}) collective-permute-start(bf16[1024,128]{1,0:T(8,128)(2,1)S(1)} %bitcast.19), channel_id=1, source_target_pairs={{0,16},{16,0},{32,48},{48,32},{1,17},{17,1},{33,49},{49,33},{2,18}... | collective-permute-start | bytes 786440 | tf_op jit(solution)/shard_map/ppermute | solution.py:317
  39.0 22.3 %all-to-all-start.1 = ((bf16[16,32,1024]{2,1,0:T(8,128)(2,1)}), bf16[16,32,1024]{2,1,0:T(8,128)(2,1)S(1)}, u32[]{:S(2)}, u32[]{:S(2)}) async-start(bf16[16,32,1024]{2,1,0:T(8,128)(2,1)} %meet.1), calls=%async_computation.1 | async-start | bytes 2097152 | tf_op jit(solution)/shard_map/all_to_all | solution.py:351
  42.7 27.2 %collective-permute-start.10 = (bf16[128,2048]{1,0:T(8,128)(2,1)}, bf16[128,2048]{1,0:T(8,128)(2,1)S(1)}, u32[]{:S(2)}, u32[]{:S(2)}) collective-permute-start(bf16[128,2048]{1,0:T(8,128)(2,1)} %pad_maximum_fusion), channel_id=1, source_target_pairs={{1,2},{2,1},{3,4},{4,3},{5,6},{6,5},{7,8},{8,7},{9,10},{10,9},{11,... | collective-permute-start | bytes 1572872 | tf_op jit(solution)/shard_map/ppermute | solution.py:355
  43.4 26.5 %collective-permute-start.9 = (bf16[128,2048]{1,0:T(8,128)(2,1)}, bf16[128,2048]{1,0:T(8,128)(2,1)}, u32[]{:S(2)}, u32[]{:S(2)}) collective-permute-start(bf16[128,2048]{1,0:T(8,128)(2,1)} %pad_maximum_fusion), channel_id=1, source_target_pairs={{0,1},{1,0},{2,3},{3,2},{4,5},{5,4},{6,7},{7,6},{8,9},{9,8},{10,11... | collective-permute-start | bytes 1572872 | tf_op jit(solution)/shard_map/ppermute | solution.py:354
  60.2 9.7 %copy-start.6 = (bf16[1,128,1024]{2,1,0:T(8,128)(2,1)S(1)}, bf16[1,128,1024]{2,1,0:T(8,128)(2,1)}, u32[]{:S(2)}) copy-start(bf16[1,128,1024]{2,1,0:T(8,128)(2,1)} %param.10) | copy-start | bytes 786436
  61.3 17.3 %all-to-all-start.2 = ((bf16[16,64,128]{2,1,0:T(8,128)(2,1)}), bf16[16,64,128]{2,1,0:T(8,128)(2,1)S(1)}, u32[]{:S(2)}, u32[]{:S(2)}) async-start(bf16[16,64,128]{2,1,0:T(8,128)(2,1)} %heavy.1), calls=%async_computation.2 | async-start | bytes 524288 | tf_op jit(solution)/shard_map/all_to_all | solution.py:359
  72.9 5.7 %copy-start.4 = (s32[1,64]{1,0:T(1,128)S(1)}, s32[1,64]{1,0:T(1,128)}, u32[]{:S(2)}) copy-start(s32[1,64]{1,0:T(1,128)} %ids.3) | copy-start | bytes 772

commit v10 on v9

--- a/solution.py
+++ b/solution.py
@@ -100,22 +100,12 @@
     return total, peak
 
 
-def heavy_kernel(q, kv0, kv1, kv2, kv3, out, others, sem):
-    copies = [pltpu.make_async_copy(kv, others.at[n], sem.at[n]) for n, kv in enumerate((kv1, kv2, kv3))]
-    for copy in copies:
-        copy.start()
-
-    def arriving():
-        yield kv0[...]
-        for n, copy in enumerate(copies):
-            copy.wait()
-            yield others[n]
-
+def heavy_kernel(q, kv0, kv1, kv2, kv3, out):
     rows = q.shape[0] * HALF
     both = q[:, BLOCK:].reshape(rows, LANES)
     zero = jnp.zeros((rows, HEAD), bf16)
-    a, _ = summed(jnp.concatenate([both[:, :HEAD], zero], axis=1), arriving())
-    keys = [kv0[...]] + [others[n] for n in range(len(copies))]
+    keys = [kv[...] for kv in (kv0, kv1, kv2, kv3)]
+    a, _ = summed(jnp.concatenate([both[:, :HEAD], zero], axis=1), keys)
     b, _ = summed(jnp.concatenate([both[:, HEAD:], zero], axis=1), keys)
     low = lane_ids(a.shape) < HEAD
     top = jnp.where(low, pltpu.roll(a, HEAD, 1), b)
@@ -124,22 +114,13 @@
 
 
 def heavy_attend(q_kv, kvs):
-    blocks = q_kv.shape[0]
-    vmem = pl.BlockSpec(memory_space=pltpu.VMEM)
-    hbm = pl.BlockSpec(memory_space=pl.ANY)
-    others = kvs[1:]
     return pl.pallas_call(
         heavy_kernel,
-        in_specs=[vmem] * 2 + [hbm] * len(others),
-        out_shape=jax.ShapeDtypeStruct((blocks, HALF, LANES), bf16),
-        scratch_shapes=[
-            pltpu.VMEM((len(others),) + kvs[0].shape, bf16),
-            pltpu.SemaphoreType.DMA((len(others),)),
-        ],
+        out_shape=jax.ShapeDtypeStruct((q_kv.shape[0], HALF, LANES), bf16),
         compiler_params=params(28),
         cost_estimate=pl.CostEstimate(flops=10_000_000_000, transcendentals=8_000_000, bytes_accessed=2_000_000),
         name="heavy",
-    )(q_kv, kvs[0], *others)
+    )(q_kv, *kvs)
 
 
 def light_kernel(q, k, v, even, odd, rows_in, out, rows_out, sem):
@@ -193,19 +174,28 @@
     )(q, k, v, even, odd, decoded)
 
 
-def join_kernel(ids, light, heavy, out):
+def join_kernel(ids, light, heavy, out, both, sem):
     here = lax.axis_index(TOKENS)
     count = jnp.int32(0)
     for n in range(ids.shape[1]):
         count = count + jnp.where(ids[0, n] == here, 1, 0)
     scale = count.astype(f32)
-    for p in range(heavy.shape[0] // 2):
+    pairs = heavy.shape[0] // 2
+    step = pairs // 4
+    copies = []
+    for p in range(pairs):
         e, o = heavy[2 * p], heavy[2 * p + 1]
+        cols = slice(p * LANES, (p + 1) * LANES)
         for n in range(2):
             rows, lanes = slice(n * HALF, (n + 1) * HALF), slice(n * HEAD, (n + 1) * HEAD)
-            cols = slice(p * LANES, (p + 1) * LANES)
-            both = jnp.concatenate([e[:, lanes], o[:, lanes]], axis=1)
-            out[rows, cols] = (light[rows, cols] + both.astype(f32) * scale).astype(bf16)
+            added = jnp.concatenate([e[:, lanes], o[:, lanes]], axis=1)
+            both[rows, cols] = (light[rows, cols] + added.astype(f32) * scale).astype(bf16)
+        if p % step == step - 1:
+            part = pl.ds((p + 1 - step) * LANES, step * LANES)
+            copies.append(pltpu.make_async_copy(both.at[:, part], out.at[:, part], sem.at[p // step]))
+            copies[-1].start()
+    for copy in copies:
+        copy.wait()
 
 
 def join(ids, light, heavy):
@@ -213,7 +203,9 @@
     return pl.pallas_call(
         join_kernel,
         in_specs=[pl.BlockSpec(memory_space=pltpu.SMEM), vmem, vmem],
+        out_specs=pl.BlockSpec(memory_space=pl.ANY),
         out_shape=jax.ShapeDtypeStruct(light.shape, bf16),
+        scratch_shapes=[pltpu.VMEM(light.shape, bf16), pltpu.SemaphoreType.DMA((4,))],
         compiler_params=params(6),
         name="join",
     )(ids, light, heavy)
@@ -350,11 +342,10 @@
     share = meet([after_all(part, own)] + parts, n_fine, dec_rows, width)
     decoded = lax.all_to_all(share, "fine", 0, 0, tiled=True)
 
-    light_kv = after_all(light_kv, share)
     even = lax.ppermute(light_kv, TOKENS, [(i, i ^ 1) for i in range(n_seq)])
-    odd = lax.ppermute(light_kv, TOKENS, [(i, (i - 1 ^ 1) + 1) for i in range(1, n_seq - 1)])
-
-    heavy = heavy_attend(group, routed)
+    odd = lax.ppermute(after_all(light_kv, share), TOKENS, [(i, (i - 1 ^ 1) + 1) for i in range(1, n_seq - 1)])
+
+    heavy = heavy_attend(after_all(group, even), routed)
     heavy, decoded = lax.optimization_barrier((heavy, decoded))
     heavy = lax.all_to_all(heavy, "fine", 0, 0, tiled=True)
     light, decoded = light_attend(

time: 80.5 us -> 81.2 us (level)
  the two profiles are of different devices: /device:TPU:0 before, /device:TPU:64 now
where the time goes in v10:
time: 81.2 us; the launch traced here: 80.7 us
  starting transfers between devices  44.1 us (54%)
  Pallas kernels  22.1 us (27%)
  waiting for transfers between devices  12.7 us (16%)
  between operations  1.01 us (1%)
  other arithmetic  0.85 us (1%)
    ppermute x12, starting transfers between devices, around(): return [lax.ppermute(value, axis, pairs(d)) for d in range(1, ring)]  16.7 us
    pallas_call x1, Pallas kernels, heavy_attend(): pl.pallas_call(heavy_kernel, out_shape=jax.ShapeDtypeStruct((q_kv.shape[0...  11.4 us
    ppermute x1, starting transfers between devices, local(): lax.ppermute(after_all(light_kv, share), TOKENS, [(i, (i - 1 ^ 1) + 1) fo...  8.24 us
    all_to_all x1, starting transfers between devices, local(): heavy = lax.all_to_all(heavy, 'fine', 0, 0, tiled=True)  7.37 us
    all_to_all x1, starting transfers between devices, local(): group = lax.all_to_all(after_all(chunks, enc[0]), 'fine', 0, 0, tiled=True)  6.03 us
    all_to_all x1, waiting for transfers between devices, local(): heavy = lax.all_to_all(heavy, 'fine', 0, 0, tiled=True)  6.03 us
    all_to_all x1, waiting for transfers between devices, local(): group = lax.all_to_all(after_all(chunks, enc[0]), 'fine', 0, 0, tiled=True)  4.6 us
    all_to_all x1, starting transfers between devices, local(): decoded = lax.all_to_all(share, 'fine', 0, 0, tiled=True)  3.85 us
  transfers between devices with their start and end apart: 17, of which 3 were waited for; matrix products, arithmetic and copies ran while one was open for 1% of the time, Pallas kernels for 26%

profile of v10, /device:TPU:64, one launch (start us, length us, event | category | flops | bytes accessed | tf_op | source)
XLA Modules:
  0.0 80.7 jit_solution(5205125487203853112)
XLA Ops:
  0.6 2.8 %collective-permute-start.3 = (bf16[128,128]{1,0:T(8,128)(2,1)}, bf16[128,128]{1,0:T(8,128)(2,1)S(1)}, u32[]{:S(2)}, u32[]{:S(2)}) collective-permute-start(bf16[128,128]{1,0:T(8,128)(2,1)} %bitcast.21), channel_id=1, source_target_pairs={{0,3},{1,2},{2,1},{3,0},{4,7},{5,6},{6,5},{7,4},{8,11},{9,10},{10,... | collective-permute-start | bytes 98312 | tf_op jit(solution)/shard_map/ppermute | solution.py:309
  3.5 0.8 collective-permute-start.2
  4.3 0.5 collective-permute-start.1
  4.8 2.3 %pack.1.refs_4_ = bf16[16,192,128]{2,1,0:T(8,128)(2,1)} custom-call(bf16[128,1024]{1,0:T(8,128)(2,1)} %bitcast.27, bf16[128,1024]{1,0:T(8,128)(2,1)} %bitcast.28, bf16[128,1024]{1,0:T(8,128)(2,1)} %bitcast.29), custom_call_target="tpu_custom_call" | custom-call | tf_op jit(solution)/shard_map/pack/pallas_call | solution.py:60
  7.1 2.0 %collective-permute-done.2.refs_2_ = bf16[128,128]{1,0:T(8,128)(2,1)S(1)} collective-permute-done((bf16[128,128]{1,0:T(8,128)(2,1)}, bf16[128,128]{1,0:T(8,128)(2,1)S(1)}, u32[]{:S(2)}, u32[]{:S(2)}) %collective-permute-start.2) | collective-permute-done | bytes 32800 | tf_op jit(solution)/shard_map/ppermute | solution.py:309
  9.1 0.0 copy-start.5
  9.1 3.1 %collective-permute-start.6 = (bf16[512,128]{1,0:T(8,128)(2,1)S(1)}, bf16[512,128]{1,0:T(8,128)(2,1)S(1)}, u32[]{:S(2)}, u32[]{:S(2)}) collective-permute-start(bf16[512,128]{1,0:T(8,128)(2,1)S(1)} %stack.1.e0), channel_id=1, source_target_pairs={{0,12},{1,13},{2,14},{3,15},{4,8},{5,9},{6,10},{7,11},{8,4},{9,5},... | collective-permute-start | bytes 393224 | tf_op jit(solution)/shard_map/ppermute | solution.py:309
  12.2 0.6 collective-permute-start.5
  12.9 0.5 collective-permute-start.4
  13.3 6.0 %all-to-all-start = ((bf16[16,192,128]{2,1,0:T(8,128)(2,1)}), bf16[16,192,128]{2,1,0:T(8,128)(2,1)S(1)}, u32[]{:S(2)}, u32[]{:S(2)}) async-start(bf16[16,192,128]{2,1,0:T(8,128)(2,1)} %pack.1.refs_4_), calls=%async_computation | async-start | bytes 1572864 | tf_op jit(solution)/shard_map/all_to_all | solution.py:334
  19.4 0.0 copy-start
  19.4 0.0 copy-start.1
  19.4 1.8 %decode.1.a = bf16[512,128]{1,0:T(8,128)(2,1)S(1)} custom-call(bf16[512,1024]{1,0:T(8,128)(2,1)S(1)} %bitcast.25, bf16[512,128]{1,0:T(8,128)(2,1)S(1)} %stack.1.e0, bf16[512,128]{1,0:T(8,128)(2,1)S(1)} %collective-permute-done.4.e1, bf16[512,128]{1,0:T(8,128)(2,1)S(1)} %collective-permute-done.5.e2, bf16[512,128]{1,0:T(8,128)(2,1)S(1)} %collective-permute-done.6.e3), custom_call_target="tpu_custom_call" | custom-call | flops 30000001024 | bytes 1000000 | tf_op jit(solution)/shard_map/decode/pallas_call | solution.py:243
  21.2 0.2 collective-permute-start.9
  21.4 3.6 %collective-permute-start.8 = (bf16[512,128]{1,0:T(8,128)(2,1)S(1)}, bf16[512,128]{1,0:T(8,128)(2,1)S(1)}, u32[]{:S(2)}, u32[]{:S(2)}) collective-permute-start(bf16[512,128]{1,0:T(8,128)(2,1)S(1)} %decode.1.a), channel_id=1, source_target_pairs={{0,32},{16,48},{32,0},{48,16},{1,33},{17,49},{33,1},{49,17},{2,34}... | collective-permute-start | bytes 393224 | tf_op jit(solution)/shard_map/ppermute | solution.py:309
  25.0 0.4 collective-permute-start.7
  25.4 0.8 %pad_maximum_fusion = bf16[128,2048]{1,0:T(8,128)(2,1)} fusion(bf16[128,1024]{1,0:T(8,128)(2,1)S(1)} %bitcast.15, bf16[128,1024]{1,0:T(8,128)(2,1)S(1)} %bitcast.13), kind=kLoop, calls=%fused_computation | loop fusion | flops 1048576 | bytes 1048576 | tf_op jit(solution)/shard_map/concatenate | solution.py:324
  26.2 1.9 %collective-permute-start = (bf16[128,2048]{1,0:T(8,128)(2,1)}, bf16[128,2048]{1,0:T(8,128)(2,1)S(1)}, u32[]{:S(2)}, u32[]{:S(2)}) collective-permute-start(bf16[128,2048]{1,0:T(8,128)(2,1)} %pad_maximum_fusion), channel_id=1, source_target_pairs={{0,1},{1,0},{2,3},{3,2},{4,5},{5,4},{6,7},{7,6},{8,9},{9,8},{10,11... | collective-permute-start | bytes 1572872 | tf_op jit(solution)/shard_map/ppermute | solution.py:345
  28.2 4.6 %all-to-all-done.kv.q = bf16[16,192,128]{2,1,0:T(8,128)(2,1)S(1)} async-done(((bf16[16,192,128]{2,1,0:T(8,128)(2,1)}), bf16[16,192,128]{2,1,0:T(8,128)(2,1)S(1)}, u32[]{:S(2)}, u32[]{:S(2)}) %all-to-all-start) | async-done | bytes 786464 | tf_op jit(solution)/shard_map/all_to_all | solution.py:334
  32.8 0.6 pick.1
  33.4 0.1 collective-permute-start.13
  33.5 3.7 %collective-permute-start.12 = (bf16[1024,128]{1,0:T(8,128)(2,1)S(1)}, bf16[1024,128]{1,0:T(8,128)(2,1)}, u32[]{:S(2)}, u32[]{:S(2)}) collective-permute-start(bf16[1024,128]{1,0:T(8,128)(2,1)S(1)} %bitcast.18), channel_id=1, source_target_pairs={{0,32},{16,48},{32,0},{48,16},{1,33},{17,49},{33,1},{49,17},{2,34}... | collective-permute-start | bytes 786440 | tf_op jit(solution)/shard_map/ppermute | solution.py:309
  37.1 0.4 collective-permute-start.11
  37.5 2.0 %meet.1 = bf16[16,32,1024]{2,1,0:T(8,128)(2,1)} custom-call(bf16[512,128]{1,0:T(8,128)(2,1)S(1)} %decode.1.a, bf16[512,128]{1,0:T(8,128)(2,1)S(1)} %collective-permute-done.7.b, bf16[512,128]{1,0:T(8,128)(2,1)S(1)} %collective-permute-done.8.c, bf16[512,128]{1,0:T(8,128)(2,1)S(1)} %collective-permute-done.9.d), custom_call_target="tpu_custom_call" | custom-call | flops 30000001024 | bytes 2000000 | tf_op jit(solution)/shard_map/meet/pallas_call | solution.py:274
  39.6 3.9 %all-to-all-start.1 = ((bf16[16,32,1024]{2,1,0:T(8,128)(2,1)}), bf16[16,32,1024]{2,1,0:T(8,128)(2,1)S(1)}, u32[]{:S(2)}, u32[]{:S(2)}) async-start(bf16[16,32,1024]{2,1,0:T(8,128)(2,1)} %meet.1), calls=%async_computation.1 | async-start | bytes 2097152 | tf_op jit(solution)/shard_map/all_to_all | solution.py:343
  43.4 8.2 %collective-permute-start.10 = (bf16[128,2048]{1,0:T(8,128)(2,1)}, bf16[128,2048]{1,0:T(8,128)(2,1)}, u32[]{:S(2)}, u32[]{:S(2)}) collective-permute-start(bf16[128,2048]{1,0:T(8,128)(2,1)} %pad_maximum_fusion), channel_id=1, source_target_pairs={{1,2},{2,1},{3,4},{4,3},{5,6},{6,5},{7,8},{8,7},{9,10},{10,9},{11,... | collective-permute-start | bytes 1572872 | tf_op jit(solution)/shard_map/ppermute | solution.py:346
  51.7 11.4 %heavy.1 = bf16[16,64,128]{2,1,0:T(8,128)(2,1)} custom-call(bf16[16,192,128]{2,1,0:T(8,128)(2,1)S(1)} %all-to-all-done.kv.q, bf16[1024,128]{1,0:T(8,128)(2,1)S(1)} %bitcast.20, bf16[1024,128]{1,0:T(8,128)(2,1)} %collective-permute-done.11.kv1, bf16[1024,128]{1,0:T(8,128)(2,1)} %collective-permute-done.12.kv2, bf16[1024,128]{1,0:T(8,128)(2,1)S(1)} %collective-permute-done.13.kv3), custom_call_target="tpu_custom_call" | custom-call | flops 10000000000 | bytes 2000000 | tf_op jit(solution)/shard_map/heavy/pallas_call | solution.py:117
  63.1 7.4 %all-to-all-start.2 = ((bf16[16,64,128]{2,1,0:T(8,128)(2,1)}), bf16[16,64,128]{2,1,0:T(8,128)(2,1)S(1)}, u32[]{:S(2)}, u32[]{:S(2)}) async-start(bf16[16,64,128]{2,1,0:T(8,128)(2,1)} %heavy.1), calls=%async_computation.2 | async-start | bytes 524288 | tf_op jit(solution)/shard_map/all_to_all | solution.py:350
  70.5 2.6 %light.1 = (f32[128,1024]{1,0:T(8,128)S(1)}, bf16[512,1024]{1,0:T(8,128)(2,1)}) custom-call(bf16[128,1024]{1,0:T(8,128)(2,1)S(1)} %bitcast.26, bf16[128,1024]{1,0:T(8,128)(2,1)S(1)} %bitcast.14, bf16[128,1024]{1,0:T(8,128)(2,1)S(1)} %bitcast.16, bf16[128,2048]{1,0:T(8,128)(2,1)S(1)} %collective-permute-done.even, ...), custom_call_target="tpu_custom_call" | custom-call | flops 3000000000 | bytes 2000000 | tf_op jit(solution)/shard_map/light/pallas_call | solution.py:165
  73.1 0.0 copy-start.4
  73.1 6.0 %all-to-all-done.2.heavy = bf16[16,64,128]{2,1,0:T(8,128)(2,1)S(1)} async-done(((bf16[16,64,128]{2,1,0:T(8,128)(2,1)}), bf16[16,64,128]{2,1,0:T(8,128)(2,1)S(1)}, u32[]{:S(2)}, u32[]{:S(2)}) %all-to-all-start.2) | async-done | bytes 262176 | tf_op jit(solution)/shard_map/all_to_all | solution.py:350
  79.2 1.4 %join.1 = bf16[128,1024]{1,0:T(8,128)(2,1)} custom-call(s32[1,64]{1,0:T(1,128)S(1)} %copy-done.4, f32[128,1024]{1,0:T(8,128)S(1)} %get-tuple-element.17.light, bf16[16,64,128]{2,1,0:T(8,128)(2,1)S(1)} %all-to-all-done.2.heavy), custom_call_target="tpu_custom_call" | custom-call | tf_op jit(solution)/shard_map/join/pallas_call | solution.py:203
  (25 shorter events, 0.1 us)
Async XLA Ops:
  0.6 6.5 %collective-permute-start.3 = (bf16[128,128]{1,0:T(8,128)(2,1)}, bf16[128,128]{1,0:T(8,128)(2,1)S(1)}, u32[]{:S(2)}, u32[]{:S(2)}) collective-permute-start(bf16[128,128]{1,0:T(8,128)(2,1)} %bitcast.21), channel_id=1, source_target_pairs={{0,3},{1,2},{2,1},{3,0},{4,7},{5,6},{6,5},{7,4},{8,11},{9,10},{10,... | collective-permute-start | bytes 98312 | tf_op jit(solution)/shard_map/ppermute | solution.py:309
  3.5 5.6 %collective-permute-start.2 = (bf16[128,128]{1,0:T(8,128)(2,1)}, bf16[128,128]{1,0:T(8,128)(2,1)S(1)}, u32[]{:S(2)}, u32[]{:S(2)}) collective-permute-start(bf16[128,128]{1,0:T(8,128)(2,1)} %bitcast.22), channel_id=1, source_target_pairs={{0,2},{1,3},{2,0},{3,1},{4,6},{5,7},{6,4},{7,5},{8,10},{9,11},{10,... | collective-permute-start | bytes 98312 | tf_op jit(solution)/shard_map/ppermute | solution.py:309
  4.3 4.8 %collective-permute-start.1 = (bf16[128,128]{1,0:T(8,128)(2,1)}, bf16[128,128]{1,0:T(8,128)(2,1)S(1)}, u32[]{:S(2)}, u32[]{:S(2)}) collective-permute-start(bf16[128,128]{1,0:T(8,128)(2,1)} %bitcast.23), channel_id=1, source_target_pairs={{0,1},{1,0},{2,3},{3,2},{4,5},{5,4},{6,7},{7,6},{8,9},{9,8},{10,11... | collective-permute-start | bytes 98312 | tf_op jit(solution)/shard_map/ppermute | solution.py:309
  4.8 4.3 %copy-start.2 = (bf16[1,128,128]{2,1,0:T(8,128)(2,1)S(1)}, bf16[1,128,128]{2,1,0:T(8,128)(2,1)}, u32[]{:S(2)}) copy-start(bf16[1,128,128]{2,1,0:T(8,128)(2,1)} %param.16) | copy-start | bytes 98308
  9.1 10.3 %copy-start.5 = (bf16[1,512,1024]{2,1,0:T(8,128)(2,1)S(1)}, bf16[1,512,1024]{2,1,0:T(8,128)(2,1)}, u32[]{:S(2)}) copy-start(bf16[1,512,1024]{2,1,0:T(8,128)(2,1)} %param.17) | copy-start | bytes 3145732
  9.1 10.2 %collective-permute-start.6 = (bf16[512,128]{1,0:T(8,128)(2,1)S(1)}, bf16[512,128]{1,0:T(8,128)(2,1)S(1)}, u32[]{:S(2)}, u32[]{:S(2)}) collective-permute-start(bf16[512,128]{1,0:T(8,128)(2,1)S(1)} %stack.1.e0), channel_id=1, source_target_pairs={{0,12},{1,13},{2,14},{3,15},{4,8},{5,9},{6,10},{7,11},{8,4},{9,5},... | collective-permute-start | bytes 393224 | tf_op jit(solution)/shard_map/ppermute | solution.py:309
  12.2 7.1 %collective-permute-start.5 = (bf16[512,128]{1,0:T(8,128)(2,1)S(1)}, bf16[512,128]{1,0:T(8,128)(2,1)S(1)}, u32[]{:S(2)}, u32[]{:S(2)}) collective-permute-start(bf16[512,128]{1,0:T(8,128)(2,1)S(1)} %stack.1.e0), channel_id=1, source_target_pairs={{0,8},{1,9},{2,10},{3,11},{4,12},{5,13},{6,14},{7,15},{8,0},{9,1},... | collective-permute-start | bytes 393224 | tf_op jit(solution)/shard_map/ppermute | solution.py:309
  12.9 6.5 %collective-permute-start.4 = (bf16[512,128]{1,0:T(8,128)(2,1)S(1)}, bf16[512,128]{1,0:T(8,128)(2,1)S(1)}, u32[]{:S(2)}, u32[]{:S(2)}) collective-permute-start(bf16[512,128]{1,0:T(8,128)(2,1)S(1)} %stack.1.e0), channel_id=1, source_target_pairs={{0,4},{1,5},{2,6},{3,7},{4,0},{5,1},{6,2},{7,3},{8,12},{9,13},{10,... | collective-permute-start | bytes 393224 | tf_op jit(solution)/shard_map/ppermute | solution.py:309
  13.3 19.5 %all-to-all-start = ((bf16[16,192,128]{2,1,0:T(8,128)(2,1)}), bf16[16,192,128]{2,1,0:T(8,128)(2,1)S(1)}, u32[]{:S(2)}, u32[]{:S(2)}) async-start(bf16[16,192,128]{2,1,0:T(8,128)(2,1)} %pack.1.refs_4_), calls=%async_computation | async-start | bytes 1572864 | tf_op jit(solution)/shard_map/all_to_all | solution.py:334
  19.4 6.0 %copy-start = (bf16[1,128,1024]{2,1,0:T(8,128)(2,1)S(1)}, bf16[1,128,1024]{2,1,0:T(8,128)(2,1)}, u32[]{:S(2)}) copy-start(bf16[1,128,1024]{2,1,0:T(8,128)(2,1)} %param.11) | copy-start | bytes 786436
  19.4 6.0 %copy-start.1 = (bf16[1,128,1024]{2,1,0:T(8,128)(2,1)S(1)}, bf16[1,128,1024]{2,1,0:T(8,128)(2,1)}, u32[]{:S(2)}) copy-start(bf16[1,128,1024]{2,1,0:T(8,128)(2,1)} %param.12) | copy-start | bytes 786436
  21.2 12.2 %collective-permute-start.9 = (bf16[512,128]{1,0:T(8,128)(2,1)S(1)}, bf16[512,128]{1,0:T(8,128)(2,1)S(1)}, u32[]{:S(2)}, u32[]{:S(2)}) collective-permute-start(bf16[512,128]{1,0:T(8,128)(2,1)S(1)} %decode.1.a), channel_id=1, source_target_pairs={{0,48},{16,32},{32,16},{48,0},{1,49},{17,33},{33,17},{49,1},{2,50}... | collective-permute-start | bytes 393224 | tf_op jit(solution)/shard_map/ppermute | solution.py:309
  21.4 15.7 %collective-permute-start.8 = (bf16[512,128]{1,0:T(8,128)(2,1)S(1)}, bf16[512,128]{1,0:T(8,128)(2,1)S(1)}, u32[]{:S(2)}, u32[]{:S(2)}) collective-permute-start(bf16[512,128]{1,0:T(8,128)(2,1)S(1)} %decode.1.a), channel_id=1, source_target_pairs={{0,32},{16,48},{32,0},{48,16},{1,33},{17,49},{33,1},{49,17},{2,34}... | collective-permute-start | bytes 393224 | tf_op jit(solution)/shard_map/ppermute | solution.py:309
  25.0 12.6 %collective-permute-start.7 = (bf16[512,128]{1,0:T(8,128)(2,1)S(1)}, bf16[512,128]{1,0:T(8,128)(2,1)S(1)}, u32[]{:S(2)}, u32[]{:S(2)}) collective-permute-start(bf16[512,128]{1,0:T(8,128)(2,1)S(1)} %decode.1.a), channel_id=1, source_target_pairs={{0,16},{16,0},{32,48},{48,32},{1,17},{17,1},{33,49},{49,33},{2,18}... | collective-permute-start | bytes 393224 | tf_op jit(solution)/shard_map/ppermute | solution.py:309
  25.4 7.4 %copy-start.3 = (s32[1,32]{1,0:T(1,128)S(1)}, s32[1,32]{1,0:T(1,128)}, u32[]{:S(2)}) copy-start(s32[1,32]{1,0:T(1,128)} %ids.2) | copy-start | bytes 388
  26.2 17.2 %collective-permute-start = (bf16[128,2048]{1,0:T(8,128)(2,1)}, bf16[128,2048]{1,0:T(8,128)(2,1)S(1)}, u32[]{:S(2)}, u32[]{:S(2)}) collective-permute-start(bf16[128,2048]{1,0:T(8,128)(2,1)} %pad_maximum_fusion), channel_id=1, source_target_pairs={{0,1},{1,0},{2,3},{3,2},{4,5},{5,4},{6,7},{7,6},{8,9},{9,8},{10,11... | collective-permute-start | bytes 1572872 | tf_op jit(solution)/shard_map/ppermute | solution.py:345
  33.4 18.3 %collective-permute-start.13 = (bf16[1024,128]{1,0:T(8,128)(2,1)S(1)}, bf16[1024,128]{1,0:T(8,128)(2,1)S(1)}, u32[]{:S(2)}, u32[]{:S(2)}) collective-permute-start(bf16[1024,128]{1,0:T(8,128)(2,1)S(1)} %bitcast.17), channel_id=1, source_target_pairs={{0,48},{16,32},{32,16},{48,0},{1,49},{17,33},{33,17},{49,1},{2,50}... | collective-permute-start | bytes 786440 | tf_op jit(solution)/shard_map/ppermute | solution.py:309
  33.5 18.2 %collective-permute-start.12 = (bf16[1024,128]{1,0:T(8,128)(2,1)S(1)}, bf16[1024,128]{1,0:T(8,128)(2,1)}, u32[]{:S(2)}, u32[]{:S(2)}) collective-permute-start(bf16[1024,128]{1,0:T(8,128)(2,1)S(1)} %bitcast.18), channel_id=1, source_target_pairs={{0,32},{16,48},{32,0},{48,16},{1,33},{17,49},{33,1},{49,17},{2,34}... | collective-permute-start | bytes 786440 | tf_op jit(solution)/shard_map/ppermute | solution.py:309
  37.1 14.6 %collective-permute-start.11 = (bf16[1024,128]{1,0:T(8,128)(2,1)S(1)}, bf16[1024,128]{1,0:T(8,128)(2,1)}, u32[]{:S(2)}, u32[]{:S(2)}) collective-permute-start(bf16[1024,128]{1,0:T(8,128)(2,1)S(1)} %bitcast.19), channel_id=1, source_target_pairs={{0,16},{16,0},{32,48},{48,32},{1,17},{17,1},{33,49},{49,33},{2,18}... | collective-permute-start | bytes 786440 | tf_op jit(solution)/shard_map/ppermute | solution.py:309
  39.6 23.5 %all-to-all-start.1 = ((bf16[16,32,1024]{2,1,0:T(8,128)(2,1)}), bf16[16,32,1024]{2,1,0:T(8,128)(2,1)S(1)}, u32[]{:S(2)}, u32[]{:S(2)}) async-start(bf16[16,32,1024]{2,1,0:T(8,128)(2,1)} %meet.1), calls=%async_computation.1 | async-start | bytes 2097152 | tf_op jit(solution)/shard_map/all_to_all | solution.py:343
  43.4 27.0 %collective-permute-start.10 = (bf16[128,2048]{1,0:T(8,128)(2,1)}, bf16[128,2048]{1,0:T(8,128)(2,1)}, u32[]{:S(2)}, u32[]{:S(2)}) collective-permute-start(bf16[128,2048]{1,0:T(8,128)(2,1)} %pad_maximum_fusion), channel_id=1, source_target_pairs={{1,2},{2,1},{3,4},{4,3},{5,6},{6,5},{7,8},{8,7},{9,10},{10,9},{11,... | collective-permute-start | bytes 1572872 | tf_op jit(solution)/shard_map/ppermute | solution.py:346
  63.1 7.4 %copy-start.6 = (bf16[1,128,1024]{2,1,0:T(8,128)(2,1)S(1)}, bf16[1,128,1024]{2,1,0:T(8,128)(2,1)}, u32[]{:S(2)}) copy-start(bf16[1,128,1024]{2,1,0:T(8,128)(2,1)} %param.10) | copy-start | bytes 786436
  63.1 16.1 %all-to-all-start.2 = ((bf16[16,64,128]{2,1,0:T(8,128)(2,1)}), bf16[16,64,128]{2,1,0:T(8,128)(2,1)S(1)}, u32[]{:S(2)}, u32[]{:S(2)}) async-start(bf16[16,64,128]{2,1,0:T(8,128)(2,1)} %heavy.1), calls=%async_computation.2 | async-start | bytes 524288 | tf_op jit(solution)/shard_map/all_to_all | solution.py:350
  73.1 6.0 %copy-start.4 = (s32[1,64]{1,0:T(1,128)S(1)}, s32[1,64]{1,0:T(1,128)}, u32[]{:S(2)}) copy-start(s32[1,64]{1,0:T(1,128)} %ids.3) | copy-start | bytes 772

commit v11 on v10

--- a/solution.py
+++ b/solution.py
@@ -100,12 +100,23 @@
     return total, peak
 
 
-def heavy_kernel(q, kv0, kv1, kv2, kv3, out):
+def heavy_kernel(q, kv0, kv1, kv2, kv3, out, late, sem):
+    copies = [pltpu.make_async_copy(kv, late.at[n], sem.at[n]) for n, kv in enumerate((kv1, kv2))]
+    for copy in copies:
+        copy.start()
+
+    def arriving():
+        yield kv0[...]
+        yield kv3[...]
+        for n, copy in enumerate(copies):
+            copy.wait()
+            yield late[n]
+
     rows = q.shape[0] * HALF
     both = q[:, BLOCK:].reshape(rows, LANES)
     zero = jnp.zeros((rows, HEAD), bf16)
-    keys = [kv[...] for kv in (kv0, kv1, kv2, kv3)]
-    a, _ = summed(jnp.concatenate([both[:, :HEAD], zero], axis=1), keys)
+    a, _ = summed(jnp.concatenate([both[:, :HEAD], zero], axis=1), arriving())
+    keys = [kv0[...], kv3[...]] + [late[n] for n in range(len(copies))]
     b, _ = summed(jnp.concatenate([both[:, HEAD:], zero], axis=1), keys)
     low = lane_ids(a.shape) < HEAD
     top = jnp.where(low, pltpu.roll(a, HEAD, 1), b)
@@ -114,9 +125,13 @@
 
 
 def heavy_attend(q_kv, kvs):
+    vmem = pl.BlockSpec(memory_space=pltpu.VMEM)
+    own = kvs[0]
     return pl.pallas_call(
         heavy_kernel,
+        in_specs=[vmem] * 2 + [pl.BlockSpec(memory_space=pl.ANY)] * 2 + [vmem],
         out_shape=jax.ShapeDtypeStruct((q_kv.shape[0], HALF, LANES), bf16),
+        scratch_shapes=[pltpu.VMEM((2,) + own.shape, bf16), pltpu.SemaphoreType.DMA((2,))],
         compiler_params=params(28),
         cost_estimate=pl.CostEstimate(flops=10_000_000_000, transcendentals=8_000_000, bytes_accessed=2_000_000),
         name="heavy",

time: 81.2 us -> 81.2 us (level)
  transfers between devices with their start and end apart: 17 -> 17, of which waited for: 3 -> 3; matrix products, arithmetic and copies ran while one was open for 1% -> 1% of each run, Pallas kernels for 26% -> 25%
where the time goes in v11:
time: 81.2 us; the launch traced here: 80.7 us
  starting transfers between devices  44.5 us (55%)
  Pallas kernels  21.7 us (27%)
  waiting for transfers between devices  12.7 us (16%)
  between operations  1.03 us (1%)
  other arithmetic  0.85 us (1%)
    ppermute x12, starting transfers between devices, around(): return [lax.ppermute(value, axis, pairs(d)) for d in range(1, ring)]  16.7 us
    pallas_call x1, Pallas kernels, heavy_attend(): pl.pallas_call(heavy_kernel, in_specs=[vmem] * 2 + [pl.BlockSpec(memory_s...  11 us
    ppermute x1, starting transfers between devices, local(): lax.ppermute(after_all(light_kv, share), TOKENS, [(i, (i - 1 ^ 1) + 1) fo...  8.24 us
    all_to_all x1, starting transfers between devices, local(): heavy = lax.all_to_all(heavy, 'fine', 0, 0, tiled=True)  7.75 us
    all_to_all x1, starting transfers between devices, local(): group = lax.all_to_all(after_all(chunks, enc[0]), 'fine', 0, 0, tiled=True)  6.03 us
    all_to_all x1, waiting for transfers between devices, local(): heavy = lax.all_to_all(heavy, 'fine', 0, 0, tiled=True)  6.03 us
    all_to_all x1, waiting for transfers between devices, local(): group = lax.all_to_all(after_all(chunks, enc[0]), 'fine', 0, 0, tiled=True)  4.6 us
    all_to_all x1, starting transfers between devices, local(): decoded = lax.all_to_all(share, 'fine', 0, 0, tiled=True)  3.85 us
  transfers between devices with their start and end apart: 17, of which 3 were waited for; matrix products, arithmetic and copies ran while one was open for 1% of the time, Pallas kernels for 25%

profile of v11, /device:TPU:64, one launch (start us, length us, event | category | flops | bytes accessed | tf_op | source)
XLA Modules:
  0.0 80.7 jit_solution(12967187536880069519)
XLA Ops:
  0.6 2.8 %collective-permute-start.3 = (bf16[128,128]{1,0:T(8,128)(2,1)}, bf16[128,128]{1,0:T(8,128)(2,1)S(1)}, u32[]{:S(2)}, u32[]{:S(2)}) collective-permute-start(bf16[128,128]{1,0:T(8,128)(2,1)} %bitcast.21), channel_id=1, source_target_pairs={{0,3},{1,2},{2,1},{3,0},{4,7},{5,6},{6,5},{7,4},{8,11},{9,10},{10,... | collective-permute-start | bytes 98312 | tf_op jit(solution)/shard_map/ppermute | solution.py:324
  3.5 0.8 collective-permute-start.2
  4.3 0.5 collective-permute-start.1
  4.8 2.3 %pack.1.refs_4_ = bf16[16,192,128]{2,1,0:T(8,128)(2,1)} custom-call(bf16[128,1024]{1,0:T(8,128)(2,1)} %bitcast.27, bf16[128,1024]{1,0:T(8,128)(2,1)} %bitcast.28, bf16[128,1024]{1,0:T(8,128)(2,1)} %bitcast.29), custom_call_target="tpu_custom_call" | custom-call | tf_op jit(solution)/shard_map/pack/pallas_call | solution.py:60
  7.1 2.0 %collective-permute-done.2.refs_2_ = bf16[128,128]{1,0:T(8,128)(2,1)S(1)} collective-permute-done((bf16[128,128]{1,0:T(8,128)(2,1)}, bf16[128,128]{1,0:T(8,128)(2,1)S(1)}, u32[]{:S(2)}, u32[]{:S(2)}) %collective-permute-start.2) | collective-permute-done | bytes 32800 | tf_op jit(solution)/shard_map/ppermute | solution.py:324
  9.1 0.0 copy-start.5
  9.1 3.1 %collective-permute-start.6 = (bf16[512,128]{1,0:T(8,128)(2,1)S(1)}, bf16[512,128]{1,0:T(8,128)(2,1)S(1)}, u32[]{:S(2)}, u32[]{:S(2)}) collective-permute-start(bf16[512,128]{1,0:T(8,128)(2,1)S(1)} %stack.1.e0), channel_id=1, source_target_pairs={{0,12},{1,13},{2,14},{3,15},{4,8},{5,9},{6,10},{7,11},{8,4},{9,5},... | collective-permute-start | bytes 393224 | tf_op jit(solution)/shard_map/ppermute | solution.py:324
  12.2 0.6 collective-permute-start.5
  12.9 0.5 collective-permute-start.4
  13.3 6.0 %all-to-all-start = ((bf16[16,192,128]{2,1,0:T(8,128)(2,1)}), bf16[16,192,128]{2,1,0:T(8,128)(2,1)S(1)}, u32[]{:S(2)}, u32[]{:S(2)}) async-start(bf16[16,192,128]{2,1,0:T(8,128)(2,1)} %pack.1.refs_4_), calls=%async_computation | async-start | bytes 1572864 | tf_op jit(solution)/shard_map/all_to_all | solution.py:349
  19.4 0.0 copy-start
  19.4 0.0 copy-start.1
  19.4 1.8 %decode.1.a = bf16[512,128]{1,0:T(8,128)(2,1)S(1)} custom-call(bf16[512,1024]{1,0:T(8,128)(2,1)S(1)} %bitcast.25, bf16[512,128]{1,0:T(8,128)(2,1)S(1)} %stack.1.e0, bf16[512,128]{1,0:T(8,128)(2,1)S(1)} %collective-permute-done.4.e1, bf16[512,128]{1,0:T(8,128)(2,1)S(1)} %collective-permute-done.5.e2, bf16[512,128]{1,0:T(8,128)(2,1)S(1)} %collective-permute-done.6.e3), custom_call_target="tpu_custom_call" | custom-call | flops 30000001024 | bytes 1000000 | tf_op jit(solution)/shard_map/decode/pallas_call | solution.py:258
  21.2 0.2 collective-permute-start.9
  21.4 3.6 %collective-permute-start.8 = (bf16[512,128]{1,0:T(8,128)(2,1)S(1)}, bf16[512,128]{1,0:T(8,128)(2,1)S(1)}, u32[]{:S(2)}, u32[]{:S(2)}) collective-permute-start(bf16[512,128]{1,0:T(8,128)(2,1)S(1)} %decode.1.a), channel_id=1, source_target_pairs={{0,32},{16,48},{32,0},{48,16},{1,33},{17,49},{33,1},{49,17},{2,34}... | collective-permute-start | bytes 393224 | tf_op jit(solution)/shard_map/ppermute | solution.py:324
  25.0 0.4 collective-permute-start.7
  25.4 0.8 %pad_maximum_fusion = bf16[128,2048]{1,0:T(8,128)(2,1)} fusion(bf16[128,1024]{1,0:T(8,128)(2,1)S(1)} %bitcast.15, bf16[128,1024]{1,0:T(8,128)(2,1)S(1)} %bitcast.13), kind=kLoop, calls=%fused_computation | loop fusion | flops 1048576 | bytes 1048576 | tf_op jit(solution)/shard_map/concatenate | solution.py:339
  26.2 1.9 %collective-permute-start = (bf16[128,2048]{1,0:T(8,128)(2,1)}, bf16[128,2048]{1,0:T(8,128)(2,1)S(1)}, u32[]{:S(2)}, u32[]{:S(2)}) collective-permute-start(bf16[128,2048]{1,0:T(8,128)(2,1)} %pad_maximum_fusion), channel_id=1, source_target_pairs={{0,1},{1,0},{2,3},{3,2},{4,5},{5,4},{6,7},{7,6},{8,9},{9,8},{10,11... | collective-permute-start | bytes 1572872 | tf_op jit(solution)/shard_map/ppermute | solution.py:360
  28.2 4.6 %all-to-all-done.kv.q = bf16[16,192,128]{2,1,0:T(8,128)(2,1)S(1)} async-done(((bf16[16,192,128]{2,1,0:T(8,128)(2,1)}), bf16[16,192,128]{2,1,0:T(8,128)(2,1)S(1)}, u32[]{:S(2)}, u32[]{:S(2)}) %all-to-all-start) | async-done | bytes 786464 | tf_op jit(solution)/shard_map/all_to_all | solution.py:349
  32.8 0.6 pick.1
  33.4 0.1 collective-permute-start.13
  33.5 3.7 %collective-permute-start.12 = (bf16[1024,128]{1,0:T(8,128)(2,1)S(1)}, bf16[1024,128]{1,0:T(8,128)(2,1)}, u32[]{:S(2)}, u32[]{:S(2)}) collective-permute-start(bf16[1024,128]{1,0:T(8,128)(2,1)S(1)} %bitcast.18), channel_id=1, source_target_pairs={{0,32},{16,48},{32,0},{48,16},{1,33},{17,49},{33,1},{49,17},{2,34}... | collective-permute-start | bytes 786440 | tf_op jit(solution)/shard_map/ppermute | solution.py:324
  37.1 0.4 collective-permute-start.11
  37.5 2.0 %meet.1 = bf16[16,32,1024]{2,1,0:T(8,128)(2,1)} custom-call(bf16[512,128]{1,0:T(8,128)(2,1)S(1)} %decode.1.a, bf16[512,128]{1,0:T(8,128)(2,1)S(1)} %collective-permute-done.7.b, bf16[512,128]{1,0:T(8,128)(2,1)S(1)} %collective-permute-done.8.c, bf16[512,128]{1,0:T(8,128)(2,1)S(1)} %collective-permute-done.9.d), custom_call_target="tpu_custom_call" | custom-call | flops 30000001024 | bytes 2000000 | tf_op jit(solution)/shard_map/meet/pallas_call | solution.py:289
  39.6 3.9 %all-to-all-start.1 = ((bf16[16,32,1024]{2,1,0:T(8,128)(2,1)}), bf16[16,32,1024]{2,1,0:T(8,128)(2,1)S(1)}, u32[]{:S(2)}, u32[]{:S(2)}) async-start(bf16[16,32,1024]{2,1,0:T(8,128)(2,1)} %meet.1), calls=%async_computation.1 | async-start | bytes 2097152 | tf_op jit(solution)/shard_map/all_to_all | solution.py:358
  43.4 8.2 %collective-permute-start.10 = (bf16[128,2048]{1,0:T(8,128)(2,1)}, bf16[128,2048]{1,0:T(8,128)(2,1)}, u32[]{:S(2)}, u32[]{:S(2)}) collective-permute-start(bf16[128,2048]{1,0:T(8,128)(2,1)} %pad_maximum_fusion), channel_id=1, source_target_pairs={{1,2},{2,1},{3,4},{4,3},{5,6},{6,5},{7,8},{8,7},{9,10},{10,9},{11,... | collective-permute-start | bytes 1572872 | tf_op jit(solution)/shard_map/ppermute | solution.py:361
  51.7 11.0 %heavy.1 = bf16[16,64,128]{2,1,0:T(8,128)(2,1)} custom-call(bf16[16,192,128]{2,1,0:T(8,128)(2,1)S(1)} %all-to-all-done.kv.q, bf16[1024,128]{1,0:T(8,128)(2,1)S(1)} %bitcast.20, bf16[1024,128]{1,0:T(8,128)(2,1)} %collective-permute-done.11.kv1, bf16[1024,128]{1,0:T(8,128)(2,1)} %collective-permute-done.12.kv2, bf16[1024,128]{1,0:T(8,128)(2,1)S(1)} %collective-permute-done.13.kv3), custom_call_target="tpu_custom_call" | custom-call | flops 10000000000 | bytes 2000000 | tf_op jit(solution)/shard_map/heavy/pallas_call | solution.py:130
  62.7 0.0 copy-start.6
  62.7 7.7 %all-to-all-start.2 = ((bf16[16,64,128]{2,1,0:T(8,128)(2,1)}), bf16[16,64,128]{2,1,0:T(8,128)(2,1)S(1)}, u32[]{:S(2)}, u32[]{:S(2)}) async-start(bf16[16,64,128]{2,1,0:T(8,128)(2,1)} %heavy.1), calls=%async_computation.2 | async-start | bytes 524288 | tf_op jit(solution)/shard_map/all_to_all | solution.py:365
  70.5 2.6 %light.1 = (f32[128,1024]{1,0:T(8,128)S(1)}, bf16[512,1024]{1,0:T(8,128)(2,1)}) custom-call(bf16[128,1024]{1,0:T(8,128)(2,1)S(1)} %bitcast.26, bf16[128,1024]{1,0:T(8,128)(2,1)S(1)} %bitcast.14, bf16[128,1024]{1,0:T(8,128)(2,1)S(1)} %bitcast.16, bf16[128,2048]{1,0:T(8,128)(2,1)S(1)} %collective-permute-done.even, ...), custom_call_target="tpu_custom_call" | custom-call | flops 3000000000 | bytes 2000000 | tf_op jit(solution)/shard_map/light/pallas_call | solution.py:180
  73.1 6.0 %all-to-all-done.2.heavy = bf16[16,64,128]{2,1,0:T(8,128)(2,1)S(1)} async-done(((bf16[16,64,128]{2,1,0:T(8,128)(2,1)}), bf16[16,64,128]{2,1,0:T(8,128)(2,1)S(1)}, u32[]{:S(2)}, u32[]{:S(2)}) %all-to-all-start.2) | async-done | bytes 262176 | tf_op jit(solution)/shard_map/all_to_all | solution.py:365
  79.2 1.4 %join.1 = bf16[128,1024]{1,0:T(8,128)(2,1)} custom-call(s32[1,64]{1,0:T(1,128)S(1)} %copy-done.4, f32[128,1024]{1,0:T(8,128)S(1)} %get-tuple-element.17.light, bf16[16,64,128]{2,1,0:T(8,128)(2,1)S(1)} %all-to-all-done.2.heavy), custom_call_target="tpu_custom_call" | custom-call | tf_op jit(solution)/shard_map/join/pallas_call | solution.py:218
  (25 shorter events, 0.1 us)
Async XLA Ops:
  0.6 6.5 %collective-permute-start.3 = (bf16[128,128]{1,0:T(8,128)(2,1)}, bf16[128,128]{1,0:T(8,128)(2,1)S(1)}, u32[]{:S(2)}, u32[]{:S(2)}) collective-permute-start(bf16[128,128]{1,0:T(8,128)(2,1)} %bitcast.21), channel_id=1, source_target_pairs={{0,3},{1,2},{2,1},{3,0},{4,7},{5,6},{6,5},{7,4},{8,11},{9,10},{10,... | collective-permute-start | bytes 98312 | tf_op jit(solution)/shard_map/ppermute | solution.py:324
  3.5 5.6 %collective-permute-start.2 = (bf16[128,128]{1,0:T(8,128)(2,1)}, bf16[128,128]{1,0:T(8,128)(2,1)S(1)}, u32[]{:S(2)}, u32[]{:S(2)}) collective-permute-start(bf16[128,128]{1,0:T(8,128)(2,1)} %bitcast.22), channel_id=1, source_target_pairs={{0,2},{1,3},{2,0},{3,1},{4,6},{5,7},{6,4},{7,5},{8,10},{9,11},{10,... | collective-permute-start | bytes 98312 | tf_op jit(solution)/shard_map/ppermute | solution.py:324
  4.3 4.8 %collective-permute-start.1 = (bf16[128,128]{1,0:T(8,128)(2,1)}, bf16[128,128]{1,0:T(8,128)(2,1)S(1)}, u32[]{:S(2)}, u32[]{:S(2)}) collective-permute-start(bf16[128,128]{1,0:T(8,128)(2,1)} %bitcast.23), channel_id=1, source_target_pairs={{0,1},{1,0},{2,3},{3,2},{4,5},{5,4},{6,7},{7,6},{8,9},{9,8},{10,11... | collective-permute-start | bytes 98312 | tf_op jit(solution)/shard_map/ppermute | solution.py:324
  4.8 4.3 %copy-start.2 = (bf16[1,128,128]{2,1,0:T(8,128)(2,1)S(1)}, bf16[1,128,128]{2,1,0:T(8,128)(2,1)}, u32[]{:S(2)}) copy-start(bf16[1,128,128]{2,1,0:T(8,128)(2,1)} %param.16) | copy-start | bytes 98308
  9.1 10.3 %copy-start.5 = (bf16[1,512,1024]{2,1,0:T(8,128)(2,1)S(1)}, bf16[1,512,1024]{2,1,0:T(8,128)(2,1)}, u32[]{:S(2)}) copy-start(bf16[1,512,1024]{2,1,0:T(8,128)(2,1)} %param.17) | copy-start | bytes 3145732
  9.1 10.2 %collective-permute-start.6 = (bf16[512,128]{1,0:T(8,128)(2,1)S(1)}, bf16[512,128]{1,0:T(8,128)(2,1)S(1)}, u32[]{:S(2)}, u32[]{:S(2)}) collective-permute-start(bf16[512,128]{1,0:T(8,128)(2,1)S(1)} %stack.1.e0), channel_id=1, source_target_pairs={{0,12},{1,13},{2,14},{3,15},{4,8},{5,9},{6,10},{7,11},{8,4},{9,5},... | collective-permute-start | bytes 393224 | tf_op jit(solution)/shard_map/ppermute | solution.py:324
  12.2 7.1 %collective-permute-start.5 = (bf16[512,128]{1,0:T(8,128)(2,1)S(1)}, bf16[512,128]{1,0:T(8,128)(2,1)S(1)}, u32[]{:S(2)}, u32[]{:S(2)}) collective-permute-start(bf16[512,128]{1,0:T(8,128)(2,1)S(1)} %stack.1.e0), channel_id=1, source_target_pairs={{0,8},{1,9},{2,10},{3,11},{4,12},{5,13},{6,14},{7,15},{8,0},{9,1},... | collective-permute-start | bytes 393224 | tf_op jit(solution)/shard_map/ppermute | solution.py:324
  12.9 6.5 %collective-permute-start.4 = (bf16[512,128]{1,0:T(8,128)(2,1)S(1)}, bf16[512,128]{1,0:T(8,128)(2,1)S(1)}, u32[]{:S(2)}, u32[]{:S(2)}) collective-permute-start(bf16[512,128]{1,0:T(8,128)(2,1)S(1)} %stack.1.e0), channel_id=1, source_target_pairs={{0,4},{1,5},{2,6},{3,7},{4,0},{5,1},{6,2},{7,3},{8,12},{9,13},{10,... | collective-permute-start | bytes 393224 | tf_op jit(solution)/shard_map/ppermute | solution.py:324
  13.3 19.5 %all-to-all-start = ((bf16[16,192,128]{2,1,0:T(8,128)(2,1)}), bf16[16,192,128]{2,1,0:T(8,128)(2,1)S(1)}, u32[]{:S(2)}, u32[]{:S(2)}) async-start(bf16[16,192,128]{2,1,0:T(8,128)(2,1)} %pack.1.refs_4_), calls=%async_computation | async-start | bytes 1572864 | tf_op jit(solution)/shard_map/all_to_all | solution.py:349
  19.4 6.0 %copy-start = (bf16[1,128,1024]{2,1,0:T(8,128)(2,1)S(1)}, bf16[1,128,1024]{2,1,0:T(8,128)(2,1)}, u32[]{:S(2)}) copy-start(bf16[1,128,1024]{2,1,0:T(8,128)(2,1)} %param.11) | copy-start | bytes 786436
  19.4 6.0 %copy-start.1 = (bf16[1,128,1024]{2,1,0:T(8,128)(2,1)S(1)}, bf16[1,128,1024]{2,1,0:T(8,128)(2,1)}, u32[]{:S(2)}) copy-start(bf16[1,128,1024]{2,1,0:T(8,128)(2,1)} %param.12) | copy-start | bytes 786436
  21.2 12.2 %collective-permute-start.9 = (bf16[512,128]{1,0:T(8,128)(2,1)S(1)}, bf16[512,128]{1,0:T(8,128)(2,1)S(1)}, u32[]{:S(2)}, u32[]{:S(2)}) collective-permute-start(bf16[512,128]{1,0:T(8,128)(2,1)S(1)} %decode.1.a), channel_id=1, source_target_pairs={{0,48},{16,32},{32,16},{48,0},{1,49},{17,33},{33,17},{49,1},{2,50}... | collective-permute-start | bytes 393224 | tf_op jit(solution)/shard_map/ppermute | solution.py:324
  21.4 15.7 %collective-permute-start.8 = (bf16[512,128]{1,0:T(8,128)(2,1)S(1)}, bf16[512,128]{1,0:T(8,128)(2,1)S(1)}, u32[]{:S(2)}, u32[]{:S(2)}) collective-permute-start(bf16[512,128]{1,0:T(8,128)(2,1)S(1)} %decode.1.a), channel_id=1, source_target_pairs={{0,32},{16,48},{32,0},{48,16},{1,33},{17,49},{33,1},{49,17},{2,34}... | collective-permute-start | bytes 393224 | tf_op jit(solution)/shard_map/ppermute | solution.py:324
  25.0 12.6 %collective-permute-start.7 = (bf16[512,128]{1,0:T(8,128)(2,1)S(1)}, bf16[512,128]{1,0:T(8,128)(2,1)S(1)}, u32[]{:S(2)}, u32[]{:S(2)}) collective-permute-start(bf16[512,128]{1,0:T(8,128)(2,1)S(1)} %decode.1.a), channel_id=1, source_target_pairs={{0,16},{16,0},{32,48},{48,32},{1,17},{17,1},{33,49},{49,33},{2,18}... | collective-permute-start | bytes 393224 | tf_op jit(solution)/shard_map/ppermute | solution.py:324
  25.4 7.4 %copy-start.3 = (s32[1,32]{1,0:T(1,128)S(1)}, s32[1,32]{1,0:T(1,128)}, u32[]{:S(2)}) copy-start(s32[1,32]{1,0:T(1,128)} %ids.2) | copy-start | bytes 388
  26.2 17.2 %collective-permute-start = (bf16[128,2048]{1,0:T(8,128)(2,1)}, bf16[128,2048]{1,0:T(8,128)(2,1)S(1)}, u32[]{:S(2)}, u32[]{:S(2)}) collective-permute-start(bf16[128,2048]{1,0:T(8,128)(2,1)} %pad_maximum_fusion), channel_id=1, source_target_pairs={{0,1},{1,0},{2,3},{3,2},{4,5},{5,4},{6,7},{7,6},{8,9},{9,8},{10,11... | collective-permute-start | bytes 1572872 | tf_op jit(solution)/shard_map/ppermute | solution.py:360
  33.4 18.3 %collective-permute-start.13 = (bf16[1024,128]{1,0:T(8,128)(2,1)S(1)}, bf16[1024,128]{1,0:T(8,128)(2,1)S(1)}, u32[]{:S(2)}, u32[]{:S(2)}) collective-permute-start(bf16[1024,128]{1,0:T(8,128)(2,1)S(1)} %bitcast.17), channel_id=1, source_target_pairs={{0,48},{16,32},{32,16},{48,0},{1,49},{17,33},{33,17},{49,1},{2,50}... | collective-permute-start | bytes 786440 | tf_op jit(solution)/shard_map/ppermute | solution.py:324
  33.5 18.2 %collective-permute-start.12 = (bf16[1024,128]{1,0:T(8,128)(2,1)S(1)}, bf16[1024,128]{1,0:T(8,128)(2,1)}, u32[]{:S(2)}, u32[]{:S(2)}) collective-permute-start(bf16[1024,128]{1,0:T(8,128)(2,1)S(1)} %bitcast.18), channel_id=1, source_target_pairs={{0,32},{16,48},{32,0},{48,16},{1,33},{17,49},{33,1},{49,17},{2,34}... | collective-permute-start | bytes 786440 | tf_op jit(solution)/shard_map/ppermute | solution.py:324
  37.1 14.6 %collective-permute-start.11 = (bf16[1024,128]{1,0:T(8,128)(2,1)S(1)}, bf16[1024,128]{1,0:T(8,128)(2,1)}, u32[]{:S(2)}, u32[]{:S(2)}) collective-permute-start(bf16[1024,128]{1,0:T(8,128)(2,1)S(1)} %bitcast.19), channel_id=1, source_target_pairs={{0,16},{16,0},{32,48},{48,32},{1,17},{17,1},{33,49},{49,33},{2,18}... | collective-permute-start | bytes 786440 | tf_op jit(solution)/shard_map/ppermute | solution.py:324
  39.6 23.1 %all-to-all-start.1 = ((bf16[16,32,1024]{2,1,0:T(8,128)(2,1)}), bf16[16,32,1024]{2,1,0:T(8,128)(2,1)S(1)}, u32[]{:S(2)}, u32[]{:S(2)}) async-start(bf16[16,32,1024]{2,1,0:T(8,128)(2,1)} %meet.1), calls=%async_computation.1 | async-start | bytes 2097152 | tf_op jit(solution)/shard_map/all_to_all | solution.py:358
  43.4 27.0 %collective-permute-start.10 = (bf16[128,2048]{1,0:T(8,128)(2,1)}, bf16[128,2048]{1,0:T(8,128)(2,1)}, u32[]{:S(2)}, u32[]{:S(2)}) collective-permute-start(bf16[128,2048]{1,0:T(8,128)(2,1)} %pad_maximum_fusion), channel_id=1, source_target_pairs={{1,2},{2,1},{3,4},{4,3},{5,6},{6,5},{7,8},{8,7},{9,10},{10,9},{11,... | collective-permute-start | bytes 1572872 | tf_op jit(solution)/shard_map/ppermute | solution.py:361
  62.7 7.8 %copy-start.6 = (bf16[1,128,1024]{2,1,0:T(8,128)(2,1)S(1)}, bf16[1,128,1024]{2,1,0:T(8,128)(2,1)}, u32[]{:S(2)}) copy-start(bf16[1,128,1024]{2,1,0:T(8,128)(2,1)} %param.10) | copy-start | bytes 786436
  62.7 16.4 %all-to-all-start.2 = ((bf16[16,64,128]{2,1,0:T(8,128)(2,1)}), bf16[16,64,128]{2,1,0:T(8,128)(2,1)S(1)}, u32[]{:S(2)}, u32[]{:S(2)}) async-start(bf16[16,64,128]{2,1,0:T(8,128)(2,1)} %heavy.1), calls=%async_computation.2 | async-start | bytes 524288 | tf_op jit(solution)/shard_map/all_to_all | solution.py:365
  73.1 6.0 %copy-start.4 = (s32[1,64]{1,0:T(1,128)S(1)}, s32[1,64]{1,0:T(1,128)}, u32[]{:S(2)}) copy-start(s32[1,64]{1,0:T(1,128)} %ids.3) | copy-start | bytes 772

commit v12 on v11

--- a/solution.py
+++ b/solution.py
@@ -138,7 +138,7 @@
     )(q_kv, *kvs)
 
 
-def light_kernel(q, k, v, even, odd, rows_in, out, rows_out, sem):
+def light_kernel(q, k, v, even, odd, cross, rows_in, out, rows_out, sem):
     count = rows_in.shape[0] // 4
     copies = [
         pltpu.make_async_copy(rows_in.at[pl.ds(n * count, count)], rows_out.at[pl.ds(n * count, count)], sem.at[n])
@@ -163,30 +163,30 @@
         two = jnp.concatenate([jnp.where(low, qq, zero), jnp.where(low, zero, qq)], axis=0)
         own = nt(two, k[:, c])
         first = jnp.where(sees_even, nt(two, even[:, c]), f32(-1e30))
-        second = jnp.where(sees_odd, nt(two, odd[:, c]), f32(-1e30))
+        second = jnp.where(sees_odd, nt(two, odd[:, c] + cross[:, c]), f32(-1e30))
         peak = jnp.maximum(jnp.maximum(own, first), second).max(axis=1, keepdims=True)
         po, pe, pd = (jnp.exp2((s - peak) * (SCALE * LOG2E)) for s in (own, first, second))
         total = (po + pe + pd).sum(axis=1, keepdims=True)
-        o = nn(po.astype(bf16), v[:, c]) + nn(pe.astype(bf16), even[:, cv]) + nn(pd.astype(bf16), odd[:, cv])
+        o = nn(po.astype(bf16), v[:, c]) + nn(pe.astype(bf16), even[:, cv]) + nn(pd.astype(bf16), odd[:, cv] + cross[:, cv])
         o = o / total
         out[:, c] = jnp.where(low, o[:rows], o[rows:])
     for copy in copies:
         copy.wait()
 
 
-def light_attend(q, k, v, even, odd, decoded):
+def light_attend(q, k, v, even, odd, cross, decoded):
     vmem = pl.BlockSpec(memory_space=pltpu.VMEM)
     hbm = pl.BlockSpec(memory_space=pl.ANY)
     return pl.pallas_call(
         light_kernel,
-        in_specs=[vmem] * 5 + [hbm],
+        in_specs=[vmem] * 6 + [hbm],
         out_specs=(vmem, hbm),
         out_shape=(jax.ShapeDtypeStruct(q.shape, f32), jax.ShapeDtypeStruct(decoded.shape, bf16)),
         scratch_shapes=[pltpu.SemaphoreType.DMA((4,))],
         compiler_params=params(12),
         cost_estimate=pl.CostEstimate(flops=3_000_000_000, transcendentals=800_000, bytes_accessed=2_000_000),
         name="light",
-    )(q, k, v, even, odd, decoded)
+    )(q, k, v, even, odd, cross, decoded)
 
 
 def join_kernel(ids, light, heavy, out, both, sem):
@@ -336,8 +336,6 @@
     side = 4
     width = q_light.shape[2]
 
-    light_kv = jnp.concatenate([k_light[0], v_light[0]], axis=1)
-
     def rows_of(value):
         return [value] + around(value, "fine", 1, side)
 
@@ -346,25 +344,28 @@
 
     chunks = pack(q_heavy[0], k_heavy[0], v_heavy[0])
     enc = square(stack(rows_of(enc_kv[0]), chunks))
+    light_kv = jnp.concatenate([after_all(k_light[0], enc[0]), v_light[0]], axis=1)
+    odd_pairs = [(i, (i - 1 ^ 1) + 1) for i in range(1, n_seq - 1)]
+    even = lax.ppermute(light_kv, TOKENS, [(i, i ^ 1) for i in range(n_seq)])
+    odd = lax.ppermute(light_kv, TOKENS, [(i, j) for i, j in odd_pairs if i // n_fine == j // n_fine])
+    cross = lax.ppermute(light_kv, TOKENS, [(i, j) for i, j in odd_pairs if i // n_fine != j // n_fine])
+
     group = lax.all_to_all(after_all(chunks, enc[0]), "fine", 0, 0, tiled=True)
 
     dec_rows = dec_queries.shape[1] // n_fine
     part = decode(dec_queries[0], enc, dec_rows)
 
     parts = around(part, "coarse")
-    own = pick(key_ids, after_all(group, part, light_kv)).reshape(KGRP * BLOCK, LANES)
+    own = pick(key_ids, after_all(group, part, cross)).reshape(KGRP * BLOCK, LANES)
     routed = [own] + around(own, "coarse")
     share = meet([after_all(part, own)] + parts, n_fine, dec_rows, width)
     decoded = lax.all_to_all(share, "fine", 0, 0, tiled=True)
 
-    even = lax.ppermute(light_kv, TOKENS, [(i, i ^ 1) for i in range(n_seq)])
-    odd = lax.ppermute(after_all(light_kv, share), TOKENS, [(i, (i - 1 ^ 1) + 1) for i in range(1, n_seq - 1)])
-
-    heavy = heavy_attend(after_all(group, even), routed)
+    heavy = heavy_attend(after_all(group, even, odd), routed)
     heavy, decoded = lax.optimization_barrier((heavy, decoded))
     heavy = lax.all_to_all(heavy, "fine", 0, 0, tiled=True)
     light, decoded = light_attend(
-        q_light[0], k_light[0], v_light[0], even, odd, decoded.reshape(-1, width)
+        q_light[0], k_light[0], v_light[0], even, odd, cross, decoded.reshape(-1, width)
     )
     encoded = join(query_ids, light, heavy)[None]
     return (encoded, decoded[None])

time: 81.2 us -> 88 us (1.084)
  the two profiles are of different devices: /device:TPU:64 before, /device:TPU:0 now
where the time goes in v12:
time: 88 us; the launch traced here: 87.5 us
  starting transfers between devices  41.5 us (47%)
  Pallas kernels  22.5 us (26%)
  waiting for transfers between devices  19 us (22%)
  local copies, waits for them, and re-layouts  2.54 us (3%)
  between operations  1.02 us (1%)
    ppermute x12, starting transfers between devices, around(): return [lax.ppermute(value, axis, pairs(d)) for d in range(1, ring)]  19.5 us
    pallas_call x1, Pallas kernels, heavy_attend(): pl.pallas_call(heavy_kernel, in_specs=[vmem] * 2 + [pl.BlockSpec(memory_s...  11.8 us
    all_to_all x1, starting transfers between devices, local(): group = lax.all_to_all(after_all(chunks, enc[0]), 'fine', 0, 0, tiled=True)  9.31 us
    ppermute x12, waiting for transfers between devices, around(): return [lax.ppermute(value, axis, pairs(d)) for d in range(1, ring)]  9.21 us
    all_to_all x1, waiting for transfers between devices, local(): heavy = lax.all_to_all(heavy, 'fine', 0, 0, tiled=True)  4.99 us
    all_to_all x1, starting transfers between devices, local(): decoded = lax.all_to_all(share, 'fine', 0, 0, tiled=True)  4.89 us
    all_to_all x1, waiting for transfers between devices, local(): group = lax.all_to_all(after_all(chunks, enc[0]), 'fine', 0, 0, tiled=True)  4.83 us
    all_to_all x1, starting transfers between devices, local(): heavy = lax.all_to_all(heavy, 'fine', 0, 0, tiled=True)  3.68 us
  transfers between devices with their start and end apart: 18, of which 6 were waited for; matrix products, arithmetic and copies ran while one was open for 1% of the time, Pallas kernels for 24%

profile of v12, /device:TPU:0, one launch (start us, length us, event | category | flops | bytes accessed | tf_op | source)
XLA Modules:
  0.0 87.5 jit_solution(11039606325808309017)
XLA Ops:
  0.6 1.7 %collective-permute-start = (bf16[128,128]{1,0:T(8,128)(2,1)}, bf16[128,128]{1,0:T(8,128)(2,1)S(1)}, u32[]{:S(2)}, u32[]{:S(2)}) collective-permute-start(bf16[128,128]{1,0:T(8,128)(2,1)} %bitcast.21), channel_id=1, source_target_pairs={{0,1},{1,0},{2,3},{3,2},{4,5},{5,4},{6,7},{7,6},{8,9},{9,8},{10,11... | collective-permute-start | bytes 98312 | tf_op jit(solution)/shard_map/ppermute | solution.py:324
  2.3 2.7 %collective-permute-start.1 = (bf16[128,128]{1,0:T(8,128)(2,1)}, bf16[128,128]{1,0:T(8,128)(2,1)S(1)}, u32[]{:S(2)}, u32[]{:S(2)}) collective-permute-start(bf16[128,128]{1,0:T(8,128)(2,1)} %bitcast.22), channel_id=1, source_target_pairs={{0,2},{1,3},{2,0},{3,1},{4,6},{5,7},{6,4},{7,5},{8,10},{9,11},{10,... | collective-permute-start | bytes 98312 | tf_op jit(solution)/shard_map/ppermute | solution.py:324
  5.0 0.4 collective-permute-start.2
  5.4 2.3 %pack.1.refs_4_ = bf16[16,192,128]{2,1,0:T(8,128)(2,1)} custom-call(bf16[128,1024]{1,0:T(8,128)(2,1)} %bitcast.27, bf16[128,1024]{1,0:T(8,128)(2,1)} %bitcast.28, bf16[128,1024]{1,0:T(8,128)(2,1)} %bitcast.29), custom_call_target="tpu_custom_call" | custom-call | tf_op jit(solution)/shard_map/pack/pallas_call | solution.py:60
  7.9 2.4 %collective-permute-done.2.refs_3_ = bf16[128,128]{1,0:T(8,128)(2,1)S(1)} collective-permute-done((bf16[128,128]{1,0:T(8,128)(2,1)}, bf16[128,128]{1,0:T(8,128)(2,1)S(1)}, u32[]{:S(2)}, u32[]{:S(2)}) %collective-permute-start.2) | collective-permute-done | bytes 32800 | tf_op jit(solution)/shard_map/ppermute | solution.py:324
  10.4 1.7 %collective-permute-start.6 = (bf16[512,128]{1,0:T(8,128)(2,1)S(1)}, bf16[512,128]{1,0:T(8,128)(2,1)S(1)}, u32[]{:S(2)}, u32[]{:S(2)}) collective-permute-start(bf16[512,128]{1,0:T(8,128)(2,1)S(1)} %stack.1.e0), channel_id=1, source_target_pairs={{0,4},{1,5},{2,6},{3,7},{4,0},{5,1},{6,2},{7,3},{8,12},{9,13},{10,... | collective-permute-start | bytes 393224 | tf_op jit(solution)/shard_map/ppermute | solution.py:324
  12.0 2.9 %collective-permute-start.7 = (bf16[512,128]{1,0:T(8,128)(2,1)S(1)}, bf16[512,128]{1,0:T(8,128)(2,1)S(1)}, u32[]{:S(2)}, u32[]{:S(2)}) collective-permute-start(bf16[512,128]{1,0:T(8,128)(2,1)S(1)} %stack.1.e0), channel_id=1, source_target_pairs={{0,8},{1,9},{2,10},{3,11},{4,12},{5,13},{6,14},{7,15},{8,0},{9,1},... | collective-permute-start | bytes 393224 | tf_op jit(solution)/shard_map/ppermute | solution.py:324
  15.2 0.8 pad_maximum_fusion
  16.0 0.8 collective-permute-start.5
  16.8 9.3 %all-to-all-start = ((bf16[16,192,128]{2,1,0:T(8,128)(2,1)}), bf16[16,192,128]{2,1,0:T(8,128)(2,1)S(1)}, u32[]{:S(2)}, u32[]{:S(2)}) async-start(bf16[16,192,128]{2,1,0:T(8,128)(2,1)} %pack.1.refs_4_), calls=%async_computation | async-start | bytes 1572864 | tf_op jit(solution)/shard_map/all_to_all | solution.py:353
  26.2 0.6 copy-done.9
  26.8 0.9 %copy-done.10 = bf16[512,128]{1,0:T(8,128)(2,1)S(1)} copy-done((bf16[512,128]{1,0:T(8,128)(2,1)S(1)}, bf16[512,128]{1,0:T(8,128)(2,1)}, u32[]{:S(2)}) %copy-start.10) | copy-done | bytes 131096
  27.7 1.8 %decode.1.a = bf16[512,128]{1,0:T(8,128)(2,1)S(1)} custom-call(bf16[512,1024]{1,0:T(8,128)(2,1)S(1)} %bitcast.25, bf16[512,128]{1,0:T(8,128)(2,1)S(1)} %stack.1.e0, bf16[512,128]{1,0:T(8,128)(2,1)S(1)} %collective-permute-done.6.e1, bf16[512,128]{1,0:T(8,128)(2,1)S(1)} %collective-permute-done.7.e2, bf16[512,128]{1,0:T(8,128)(2,1)S(1)} %copy-done.10), custom_call_target="tpu_custom_call" | custom-call | flops 30000001024 | bytes 1000000 | tf_op jit(solution)/shard_map/decode/pallas_call | solution.py:258
  29.5 2.0 %collective-permute-start.12 = (bf16[512,128]{1,0:T(8,128)(2,1)S(1)}, bf16[512,128]{1,0:T(8,128)(2,1)S(1)}, u32[]{:S(2)}, u32[]{:S(2)}) collective-permute-start(bf16[512,128]{1,0:T(8,128)(2,1)S(1)} %decode.1.a), channel_id=1, source_target_pairs={{0,16},{16,0},{32,48},{48,32},{1,17},{17,1},{33,49},{49,33},{2,18}... | collective-permute-start | bytes 393224 | tf_op jit(solution)/shard_map/ppermute | solution.py:324
  31.5 1.9 %collective-permute-start.13 = (bf16[512,128]{1,0:T(8,128)(2,1)S(1)}, bf16[512,128]{1,0:T(8,128)(2,1)S(1)}, u32[]{:S(2)}, u32[]{:S(2)}) collective-permute-start(bf16[512,128]{1,0:T(8,128)(2,1)S(1)} %decode.1.a), channel_id=1, source_target_pairs={{0,32},{16,48},{32,0},{48,16},{1,33},{17,49},{33,1},{49,17},{2,34}... | collective-permute-start | bytes 393224 | tf_op jit(solution)/shard_map/ppermute | solution.py:324
  33.4 0.9 %collective-permute-start.14 = (bf16[512,128]{1,0:T(8,128)(2,1)S(1)}, bf16[512,128]{1,0:T(8,128)(2,1)S(1)}, u32[]{:S(2)}, u32[]{:S(2)}) collective-permute-start(bf16[512,128]{1,0:T(8,128)(2,1)S(1)} %decode.1.a), channel_id=1, source_target_pairs={{0,48},{16,32},{32,16},{48,0},{1,49},{17,33},{33,17},{49,1},{2,50}... | collective-permute-start | bytes 393224 | tf_op jit(solution)/shard_map/ppermute | solution.py:324
  34.3 1.9 %collective-permute-start.3 = (bf16[128,2048]{1,0:T(8,128)(2,1)}, bf16[128,2048]{1,0:T(8,128)(2,1)S(1)}, u32[]{:S(2)}, u32[]{:S(2)}) collective-permute-start(bf16[128,2048]{1,0:T(8,128)(2,1)} %pad_maximum_fusion), channel_id=1, source_target_pairs={{0,1},{1,0},{2,3},{3,2},{4,5},{5,4},{6,7},{7,6},{8,9},{9,8},{10,11... | collective-permute-start | bytes 1572872 | tf_op jit(solution)/shard_map/ppermute | solution.py:349
  36.2 1.5 %collective-permute-start.4 = (bf16[128,2048]{1,0:T(8,128)(2,1)}, bf16[128,2048]{1,0:T(8,128)(2,1)}, u32[]{:S(2)}, u32[]{:S(2)}) collective-permute-start(bf16[128,2048]{1,0:T(8,128)(2,1)} %pad_maximum_fusion), channel_id=1, source_target_pairs={{1,2},{2,1},{3,4},{4,3},{5,6},{6,5},{7,8},{8,7},{9,10},{10,9},{11,... | collective-permute-start | bytes 1572872 | tf_op jit(solution)/shard_map/ppermute | solution.py:350
  37.7 4.8 %all-to-all-done.kv.q = bf16[16,192,128]{2,1,0:T(8,128)(2,1)S(1)} async-done(((bf16[16,192,128]{2,1,0:T(8,128)(2,1)}), bf16[16,192,128]{2,1,0:T(8,128)(2,1)S(1)}, u32[]{:S(2)}, u32[]{:S(2)}) %all-to-all-start) | async-done | bytes 786464 | tf_op jit(solution)/shard_map/all_to_all | solution.py:353
  42.5 0.6 pick.1
  43.1 2.0 %collective-permute-start.9 = (bf16[1024,128]{1,0:T(8,128)(2,1)S(1)}, bf16[1024,128]{1,0:T(8,128)(2,1)S(1)}, u32[]{:S(2)}, u32[]{:S(2)}) collective-permute-start(bf16[1024,128]{1,0:T(8,128)(2,1)S(1)} %bitcast.17), channel_id=1, source_target_pairs={{0,16},{16,0},{32,48},{48,32},{1,17},{17,1},{33,49},{49,33},{2,18}... | collective-permute-start | bytes 786440 | tf_op jit(solution)/shard_map/ppermute | solution.py:324
  45.1 3.1 %collective-permute-start.10 = (bf16[1024,128]{1,0:T(8,128)(2,1)S(1)}, bf16[1024,128]{1,0:T(8,128)(2,1)}, u32[]{:S(2)}, u32[]{:S(2)}) collective-permute-start(bf16[1024,128]{1,0:T(8,128)(2,1)S(1)} %bitcast.18), channel_id=1, source_target_pairs={{0,32},{16,48},{32,0},{48,16},{1,33},{17,49},{33,1},{49,17},{2,34}... | collective-permute-start | bytes 786440 | tf_op jit(solution)/shard_map/ppermute | solution.py:324
  48.2 2.0 %meet.1 = bf16[16,32,1024]{2,1,0:T(8,128)(2,1)} custom-call(bf16[512,128]{1,0:T(8,128)(2,1)S(1)} %decode.1.a, bf16[512,128]{1,0:T(8,128)(2,1)S(1)} %collective-permute-done.12.b, bf16[512,128]{1,0:T(8,128)(2,1)S(1)} %collective-permute-done.13.c, bf16[512,128]{1,0:T(8,128)(2,1)S(1)} %collective-permute-done.14.d), custom_call_target="tpu_custom_call" | custom-call | flops 30000001024 | bytes 2000000 | tf_op jit(solution)/shard_map/meet/pallas_call | solution.py:289
  50.3 4.9 %all-to-all-start.1 = ((bf16[16,32,1024]{2,1,0:T(8,128)(2,1)}), bf16[16,32,1024]{2,1,0:T(8,128)(2,1)S(1)}, u32[]{:S(2)}, u32[]{:S(2)}) async-start(bf16[16,32,1024]{2,1,0:T(8,128)(2,1)} %meet.1), calls=%async_computation.1 | async-start | bytes 2097152 | tf_op jit(solution)/shard_map/all_to_all | solution.py:362
  55.2 3.9 %collective-permute-done.10.kv2 = bf16[1024,128]{1,0:T(8,128)(2,1)} collective-permute-done((bf16[1024,128]{1,0:T(8,128)(2,1)S(1)}, bf16[1024,128]{1,0:T(8,128)(2,1)}, u32[]{:S(2)}, u32[]{:S(2)}) %collective-permute-start.10) | collective-permute-done | bytes 262176 | tf_op jit(solution)/shard_map/ppermute | solution.py:324
  59.1 2.7 %collective-permute-done.11.kv3 = bf16[1024,128]{1,0:T(8,128)(2,1)} collective-permute-done((bf16[1024,128]{1,0:T(8,128)(2,1)S(1)}, bf16[1024,128]{1,0:T(8,128)(2,1)}, u32[]{:S(2)}, u32[]{:S(2)}) %collective-permute-start.11) | collective-permute-done | bytes 262176 | tf_op jit(solution)/shard_map/ppermute | solution.py:324
  61.8 11.8 %heavy.1 = bf16[16,64,128]{2,1,0:T(8,128)(2,1)} custom-call(bf16[16,192,128]{2,1,0:T(8,128)(2,1)S(1)} %all-to-all-done.kv.q, bf16[1024,128]{1,0:T(8,128)(2,1)S(1)} %bitcast.20, bf16[1024,128]{1,0:T(8,128)(2,1)S(1)} %collective-permute-done.9.kv1, bf16[1024,128]{1,0:T(8,128)(2,1)} %collective-permute-done.10.kv2, bf16[1024,128]{1,0:T(8,128)(2,1)} %collective-permute-done.11.kv3), custom_call_target="tpu_custom_call" | custom-call | flops 10000000000 | bytes 2000000 | tf_op jit(solution)/shard_map/heavy/pallas_call | solution.py:130
  73.5 3.7 %all-to-all-start.2 = ((bf16[16,64,128]{2,1,0:T(8,128)(2,1)}), bf16[16,64,128]{2,1,0:T(8,128)(2,1)S(1)}, u32[]{:S(2)}, u32[]{:S(2)}) async-start(bf16[16,64,128]{2,1,0:T(8,128)(2,1)} %heavy.1), calls=%async_computation.2 | async-start | bytes 524288 | tf_op jit(solution)/shard_map/all_to_all | solution.py:366
  77.2 0.9 %copy-done.8 = bf16[1,128,1024]{2,1,0:T(8,128)(2,1)S(1)} copy-done((bf16[1,128,1024]{2,1,0:T(8,128)(2,1)S(1)}, bf16[1,128,1024]{2,1,0:T(8,128)(2,1)}, u32[]{:S(2)}) %copy-start.8) | copy-done | bytes 262168
  78.2 2.7 %light.1 = (f32[128,1024]{1,0:T(8,128)S(1)}, bf16[512,1024]{1,0:T(8,128)(2,1)}) custom-call(bf16[128,1024]{1,0:T(8,128)(2,1)S(1)} %bitcast.26, bf16[128,1024]{1,0:T(8,128)(2,1)S(1)} %bitcast.14, bf16[128,1024]{1,0:T(8,128)(2,1)S(1)} %bitcast.16, bf16[128,2048]{1,0:T(8,128)(2,1)S(1)} %collective-permute-done.3.even, ...), custom_call_target="tpu_custom_call" | custom-call | flops 3000000000 | bytes 2000000 | tf_op jit(solution)/shard_map/light/pallas_call | solution.py:180
  80.9 5.0 %all-to-all-done.2.heavy = bf16[16,64,128]{2,1,0:T(8,128)(2,1)S(1)} async-done(((bf16[16,64,128]{2,1,0:T(8,128)(2,1)}), bf16[16,64,128]{2,1,0:T(8,128)(2,1)S(1)}, u32[]{:S(2)}, u32[]{:S(2)}) %all-to-all-start.2) | async-done | bytes 262176 | tf_op jit(solution)/shard_map/all_to_all | solution.py:366
  85.9 1.4 %join.1 = bf16[128,1024]{1,0:T(8,128)(2,1)} custom-call(s32[1,64]{1,0:T(1,128)S(1)} %copy-done.4, f32[128,1024]{1,0:T(8,128)S(1)} %get-tuple-element.17.light, bf16[16,64,128]{2,1,0:T(8,128)(2,1)S(1)} %all-to-all-done.2.heavy), custom_call_target="tpu_custom_call" | custom-call | tf_op jit(solution)/shard_map/join/pallas_call | solution.py:218
  (35 shorter events, 0.5 us)
Async XLA Ops:
  0.6 7.1 %collective-permute-start = (bf16[128,128]{1,0:T(8,128)(2,1)}, bf16[128,128]{1,0:T(8,128)(2,1)S(1)}, u32[]{:S(2)}, u32[]{:S(2)}) collective-permute-start(bf16[128,128]{1,0:T(8,128)(2,1)} %bitcast.21), channel_id=1, source_target_pairs={{0,1},{1,0},{2,3},{3,2},{4,5},{5,4},{6,7},{7,6},{8,9},{9,8},{10,11... | collective-permute-start | bytes 98312 | tf_op jit(solution)/shard_map/ppermute | solution.py:324
  2.3 5.6 %collective-permute-start.1 = (bf16[128,128]{1,0:T(8,128)(2,1)}, bf16[128,128]{1,0:T(8,128)(2,1)S(1)}, u32[]{:S(2)}, u32[]{:S(2)}) collective-permute-start(bf16[128,128]{1,0:T(8,128)(2,1)} %bitcast.22), channel_id=1, source_target_pairs={{0,2},{1,3},{2,0},{3,1},{4,6},{5,7},{6,4},{7,5},{8,10},{9,11},{10,... | collective-permute-start | bytes 98312 | tf_op jit(solution)/shard_map/ppermute | solution.py:324
  5.0 5.3 %collective-permute-start.2 = (bf16[128,128]{1,0:T(8,128)(2,1)}, bf16[128,128]{1,0:T(8,128)(2,1)S(1)}, u32[]{:S(2)}, u32[]{:S(2)}) collective-permute-start(bf16[128,128]{1,0:T(8,128)(2,1)} %bitcast.23), channel_id=1, source_target_pairs={{0,3},{1,2},{2,1},{3,0},{4,7},{5,6},{6,5},{7,4},{8,11},{9,10},{10,... | collective-permute-start | bytes 98312 | tf_op jit(solution)/shard_map/ppermute | solution.py:324
  5.4 4.9 %copy-start.2 = (bf16[1,128,128]{2,1,0:T(8,128)(2,1)S(1)}, bf16[1,128,128]{2,1,0:T(8,128)(2,1)}, u32[]{:S(2)}) copy-start(bf16[1,128,128]{2,1,0:T(8,128)(2,1)} %param.16) | copy-start | bytes 98308
  7.7 7.4 %copy-start = (bf16[1,128,1024]{2,1,0:T(8,128)(2,1)S(1)}, bf16[1,128,1024]{2,1,0:T(8,128)(2,1)}, u32[]{:S(2)}) copy-start(bf16[1,128,1024]{2,1,0:T(8,128)(2,1)} %param.11) | copy-start | bytes 786436
  7.7 7.4 %copy-start.1 = (bf16[1,128,1024]{2,1,0:T(8,128)(2,1)S(1)}, bf16[1,128,1024]{2,1,0:T(8,128)(2,1)}, u32[]{:S(2)}) copy-start(bf16[1,128,1024]{2,1,0:T(8,128)(2,1)} %param.12) | copy-start | bytes 786436
  10.4 15.8 %collective-permute-start.6 = (bf16[512,128]{1,0:T(8,128)(2,1)S(1)}, bf16[512,128]{1,0:T(8,128)(2,1)S(1)}, u32[]{:S(2)}, u32[]{:S(2)}) collective-permute-start(bf16[512,128]{1,0:T(8,128)(2,1)S(1)} %stack.1.e0), channel_id=1, source_target_pairs={{0,4},{1,5},{2,6},{3,7},{4,0},{5,1},{6,2},{7,3},{8,12},{9,13},{10,... | collective-permute-start | bytes 393224 | tf_op jit(solution)/shard_map/ppermute | solution.py:324
  12.0 14.1 %collective-permute-start.7 = (bf16[512,128]{1,0:T(8,128)(2,1)S(1)}, bf16[512,128]{1,0:T(8,128)(2,1)S(1)}, u32[]{:S(2)}, u32[]{:S(2)}) collective-permute-start(bf16[512,128]{1,0:T(8,128)(2,1)S(1)} %stack.1.e0), channel_id=1, source_target_pairs={{0,8},{1,9},{2,10},{3,11},{4,12},{5,13},{6,14},{7,15},{8,0},{9,1},... | collective-permute-start | bytes 393224 | tf_op jit(solution)/shard_map/ppermute | solution.py:324
  14.9 11.2 %collective-permute-start.8 = (bf16[512,128]{1,0:T(8,128)(2,1)S(1)}, bf16[512,128]{1,0:T(8,128)(2,1)S(1)}, u32[]{:S(2)}, u32[]{:S(2)}) collective-permute-start(bf16[512,128]{1,0:T(8,128)(2,1)S(1)} %stack.1.e0), channel_id=1, source_target_pairs={{0,12},{1,13},{2,14},{3,15},{4,8},{5,9},{6,10},{7,11},{8,4},{9,5},... | collective-permute-start | bytes 393224 | tf_op jit(solution)/shard_map/ppermute | solution.py:324
  16.0 10.8 %copy-start.5 = (bf16[1,512,1024]{2,1,0:T(8,128)(2,1)S(1)}, bf16[1,512,1024]{2,1,0:T(8,128)(2,1)}, u32[]{:S(2)}) copy-start(bf16[1,512,1024]{2,1,0:T(8,128)(2,1)} %param.17) | copy-start | bytes 3145732
  16.0 20.2 %collective-permute-start.5 = (bf16[128,2048]{1,0:T(8,128)(2,1)}, bf16[128,2048]{1,0:T(8,128)(2,1)S(1)}, u32[]{:S(2)}, u32[]{:S(2)}) collective-permute-start(bf16[128,2048]{1,0:T(8,128)(2,1)} %pad_maximum_fusion), channel_id=1, source_target_pairs={{15,16},{16,15},{31,32},{32,31},{47,48},{48,47},{79,80},{80,79},{9... | collective-permute-start | bytes 1572872 | tf_op jit(solution)/shard_map/ppermute | solution.py:351
  16.8 25.7 %all-to-all-start = ((bf16[16,192,128]{2,1,0:T(8,128)(2,1)}), bf16[16,192,128]{2,1,0:T(8,128)(2,1)S(1)}, u32[]{:S(2)}, u32[]{:S(2)}) async-start(bf16[16,192,128]{2,1,0:T(8,128)(2,1)} %pack.1.refs_4_), calls=%async_computation | async-start | bytes 1572864 | tf_op jit(solution)/shard_map/all_to_all | solution.py:353
  26.2 0.7 copy-start.9
  26.8 0.9 %copy-start.10 = (bf16[512,128]{1,0:T(8,128)(2,1)S(1)}, bf16[512,128]{1,0:T(8,128)(2,1)}, u32[]{:S(2)}) copy-start(bf16[512,128]{1,0:T(8,128)(2,1)} %copy-done.9) | copy-start | bytes 393220
  27.7 14.8 %copy-start.3 = (s32[1,32]{1,0:T(1,128)S(1)}, s32[1,32]{1,0:T(1,128)}, u32[]{:S(2)}) copy-start(s32[1,32]{1,0:T(1,128)} %ids.2) | copy-start | bytes 388
  29.5 13.6 %collective-permute-start.12 = (bf16[512,128]{1,0:T(8,128)(2,1)S(1)}, bf16[512,128]{1,0:T(8,128)(2,1)S(1)}, u32[]{:S(2)}, u32[]{:S(2)}) collective-permute-start(bf16[512,128]{1,0:T(8,128)(2,1)S(1)} %decode.1.a), channel_id=1, source_target_pairs={{0,16},{16,0},{32,48},{48,32},{1,17},{17,1},{33,49},{49,33},{2,18}... | collective-permute-start | bytes 393224 | tf_op jit(solution)/shard_map/ppermute | solution.py:324
  31.5 13.6 %collective-permute-start.13 = (bf16[512,128]{1,0:T(8,128)(2,1)S(1)}, bf16[512,128]{1,0:T(8,128)(2,1)S(1)}, u32[]{:S(2)}, u32[]{:S(2)}) collective-permute-start(bf16[512,128]{1,0:T(8,128)(2,1)S(1)} %decode.1.a), channel_id=1, source_target_pairs={{0,32},{16,48},{32,0},{48,16},{1,33},{17,49},{33,1},{49,17},{2,34}... | collective-permute-start | bytes 393224 | tf_op jit(solution)/shard_map/ppermute | solution.py:324
  33.4 14.9 %collective-permute-start.14 = (bf16[512,128]{1,0:T(8,128)(2,1)S(1)}, bf16[512,128]{1,0:T(8,128)(2,1)S(1)}, u32[]{:S(2)}, u32[]{:S(2)}) collective-permute-start(bf16[512,128]{1,0:T(8,128)(2,1)S(1)} %decode.1.a), channel_id=1, source_target_pairs={{0,48},{16,32},{32,16},{48,0},{1,49},{17,33},{33,17},{49,1},{2,50}... | collective-permute-start | bytes 393224 | tf_op jit(solution)/shard_map/ppermute | solution.py:324
  34.3 20.9 %collective-permute-start.3 = (bf16[128,2048]{1,0:T(8,128)(2,1)}, bf16[128,2048]{1,0:T(8,128)(2,1)S(1)}, u32[]{:S(2)}, u32[]{:S(2)}) collective-permute-start(bf16[128,2048]{1,0:T(8,128)(2,1)} %pad_maximum_fusion), channel_id=1, source_target_pairs={{0,1},{1,0},{2,3},{3,2},{4,5},{5,4},{6,7},{7,6},{8,9},{9,8},{10,11... | collective-permute-start | bytes 1572872 | tf_op jit(solution)/shard_map/ppermute | solution.py:349
  36.2 6.9 %copy-start.6 = (bf16[128,2048]{1,0:T(8,128)(2,1)}, bf16[128,2048]{1,0:T(8,128)(2,1)S(1)}, u32[]{:S(2)}) copy-start(bf16[128,2048]{1,0:T(8,128)(2,1)S(1)} %collective-permute-done.5.cross) | copy-start | bytes 1572868
  36.2 19.0 %collective-permute-start.4 = (bf16[128,2048]{1,0:T(8,128)(2,1)}, bf16[128,2048]{1,0:T(8,128)(2,1)}, u32[]{:S(2)}, u32[]{:S(2)}) collective-permute-start(bf16[128,2048]{1,0:T(8,128)(2,1)} %pad_maximum_fusion), channel_id=1, source_target_pairs={{1,2},{2,1},{3,4},{4,3},{5,6},{6,5},{7,8},{8,7},{9,10},{10,9},{11,... | collective-permute-start | bytes 1572872 | tf_op jit(solution)/shard_map/ppermute | solution.py:350
  43.1 12.1 %collective-permute-start.9 = (bf16[1024,128]{1,0:T(8,128)(2,1)S(1)}, bf16[1024,128]{1,0:T(8,128)(2,1)S(1)}, u32[]{:S(2)}, u32[]{:S(2)}) collective-permute-start(bf16[1024,128]{1,0:T(8,128)(2,1)S(1)} %bitcast.17), channel_id=1, source_target_pairs={{0,16},{16,0},{32,48},{48,32},{1,17},{17,1},{33,49},{49,33},{2,18}... | collective-permute-start | bytes 786440 | tf_op jit(solution)/shard_map/ppermute | solution.py:324
  45.1 14.0 %collective-permute-start.10 = (bf16[1024,128]{1,0:T(8,128)(2,1)S(1)}, bf16[1024,128]{1,0:T(8,128)(2,1)}, u32[]{:S(2)}, u32[]{:S(2)}) collective-permute-start(bf16[1024,128]{1,0:T(8,128)(2,1)S(1)} %bitcast.18), channel_id=1, source_target_pairs={{0,32},{16,48},{32,0},{48,16},{1,33},{17,49},{33,1},{49,17},{2,34}... | collective-permute-start | bytes 786440 | tf_op jit(solution)/shard_map/ppermute | solution.py:324
  48.2 13.5 %collective-permute-start.11 = (bf16[1024,128]{1,0:T(8,128)(2,1)S(1)}, bf16[1024,128]{1,0:T(8,128)(2,1)}, u32[]{:S(2)}, u32[]{:S(2)}) collective-permute-start(bf16[1024,128]{1,0:T(8,128)(2,1)S(1)} %bitcast.19), channel_id=1, source_target_pairs={{0,48},{16,32},{32,16},{48,0},{1,49},{17,33},{33,17},{49,1},{2,50}... | collective-permute-start | bytes 786440 | tf_op jit(solution)/shard_map/ppermute | solution.py:324
  50.3 23.3 %all-to-all-start.1 = ((bf16[16,32,1024]{2,1,0:T(8,128)(2,1)}), bf16[16,32,1024]{2,1,0:T(8,128)(2,1)S(1)}, u32[]{:S(2)}, u32[]{:S(2)}) async-start(bf16[16,32,1024]{2,1,0:T(8,128)(2,1)} %meet.1), calls=%async_computation.1 | async-start | bytes 2097152 | tf_op jit(solution)/shard_map/all_to_all | solution.py:362
  73.5 3.7 %copy-start.7 = (bf16[128,2048]{1,0:T(8,128)(2,1)S(1)}, bf16[128,2048]{1,0:T(8,128)(2,1)}, u32[]{:S(2)}) copy-start(bf16[128,2048]{1,0:T(8,128)(2,1)} %copy-done.6) | copy-start | bytes 1572868
  73.5 12.3 %all-to-all-start.2 = ((bf16[16,64,128]{2,1,0:T(8,128)(2,1)}), bf16[16,64,128]{2,1,0:T(8,128)(2,1)S(1)}, u32[]{:S(2)}, u32[]{:S(2)}) async-start(bf16[16,64,128]{2,1,0:T(8,128)(2,1)} %heavy.1), calls=%async_computation.2 | async-start | bytes 524288 | tf_op jit(solution)/shard_map/all_to_all | solution.py:366
  77.2 1.0 %copy-start.8 = (bf16[1,128,1024]{2,1,0:T(8,128)(2,1)S(1)}, bf16[1,128,1024]{2,1,0:T(8,128)(2,1)}, u32[]{:S(2)}) copy-start(bf16[1,128,1024]{2,1,0:T(8,128)(2,1)} %param.10) | copy-start | bytes 786436
  80.9 5.0 %copy-start.4 = (s32[1,64]{1,0:T(1,128)S(1)}, s32[1,64]{1,0:T(1,128)}, u32[]{:S(2)}) copy-start(s32[1,64]{1,0:T(1,128)} %ids.3) | copy-start | bytes 772

commit v13 on v11

--- a/solution.py
+++ b/solution.py
@@ -357,10 +357,11 @@
     share = meet([after_all(part, own)] + parts, n_fine, dec_rows, width)
     decoded = lax.all_to_all(share, "fine", 0, 0, tiled=True)
 
+    light_kv = after_all(light_kv, share)
     even = lax.ppermute(light_kv, TOKENS, [(i, i ^ 1) for i in range(n_seq)])
-    odd = lax.ppermute(after_all(light_kv, share), TOKENS, [(i, (i - 1 ^ 1) + 1) for i in range(1, n_seq - 1)])
-
-    heavy = heavy_attend(after_all(group, even), routed)
+    odd = lax.ppermute(light_kv, TOKENS, [(i, (i - 1 ^ 1) + 1) for i in range(1, n_seq - 1)])
+
+    heavy = heavy_attend(group, routed)
     heavy, decoded = lax.optimization_barrier((heavy, decoded))
     heavy = lax.all_to_all(heavy, "fine", 0, 0, tiled=True)
     light, decoded = light_attend(

time: 81.2 us -> 79.6 us (0.980)
  the two profiles are of different devices: /device:TPU:64 before, /device:TPU:0 now
where the time goes in v13:
time: 79.6 us; the launch traced here: 79.1 us
  starting transfers between devices  41.2 us (52%)
  Pallas kernels  22.1 us (28%)
  waiting for transfers between devices  14 us (18%)
  between operations  0.99 us (1%)
  other arithmetic  0.85 us (1%)
    ppermute x12, starting transfers between devices, around(): return [lax.ppermute(value, axis, pairs(d)) for d in range(1, ring)]  18.5 us
    pallas_call x1, Pallas kernels, heavy_attend(): pl.pallas_call(heavy_kernel, in_specs=[vmem] * 2 + [pl.BlockSpec(memory_s...  11 us
    all_to_all x1, starting transfers between devices, local(): heavy = lax.all_to_all(heavy, 'fine', 0, 0, tiled=True)  7.56 us
    all_to_all x1, starting transfers between devices, local(): group = lax.all_to_all(after_all(chunks, enc[0]), 'fine', 0, 0, tiled=True)  6.03 us
    all_to_all x1, waiting for transfers between devices, local(): heavy = lax.all_to_all(heavy, 'fine', 0, 0, tiled=True)  5.65 us
    ppermute x1, starting transfers between devices, local(): even = lax.ppermute(light_kv, TOKENS, [(i, i ^ 1) for i in range(n_seq)])  4.74 us
    all_to_all x1, waiting for transfers between devices, local(): group = lax.all_to_all(after_all(chunks, enc[0]), 'fine', 0, 0, tiled=True)  4.13 us
    all_to_all x1, starting transfers between devices, local(): decoded = lax.all_to_all(share, 'fine', 0, 0, tiled=True)  3.66 us
  transfers between devices with their start and end apart: 17, of which 4 were waited for; matrix products, arithmetic and copies ran while one was open for 1% of the time, Pallas kernels for 26%

profile of v13, /device:TPU:0, one launch (start us, length us, event | category | flops | bytes accessed | tf_op | source)
XLA Modules:
  0.0 79.1 jit_solution(2425826560619845663)
XLA Ops:
  0.6 2.9 %collective-permute-start.2 = (bf16[128,128]{1,0:T(8,128)(2,1)}, bf16[128,128]{1,0:T(8,128)(2,1)S(1)}, u32[]{:S(2)}, u32[]{:S(2)}) collective-permute-start(bf16[128,128]{1,0:T(8,128)(2,1)} %bitcast.21), channel_id=1, source_target_pairs={{0,3},{1,2},{2,1},{3,0},{4,7},{5,6},{6,5},{7,4},{8,11},{9,10},{10,... | collective-permute-start | bytes 98312 | tf_op jit(solution)/shard_map/ppermute | solution.py:324
  3.6 0.8 %collective-permute-start.1 = (bf16[128,128]{1,0:T(8,128)(2,1)}, bf16[128,128]{1,0:T(8,128)(2,1)S(1)}, u32[]{:S(2)}, u32[]{:S(2)}) collective-permute-start(bf16[128,128]{1,0:T(8,128)(2,1)} %bitcast.22), channel_id=1, source_target_pairs={{0,2},{1,3},{2,0},{3,1},{4,6},{5,7},{6,4},{7,5},{8,10},{9,11},{10,... | collective-permute-start | bytes 98312 | tf_op jit(solution)/shard_map/ppermute | solution.py:324
  4.4 0.5 collective-permute-start
  4.8 2.3 %pack.1.refs_4_ = bf16[16,192,128]{2,1,0:T(8,128)(2,1)} custom-call(bf16[128,1024]{1,0:T(8,128)(2,1)} %bitcast.27, bf16[128,1024]{1,0:T(8,128)(2,1)} %bitcast.28, bf16[128,1024]{1,0:T(8,128)(2,1)} %bitcast.29), custom_call_target="tpu_custom_call" | custom-call | tf_op jit(solution)/shard_map/pack/pallas_call | solution.py:60
  7.1 2.1 %collective-permute-done.1.refs_2_ = bf16[128,128]{1,0:T(8,128)(2,1)S(1)} collective-permute-done((bf16[128,128]{1,0:T(8,128)(2,1)}, bf16[128,128]{1,0:T(8,128)(2,1)S(1)}, u32[]{:S(2)}, u32[]{:S(2)}) %collective-permute-start.1) | collective-permute-done | bytes 32800 | tf_op jit(solution)/shard_map/ppermute | solution.py:324
  9.2 0.0 copy-start.5
  9.2 3.1 %collective-permute-start.5 = (bf16[512,128]{1,0:T(8,128)(2,1)S(1)}, bf16[512,128]{1,0:T(8,128)(2,1)S(1)}, u32[]{:S(2)}, u32[]{:S(2)}) collective-permute-start(bf16[512,128]{1,0:T(8,128)(2,1)S(1)} %stack.1.e0), channel_id=1, source_target_pairs={{0,12},{1,13},{2,14},{3,15},{4,8},{5,9},{6,10},{7,11},{8,4},{9,5},... | collective-permute-start | bytes 393224 | tf_op jit(solution)/shard_map/ppermute | solution.py:324
  12.3 0.6 collective-permute-start.4
  12.9 0.5 collective-permute-start.3
  13.4 6.0 %all-to-all-start = ((bf16[16,192,128]{2,1,0:T(8,128)(2,1)}), bf16[16,192,128]{2,1,0:T(8,128)(2,1)S(1)}, u32[]{:S(2)}, u32[]{:S(2)}) async-start(bf16[16,192,128]{2,1,0:T(8,128)(2,1)} %pack.1.refs_4_), calls=%async_computation | async-start | bytes 1572864 | tf_op jit(solution)/shard_map/all_to_all | solution.py:349
  19.5 0.0 copy-start
  19.5 0.0 copy-start.1
  19.5 1.8 %decode.1.a = bf16[512,128]{1,0:T(8,128)(2,1)S(1)} custom-call(bf16[512,1024]{1,0:T(8,128)(2,1)S(1)} %bitcast.25, bf16[512,128]{1,0:T(8,128)(2,1)S(1)} %stack.1.e0, bf16[512,128]{1,0:T(8,128)(2,1)S(1)} %collective-permute-done.3.e1, bf16[512,128]{1,0:T(8,128)(2,1)S(1)} %collective-permute-done.4.e2, bf16[512,128]{1,0:T(8,128)(2,1)S(1)} %collective-permute-done.5.e3), custom_call_target="tpu_custom_call" | custom-call | flops 30000001024 | bytes 1000000 | tf_op jit(solution)/shard_map/decode/pallas_call | solution.py:258
  21.3 4.1 %collective-permute-start.8 = (bf16[512,128]{1,0:T(8,128)(2,1)S(1)}, bf16[512,128]{1,0:T(8,128)(2,1)S(1)}, u32[]{:S(2)}, u32[]{:S(2)}) collective-permute-start(bf16[512,128]{1,0:T(8,128)(2,1)S(1)} %decode.1.a), channel_id=1, source_target_pairs={{0,48},{16,32},{32,16},{48,0},{1,49},{17,33},{33,17},{49,1},{2,50}... | collective-permute-start | bytes 393224 | tf_op jit(solution)/shard_map/ppermute | solution.py:324
  25.4 0.9 %collective-permute-start.6 = (bf16[512,128]{1,0:T(8,128)(2,1)S(1)}, bf16[512,128]{1,0:T(8,128)(2,1)S(1)}, u32[]{:S(2)}, u32[]{:S(2)}) collective-permute-start(bf16[512,128]{1,0:T(8,128)(2,1)S(1)} %decode.1.a), channel_id=1, source_target_pairs={{0,16},{16,0},{32,48},{48,32},{1,17},{17,1},{33,49},{49,33},{2,18}... | collective-permute-start | bytes 393224 | tf_op jit(solution)/shard_map/ppermute | solution.py:324
  26.4 0.8 %pad_maximum_fusion = bf16[128,2048]{1,0:T(8,128)(2,1)} fusion(bf16[128,1024]{1,0:T(8,128)(2,1)S(1)} %bitcast.15, bf16[128,1024]{1,0:T(8,128)(2,1)S(1)} %bitcast.13), kind=kLoop, calls=%fused_computation | loop fusion | flops 1048576 | bytes 1048576 | tf_op jit(solution)/shard_map/concatenate | solution.py:339
  27.2 4.1 %all-to-all-done.kv.q = bf16[16,192,128]{2,1,0:T(8,128)(2,1)S(1)} async-done(((bf16[16,192,128]{2,1,0:T(8,128)(2,1)}), bf16[16,192,128]{2,1,0:T(8,128)(2,1)S(1)}, u32[]{:S(2)}, u32[]{:S(2)}) %all-to-all-start) | async-done | bytes 786464 | tf_op jit(solution)/shard_map/all_to_all | solution.py:349
  31.4 0.6 pick.1
  31.9 4.1 %collective-permute-start.13 = (bf16[1024,128]{1,0:T(8,128)(2,1)S(1)}, bf16[1024,128]{1,0:T(8,128)(2,1)S(1)}, u32[]{:S(2)}, u32[]{:S(2)}) collective-permute-start(bf16[1024,128]{1,0:T(8,128)(2,1)S(1)} %bitcast.17), channel_id=1, source_target_pairs={{0,48},{16,32},{32,16},{48,0},{1,49},{17,33},{33,17},{49,1},{2,50}... | collective-permute-start | bytes 786440 | tf_op jit(solution)/shard_map/ppermute | solution.py:324
  36.1 0.9 %collective-permute-start.11 = (bf16[1024,128]{1,0:T(8,128)(2,1)S(1)}, bf16[1024,128]{1,0:T(8,128)(2,1)}, u32[]{:S(2)}, u32[]{:S(2)}) collective-permute-start(bf16[1024,128]{1,0:T(8,128)(2,1)S(1)} %bitcast.19), channel_id=1, source_target_pairs={{0,16},{16,0},{32,48},{48,32},{1,17},{17,1},{33,49},{49,33},{2,18}... | collective-permute-start | bytes 786440 | tf_op jit(solution)/shard_map/ppermute | solution.py:324
  37.0 2.0 %meet.1 = bf16[16,32,1024]{2,1,0:T(8,128)(2,1)} custom-call(bf16[512,128]{1,0:T(8,128)(2,1)S(1)} %decode.1.a, bf16[512,128]{1,0:T(8,128)(2,1)S(1)} %collective-permute-done.6.b, bf16[512,128]{1,0:T(8,128)(2,1)S(1)} %collective-permute-done.7.c, bf16[512,128]{1,0:T(8,128)(2,1)S(1)} %collective-permute-done.8.d), custom_call_target="tpu_custom_call" | custom-call | flops 30000001024 | bytes 2000000 | tf_op jit(solution)/shard_map/meet/pallas_call | solution.py:289
  39.0 3.7 %all-to-all-start.1 = ((bf16[16,32,1024]{2,1,0:T(8,128)(2,1)}), bf16[16,32,1024]{2,1,0:T(8,128)(2,1)S(1)}, u32[]{:S(2)}, u32[]{:S(2)}) async-start(bf16[16,32,1024]{2,1,0:T(8,128)(2,1)} %meet.1), calls=%async_computation.1 | async-start | bytes 2097152 | tf_op jit(solution)/shard_map/all_to_all | solution.py:358
  42.7 0.7 collective-permute-start.10
  43.4 4.7 %collective-permute-start.9 = (bf16[128,2048]{1,0:T(8,128)(2,1)}, bf16[128,2048]{1,0:T(8,128)(2,1)}, u32[]{:S(2)}, u32[]{:S(2)}) collective-permute-start(bf16[128,2048]{1,0:T(8,128)(2,1)} %pad_maximum_fusion), channel_id=1, source_target_pairs={{0,1},{1,0},{2,3},{3,2},{4,5},{5,4},{6,7},{7,6},{8,9},{9,8},{10,11... | collective-permute-start | bytes 1572872 | tf_op jit(solution)/shard_map/ppermute | solution.py:361
  48.1 11.0 %heavy.1 = bf16[16,64,128]{2,1,0:T(8,128)(2,1)} custom-call(bf16[16,192,128]{2,1,0:T(8,128)(2,1)S(1)} %all-to-all-done.kv.q, bf16[1024,128]{1,0:T(8,128)(2,1)S(1)} %bitcast.20, bf16[1024,128]{1,0:T(8,128)(2,1)} %collective-permute-done.11.kv1, bf16[1024,128]{1,0:T(8,128)(2,1)} %collective-permute-done.12.kv2, bf16[1024,128]{1,0:T(8,128)(2,1)S(1)} %collective-permute-done.13.kv3), custom_call_target="tpu_custom_call" | custom-call | flops 10000000000 | bytes 2000000 | tf_op jit(solution)/shard_map/heavy/pallas_call | solution.py:130
  59.1 0.0 copy-start.6
  59.1 2.2 %all-to-all-done.1 = bf16[16,32,1024]{2,1,0:T(8,128)(2,1)S(1)} async-done(((bf16[16,32,1024]{2,1,0:T(8,128)(2,1)}), bf16[16,32,1024]{2,1,0:T(8,128)(2,1)S(1)}, u32[]{:S(2)}, u32[]{:S(2)}) %all-to-all-start.1) | async-done | bytes 1048608 | tf_op jit(solution)/shard_map/all_to_all | solution.py:358
  61.3 7.6 %all-to-all-start.2 = ((bf16[16,64,128]{2,1,0:T(8,128)(2,1)}), bf16[16,64,128]{2,1,0:T(8,128)(2,1)S(1)}, u32[]{:S(2)}, u32[]{:S(2)}) async-start(bf16[16,64,128]{2,1,0:T(8,128)(2,1)} %heavy.1), calls=%async_computation.2 | async-start | bytes 524288 | tf_op jit(solution)/shard_map/all_to_all | solution.py:366
  68.9 3.0 %light.1 = (f32[128,1024]{1,0:T(8,128)S(1)}, bf16[512,1024]{1,0:T(8,128)(2,1)}) custom-call(bf16[128,1024]{1,0:T(8,128)(2,1)S(1)} %bitcast.26, bf16[128,1024]{1,0:T(8,128)(2,1)S(1)} %bitcast.14, bf16[128,1024]{1,0:T(8,128)(2,1)S(1)} %bitcast.16, bf16[128,2048]{1,0:T(8,128)(2,1)} %collective-permute-done.9.even, ...), custom_call_target="tpu_custom_call" | custom-call | flops 3000000000 | bytes 2000000 | tf_op jit(solution)/shard_map/light/pallas_call | solution.py:180
  71.9 0.0 copy-start.4
  71.9 5.6 %all-to-all-done.2.heavy = bf16[16,64,128]{2,1,0:T(8,128)(2,1)S(1)} async-done(((bf16[16,64,128]{2,1,0:T(8,128)(2,1)}), bf16[16,64,128]{2,1,0:T(8,128)(2,1)S(1)}, u32[]{:S(2)}, u32[]{:S(2)}) %all-to-all-start.2) | async-done | bytes 262176 | tf_op jit(solution)/shard_map/all_to_all | solution.py:366
  77.6 1.4 %join.1 = bf16[128,1024]{1,0:T(8,128)(2,1)} custom-call(s32[1,64]{1,0:T(1,128)S(1)} %copy-done.4, f32[128,1024]{1,0:T(8,128)S(1)} %get-tuple-element.15.light, bf16[16,64,128]{2,1,0:T(8,128)(2,1)S(1)} %all-to-all-done.2.heavy), custom_call_target="tpu_custom_call" | custom-call | tf_op jit(solution)/shard_map/join/pallas_call | solution.py:218
  (25 shorter events, 0.1 us)
Async XLA Ops:
  0.6 6.5 %collective-permute-start.2 = (bf16[128,128]{1,0:T(8,128)(2,1)}, bf16[128,128]{1,0:T(8,128)(2,1)S(1)}, u32[]{:S(2)}, u32[]{:S(2)}) collective-permute-start(bf16[128,128]{1,0:T(8,128)(2,1)} %bitcast.21), channel_id=1, source_target_pairs={{0,3},{1,2},{2,1},{3,0},{4,7},{5,6},{6,5},{7,4},{8,11},{9,10},{10,... | collective-permute-start | bytes 98312 | tf_op jit(solution)/shard_map/ppermute | solution.py:324
  3.6 5.6 %collective-permute-start.1 = (bf16[128,128]{1,0:T(8,128)(2,1)}, bf16[128,128]{1,0:T(8,128)(2,1)S(1)}, u32[]{:S(2)}, u32[]{:S(2)}) collective-permute-start(bf16[128,128]{1,0:T(8,128)(2,1)} %bitcast.22), channel_id=1, source_target_pairs={{0,2},{1,3},{2,0},{3,1},{4,6},{5,7},{6,4},{7,5},{8,10},{9,11},{10,... | collective-permute-start | bytes 98312 | tf_op jit(solution)/shard_map/ppermute | solution.py:324
  4.4 4.8 %collective-permute-start = (bf16[128,128]{1,0:T(8,128)(2,1)}, bf16[128,128]{1,0:T(8,128)(2,1)S(1)}, u32[]{:S(2)}, u32[]{:S(2)}) collective-permute-start(bf16[128,128]{1,0:T(8,128)(2,1)} %bitcast.23), channel_id=1, source_target_pairs={{0,1},{1,0},{2,3},{3,2},{4,5},{5,4},{6,7},{7,6},{8,9},{9,8},{10,11... | collective-permute-start | bytes 98312 | tf_op jit(solution)/shard_map/ppermute | solution.py:324
  4.8 4.4 %copy-start.2 = (bf16[1,128,128]{2,1,0:T(8,128)(2,1)S(1)}, bf16[1,128,128]{2,1,0:T(8,128)(2,1)}, u32[]{:S(2)}) copy-start(bf16[1,128,128]{2,1,0:T(8,128)(2,1)} %param.16) | copy-start | bytes 98308
  9.2 10.3 %copy-start.5 = (bf16[1,512,1024]{2,1,0:T(8,128)(2,1)S(1)}, bf16[1,512,1024]{2,1,0:T(8,128)(2,1)}, u32[]{:S(2)}) copy-start(bf16[1,512,1024]{2,1,0:T(8,128)(2,1)} %param.17) | copy-start | bytes 3145732
  9.2 10.2 %collective-permute-start.5 = (bf16[512,128]{1,0:T(8,128)(2,1)S(1)}, bf16[512,128]{1,0:T(8,128)(2,1)S(1)}, u32[]{:S(2)}, u32[]{:S(2)}) collective-permute-start(bf16[512,128]{1,0:T(8,128)(2,1)S(1)} %stack.1.e0), channel_id=1, source_target_pairs={{0,12},{1,13},{2,14},{3,15},{4,8},{5,9},{6,10},{7,11},{8,4},{9,5},... | collective-permute-start | bytes 393224 | tf_op jit(solution)/shard_map/ppermute | solution.py:324
  12.3 7.1 %collective-permute-start.4 = (bf16[512,128]{1,0:T(8,128)(2,1)S(1)}, bf16[512,128]{1,0:T(8,128)(2,1)S(1)}, u32[]{:S(2)}, u32[]{:S(2)}) collective-permute-start(bf16[512,128]{1,0:T(8,128)(2,1)S(1)} %stack.1.e0), channel_id=1, source_target_pairs={{0,8},{1,9},{2,10},{3,11},{4,12},{5,13},{6,14},{7,15},{8,0},{9,1},... | collective-permute-start | bytes 393224 | tf_op jit(solution)/shard_map/ppermute | solution.py:324
  12.9 6.5 %collective-permute-start.3 = (bf16[512,128]{1,0:T(8,128)(2,1)S(1)}, bf16[512,128]{1,0:T(8,128)(2,1)S(1)}, u32[]{:S(2)}, u32[]{:S(2)}) collective-permute-start(bf16[512,128]{1,0:T(8,128)(2,1)S(1)} %stack.1.e0), channel_id=1, source_target_pairs={{0,4},{1,5},{2,6},{3,7},{4,0},{5,1},{6,2},{7,3},{8,12},{9,13},{10,... | collective-permute-start | bytes 393224 | tf_op jit(solution)/shard_map/ppermute | solution.py:324
  13.4 18.0 %all-to-all-start = ((bf16[16,192,128]{2,1,0:T(8,128)(2,1)}), bf16[16,192,128]{2,1,0:T(8,128)(2,1)S(1)}, u32[]{:S(2)}, u32[]{:S(2)}) async-start(bf16[16,192,128]{2,1,0:T(8,128)(2,1)} %pack.1.refs_4_), calls=%async_computation | async-start | bytes 1572864 | tf_op jit(solution)/shard_map/all_to_all | solution.py:349
  19.5 6.9 %copy-start = (bf16[1,128,1024]{2,1,0:T(8,128)(2,1)S(1)}, bf16[1,128,1024]{2,1,0:T(8,128)(2,1)}, u32[]{:S(2)}) copy-start(bf16[1,128,1024]{2,1,0:T(8,128)(2,1)} %param.11) | copy-start | bytes 786436
  19.5 6.9 %copy-start.1 = (bf16[1,128,1024]{2,1,0:T(8,128)(2,1)S(1)}, bf16[1,128,1024]{2,1,0:T(8,128)(2,1)}, u32[]{:S(2)}) copy-start(bf16[1,128,1024]{2,1,0:T(8,128)(2,1)} %param.12) | copy-start | bytes 786436
  21.3 14.8 %collective-permute-start.8 = (bf16[512,128]{1,0:T(8,128)(2,1)S(1)}, bf16[512,128]{1,0:T(8,128)(2,1)S(1)}, u32[]{:S(2)}, u32[]{:S(2)}) collective-permute-start(bf16[512,128]{1,0:T(8,128)(2,1)S(1)} %decode.1.a), channel_id=1, source_target_pairs={{0,48},{16,32},{32,16},{48,0},{1,49},{17,33},{33,17},{49,1},{2,50}... | collective-permute-start | bytes 393224 | tf_op jit(solution)/shard_map/ppermute | solution.py:324
  25.4 11.6 %collective-permute-start.7 = (bf16[512,128]{1,0:T(8,128)(2,1)S(1)}, bf16[512,128]{1,0:T(8,128)(2,1)S(1)}, u32[]{:S(2)}, u32[]{:S(2)}) collective-permute-start(bf16[512,128]{1,0:T(8,128)(2,1)S(1)} %decode.1.a), channel_id=1, source_target_pairs={{0,32},{16,48},{32,0},{48,16},{1,33},{17,49},{33,1},{49,17},{2,34}... | collective-permute-start | bytes 393224 | tf_op jit(solution)/shard_map/ppermute | solution.py:324
  25.4 11.6 %collective-permute-start.6 = (bf16[512,128]{1,0:T(8,128)(2,1)S(1)}, bf16[512,128]{1,0:T(8,128)(2,1)S(1)}, u32[]{:S(2)}, u32[]{:S(2)}) collective-permute-start(bf16[512,128]{1,0:T(8,128)(2,1)S(1)} %decode.1.a), channel_id=1, source_target_pairs={{0,16},{16,0},{32,48},{48,32},{1,17},{17,1},{33,49},{49,33},{2,18}... | collective-permute-start | bytes 393224 | tf_op jit(solution)/shard_map/ppermute | solution.py:324
  26.4 5.0 %copy-start.3 = (s32[1,32]{1,0:T(1,128)S(1)}, s32[1,32]{1,0:T(1,128)}, u32[]{:S(2)}) copy-start(s32[1,32]{1,0:T(1,128)} %ids.2) | copy-start | bytes 388
  31.9 16.2 %collective-permute-start.13 = (bf16[1024,128]{1,0:T(8,128)(2,1)S(1)}, bf16[1024,128]{1,0:T(8,128)(2,1)S(1)}, u32[]{:S(2)}, u32[]{:S(2)}) collective-permute-start(bf16[1024,128]{1,0:T(8,128)(2,1)S(1)} %bitcast.17), channel_id=1, source_target_pairs={{0,48},{16,32},{32,16},{48,0},{1,49},{17,33},{33,17},{49,1},{2,50}... | collective-permute-start | bytes 786440 | tf_op jit(solution)/shard_map/ppermute | solution.py:324
  36.1 12.1 %collective-permute-start.12 = (bf16[1024,128]{1,0:T(8,128)(2,1)S(1)}, bf16[1024,128]{1,0:T(8,128)(2,1)}, u32[]{:S(2)}, u32[]{:S(2)}) collective-permute-start(bf16[1024,128]{1,0:T(8,128)(2,1)S(1)} %bitcast.18), channel_id=1, source_target_pairs={{0,32},{16,48},{32,0},{48,16},{1,33},{17,49},{33,1},{49,17},{2,34}... | collective-permute-start | bytes 786440 | tf_op jit(solution)/shard_map/ppermute | solution.py:324
  36.1 12.1 %collective-permute-start.11 = (bf16[1024,128]{1,0:T(8,128)(2,1)S(1)}, bf16[1024,128]{1,0:T(8,128)(2,1)}, u32[]{:S(2)}, u32[]{:S(2)}) collective-permute-start(bf16[1024,128]{1,0:T(8,128)(2,1)S(1)} %bitcast.19), channel_id=1, source_target_pairs={{0,16},{16,0},{32,48},{48,32},{1,17},{17,1},{33,49},{49,33},{2,18}... | collective-permute-start | bytes 786440 | tf_op jit(solution)/shard_map/ppermute | solution.py:324
  39.0 22.3 %all-to-all-start.1 = ((bf16[16,32,1024]{2,1,0:T(8,128)(2,1)}), bf16[16,32,1024]{2,1,0:T(8,128)(2,1)S(1)}, u32[]{:S(2)}, u32[]{:S(2)}) async-start(bf16[16,32,1024]{2,1,0:T(8,128)(2,1)} %meet.1), calls=%async_computation.1 | async-start | bytes 2097152 | tf_op jit(solution)/shard_map/all_to_all | solution.py:358
  42.7 26.2 %collective-permute-start.10 = (bf16[128,2048]{1,0:T(8,128)(2,1)}, bf16[128,2048]{1,0:T(8,128)(2,1)S(1)}, u32[]{:S(2)}, u32[]{:S(2)}) collective-permute-start(bf16[128,2048]{1,0:T(8,128)(2,1)} %pad_maximum_fusion), channel_id=1, source_target_pairs={{1,2},{2,1},{3,4},{4,3},{5,6},{6,5},{7,8},{8,7},{9,10},{10,9},{11,... | collective-permute-start | bytes 1572872 | tf_op jit(solution)/shard_map/ppermute | solution.py:362
  43.4 25.5 %collective-permute-start.9 = (bf16[128,2048]{1,0:T(8,128)(2,1)}, bf16[128,2048]{1,0:T(8,128)(2,1)}, u32[]{:S(2)}, u32[]{:S(2)}) collective-permute-start(bf16[128,2048]{1,0:T(8,128)(2,1)} %pad_maximum_fusion), channel_id=1, source_target_pairs={{0,1},{1,0},{2,3},{3,2},{4,5},{5,4},{6,7},{7,6},{8,9},{9,8},{10,11... | collective-permute-start | bytes 1572872 | tf_op jit(solution)/shard_map/ppermute | solution.py:361
  59.1 9.8 %copy-start.6 = (bf16[1,128,1024]{2,1,0:T(8,128)(2,1)S(1)}, bf16[1,128,1024]{2,1,0:T(8,128)(2,1)}, u32[]{:S(2)}) copy-start(bf16[1,128,1024]{2,1,0:T(8,128)(2,1)} %param.10) | copy-start | bytes 786436
  61.3 16.3 %all-to-all-start.2 = ((bf16[16,64,128]{2,1,0:T(8,128)(2,1)}), bf16[16,64,128]{2,1,0:T(8,128)(2,1)S(1)}, u32[]{:S(2)}, u32[]{:S(2)}) async-start(bf16[16,64,128]{2,1,0:T(8,128)(2,1)} %heavy.1), calls=%async_computation.2 | async-start | bytes 524288 | tf_op jit(solution)/shard_map/all_to_all | solution.py:366
  71.9 5.7 %copy-start.4 = (s32[1,64]{1,0:T(1,128)S(1)}, s32[1,64]{1,0:T(1,128)}, u32[]{:S(2)}) copy-start(s32[1,64]{1,0:T(1,128)} %ids.3) | copy-start | bytes 772

commit v14 on v13

--- a/solution.py
+++ b/solution.py
@@ -266,7 +266,7 @@
     )(q, *enc)
 
 
-def meet_kernel(a, b, c, d, out):
+def meet_kernel(a, b, c, d, out, share, sem):
     parts = [x[...].astype(f32) for x in (a, b, c, d)]
     levels = [x[:, 0:1] + x[:, 16:17] + x[:, 32:33] for x in parts]
     peak = jnp.maximum(jnp.maximum(levels[0], levels[1]), jnp.maximum(levels[2], levels[3]))
@@ -276,18 +276,23 @@
     for x, s in zip(parts[1:], scales[1:]):
         value = value + x * s
     value = (value / total).astype(bf16)
-    copies, rows, width = out.shape
+    rows, width = share.shape
     for p in range(width // LANES):
         e = value[2 * p * rows : (2 * p + 1) * rows, HEAD:]
         o = value[(2 * p + 1) * rows : (2 * p + 2) * rows, HEAD:]
-        both = jnp.concatenate([e, o], axis=1)
-        for n in range(copies):
-            out[n, :, p * LANES : (p + 1) * LANES] = both
+        share[:, p * LANES : (p + 1) * LANES] = jnp.concatenate([e, o], axis=1)
+    copies = [pltpu.make_async_copy(share, out.at[n], sem.at[n]) for n in range(out.shape[0])]
+    for copy in copies:
+        copy.start()
+    for copy in copies:
+        copy.wait()
 
 
 def meet(parts, copies, rows, width):
     return pl.pallas_call(
         meet_kernel,
+        out_specs=pl.BlockSpec(memory_space=pl.ANY),
+        scratch_shapes=[pltpu.VMEM((rows, width), bf16), pltpu.SemaphoreType.DMA((copies,))],
         out_shape=jax.ShapeDtypeStruct((copies, rows, width), bf16),
         compiler_params=params(8),
         cost_estimate=pl.CostEstimate(flops=30_000_000_000, transcendentals=0, bytes_accessed=2_000_000),

time: 79.6 us -> 79.5 us (level)
  no operation moved by 1% of the time
where the time goes in v14:
time: 79.5 us; the launch traced here: 79.1 us
  starting transfers between devices  41.2 us (52%)
  Pallas kernels  22 us (28%)
  waiting for transfers between devices  14 us (18%)
  between operations  1 us (1%)
  other arithmetic  0.85 us (1%)
    ppermute x12, starting transfers between devices, around(): return [lax.ppermute(value, axis, pairs(d)) for d in range(1, ring)]  18.5 us
    pallas_call x1, Pallas kernels, heavy_attend(): pl.pallas_call(heavy_kernel, in_specs=[vmem] * 2 + [pl.BlockSpec(memory_s...  11 us
    all_to_all x1, starting transfers between devices, local(): heavy = lax.all_to_all(heavy, 'fine', 0, 0, tiled=True)  7.55 us
    all_to_all x1, starting transfers between devices, local(): group = lax.all_to_all(after_all(chunks, enc[0]), 'fine', 0, 0, tiled=True)  6.03 us
    all_to_all x1, waiting for transfers between devices, local(): heavy = lax.all_to_all(heavy, 'fine', 0, 0, tiled=True)  5.65 us
    ppermute x1, starting transfers between devices, local(): even = lax.ppermute(light_kv, TOKENS, [(i, i ^ 1) for i in range(n_seq)])  4.74 us
    all_to_all x1, waiting for transfers between devices, local(): group = lax.all_to_all(after_all(chunks, enc[0]), 'fine', 0, 0, tiled=True)  4.13 us
    all_to_all x1, starting transfers between devices, local(): decoded = lax.all_to_all(share, 'fine', 0, 0, tiled=True)  3.67 us
  transfers between devices with their start and end apart: 17, of which 4 were waited for; matrix products, arithmetic and copies ran while one was open for 1% of the time, Pallas kernels for 26%

profile of v14, /device:TPU:0, one launch (start us, length us, event | category | flops | bytes accessed | tf_op | source)
XLA Modules:
  0.0 79.1 jit_solution(9916337104356282920)
XLA Ops:
  0.6 2.9 %collective-permute-start.2 = (bf16[128,128]{1,0:T(8,128)(2,1)}, bf16[128,128]{1,0:T(8,128)(2,1)S(1)}, u32[]{:S(2)}, u32[]{:S(2)}) collective-permute-start(bf16[128,128]{1,0:T(8,128)(2,1)} %bitcast.21), channel_id=1, source_target_pairs={{0,3},{1,2},{2,1},{3,0},{4,7},{5,6},{6,5},{7,4},{8,11},{9,10},{10,... | collective-permute-start | bytes 98312 | tf_op jit(solution)/shard_map/ppermute | solution.py:329
  3.6 0.8 %collective-permute-start.1 = (bf16[128,128]{1,0:T(8,128)(2,1)}, bf16[128,128]{1,0:T(8,128)(2,1)S(1)}, u32[]{:S(2)}, u32[]{:S(2)}) collective-permute-start(bf16[128,128]{1,0:T(8,128)(2,1)} %bitcast.22), channel_id=1, source_target_pairs={{0,2},{1,3},{2,0},{3,1},{4,6},{5,7},{6,4},{7,5},{8,10},{9,11},{10,... | collective-permute-start | bytes 98312 | tf_op jit(solution)/shard_map/ppermute | solution.py:329
  4.4 0.5 collective-permute-start
  4.8 2.3 %pack.1.refs_4_ = bf16[16,192,128]{2,1,0:T(8,128)(2,1)} custom-call(bf16[128,1024]{1,0:T(8,128)(2,1)} %bitcast.27, bf16[128,1024]{1,0:T(8,128)(2,1)} %bitcast.28, bf16[128,1024]{1,0:T(8,128)(2,1)} %bitcast.29), custom_call_target="tpu_custom_call" | custom-call | tf_op jit(solution)/shard_map/pack/pallas_call | solution.py:60
  7.1 2.1 %collective-permute-done.1.refs_2_ = bf16[128,128]{1,0:T(8,128)(2,1)S(1)} collective-permute-done((bf16[128,128]{1,0:T(8,128)(2,1)}, bf16[128,128]{1,0:T(8,128)(2,1)S(1)}, u32[]{:S(2)}, u32[]{:S(2)}) %collective-permute-start.1) | collective-permute-done | bytes 32800 | tf_op jit(solution)/shard_map/ppermute | solution.py:329
  9.2 0.0 copy-start.5
  9.2 3.1 %collective-permute-start.5 = (bf16[512,128]{1,0:T(8,128)(2,1)S(1)}, bf16[512,128]{1,0:T(8,128)(2,1)S(1)}, u32[]{:S(2)}, u32[]{:S(2)}) collective-permute-start(bf16[512,128]{1,0:T(8,128)(2,1)S(1)} %stack.1.e0), channel_id=1, source_target_pairs={{0,12},{1,13},{2,14},{3,15},{4,8},{5,9},{6,10},{7,11},{8,4},{9,5},... | collective-permute-start | bytes 393224 | tf_op jit(solution)/shard_map/ppermute | solution.py:329
  12.3 0.6 collective-permute-start.4
  12.9 0.5 collective-permute-start.3
  13.4 6.0 %all-to-all-start = ((bf16[16,192,128]{2,1,0:T(8,128)(2,1)}), bf16[16,192,128]{2,1,0:T(8,128)(2,1)S(1)}, u32[]{:S(2)}, u32[]{:S(2)}) async-start(bf16[16,192,128]{2,1,0:T(8,128)(2,1)} %pack.1.refs_4_), calls=%async_computation | async-start | bytes 1572864 | tf_op jit(solution)/shard_map/all_to_all | solution.py:354
  19.5 0.0 copy-start
  19.5 0.0 copy-start.1
  19.5 1.8 %decode.1.a = bf16[512,128]{1,0:T(8,128)(2,1)S(1)} custom-call(bf16[512,1024]{1,0:T(8,128)(2,1)S(1)} %bitcast.25, bf16[512,128]{1,0:T(8,128)(2,1)S(1)} %stack.1.e0, bf16[512,128]{1,0:T(8,128)(2,1)S(1)} %collective-permute-done.3.e1, bf16[512,128]{1,0:T(8,128)(2,1)S(1)} %collective-permute-done.4.e2, bf16[512,128]{1,0:T(8,128)(2,1)S(1)} %collective-permute-done.5.e3), custom_call_target="tpu_custom_call" | custom-call | flops 30000001024 | bytes 1000000 | tf_op jit(solution)/shard_map/decode/pallas_call | solution.py:258
  21.3 4.1 %collective-permute-start.8 = (bf16[512,128]{1,0:T(8,128)(2,1)S(1)}, bf16[512,128]{1,0:T(8,128)(2,1)S(1)}, u32[]{:S(2)}, u32[]{:S(2)}) collective-permute-start(bf16[512,128]{1,0:T(8,128)(2,1)S(1)} %decode.1.a), channel_id=1, source_target_pairs={{0,48},{16,32},{32,16},{48,0},{1,49},{17,33},{33,17},{49,1},{2,50}... | collective-permute-start | bytes 393224 | tf_op jit(solution)/shard_map/ppermute | solution.py:329
  25.4 0.9 %collective-permute-start.6 = (bf16[512,128]{1,0:T(8,128)(2,1)S(1)}, bf16[512,128]{1,0:T(8,128)(2,1)S(1)}, u32[]{:S(2)}, u32[]{:S(2)}) collective-permute-start(bf16[512,128]{1,0:T(8,128)(2,1)S(1)} %decode.1.a), channel_id=1, source_target_pairs={{0,16},{16,0},{32,48},{48,32},{1,17},{17,1},{33,49},{49,33},{2,18}... | collective-permute-start | bytes 393224 | tf_op jit(solution)/shard_map/ppermute | solution.py:329
  26.4 0.8 %pad_maximum_fusion = bf16[128,2048]{1,0:T(8,128)(2,1)} fusion(bf16[128,1024]{1,0:T(8,128)(2,1)S(1)} %bitcast.15, bf16[128,1024]{1,0:T(8,128)(2,1)S(1)} %bitcast.13), kind=kLoop, calls=%fused_computation | loop fusion | flops 1048576 | bytes 1048576 | tf_op jit(solution)/shard_map/concatenate | solution.py:344
  27.2 4.1 %all-to-all-done.kv.q = bf16[16,192,128]{2,1,0:T(8,128)(2,1)S(1)} async-done(((bf16[16,192,128]{2,1,0:T(8,128)(2,1)}), bf16[16,192,128]{2,1,0:T(8,128)(2,1)S(1)}, u32[]{:S(2)}, u32[]{:S(2)}) %all-to-all-start) | async-done | bytes 786464 | tf_op jit(solution)/shard_map/all_to_all | solution.py:354
  31.4 0.6 pick.1
  31.9 4.1 %collective-permute-start.13 = (bf16[1024,128]{1,0:T(8,128)(2,1)S(1)}, bf16[1024,128]{1,0:T(8,128)(2,1)S(1)}, u32[]{:S(2)}, u32[]{:S(2)}) collective-permute-start(bf16[1024,128]{1,0:T(8,128)(2,1)S(1)} %bitcast.17), channel_id=1, source_target_pairs={{0,48},{16,32},{32,16},{48,0},{1,49},{17,33},{33,17},{49,1},{2,50}... | collective-permute-start | bytes 786440 | tf_op jit(solution)/shard_map/ppermute | solution.py:329
  36.1 0.9 %collective-permute-start.11 = (bf16[1024,128]{1,0:T(8,128)(2,1)S(1)}, bf16[1024,128]{1,0:T(8,128)(2,1)}, u32[]{:S(2)}, u32[]{:S(2)}) collective-permute-start(bf16[1024,128]{1,0:T(8,128)(2,1)S(1)} %bitcast.19), channel_id=1, source_target_pairs={{0,16},{16,0},{32,48},{48,32},{1,17},{17,1},{33,49},{49,33},{2,18}... | collective-permute-start | bytes 786440 | tf_op jit(solution)/shard_map/ppermute | solution.py:329
  37.0 1.9 %meet.1 = bf16[16,32,1024]{2,1,0:T(8,128)(2,1)} custom-call(bf16[512,128]{1,0:T(8,128)(2,1)S(1)} %decode.1.a, bf16[512,128]{1,0:T(8,128)(2,1)S(1)} %collective-permute-done.6.b, bf16[512,128]{1,0:T(8,128)(2,1)S(1)} %collective-permute-done.7.c, bf16[512,128]{1,0:T(8,128)(2,1)S(1)} %collective-permute-done.8.d), custom_call_target="tpu_custom_call" | custom-call | flops 30000001024 | bytes 2000000 | tf_op jit(solution)/shard_map/meet/pallas_call | solution.py:292
  39.0 3.7 %all-to-all-start.1 = ((bf16[16,32,1024]{2,1,0:T(8,128)(2,1)}), bf16[16,32,1024]{2,1,0:T(8,128)(2,1)S(1)}, u32[]{:S(2)}, u32[]{:S(2)}) async-start(bf16[16,32,1024]{2,1,0:T(8,128)(2,1)} %meet.1), calls=%async_computation.1 | async-start | bytes 2097152 | tf_op jit(solution)/shard_map/all_to_all | solution.py:363
  42.6 0.7 collective-permute-start.10
  43.3 4.7 %collective-permute-start.9 = (bf16[128,2048]{1,0:T(8,128)(2,1)}, bf16[128,2048]{1,0:T(8,128)(2,1)}, u32[]{:S(2)}, u32[]{:S(2)}) collective-permute-start(bf16[128,2048]{1,0:T(8,128)(2,1)} %pad_maximum_fusion), channel_id=1, source_target_pairs={{0,1},{1,0},{2,3},{3,2},{4,5},{5,4},{6,7},{7,6},{8,9},{9,8},{10,11... | collective-permute-start | bytes 1572872 | tf_op jit(solution)/shard_map/ppermute | solution.py:366
  48.1 11.0 %heavy.1 = bf16[16,64,128]{2,1,0:T(8,128)(2,1)} custom-call(bf16[16,192,128]{2,1,0:T(8,128)(2,1)S(1)} %all-to-all-done.kv.q, bf16[1024,128]{1,0:T(8,128)(2,1)S(1)} %bitcast.20, bf16[1024,128]{1,0:T(8,128)(2,1)} %collective-permute-done.11.kv1, bf16[1024,128]{1,0:T(8,128)(2,1)} %collective-permute-done.12.kv2, bf16[1024,128]{1,0:T(8,128)(2,1)S(1)} %collective-permute-done.13.kv3), custom_call_target="tpu_custom_call" | custom-call | flops 10000000000 | bytes 2000000 | tf_op jit(solution)/shard_map/heavy/pallas_call | solution.py:130
  59.1 0.0 copy-start.6
  59.1 2.2 %all-to-all-done.1 = bf16[16,32,1024]{2,1,0:T(8,128)(2,1)S(1)} async-done(((bf16[16,32,1024]{2,1,0:T(8,128)(2,1)}), bf16[16,32,1024]{2,1,0:T(8,128)(2,1)S(1)}, u32[]{:S(2)}, u32[]{:S(2)}) %all-to-all-start.1) | async-done | bytes 1048608 | tf_op jit(solution)/shard_map/all_to_all | solution.py:363
  61.2 7.6 %all-to-all-start.2 = ((bf16[16,64,128]{2,1,0:T(8,128)(2,1)}), bf16[16,64,128]{2,1,0:T(8,128)(2,1)S(1)}, u32[]{:S(2)}, u32[]{:S(2)}) async-start(bf16[16,64,128]{2,1,0:T(8,128)(2,1)} %heavy.1), calls=%async_computation.2 | async-start | bytes 524288 | tf_op jit(solution)/shard_map/all_to_all | solution.py:371
  68.8 3.0 %light.1 = (f32[128,1024]{1,0:T(8,128)S(1)}, bf16[512,1024]{1,0:T(8,128)(2,1)}) custom-call(bf16[128,1024]{1,0:T(8,128)(2,1)S(1)} %bitcast.26, bf16[128,1024]{1,0:T(8,128)(2,1)S(1)} %bitcast.14, bf16[128,1024]{1,0:T(8,128)(2,1)S(1)} %bitcast.16, bf16[128,2048]{1,0:T(8,128)(2,1)} %collective-permute-done.9.even, ...), custom_call_target="tpu_custom_call" | custom-call | flops 3000000000 | bytes 2000000 | tf_op jit(solution)/shard_map/light/pallas_call | solution.py:180
  71.8 0.0 copy-start.4
  71.8 5.6 %all-to-all-done.2.heavy = bf16[16,64,128]{2,1,0:T(8,128)(2,1)S(1)} async-done(((bf16[16,64,128]{2,1,0:T(8,128)(2,1)}), bf16[16,64,128]{2,1,0:T(8,128)(2,1)S(1)}, u32[]{:S(2)}, u32[]{:S(2)}) %all-to-all-start.2) | async-done | bytes 262176 | tf_op jit(solution)/shard_map/all_to_all | solution.py:371
  77.5 1.4 %join.1 = bf16[128,1024]{1,0:T(8,128)(2,1)} custom-call(s32[1,64]{1,0:T(1,128)S(1)} %copy-done.4, f32[128,1024]{1,0:T(8,128)S(1)} %get-tuple-element.15.light, bf16[16,64,128]{2,1,0:T(8,128)(2,1)S(1)} %all-to-all-done.2.heavy), custom_call_target="tpu_custom_call" | custom-call | tf_op jit(solution)/shard_map/join/pallas_call | solution.py:218
  (25 shorter events, 0.1 us)
Async XLA Ops:
  0.6 6.5 %collective-permute-start.2 = (bf16[128,128]{1,0:T(8,128)(2,1)}, bf16[128,128]{1,0:T(8,128)(2,1)S(1)}, u32[]{:S(2)}, u32[]{:S(2)}) collective-permute-start(bf16[128,128]{1,0:T(8,128)(2,1)} %bitcast.21), channel_id=1, source_target_pairs={{0,3},{1,2},{2,1},{3,0},{4,7},{5,6},{6,5},{7,4},{8,11},{9,10},{10,... | collective-permute-start | bytes 98312 | tf_op jit(solution)/shard_map/ppermute | solution.py:329
  3.6 5.6 %collective-permute-start.1 = (bf16[128,128]{1,0:T(8,128)(2,1)}, bf16[128,128]{1,0:T(8,128)(2,1)S(1)}, u32[]{:S(2)}, u32[]{:S(2)}) collective-permute-start(bf16[128,128]{1,0:T(8,128)(2,1)} %bitcast.22), channel_id=1, source_target_pairs={{0,2},{1,3},{2,0},{3,1},{4,6},{5,7},{6,4},{7,5},{8,10},{9,11},{10,... | collective-permute-start | bytes 98312 | tf_op jit(solution)/shard_map/ppermute | solution.py:329
  4.4 4.8 %collective-permute-start = (bf16[128,128]{1,0:T(8,128)(2,1)}, bf16[128,128]{1,0:T(8,128)(2,1)S(1)}, u32[]{:S(2)}, u32[]{:S(2)}) collective-permute-start(bf16[128,128]{1,0:T(8,128)(2,1)} %bitcast.23), channel_id=1, source_target_pairs={{0,1},{1,0},{2,3},{3,2},{4,5},{5,4},{6,7},{7,6},{8,9},{9,8},{10,11... | collective-permute-start | bytes 98312 | tf_op jit(solution)/shard_map/ppermute | solution.py:329
  4.8 4.4 %copy-start.2 = (bf16[1,128,128]{2,1,0:T(8,128)(2,1)S(1)}, bf16[1,128,128]{2,1,0:T(8,128)(2,1)}, u32[]{:S(2)}) copy-start(bf16[1,128,128]{2,1,0:T(8,128)(2,1)} %param.16) | copy-start | bytes 98308
  9.2 10.3 %copy-start.5 = (bf16[1,512,1024]{2,1,0:T(8,128)(2,1)S(1)}, bf16[1,512,1024]{2,1,0:T(8,128)(2,1)}, u32[]{:S(2)}) copy-start(bf16[1,512,1024]{2,1,0:T(8,128)(2,1)} %param.17) | copy-start | bytes 3145732
  9.2 10.2 %collective-permute-start.5 = (bf16[512,128]{1,0:T(8,128)(2,1)S(1)}, bf16[512,128]{1,0:T(8,128)(2,1)S(1)}, u32[]{:S(2)}, u32[]{:S(2)}) collective-permute-start(bf16[512,128]{1,0:T(8,128)(2,1)S(1)} %stack.1.e0), channel_id=1, source_target_pairs={{0,12},{1,13},{2,14},{3,15},{4,8},{5,9},{6,10},{7,11},{8,4},{9,5},... | collective-permute-start | bytes 393224 | tf_op jit(solution)/shard_map/ppermute | solution.py:329
  12.3 7.1 %collective-permute-start.4 = (bf16[512,128]{1,0:T(8,128)(2,1)S(1)}, bf16[512,128]{1,0:T(8,128)(2,1)S(1)}, u32[]{:S(2)}, u32[]{:S(2)}) collective-permute-start(bf16[512,128]{1,0:T(8,128)(2,1)S(1)} %stack.1.e0), channel_id=1, source_target_pairs={{0,8},{1,9},{2,10},{3,11},{4,12},{5,13},{6,14},{7,15},{8,0},{9,1},... | collective-permute-start | bytes 393224 | tf_op jit(solution)/shard_map/ppermute | solution.py:329
  12.9 6.5 %collective-permute-start.3 = (bf16[512,128]{1,0:T(8,128)(2,1)S(1)}, bf16[512,128]{1,0:T(8,128)(2,1)S(1)}, u32[]{:S(2)}, u32[]{:S(2)}) collective-permute-start(bf16[512,128]{1,0:T(8,128)(2,1)S(1)} %stack.1.e0), channel_id=1, source_target_pairs={{0,4},{1,5},{2,6},{3,7},{4,0},{5,1},{6,2},{7,3},{8,12},{9,13},{10,... | collective-permute-start | bytes 393224 | tf_op jit(solution)/shard_map/ppermute | solution.py:329
  13.4 18.0 %all-to-all-start = ((bf16[16,192,128]{2,1,0:T(8,128)(2,1)}), bf16[16,192,128]{2,1,0:T(8,128)(2,1)S(1)}, u32[]{:S(2)}, u32[]{:S(2)}) async-start(bf16[16,192,128]{2,1,0:T(8,128)(2,1)} %pack.1.refs_4_), calls=%async_computation | async-start | bytes 1572864 | tf_op jit(solution)/shard_map/all_to_all | solution.py:354
  19.5 6.9 %copy-start = (bf16[1,128,1024]{2,1,0:T(8,128)(2,1)S(1)}, bf16[1,128,1024]{2,1,0:T(8,128)(2,1)}, u32[]{:S(2)}) copy-start(bf16[1,128,1024]{2,1,0:T(8,128)(2,1)} %param.11) | copy-start | bytes 786436
  19.5 6.9 %copy-start.1 = (bf16[1,128,1024]{2,1,0:T(8,128)(2,1)S(1)}, bf16[1,128,1024]{2,1,0:T(8,128)(2,1)}, u32[]{:S(2)}) copy-start(bf16[1,128,1024]{2,1,0:T(8,128)(2,1)} %param.12) | copy-start | bytes 786436
  21.3 14.8 %collective-permute-start.8 = (bf16[512,128]{1,0:T(8,128)(2,1)S(1)}, bf16[512,128]{1,0:T(8,128)(2,1)S(1)}, u32[]{:S(2)}, u32[]{:S(2)}) collective-permute-start(bf16[512,128]{1,0:T(8,128)(2,1)S(1)} %decode.1.a), channel_id=1, source_target_pairs={{0,48},{16,32},{32,16},{48,0},{1,49},{17,33},{33,17},{49,1},{2,50}... | collective-permute-start | bytes 393224 | tf_op jit(solution)/shard_map/ppermute | solution.py:329
  25.4 11.6 %collective-permute-start.7 = (bf16[512,128]{1,0:T(8,128)(2,1)S(1)}, bf16[512,128]{1,0:T(8,128)(2,1)S(1)}, u32[]{:S(2)}, u32[]{:S(2)}) collective-permute-start(bf16[512,128]{1,0:T(8,128)(2,1)S(1)} %decode.1.a), channel_id=1, source_target_pairs={{0,32},{16,48},{32,0},{48,16},{1,33},{17,49},{33,1},{49,17},{2,34}... | collective-permute-start | bytes 393224 | tf_op jit(solution)/shard_map/ppermute | solution.py:329
  25.4 11.6 %collective-permute-start.6 = (bf16[512,128]{1,0:T(8,128)(2,1)S(1)}, bf16[512,128]{1,0:T(8,128)(2,1)S(1)}, u32[]{:S(2)}, u32[]{:S(2)}) collective-permute-start(bf16[512,128]{1,0:T(8,128)(2,1)S(1)} %decode.1.a), channel_id=1, source_target_pairs={{0,16},{16,0},{32,48},{48,32},{1,17},{17,1},{33,49},{49,33},{2,18}... | collective-permute-start | bytes 393224 | tf_op jit(solution)/shard_map/ppermute | solution.py:329
  26.4 5.0 %copy-start.3 = (s32[1,32]{1,0:T(1,128)S(1)}, s32[1,32]{1,0:T(1,128)}, u32[]{:S(2)}) copy-start(s32[1,32]{1,0:T(1,128)} %ids.2) | copy-start | bytes 388
  31.9 16.1 %collective-permute-start.13 = (bf16[1024,128]{1,0:T(8,128)(2,1)S(1)}, bf16[1024,128]{1,0:T(8,128)(2,1)S(1)}, u32[]{:S(2)}, u32[]{:S(2)}) collective-permute-start(bf16[1024,128]{1,0:T(8,128)(2,1)S(1)} %bitcast.17), channel_id=1, source_target_pairs={{0,48},{16,32},{32,16},{48,0},{1,49},{17,33},{33,17},{49,1},{2,50}... | collective-permute-start | bytes 786440 | tf_op jit(solution)/shard_map/ppermute | solution.py:329
  36.1 12.0 %collective-permute-start.12 = (bf16[1024,128]{1,0:T(8,128)(2,1)S(1)}, bf16[1024,128]{1,0:T(8,128)(2,1)}, u32[]{:S(2)}, u32[]{:S(2)}) collective-permute-start(bf16[1024,128]{1,0:T(8,128)(2,1)S(1)} %bitcast.18), channel_id=1, source_target_pairs={{0,32},{16,48},{32,0},{48,16},{1,33},{17,49},{33,1},{49,17},{2,34}... | collective-permute-start | bytes 786440 | tf_op jit(solution)/shard_map/ppermute | solution.py:329
  36.1 12.0 %collective-permute-start.11 = (bf16[1024,128]{1,0:T(8,128)(2,1)S(1)}, bf16[1024,128]{1,0:T(8,128)(2,1)}, u32[]{:S(2)}, u32[]{:S(2)}) collective-permute-start(bf16[1024,128]{1,0:T(8,128)(2,1)S(1)} %bitcast.19), channel_id=1, source_target_pairs={{0,16},{16,0},{32,48},{48,32},{1,17},{17,1},{33,49},{49,33},{2,18}... | collective-permute-start | bytes 786440 | tf_op jit(solution)/shard_map/ppermute | solution.py:329
  39.0 22.3 %all-to-all-start.1 = ((bf16[16,32,1024]{2,1,0:T(8,128)(2,1)}), bf16[16,32,1024]{2,1,0:T(8,128)(2,1)S(1)}, u32[]{:S(2)}, u32[]{:S(2)}) async-start(bf16[16,32,1024]{2,1,0:T(8,128)(2,1)} %meet.1), calls=%async_computation.1 | async-start | bytes 2097152 | tf_op jit(solution)/shard_map/all_to_all | solution.py:363
  42.6 26.2 %collective-permute-start.10 = (bf16[128,2048]{1,0:T(8,128)(2,1)}, bf16[128,2048]{1,0:T(8,128)(2,1)S(1)}, u32[]{:S(2)}, u32[]{:S(2)}) collective-permute-start(bf16[128,2048]{1,0:T(8,128)(2,1)} %pad_maximum_fusion), channel_id=1, source_target_pairs={{1,2},{2,1},{3,4},{4,3},{5,6},{6,5},{7,8},{8,7},{9,10},{10,9},{11,... | collective-permute-start | bytes 1572872 | tf_op jit(solution)/shard_map/ppermute | solution.py:367
  43.3 25.5 %collective-permute-start.9 = (bf16[128,2048]{1,0:T(8,128)(2,1)}, bf16[128,2048]{1,0:T(8,128)(2,1)}, u32[]{:S(2)}, u32[]{:S(2)}) collective-permute-start(bf16[128,2048]{1,0:T(8,128)(2,1)} %pad_maximum_fusion), channel_id=1, source_target_pairs={{0,1},{1,0},{2,3},{3,2},{4,5},{5,4},{6,7},{7,6},{8,9},{9,8},{10,11... | collective-permute-start | bytes 1572872 | tf_op jit(solution)/shard_map/ppermute | solution.py:366
  59.1 9.8 %copy-start.6 = (bf16[1,128,1024]{2,1,0:T(8,128)(2,1)S(1)}, bf16[1,128,1024]{2,1,0:T(8,128)(2,1)}, u32[]{:S(2)}) copy-start(bf16[1,128,1024]{2,1,0:T(8,128)(2,1)} %param.10) | copy-start | bytes 786436
  61.2 16.2 %all-to-all-start.2 = ((bf16[16,64,128]{2,1,0:T(8,128)(2,1)}), bf16[16,64,128]{2,1,0:T(8,128)(2,1)S(1)}, u32[]{:S(2)}, u32[]{:S(2)}) async-start(bf16[16,64,128]{2,1,0:T(8,128)(2,1)} %heavy.1), calls=%async_computation.2 | async-start | bytes 524288 | tf_op jit(solution)/shard_map/all_to_all | solution.py:371
  71.8 5.7 %copy-start.4 = (s32[1,64]{1,0:T(1,128)S(1)}, s32[1,64]{1,0:T(1,128)}, u32[]{:S(2)}) copy-start(s32[1,64]{1,0:T(1,128)} %ids.3) | copy-start | bytes 772
